TPU v7x, 32 devices: a whole 2x2x4 slice. The times are simulated.
32 devices in a mesh: dp: 8 (over y, x, core), tensor: 4 (over z).
Axes of the slice: x: 2, y: 2, z: 4, core: 2. Of those that a mesh axis runs over, the one named last changes fastest.
Arguments:
- layer_input: bfloat16 [16384, 768], P(('dp', 'tensor')), may hold values from -6 to 6
- w_qkv: bfloat16 [2, 768, 2304], P(None, 'dp', 'tensor'), may hold values from -0.3125 to 0.3125
- w_out: bfloat16 [2, 768, 768], P(None, 'tensor', 'dp'), may hold values from -0.875 to 0.875
- w_up: bfloat16 [2, 768, 3072], P(None, 'dp', 'tensor'), may hold values from -0.21875 to 0.21875
- w_down: bfloat16 [2, 3072, 768], P(None, 'tensor', 'dp'), may hold values from -0.15625 to 0.15625
- attn_gain: float32 [2, 768], replicated, may hold values from 0.25 to 1.75
- attn_shift: float32 [2, 768], replicated, may hold values from -1.5 to 1.5
- ffn_gain: float32 [2, 768], replicated, may hold values from 0.25 to 1.75
- ffn_shift: float32 [2, 768], replicated, may hold values from -1.5 to 1.5
- out_grad: bfloat16 [16384, 768], P(('dp', 'tensor')), may hold values from -6 to 6
- doc_lengths: int32 [8, 4], P('dp'), may hold values from 1 to 16, 32 in all within a row
- block_deal: int32 [8, 32], P('dp'), may hold values from 0 to 31, each once within a row
- random_blocks: int32 [8, 12, 32, 3], P('dp', 'tensor'), may hold values from 0 to 4095
Outputs:
- layer_output: bfloat16 [16384, 768], P(('dp', 'tensor'))
- input_grad: float32 [16384, 768], P(('dp', 'tensor'))
- w_qkv_grad: float32 [2, 768, 2304], P(None, 'dp', 'tensor')
- w_out_grad: float32 [2, 768, 768], P(None, 'tensor', 'dp')
- w_up_grad: float32 [2, 768, 3072], P(None, 'dp', 'tensor')
- w_down_grad: float32 [2, 3072, 768], P(None, 'tensor', 'dp')
- attn_gain_grad: float32 [2, 768], replicated
- attn_shift_grad: float32 [2, 768], replicated
- ffn_gain_grad: float32 [2, 768], replicated
- ffn_shift_grad: float32 [2, 768], replicated
Inputs may be any that keep to these rules, and one draw needn't show every extreme that they name: `doc_lengths`: each row sums to 32, and its largest entry is 16. `block_deal`: each row is a permutation of 0 to 31.
All inputs are finite; a program needn't handle non-finite values.
Results may differ from a plain program's by a relative error of at most 0.035.
The roundings to bfloat16 on the way count: a program that leaves them out, or rounds other values in their place, can miss the bound.
Values may be sent and summed in bfloat16 or wider, within the bound.
A program may use at most 192 MiB of HBM per device.

v0:
```python
import jax
import jax.numpy as jnp
from jax import lax
from jax.sharding import PartitionSpec as P

HD = 64
BLK = 64
LAYERS = 2
QROWS = 512


NORM_EPSILON = 1e-12
MASK_VALUE = -1e30


def layer_norm(summed, norm_gain, norm_shift):
    row_mean = jnp.mean(summed, axis=-1, keepdims=True)
    centred = summed - row_mean
    row_var = jnp.mean(centred * centred, axis=-1, keepdims=True)
    return centred * lax.rsqrt(row_var + NORM_EPSILON) * norm_gain + norm_shift


def gelu_tanh(values):
    return jax.nn.gelu(values, approximate=True)


def dot_right_t(left, right):
    return lax.dot_general(
        left, right, (((1,), (1,)), ((), ())), preferred_element_type=jnp.float32
    )


def dot_left_t(left, right):
    return lax.dot_general(
        left, right, (((0,), (0,)), ((), ())), preferred_element_type=jnp.float32
    )


def block_mask(doc_lengths, block_deal, random_rows):
    doc_ends = jnp.cumsum(doc_lengths)
    doc_starts = doc_ends - doc_lengths
    doc_index = jnp.sum((block_deal[:, None] >= doc_ends[None, :]).astype(jnp.int32), axis=1)
    doc_pick = (
        doc_index[:, None] == jnp.arange(doc_lengths.shape[0], dtype=jnp.int32)[None, :]
    ).astype(jnp.int32)
    first_block = jnp.sum(doc_pick * doc_starts[None, :], axis=1)
    doc_blocks = jnp.sum(doc_pick * doc_lengths[None, :], axis=1)
    local_block = block_deal - first_block
    slot_pick = (
        block_deal[:, None] == jnp.arange(block_deal.shape[0], dtype=jnp.int32)[None, :]
    ).astype(jnp.int32)
    random_picks = jnp.sum(slot_pick[None, :, :, None] * random_rows[:, None, :, :], axis=2)
    random_local = jnp.remainder(random_picks, doc_blocks[None, :, None])
    random_hit = jnp.any(random_local[:, :, :, None] == local_block[None, None, None, :], axis=2)
    same_doc = doc_index[:, None] == doc_index[None, :]
    near_pair = jnp.abs(local_block[:, None] - local_block[None, :]) <= 1
    global_pair = (local_block[:, None] < 2) | (local_block[None, :] < 2)
    return same_doc[None] & ((near_pair | global_pair)[None] | random_hit)


def masked_scores(query_block, key_rows, mask_block, score_scale):
    raw_scores = (
        jnp.einsum("qhe,khe->hqk", query_block, key_rows, preferred_element_type=jnp.float32)
        * score_scale
    )
    head_count, row_count, key_count = raw_scores.shape
    shaped = raw_scores.reshape(head_count, row_count // BLK, BLK, key_count // BLK, BLK)
    shaped = jnp.where(mask_block[:, :, None, :, None], shaped, MASK_VALUE)
    return shaped.reshape(head_count, row_count, key_count)


def split_blocks(projected, allowed):
    group_rows, head_local = (projected.shape[0], projected.shape[1])
    block_count = group_rows // QROWS
    query_blocks = projected[:, :, 0].reshape(block_count, QROWS, head_local, HD)
    mask_blocks = allowed.reshape(
        head_local, block_count, QROWS // BLK, group_rows // BLK
    ).transpose(1, 0, 2, 3)
    return (query_blocks, mask_blocks, projected[:, :, 1], projected[:, :, 2])


def attend_forward(projected, allowed, score_scale):
    group_rows, head_local = (projected.shape[0], projected.shape[1])
    query_blocks, mask_blocks, key_rows, value_rows = split_blocks(projected, allowed)

    def one_block(pieces):
        query_block, mask_block = pieces
        scores = masked_scores(query_block, key_rows, mask_block, score_scale)
        row_peak = jnp.max(scores, axis=2, keepdims=True)
        exponent = jnp.exp(scores - row_peak)
        row_total = jnp.sum(exponent, axis=2, keepdims=True)
        prob_rows = (exponent / row_total).astype(jnp.bfloat16)
        mixed_block = jnp.einsum(
            "hqk,khe->qhe", prob_rows, value_rows, preferred_element_type=jnp.float32
        )
        return (mixed_block.astype(jnp.bfloat16), (row_peak + jnp.log(row_total))[:, :, 0])

    mixed_blocks, log_total = lax.map(one_block, (query_blocks, mask_blocks))
    return (mixed_blocks.reshape(group_rows, head_local * HD), log_total)


def attend_backward(projected, allowed, score_scale, log_total, d_mixed):
    group_rows, head_local = (projected.shape[0], projected.shape[1])
    query_blocks, mask_blocks, key_rows, value_rows = split_blocks(projected, allowed)
    d_blocks = d_mixed.reshape(query_blocks.shape)

    def one_block(carry, pieces):
        key_grad, value_grad = carry
        query_block, mask_block, log_block, d_block = pieces
        scores = masked_scores(query_block, key_rows, mask_block, score_scale)
        prob_full = jnp.exp(scores - log_block[:, :, None])
        value_grad = value_grad + jnp.einsum(
            "hqk,qhe->khe",
            prob_full.astype(jnp.bfloat16),
            d_block,
            preferred_element_type=jnp.float32,
        )
        d_prob = jnp.einsum("qhe,khe->hqk", d_block, value_rows, preferred_element_type=jnp.float32)
        row_inner = jnp.sum(prob_full * d_prob, axis=2, keepdims=True)
        d_scores = (prob_full * (d_prob - row_inner)).astype(jnp.bfloat16) * score_scale
        query_grad = jnp.einsum(
            "hqk,khe->qhe", d_scores, key_rows, preferred_element_type=jnp.float32
        )
        key_grad = key_grad + jnp.einsum(
            "hqk,qhe->khe", d_scores, query_block, preferred_element_type=jnp.float32
        )
        return ((key_grad, value_grad), query_grad)

    zeros_rows = jnp.zeros((group_rows, head_local, HD), jnp.float32)
    (key_grad, value_grad), query_grads = lax.scan(
        one_block, (zeros_rows, zeros_rows), (query_blocks, mask_blocks, log_total, d_blocks)
    )
    query_grad = query_grads.reshape(group_rows, head_local, HD)
    stacked = jnp.stack([query_grad, key_grad, value_grad], axis=2).astype(jnp.bfloat16)
    return stacked.reshape(group_rows, head_local * 3 * HD)


def gather_rows(shard):
    return lax.all_gather(shard, "tensor", axis=0, tiled=True)


def gather_grads(shard):
    return lax.all_gather(shard, "tensor", axis=0, tiled=True)


def sum_rows(left, right):
    return lax.psum_scatter(
        jnp.dot(left, right, preferred_element_type=jnp.float32),
        "tensor",
        scatter_dimension=0,
        tiled=True,
    )


def input_terms(left, right):
    return lax.psum_scatter(dot_right_t(left, right), "tensor", scatter_dimension=0, tiled=True)


def local(
    layer_input,
    w_qkv,
    w_out,
    w_up,
    w_down,
    attn_gain,
    attn_shift,
    ffn_gain,
    ffn_shift,
    out_grad,
    doc_lengths,
    block_deal,
    random_blocks,
):
    head_local = random_blocks.shape[1]
    allowed = block_mask(doc_lengths[0], block_deal[0], random_blocks[0])
    score_scale = HD ** (-0.5)
    stream = layer_input.astype(jnp.float32)
    stored_layers = []
    for layer_index in range(LAYERS):
        gathered = (
            lax.all_gather(w_qkv[layer_index], "dp", axis=0, tiled=True),
            lax.all_gather(w_out[layer_index], "dp", axis=1, tiled=True),
            lax.all_gather(w_up[layer_index], "dp", axis=0, tiled=True),
            lax.all_gather(w_down[layer_index], "dp", axis=1, tiled=True),
        )
        w_proj, w_back, w_expand, w_shrink = gathered
        inputs = gather_rows(stream.astype(jnp.bfloat16))
        group_rows = inputs.shape[0]
        projected = jnp.dot(inputs, w_proj, preferred_element_type=jnp.float32).astype(jnp.bfloat16)
        projected = projected.reshape(group_rows, head_local, 3, HD)
        mixed_rows, log_total = attend_forward(projected, allowed, score_scale)
        attended = sum_rows(mixed_rows, w_back)
        summed_one = stream + attended
        normed = layer_norm(summed_one, attn_gain[layer_index], attn_shift[layer_index])
        ffn_in = gather_rows(normed.astype(jnp.bfloat16))
        pre_act = jnp.dot(ffn_in, w_expand, preferred_element_type=jnp.float32)
        activated = gelu_tanh(pre_act).astype(jnp.bfloat16)
        expanded = sum_rows(activated, w_shrink)
        summed_two = normed + expanded
        stored_layers.append(
            (
                inputs,
                projected,
                mixed_rows,
                log_total,
                summed_one,
                ffn_in,
                pre_act,
                summed_two,
                gathered,
            )
        )
        stream = layer_norm(summed_two, ffn_gain[layer_index], ffn_shift[layer_index])
    state_grad = out_grad.astype(jnp.float32)
    layer_grads = [None] * LAYERS
    norm_parts = [None] * LAYERS
    for layer_index in reversed(range(LAYERS)):
        (
            inputs,
            projected,
            mixed_rows,
            log_total,
            summed_one,
            ffn_in,
            pre_act,
            summed_two,
            gathered,
        ) = stored_layers[layer_index]
        w_proj, w_back, w_expand, w_shrink = (
            lax.all_gather(w_qkv[layer_index], "dp", axis=0, tiled=True),
            lax.all_gather(w_out[layer_index], "dp", axis=1, tiled=True),
            lax.all_gather(w_up[layer_index], "dp", axis=0, tiled=True),
            lax.all_gather(w_down[layer_index], "dp", axis=1, tiled=True),
        )
        unused_two, ffn_back = jax.vjp(
            layer_norm, summed_two, ffn_gain[layer_index], ffn_shift[layer_index]
        )
        d_two, ffn_gain_part, ffn_shift_part = ffn_back(state_grad)
        grad_rows = gather_grads(d_two.astype(jnp.bfloat16))
        activated = gelu_tanh(pre_act).astype(jnp.bfloat16)
        shrink_grad = dot_left_t(activated, grad_rows)
        unused_act, gelu_back = jax.vjp(gelu_tanh, pre_act)
        d_pre = gelu_back(dot_right_t(grad_rows, w_shrink))[0].astype(jnp.bfloat16)
        expand_grad = dot_left_t(ffn_in, d_pre)
        d_normed = d_two + input_terms(d_pre, w_expand)
        unused_one, attn_back = jax.vjp(
            layer_norm, summed_one, attn_gain[layer_index], attn_shift[layer_index]
        )
        d_one, attn_gain_part, attn_shift_part = attn_back(d_normed)
        grad_rows = gather_grads(d_one.astype(jnp.bfloat16))
        back_grad = dot_left_t(mixed_rows, grad_rows)
        d_mixed = dot_right_t(grad_rows, w_back).astype(jnp.bfloat16)
        d_projected = attend_backward(projected, allowed, score_scale, log_total, d_mixed)
        proj_grad = dot_left_t(inputs, d_projected)
        state_grad = d_one + input_terms(d_projected, w_proj)
        norm_parts[layer_index] = (attn_gain_part, attn_shift_part, ffn_gain_part, ffn_shift_part)
        layer_grads[layer_index] = (
            lax.psum_scatter(proj_grad, "dp", scatter_dimension=0, tiled=True),
            lax.psum_scatter(back_grad, "dp", scatter_dimension=1, tiled=True),
            lax.psum_scatter(expand_grad, "dp", scatter_dimension=0, tiled=True),
            lax.psum_scatter(shrink_grad, "dp", scatter_dimension=1, tiled=True),
        )
    proj_all = jnp.stack([entry[0] for entry in layer_grads])
    back_all = jnp.stack([entry[1] for entry in layer_grads])
    expand_all = jnp.stack([entry[2] for entry in layer_grads])
    shrink_all = jnp.stack([entry[3] for entry in layer_grads])
    norm_sums = lax.psum(
        (
            jnp.stack([entry[0] for entry in norm_parts]),
            jnp.stack([entry[1] for entry in norm_parts]),
            jnp.stack([entry[2] for entry in norm_parts]),
            jnp.stack([entry[3] for entry in norm_parts]),
        ),
        ("dp", "tensor"),
    )
    return (
        stream.astype(jnp.bfloat16),
        state_grad,
        proj_all,
        back_all,
        expand_all,
        shrink_all,
        norm_sums[0],
        norm_sums[1],
        norm_sums[2],
        norm_sums[3],
    )


def solution(mesh):
    placed = (
        P(("dp", "tensor"), None),
        P(None, "dp", "tensor"),
        P(None, "tensor", "dp"),
        P(None, "dp", "tensor"),
        P(None, "tensor", "dp"),
        P(),
        P(),
        P(),
        P(),
        P(("dp", "tensor"), None),
        P("dp", None),
        P("dp", None),
        P("dp", "tensor", None, None),
    )
    return jax.shard_map(
        local,
        mesh=mesh,
        in_specs=placed,
        out_specs=(
            P(("dp", "tensor"), None),
            P(("dp", "tensor"), None),
            P(None, "dp", "tensor"),
            P(None, "tensor", "dp"),
            P(None, "dp", "tensor"),
            P(None, "tensor", "dp"),
            P(),
            P(),
            P(),
            P(),
        ),
        check_vma=False,
    )
```

profile of v0, /device:TPU:0, one launch (start us, length us, event | category | flops | bytes accessed | tf_op | source)
XLA Modules:
  0.0 2581.4 jit_solution(1906324310665286945)
XLA Ops:
  18.8 11.9 all-gather.1
  33.0 11.0 all-gather
  44.0 32.6 %all-gather.21.cloned.1.call-done = bf16[2048,768]{1,0:T(8,128)(2,1)} async-done(((bf16[512,768]{1,0:T(8,128)(2,1)}), bf16[2048,768]{1,0:T(8,128)(2,1)}) %all-gather.21.cloned.1.call-update) | async-done | bytes 3145744 | tf_op jit(solution)/shard_map/all_gather | solution.py:139
  84.4 134.9 %while.54 = (s32[]{:T(128)}, bf16[4,512,3,64]{1,3,2,0:T(8,128)(2,1)}, f32[4,3,512]{2,1,0:T(4,128)S(1)}, pred[4,3,8,32]{3,2,1,0:T(8,128)(4,1)S(1)}, bf16[4,512,3,...) while((s32[]{:T(128)}, ...), condition=%wide.region_9.10_spmd, body=%wide.region_6.9_spmd.sunk | while | flops 843151872 | bytes 61792648 | solution.py:98
  89.0 16.6 broadcast_in_dim.225
  122.7 16.6 broadcast_in_dim.225
  156.3 16.6 broadcast_in_dim.225
  190.0 16.6 broadcast_in_dim.225
  228.3 107.2 %reduce-scatter.25.cloned.1.call-done = f32[512,768]{1,0:T(8,128)} async-done(((f32[2048,768]{1,0:T(8,128)}), f32[512,768]{1,0:T(8,128)}) %reduce-scatter.25.cloned.1.call-update) | async-done | bytes 1572880 | tf_op jit(solution)/shard_map/reduce_scatter | solution.py:147
  339.9 62.8 %all-gather.23.cloned.1.call-done = bf16[2048,768]{1,0:T(8,128)(2,1)} async-done(((bf16[512,768]{1,0:T(8,128)(2,1)}), bf16[2048,768]{1,0:T(8,128)(2,1)}) %all-gather.23.cloned.1.call-update) | async-done | bytes 3145744 | tf_op jit(solution)/shard_map/all_gather | solution.py:139
  410.2 17.3 all-gather.39.cloned.1.call-done
  427.5 9.6 fusion.186
  439.0 108.9 %reduce-scatter.27.cloned.1.call-done = f32[512,768]{1,0:T(8,128)} async-done(((f32[2048,768]{1,0:T(8,128)}), f32[512,768]{1,0:T(8,128)}) %reduce-scatter.27.cloned.1.call-update) | async-done | bytes 1572880 | tf_op jit(solution)/shard_map/reduce_scatter | solution.py:147
  552.4 10.4 all-gather.5
  564.4 11.0 all-gather.4
  575.4 40.9 %all-gather.25.cloned.1.call-done = bf16[2048,768]{1,0:T(8,128)(2,1)} async-done(((bf16[512,768]{1,0:T(8,128)(2,1)}), bf16[2048,768]{1,0:T(8,128)(2,1)}) %all-gather.25.cloned.1.call-update) | async-done | bytes 3145744 | tf_op jit(solution)/shard_map/all_gather | solution.py:139
  624.2 135.1 %while.55 = (s32[]{:T(128)}, bf16[4,512,3,64]{1,3,2,0:T(8,128)(2,1)}, f32[4,3,512]{2,1,0:T(4,128)S(1)}, pred[4,3,8,32]{3,2,1,0:T(8,128)(4,1)S(1)}, bf16[4,512,3,...) while((s32[]{:T(128)}, ...), condition=%wide.region_19.20_spmd, body=%wide.region_16.19_spmd.sunk | while | flops 843151872 | bytes 61792648 | solution.py:98
  629.1 16.6 broadcast_in_dim.230
  662.8 16.6 broadcast_in_dim.230
  696.4 16.6 broadcast_in_dim.230
  730.1 16.6 broadcast_in_dim.230
  766.8 108.7 %reduce-scatter.29.cloned.1.call-done = f32[512,768]{1,0:T(8,128)} async-done(((f32[2048,768]{1,0:T(8,128)}), f32[512,768]{1,0:T(8,128)}) %reduce-scatter.29.cloned.1.call-update) | async-done | bytes 1572880 | tf_op jit(solution)/shard_map/reduce_scatter | solution.py:147
  879.8 21.9 all-gather.41.cloned.1.call-done
  901.8 65.3 %all-gather.27.cloned.1.call-done = bf16[2048,768]{1,0:T(8,128)(2,1)} async-done(((bf16[512,768]{1,0:T(8,128)(2,1)}), bf16[2048,768]{1,0:T(8,128)(2,1)}) %all-gather.27.cloned.1.call-update) | async-done | bytes 3145744 | tf_op jit(solution)/shard_map/all_gather | solution.py:139
  974.7 17.2 all-gather.43.cloned.1.call-done
  991.9 9.6 fusion.176
  1001.6 110.9 %reduce-scatter.31.cloned.1.call-done = f32[512,768]{1,0:T(8,128)} async-done(((f32[2048,768]{1,0:T(8,128)}), f32[512,768]{1,0:T(8,128)}) %reduce-scatter.31.cloned.1.call-update) | async-done | bytes 1572880 | tf_op jit(solution)/shard_map/reduce_scatter | solution.py:147
  1118.7 64.1 %all-gather.29.cloned.1.call-done = bf16[2048,768]{1,0:T(8,128)(2,1)} async-done(((bf16[512,768]{1,0:T(8,128)(2,1)}), bf16[2048,768]{1,0:T(8,128)(2,1)}) %all-gather.29.cloned.1.call-update) | async-done | bytes 3145744 | tf_op jit(solution)/shard_map/all_gather | solution.py:143
  1197.4 109.5 %reduce-scatter.33.cloned.1.call-done = f32[512,768]{1,0:T(8,128)} async-done(((f32[2048,768]{1,0:T(8,128)}), f32[512,768]{1,0:T(8,128)}) %reduce-scatter.33.cloned.1.call-update) | async-done | bytes 1572880 | tf_op jit(solution)/shard_map/reduce_scatter | solution.py:156
  1312.6 63.8 %all-gather.31.cloned.1.call-done = bf16[2048,768]{1,0:T(8,128)(2,1)} async-done(((bf16[512,768]{1,0:T(8,128)(2,1)}), bf16[2048,768]{1,0:T(8,128)(2,1)}) %all-gather.31.cloned.1.call-update) | async-done | bytes 3145744 | tf_op jit(solution)/shard_map/all_gather | solution.py:143
  1382.1 299.0 %while.56 = (s32[]{:T(128)}, f32[2048,3,64]{0,2,1:T(8,128)}, f32[2048,3,64]{0,2,1:T(8,128)}, bf16[4,512,3,64]{1,3,2,0:T(8,128)(2,1)}, bf16[4,512,3,64]{1,3,2,0:T...) while((s32[]{:T(128)}, f32[2048,3,64]{0,2,1:T(8,128)}, ...), condition=%wide.region_33.34_spmd.clone, body=%wide.region_31.33_spmd.clone.sunk | while | flops 2077760512 | bytes 226906704 | solution.py:130
  1386.9 16.6 broadcast_in_dim.233
  1419.6 17.0 fusion.342
  1436.6 19.8 fusion.340
  1460.8 16.6 broadcast_in_dim.233
  1494.0 17.0 fusion.342
  1511.0 20.2 fusion.340
  1535.6 16.6 broadcast_in_dim.233
  1568.9 17.0 fusion.342
  1585.9 20.2 fusion.340
  1610.5 16.6 broadcast_in_dim.233
  1643.7 17.0 fusion.342
  1660.7 20.2 fusion.340
  1691.9 109.4 %reduce-scatter.35.cloned.1.call-done = f32[512,768]{1,0:T(8,128)} async-done(((f32[2048,768]{1,0:T(8,128)}), f32[512,768]{1,0:T(8,128)}) %reduce-scatter.35.cloned.1.call-update) | async-done | bytes 1572880 | tf_op jit(solution)/shard_map/reduce_scatter | solution.py:156
  1805.9 64.0 %all-gather.33.cloned.1.call-done = bf16[2048,768]{1,0:T(8,128)(2,1)} async-done(((bf16[512,768]{1,0:T(8,128)(2,1)}), bf16[2048,768]{1,0:T(8,128)(2,1)}) %all-gather.33.cloned.1.call-update) | async-done | bytes 3145744 | tf_op jit(solution)/shard_map/all_gather | solution.py:143
  1884.5 109.5 %reduce-scatter.37.cloned.1.call-done = f32[512,768]{1,0:T(8,128)} async-done(((f32[2048,768]{1,0:T(8,128)}), f32[512,768]{1,0:T(8,128)}) %reduce-scatter.37.cloned.1.call-update) | async-done | bytes 1572880 | tf_op jit(solution)/shard_map/reduce_scatter | solution.py:156
  2024.4 8.5 fusion.217
  2040.5 23.2 all-gather.35.cloned.1.call-done
  2069.4 306.5 %while.57 = (s32[]{:T(128)}, f32[2048,3,64]{0,2,1:T(8,128)}, f32[2048,3,64]{0,2,1:T(8,128)}, bf16[4,512,3,64]{1,3,2,0:T(8,128)(2,1)}, bf16[4,512,3,64]{1,3,2,0:T...) while((s32[]{:T(128)}, f32[2048,3,64]{0,2,1:T(8,128)}, ...), condition=%wide.region_42.43_spmd.clone, body=%wide.region_40.42_spmd.clone.sunk | while | flops 2077760512 | bytes 226906704 | solution.py:130
  2074.6 16.7 broadcast_in_dim.236
  2107.4 18.1 fusion.358
  2125.5 20.1 fusion.356
  2150.7 16.7 broadcast_in_dim.236
  2184.4 17.4 fusion.358
  2201.8 21.1 fusion.356
  2227.9 16.7 broadcast_in_dim.236
  2261.4 17.4 fusion.358
  2278.8 21.3 fusion.356
  2305.2 16.7 broadcast_in_dim.236
  2338.4 17.0 fusion.358
  2355.5 20.2 fusion.356
  2403.5 39.5 %all-reduce = (f32[2,768]{1,0:T(2,128)}, f32[2,768]{1,0:T(2,128)}, f32[2,768]{1,0:T(2,128)}, f32[2,768]{1,0:T(2,128)}) all-reduce(f32[2,768]{1,0:T(2,128)S(1)} %pad_maximum_fusion.6, f32[2,768]{1,0:T(2,128)S(1)} %pad_maximum_fusion.7, f32[2,768]{1,0:T(2,128)S(1)} %pad_maximum_fusion.8, ...), channel_id=1, replica_groups=mesh['dp'=8,'tensor'=4] {'dp','tensor'}, use_global_device_ids=true, to_apply=%region_54.55 | all-reduce | flops 6144 | bytes 49152 | tf_op jit(solution)/shard_map/psum | solution.py:267
  2444.7 13.2 reduce-scatter.49.cloned.1.call-done
  2460.1 110.9 %reduce-scatter.39.cloned.1.call-done = f32[512,768]{1,0:T(8,128)} async-done(((f32[2048,768]{1,0:T(8,128)}), f32[512,768]{1,0:T(8,128)}) %reduce-scatter.39.cloned.1.call-update) | async-done | bytes 1572880 | tf_op jit(solution)/shard_map/reduce_scatter | solution.py:156
  (583 shorter events, 521.3 us)
Async XLA Ops:
  8.0 24.3 copy-start.43
  8.0 68.6 %all-gather.21.cloned.1.call-start = ((), (), s32[]{:S(2)}) async-start(), calls=%async_computation.16 | async-start | bytes 3932160 | tf_op jit(solution)/shard_map/all_gather | solution.py:139
  8.8 326.8 %reduce-scatter.25.cloned.1.call-start = ((), (), s32[]{:S(2)}) async-start(), calls=%async_computation.17 | async-start | bytes 7864320 | tf_op jit(solution)/shard_map/reduce_scatter | solution.py:147
  44.0 36.5 %copy-start.36 = (bf16[1,768,576]{2,1,0:T(8,128)(2,1)}, bf16[1,768,576]{2,1,0:T(8,128)(2,1)S(1)}, u32[]{:S(2)}) copy-start(bf16[1,768,576]{2,1,0:T(8,128)(2,1)S(1)} %all-gather) | copy-start | bytes 2654212
  225.9 109.6 %copy-start.22 = (bf16[512,768]{1,0:T(8,128)(2,1)S(1)}, bf16[512,768]{1,0:T(8,128)(2,1)}, u32[]{:S(2)}) copy-start(bf16[512,768]{1,0:T(8,128)(2,1)} %param.21) | copy-start | bytes 2359300
  226.0 113.9 %all-gather.37.cloned.1.call-start = ((), (), s32[]{:S(2)}) async-start(), calls=%async_computation.36 | async-start | bytes 1327104 | tf_op jit(solution)/shard_map/all_gather | solution.py:183
  227.6 175.0 %all-gather.23.cloned.1.call-start = ((), (), s32[]{:S(2)}) async-start(), calls=%async_computation.18 | async-start | bytes 3932160 | tf_op jit(solution)/shard_map/all_gather | solution.py:139
  228.3 319.6 %copy-start.46 = (f32[768]{0:T(1024)}, f32[768]{0:T(1024)S(1)}, u32[]{:S(2)}) copy-start(f32[768]{0:T(1024)S(1)} %get-tuple-element.616) | copy-start | bytes 9220
  337.2 210.7 %copy-start.4 = (f32[512,768]{1,0:T(8,128)}, f32[512,768]{1,0:T(8,128)S(1)}, u32[]{:S(2)}) copy-start(f32[512,768]{1,0:T(8,128)S(1)} %get-tuple-element.588) | copy-start | bytes 4718596
  337.2 210.7 %copy-start.52 = (f32[512]{0:T(512)}, f32[512]{0:T(512)S(1)}, u32[]{:S(2)}) copy-start(f32[512]{0:T(512)S(1)} %broadcast_multiply_fusion.3) | copy-start | bytes 6148
  337.5 72.7 %copy-start.66 = (f32[512]{0:T(512)}, f32[512]{0:T(512)S(1)}, u32[]{:S(2)}) copy-start(f32[512]{0:T(512)S(1)} %multiply_reduce_fusion.11) | copy-start | bytes 6148
  337.6 210.4 %copy-start.57 = (f32[512]{0:T(512)}, f32[512]{0:T(512)S(1)}, u32[]{:S(2)}) copy-start(f32[512]{0:T(512)S(1)} %fusion.210) | copy-start | bytes 6148
  338.8 88.7 %all-gather.39.cloned.1.call-start = ((), (), s32[]{:S(2)}) async-start(), calls=%async_computation.37 | async-start | bytes 1327104 | tf_op jit(solution)/shard_map/all_gather | solution.py:184
  339.6 208.3 %reduce-scatter.27.cloned.1.call-start = ((), (), s32[]{:S(2)}) async-start(), calls=%async_computation.19 | async-start | bytes 7864320 | tf_op jit(solution)/shard_map/reduce_scatter | solution.py:147
  437.1 179.2 %all-gather.25.cloned.1.call-start = ((), (), s32[]{:S(2)}) async-start(), calls=%async_computation.20 | async-start | bytes 3932160 | tf_op jit(solution)/shard_map/all_gather | solution.py:139
  438.4 111.8 %copy-start.48 = (f32[768]{0:T(1024)}, f32[768]{0:T(1024)S(1)}, u32[]{:S(2)}) copy-start(f32[768]{0:T(1024)S(1)} %get-tuple-element.489) | copy-start | bytes 9220
  439.0 111.2 %copy-start.64 = (f32[768]{0:T(1024)}, f32[768]{0:T(1024)S(1)}, u32[]{:S(2)}) copy-start(f32[768]{0:T(1024)S(1)} %get-tuple-element.491) | copy-start | bytes 9220
  552.2 323.3 %reduce-scatter.29.cloned.1.call-start = ((), (), s32[]{:S(2)}) async-start(), calls=%async_computation.21 | async-start | bytes 7864320 | tf_op jit(solution)/shard_map/reduce_scatter | solution.py:147
  575.4 44.9 %copy-start.38 = (bf16[1,768,576]{2,1,0:T(8,128)(2,1)}, bf16[1,768,576]{2,1,0:T(8,128)(2,1)S(1)}, u32[]{:S(2)}) copy-start(bf16[1,768,576]{2,1,0:T(8,128)(2,1)S(1)} %all-gather.4) | copy-start | bytes 2654212
  766.0 109.5 %copy-start.7 = (f32[512,768]{1,0:T(8,128)S(1)}, f32[512,768]{1,0:T(8,128)}, u32[]{:S(2)}) copy-start(f32[512,768]{1,0:T(8,128)} %copy-done.6) | copy-start | bytes 4718596
  766.0 109.5 %copy-start.49 = (f32[768]{0:T(1024)S(1)}, f32[768]{0:T(1024)}, u32[]{:S(2)}) copy-start(f32[768]{0:T(1024)} %copy-done.48) | copy-start | bytes 9220
  766.0 109.5 %copy-start.55 = (f32[512]{0:T(512)S(1)}, f32[512]{0:T(512)}, u32[]{:S(2)}) copy-start(f32[512]{0:T(512)} %copy-done.54) | copy-start | bytes 6148
  766.0 109.5 %copy-start.60 = (f32[512]{0:T(512)S(1)}, f32[512]{0:T(512)}, u32[]{:S(2)}) copy-start(f32[512]{0:T(512)} %copy-done.59) | copy-start | bytes 6148
  766.0 109.5 %copy-start.65 = (f32[768]{0:T(1024)S(1)}, f32[768]{0:T(1024)}, u32[]{:S(2)}) copy-start(f32[768]{0:T(1024)} %copy-done.64) | copy-start | bytes 9220
  766.0 135.7 %all-gather.41.cloned.1.call-start = ((), (), s32[]{:S(2)}) async-start(), calls=%async_computation.38 | async-start | bytes 1327104 | tf_op jit(solution)/shard_map/all_gather | solution.py:183
  766.8 111.0 %copy-start.51 = (f32[768]{0:T(1024)S(1)}, f32[768]{0:T(1024)}, u32[]{:S(2)}) copy-start(f32[768]{0:T(1024)} %get-tuple-element.617) | copy-start | bytes 9220
  766.8 111.0 %copy-start.62 = (f32[768]{0:T(1024)S(1)}, f32[768]{0:T(1024)}, u32[]{:S(2)}) copy-start(f32[768]{0:T(1024)} %get-tuple-element.494) | copy-start | bytes 9220
  766.8 200.3 %all-gather.27.cloned.1.call-start = ((), (), s32[]{:S(2)}) async-start(), calls=%async_computation.22 | async-start | bytes 3932160 | tf_op jit(solution)/shard_map/all_gather | solution.py:139
  879.0 112.9 %all-gather.43.cloned.1.call-start = ((), (), s32[]{:S(2)}) async-start(), calls=%async_computation.39 | async-start | bytes 1327104 | tf_op jit(solution)/shard_map/all_gather | solution.py:184
  879.6 232.8 %reduce-scatter.31.cloned.1.call-start = ((), (), s32[]{:S(2)}) async-start(), calls=%async_computation.23 | async-start | bytes 7864320 | tf_op jit(solution)/shard_map/reduce_scatter | solution.py:147
  1001.5 113.2 %copy-start.23 = (bf16[512,768]{1,0:T(8,128)(2,1)S(1)}, bf16[512,768]{1,0:T(8,128)(2,1)}, u32[]{:S(2)}) copy-start(bf16[512,768]{1,0:T(8,128)(2,1)} %param.30) | copy-start | bytes 2359300
  1001.5 113.2 %copy-start.63 = (f32[768]{0:T(1024)S(1)}, f32[768]{0:T(1024)}, u32[]{:S(2)}) copy-start(f32[768]{0:T(1024)} %get-tuple-element.488) | copy-start | bytes 9220
  1001.5 181.2 %all-gather.29.cloned.1.call-start = ((), (), s32[]{:S(2)}) async-start(), calls=%async_computation.24 | async-start | bytes 3932160 | tf_op jit(solution)/shard_map/all_gather | solution.py:143
  1118.6 188.3 %reduce-scatter.33.cloned.1.call-start = ((), (), s32[]{:S(2)}) async-start(), calls=%async_computation.25 | async-start | bytes 7864320 | tf_op jit(solution)/shard_map/reduce_scatter | solution.py:156
  1197.3 179.2 %all-gather.31.cloned.1.call-start = ((), (), s32[]{:S(2)}) async-start(), calls=%async_computation.26 | async-start | bytes 3932160 | tf_op jit(solution)/shard_map/all_gather | solution.py:143
  1312.6 488.7 %reduce-scatter.35.cloned.1.call-start = ((), (), s32[]{:S(2)}) async-start(), calls=%async_computation.27 | async-start | bytes 7864320 | tf_op jit(solution)/shard_map/reduce_scatter | solution.py:156
  1691.8 109.5 %copy-start.8 = (f32[512,768]{1,0:T(8,128)S(1)}, f32[512,768]{1,0:T(8,128)}, u32[]{:S(2)}) copy-start(f32[512,768]{1,0:T(8,128)} %copy-done.6) | copy-start | bytes 4718596
  1691.8 109.5 %copy-start.16 = (f32[512,768]{1,0:T(8,128)S(1)}, f32[512,768]{1,0:T(8,128)}, u32[]{:S(2)}) copy-start(f32[512,768]{1,0:T(8,128)} %copy-done.15) | copy-start | bytes 4718596
  1691.8 109.5 %copy-start.50 = (f32[768]{0:T(1024)S(1)}, f32[768]{0:T(1024)}, u32[]{:S(2)}) copy-start(f32[768]{0:T(1024)} %copy-done.48) | copy-start | bytes 9220
  1691.8 109.5 %copy-start.56 = (f32[512]{0:T(512)S(1)}, f32[512]{0:T(512)}, u32[]{:S(2)}) copy-start(f32[512]{0:T(512)} %copy-done.54) | copy-start | bytes 6148
  1691.8 109.5 %copy-start.61 = (f32[512]{0:T(512)S(1)}, f32[512]{0:T(512)}, u32[]{:S(2)}) copy-start(f32[512]{0:T(512)} %copy-done.59) | copy-start | bytes 6148
  1691.8 109.5 %copy-start.73 = (f32[512]{0:T(512)S(1)}, f32[512]{0:T(512)}, u32[]{:S(2)}) copy-start(f32[512]{0:T(512)} %copy-done.72) | copy-start | bytes 6148
  1691.8 112.3 %copy-start.69 = (f32[512]{0:T(512)S(1)}, f32[512]{0:T(512)}, u32[]{:S(2)}) copy-start(f32[512]{0:T(512)} %copy-done.68) | copy-start | bytes 6148
  1691.8 178.1 %all-gather.33.cloned.1.call-start = ((), (), s32[]{:S(2)}) async-start(), calls=%async_computation.28 | async-start | bytes 3932160 | tf_op jit(solution)/shard_map/all_gather | solution.py:143
  1805.9 74.0 %copy-start.90 = (bf16[1,768,768]{2,1,0:T(8,128)(2,1)S(1)}, bf16[1,768,768]{2,1,0:T(8,128)(2,1)}, u32[]{:S(2)}) copy-start(bf16[1,768,768]{2,1,0:T(8,128)(2,1)} %all-gather.37.cloned.1.call-done) | copy-start | bytes 3538948
  1805.9 188.2 %reduce-scatter.37.cloned.1.call-start = ((), (), s32[]{:S(2)}) async-start(), calls=%async_computation.29 | async-start | bytes 7864320 | tf_op jit(solution)/shard_map/reduce_scatter | solution.py:156
  1884.4 109.6 %copy-start.5 = (f32[512,768]{1,0:T(8,128)S(1)}, f32[512,768]{1,0:T(8,128)}, u32[]{:S(2)}) copy-start(f32[512,768]{1,0:T(8,128)} %copy-done.4) | copy-start | bytes 4718596
  1884.4 109.6 %copy-start.47 = (f32[768]{0:T(1024)S(1)}, f32[768]{0:T(1024)}, u32[]{:S(2)}) copy-start(f32[768]{0:T(1024)} %copy-done.46) | copy-start | bytes 9220
  1884.4 109.6 %copy-start.53 = (f32[512]{0:T(512)S(1)}, f32[512]{0:T(512)}, u32[]{:S(2)}) copy-start(f32[512]{0:T(512)} %copy-done.52) | copy-start | bytes 6148
  1884.4 109.6 %copy-start.58 = (f32[512]{0:T(512)S(1)}, f32[512]{0:T(512)}, u32[]{:S(2)}) copy-start(f32[512]{0:T(512)} %copy-done.57) | copy-start | bytes 6148
  1884.5 112.4 %copy-start.67 = (f32[512]{0:T(512)S(1)}, f32[512]{0:T(512)}, u32[]{:S(2)}) copy-start(f32[512]{0:T(512)} %copy-done.66) | copy-start | bytes 6148
  1884.5 179.2 %all-gather.35.cloned.1.call-start = ((), (), s32[]{:S(2)}) async-start(), calls=%async_computation.30 | async-start | bytes 3932160 | tf_op jit(solution)/shard_map/all_gather | solution.py:143
  1999.8 397.4 %reduce-scatter.55.cloned.1.call-start = ((), (), s32[]{:S(2)}) async-start(), calls=%async_computation.43 | async-start | bytes 884736
  2004.0 394.3 %reduce-scatter.51.cloned.1.call-start = ((), (), s32[]{:S(2)}) async-start(), calls=%async_computation.41 | async-start | bytes 2211840
  2011.1 388.5 %reduce-scatter.43.cloned.1.call-start = ((), (), s32[]{:S(2)}) async-start(), calls=%async_computation.33 | async-start | bytes 2654208 | tf_op jit(solution)/shard_map/reduce_scatter | solution.py:260
  2018.2 381.4 %reduce-scatter.41.cloned.1.call-start = ((), (), s32[]{:S(2)}) async-start(), calls=%async_computation.32 | async-start | bytes 2654208 | tf_op jit(solution)/shard_map/reduce_scatter | solution.py:260
  2024.4 377.2 %reduce-scatter.47.cloned.1.call-start = ((), (), s32[]{:S(2)}) async-start(), calls=%async_computation.35 | async-start | bytes 2654208 | tf_op jit(solution)/shard_map/reduce_scatter | solution.py:261
  2032.9 368.6 %reduce-scatter.45.cloned.1.call-start = ((), (), s32[]{:S(2)}) async-start(), calls=%async_computation.34 | async-start | bytes 2654208 | tf_op jit(solution)/shard_map/reduce_scatter | solution.py:261
  2033.0 30.7 %copy-start.34 = (bf16[1,192,768]{2,1,0:T(8,128)(2,1)S(1)}, bf16[1,192,768]{2,1,0:T(8,128)(2,1)}, u32[]{:S(2)}) copy-start(bf16[1,192,768]{2,1,0:T(8,128)(2,1)} %copy.120) | copy-start | bytes 884740
  2040.4 402.6 %reduce-scatter.53.cloned.1.call-start = ((), (), s32[]{:S(2)}) async-start(), calls=%async_computation.42 | async-start | bytes 884736
  2380.5 77.4 %reduce-scatter.49.cloned.1.call-start = ((), (), s32[]{:S(2)}) async-start(), calls=%async_computation.40 | async-start | bytes 2211840
  2391.7 179.3 %reduce-scatter.39.cloned.1.call-start = ((), (), s32[]{:S(2)}) async-start(), calls=%async_computation.31 | async-start | bytes 7864320 | tf_op jit(solution)/shard_map/reduce_scatter | solution.py:156
  2398.2 172.8 %copy-start.14 = (f32[512,768]{1,0:T(8,128)S(1)}, f32[512,768]{1,0:T(8,128)}, u32[]{:S(2)}) copy-start(f32[512,768]{1,0:T(8,128)} %copy-done.13) | copy-start | bytes 4718596
  2398.2 172.8 %copy-start.71 = (f32[512]{0:T(512)S(1)}, f32[512]{0:T(512)}, u32[]{:S(2)}) copy-start(f32[512]{0:T(512)} %copy-done.70) | copy-start | bytes 6148
  (100 other events, 585.8 us)
Sparse Core Ops, SparseCore 0:
  10.4 66.1 all-gather.20
  226.1 109.4 reduce-scatter.24
  552.3 63.9 all-gather.24
  1001.6 110.7 reduce-scatter.30
  1118.7 63.9 all-gather.28
  1197.4 109.4 reduce-scatter.32
  1806.0 63.9 all-gather.32
  1884.6 109.3 reduce-scatter.36
Sparse Core Ops, SparseCore 1:
  228.9 22.4 all-gather.36
  338.9 63.8 all-gather.22
  405.0 22.4 all-gather.38
  437.2 110.7 reduce-scatter.26
  766.1 109.3 reduce-scatter.28
  877.4 24.3 all-gather.40
  903.8 63.3 all-gather.26
  969.4 22.4 all-gather.42
  1312.6 63.8 all-gather.30
  1691.9 109.3 reduce-scatter.34
  1999.9 63.8 all-gather.34
  2066.9 33.5 reduce-scatter.54
  2103.7 40.0 reduce-scatter.50
  2147.2 42.2 reduce-scatter.42
  2192.8 42.2 reduce-scatter.40
  2238.4 42.2 reduce-scatter.46
  2284.0 42.2 reduce-scatter.44
  2380.6 33.8 reduce-scatter.52
  2417.7 40.2 reduce-scatter.48
  2460.3 110.7 reduce-scatter.38
where the time goes:
time: 2590 us; the launch traced here: 2580 us
  waiting for transfers between devices  1360 us (53%)
  matrix products  636 us (25%)
  local copies, waits for them, and re-layouts  399 us (15%)
  blocking collectives  83.8 us (3%)
  other arithmetic  76.5 us (3%)
    reduce_scatter x4, waiting for transfers between devices, input_terms(): lax.psum_scatter(dot_right_t(left, right), 'tensor', scatter_dimension=0,...  439 us
    reduce_scatter x4, waiting for transfers between devices, sum_rows(): lax.psum_scatter(jnp.dot(left, right, preferred_element_type=jnp.float32)...  436 us
    broadcast_in_dim x48, local copies, waits for them, and re-layouts, masked_scores(): shaped = jnp.where(mask_block[:, :, None, :, None], shaped, MASK_VALUE)  336 us
    all_gather x4, waiting for transfers between devices, gather_grads(): return lax.all_gather(shard, 'tensor', axis=0, tiled=True)  215 us
    all_gather x4, waiting for transfers between devices, gather_rows(): return lax.all_gather(shard, 'tensor', axis=0, tiled=True)  202 us
    dot_general x8, matrix products, one_block(): jnp.einsum('hqk,qhe->khe', d_scores, query_block, preferred_element_type=...  163 us
    dot_general x8, matrix products, one_block(): jnp.einsum('hqk,khe->qhe', d_scores, key_rows, preferred_element_type=jnp...  138 us
    dot_general x16, matrix products, masked_scores(): jnp.einsum('qhe,khe->hqk', query_block, key_rows, preferred_element_type=...  70.7 us
  transfers between devices with their start and end apart: 28, of which 20 were waited for; matrix products, arithmetic and copies ran while one was open for 16% of the time, Pallas kernels for 0%

commit v1 on v0

v1 whole, which is shorter than its diff:
```python
import jax
import jax.numpy as jnp
from jax import lax
from jax.experimental import pallas as pl
from jax.experimental.pallas import tpu as pltpu
from jax.sharding import PartitionSpec as P

HD = 64
BLK = 64
LAYERS = 2
LONGEST = 16
QUAD = 4
WIDE = QUAD * HD
STEP = 4
STEPS = LONGEST // STEP

NORM_EPSILON = 1e-12
MASK_VALUE = -1e30
BF = jnp.bfloat16
F32 = jnp.float32


def layer_norm(summed, norm_gain, norm_shift):
    row_mean = jnp.mean(summed, axis=-1, keepdims=True)
    centred = summed - row_mean
    row_var = jnp.mean(centred * centred, axis=-1, keepdims=True)
    return centred * lax.rsqrt(row_var + NORM_EPSILON) * norm_gain + norm_shift


def gelu_tanh(values):
    return jax.nn.gelu(values, approximate=True)


def dot(left, right):
    return jnp.dot(left, right, preferred_element_type=F32)


def dot_right_t(left, right):
    return lax.dot_general(left, right, (((1,), (1,)), ((), ())), preferred_element_type=F32)


def dot_left_t(left, right):
    return lax.dot_general(left, right, (((0,), (0,)), ((), ())), preferred_element_type=F32)


def head_diagonal(rows):
    lane_head = lax.broadcasted_iota(jnp.int32, rows.shape, 1) // HD
    return jnp.concatenate(
        [jnp.where(lane_head == h, rows, jnp.zeros_like(rows)) for h in range(QUAD)], axis=0
    )


def diagonal_rows(full):
    lane_head = lax.broadcasted_iota(jnp.int32, (HD, WIDE), 1) // HD
    out = full[:HD]
    for h in range(1, QUAD):
        out = jnp.where(lane_head == h, full[h * HD : (h + 1) * HD], out)
    return out


def forward_kernel(keys_at, steps_of, q_ref, k_ref, v_ref, bias_ref, out_ref, log_ref, score, peak, total, mix):
    def one_block(b, carry):
        rows = pl.ds(pl.multiple_of(b * BLK, BLK), BLK)
        query = head_diagonal(q_ref[rows, :])
        steps = steps_of[b]
        peak[...] = jnp.full(peak.shape, -jnp.inf, F32)
        total[...] = jnp.zeros_like(total)
        mix[...] = jnp.zeros_like(mix)

        def block_rows(ref, t):
            return jnp.concatenate(
                [
                    ref[pl.ds(pl.multiple_of(keys_at[b, t * STEP + j] * BLK, BLK), BLK), :]
                    for j in range(STEP)
                ],
                axis=0,
            )

        def scores(t, carry):
            raw = dot_right_t(query, block_rows(k_ref, t))
            bias = bias_ref[b, t]
            for h in range(QUAD):
                piece = raw[h * BLK : (h + 1) * BLK] + bias[h : h + 1, :]
                score[t, h * BLK : (h + 1) * BLK, :] = piece
                at = slice(h * BLK, (h + 1) * BLK)
                peak[at, :] = jnp.maximum(peak[at, :], jnp.maximum(piece[:, :128], piece[:, 128:]))
            return carry

        lax.fori_loop(0, steps, scores, 0)
        row_peak = jnp.max(peak[...], axis=1, keepdims=True)

        def mixes(t, carry):
            exponent = jnp.exp(score[t] - row_peak)
            total[...] += exponent[:, :128] + exponent[:, 128:]
            mix[...] += dot(exponent.astype(BF), block_rows(v_ref, t))
            return carry

        lax.fori_loop(0, steps, mixes, 0)
        row_total = jnp.sum(total[...], axis=1, keepdims=True)
        out_ref[rows, :] = diagonal_rows(mix[...] / row_total).astype(BF)
        logs = row_peak + jnp.log(row_total)
        log_ref[b] = jnp.transpose(jnp.broadcast_to(logs, (WIDE, 128)))[0:1, :]
        return carry

    lax.fori_loop(0, q_ref.shape[0] // BLK, one_block, 0)


def backward_kernel(
    keys_at, steps_of, q_ref, k_ref, v_ref, bias_ref, log_ref, d_ref, dq_ref, dk_ref, dv_ref, prob, dprob, inner, dquery, dkey, dvalue
):
    dkey[...] = jnp.zeros_like(dkey)
    dvalue[...] = jnp.zeros_like(dvalue)

    def one_block(b, carry):
        rows = pl.ds(pl.multiple_of(b * BLK, BLK), BLK)
        query = head_diagonal(q_ref[rows, :])
        d_mixed = head_diagonal(d_ref[rows, :])
        logs = log_ref[b]
        steps = steps_of[b]
        inner[...] = jnp.zeros_like(inner)
        dquery[...] = jnp.zeros_like(dquery)

        def places(t):
            return [
                pl.ds(pl.multiple_of(keys_at[b, t * STEP + j] * BLK, BLK), BLK) for j in range(STEP)
            ]

        def probs(t, carry):
            at = places(t)
            keys = jnp.concatenate([k_ref[p, :] for p in at], axis=0)
            values = jnp.concatenate([v_ref[p, :] for p in at], axis=0)
            raw = dot_right_t(keys, query)
            back = dot_right_t(values, d_mixed)
            bias = bias_ref[b, t]
            pieces = []
            for j in range(STEP):
                own = slice(j * BLK, (j + 1) * BLK)
                full = jnp.exp(raw[own] + (bias[j : j + 1, :] - logs))
                prob[t, own, :] = full
                product = full * back[own]
                inner[...] += jnp.sum(product.reshape(BLK // 8, 8, WIDE), axis=0)
                pieces.append(full.astype(BF))
            dprob[t] = back
            grad = dot(jnp.concatenate(pieces, axis=0), d_mixed)
            for j in range(STEP):
                dvalue[at[j], :] += grad[j * BLK : (j + 1) * BLK]
            return carry

        lax.fori_loop(0, steps, probs, 0)
        row_inner = jnp.sum(inner[...], axis=0, keepdims=True)

        def grads(t, carry):
            at = places(t)
            d_score = (prob[t] * (dprob[t] - row_inner)).astype(BF)
            grad = dot(d_score, query)
            for j in range(STEP):
                dkey[at[j], :] += grad[j * BLK : (j + 1) * BLK]
            keys = jnp.concatenate([k_ref[p, :] for p in at], axis=0)
            dquery[...] += dot_left_t(d_score, keys)
            return carry

        lax.fori_loop(0, steps, grads, 0)
        dq_ref[rows, :] = (diagonal_rows(dquery[...]) * (HD**-0.5)).astype(BF)
        return carry

    lax.fori_loop(0, q_ref.shape[0] // BLK, one_block, 0)
    dk_ref[...] = dkey[...].astype(BF)
    dv_ref[...] = dvalue[...].astype(BF)


def attend_forward(query, keyval, tables):
    keys_at, steps_of, bias_rows, bias_cols = tables
    own, width = query.shape
    quads = width // WIDE
    rows = keyval.shape[0]
    blocks = own // BLK
    return pl.pallas_call(
        forward_kernel,
        grid_spec=pltpu.PrefetchScalarGridSpec(
            num_scalar_prefetch=2,
            grid=(quads,),
            in_specs=[
                pl.BlockSpec((own, WIDE), lambda i, *_: (0, i)),
                pl.BlockSpec((rows, WIDE), lambda i, *_: (0, i)),
                pl.BlockSpec((rows, WIDE), lambda i, *_: (0, i + quads)),
                pl.BlockSpec((blocks, STEPS, None, QUAD, WIDE), lambda i, *_: (0, 0, i, 0, 0)),
            ],
            out_specs=[
                pl.BlockSpec((own, WIDE), lambda i, *_: (0, i)),
                pl.BlockSpec((blocks, 1, WIDE), lambda i, *_: (0, 0, i)),
            ],
            scratch_shapes=[
                pltpu.VMEM((STEPS, WIDE, WIDE), F32),
                pltpu.VMEM((WIDE, 128), F32),
                pltpu.VMEM((WIDE, 128), F32),
                pltpu.VMEM((WIDE, WIDE), F32),
            ],
        ),
        out_shape=[
            jax.ShapeDtypeStruct((own, width), BF),
            jax.ShapeDtypeStruct((blocks, 1, width), F32),
        ],
        cost_estimate=pl.CostEstimate(
            flops=2 * 2 * own * rows * width // 2 * 4,
            bytes_accessed=2 * (own * 2 + rows * 2) * width,
            transcendentals=own * rows * width // HD // 2,
        ),
        name="attend_forward",
    )(keys_at, steps_of, query, keyval, keyval, bias_rows)


def attend_backward(query, keyval, logs, d_mixed, tables):
    keys_at, steps_of, bias_rows, bias_cols = tables
    own, width = query.shape
    quads = width // WIDE
    rows = keyval.shape[0]
    blocks = own // BLK
    return pl.pallas_call(
        backward_kernel,
        grid_spec=pltpu.PrefetchScalarGridSpec(
            num_scalar_prefetch=2,
            grid=(quads,),
            in_specs=[
                pl.BlockSpec((own, WIDE), lambda i, *_: (0, i)),
                pl.BlockSpec((rows, WIDE), lambda i, *_: (0, i)),
                pl.BlockSpec((rows, WIDE), lambda i, *_: (0, i + quads)),
                pl.BlockSpec((blocks, STEPS, STEP, WIDE), lambda i, *_: (0, 0, 0, i)),
                pl.BlockSpec((blocks, 1, WIDE), lambda i, *_: (0, 0, i)),
                pl.BlockSpec((own, WIDE), lambda i, *_: (0, i)),
            ],
            out_specs=[
                pl.BlockSpec((own, WIDE), lambda i, *_: (0, i)),
                pl.BlockSpec((rows, WIDE), lambda i, *_: (0, i)),
                pl.BlockSpec((rows, WIDE), lambda i, *_: (0, i)),
            ],
            scratch_shapes=[
                pltpu.VMEM((STEPS, WIDE, WIDE), F32),
                pltpu.VMEM((STEPS, WIDE, WIDE), F32),
                pltpu.VMEM((8, WIDE), F32),
                pltpu.VMEM((WIDE, WIDE), F32),
                pltpu.VMEM((rows, WIDE), F32),
                pltpu.VMEM((rows, WIDE), F32),
            ],
        ),
        out_shape=[
            jax.ShapeDtypeStruct((own, width), BF),
            jax.ShapeDtypeStruct((rows, width), BF),
            jax.ShapeDtypeStruct((rows, width), BF),
        ],
        cost_estimate=pl.CostEstimate(
            flops=5 * 2 * own * rows * width // 2 * 4,
            bytes_accessed=2 * (own * 3 + rows * 4) * width,
            transcendentals=own * rows * width // HD // 2,
        ),
        name="attend_backward",
    )(keys_at, steps_of, query, keyval, keyval, bias_cols, logs, d_mixed)


def attention_tables(doc_lengths, block_deal, random_rows, own_blocks, first_own):
    blocks = block_deal.shape[0]
    doc_ends = jnp.cumsum(doc_lengths)
    doc_starts = doc_ends - doc_lengths
    place = jnp.arange(blocks, dtype=jnp.int32)
    stored_at = jnp.sum(
        jnp.where(block_deal[None, :] == place[:, None], place[None, :], 0), axis=1
    )
    own = lax.dynamic_slice(block_deal, (first_own,), (own_blocks,))
    doc_index = jnp.sum((own[:, None] >= doc_ends[None, :]).astype(jnp.int32), axis=1)
    doc_pick = (
        doc_index[:, None] == jnp.arange(doc_lengths.shape[0], dtype=jnp.int32)[None, :]
    ).astype(jnp.int32)
    first_block = jnp.sum(doc_pick * doc_starts[None, :], axis=1)
    doc_blocks = jnp.sum(doc_pick * doc_lengths[None, :], axis=1)
    local = own - first_block
    other = jnp.arange(LONGEST, dtype=jnp.int32)
    wanted = jnp.minimum(first_block[:, None] + other[None, :], blocks - 1)
    keys_at = jnp.sum(
        jnp.where(wanted[:, :, None] == place[None, None, :], stored_at[None, None, :], 0), axis=2
    )
    own_pick = (own[:, None] == place[None, :]).astype(jnp.int32)
    picks = jnp.sum(own_pick[None, :, :, None] * random_rows[:, None, :, :], axis=2)
    picks = jnp.remainder(picks, doc_blocks[None, :, None])
    random_hit = jnp.any(picks[:, :, :, None] == other[None, None, None, :], axis=2)
    inside = other[None, :] < doc_blocks[:, None]
    near = jnp.abs(local[:, None] - other[None, :]) <= 1
    everywhere = (local[:, None] < 2) | (other[None, :] < 2)
    allowed = inside[None] & ((near | everywhere)[None] | random_hit)
    bias = jnp.where(allowed, 0.0, MASK_VALUE).astype(F32)
    heads = bias.shape[0]
    bias_rows = bias.reshape(heads // QUAD, QUAD, own_blocks, STEPS, STEP).transpose(2, 3, 0, 1, 4)
    bias_rows = jnp.repeat(bias_rows, BLK, axis=4)
    bias_cols = bias.transpose(1, 2, 0).reshape(own_blocks, STEPS, STEP, heads)
    bias_cols = jnp.repeat(bias_cols, BLK, axis=3)
    steps_of = (doc_blocks + STEP - 1) // STEP
    return keys_at, steps_of, bias_rows, bias_cols


def gather_tensor(shard):
    return lax.all_gather(shard, "tensor", axis=0, tiled=True)


def local(
    layer_input,
    w_qkv,
    w_out,
    w_up,
    w_down,
    attn_gain,
    attn_shift,
    ffn_gain,
    ffn_shift,
    out_grad,
    doc_lengths,
    block_deal,
    random_blocks,
):
    own_rows, width = layer_input.shape
    tensor = lax.axis_size("tensor")
    slot = lax.axis_index("tensor")
    head_local = random_blocks.shape[1]
    chunk = head_local * HD
    depth = w_qkv.shape[1]
    hidden = w_up.shape[2]
    score_scale = HD ** (-0.5)

    attn_shards = jnp.concatenate(
        [
            w_qkv.reshape(LAYERS, depth, head_local, 3, HD)
            .transpose(0, 1, 3, 2, 4)
            .reshape(LAYERS, depth, 3 * chunk),
            w_out.transpose(0, 2, 1),
        ],
        axis=2,
    )
    ffn_shards = jnp.concatenate([w_up, w_down.transpose(0, 2, 1)], axis=2)

    def spread(shards, pieces):
        gathered = lax.all_gather(shards, "tensor", axis=0)
        gathered = gathered.reshape(tensor, LAYERS, depth, pieces, -1)
        return gathered.transpose(1, 2, 3, 0, 4).reshape(LAYERS, depth, -1)

    attn_rows = spread(attn_shards, 4)
    ffn_rows = spread(ffn_shards, 2)
    attn_full = [lax.all_gather(attn_rows[l], "dp", axis=0, tiled=True) for l in range(LAYERS)]
    ffn_full = [lax.all_gather(ffn_rows[l], "dp", axis=0, tiled=True) for l in range(LAYERS)]

    random_all = lax.all_gather(random_blocks[0], "tensor", axis=0, tiled=True)
    own_blocks = own_rows // BLK
    tables = attention_tables(
        doc_lengths[0], block_deal[0], random_all, own_blocks, slot * own_blocks
    )

    stream = layer_input.astype(F32)
    stored = []
    for layer in range(LAYERS):
        attn_w, ffn_w = attn_full[layer], ffn_full[layer]
        w_query = attn_w[:, :width]
        w_keyval = attn_w[:, width : 3 * width]
        w_back_t = attn_w[:, 3 * width :]
        w_expand = ffn_w[:, : hidden * tensor]
        w_shrink_t = ffn_w[:, hidden * tensor :]
        own_inputs = stream.astype(BF)
        inputs = gather_tensor(own_inputs)
        query = (dot(own_inputs, w_query).astype(BF).astype(F32) * score_scale).astype(BF)
        keyval = dot(inputs, w_keyval).astype(BF)
        mixed, logs = attend_forward(query, keyval, tables)
        summed_one = stream + dot_right_t(mixed, w_back_t)
        normed = layer_norm(summed_one, attn_gain[layer], attn_shift[layer])
        ffn_in = normed.astype(BF)
        pre_act = dot(ffn_in, w_expand)
        activated = gelu_tanh(pre_act).astype(BF)
        summed_two = normed + dot_right_t(activated, w_shrink_t)
        stored.append(
            (own_inputs, inputs, query, keyval, mixed, logs, summed_one, ffn_in, pre_act, activated, summed_two)
        )
        stream = layer_norm(summed_two, ffn_gain[layer], ffn_shift[layer])

    state_grad = out_grad.astype(F32)
    attn_grads = [None] * LAYERS
    ffn_grads = [None] * LAYERS
    norm_parts = [None] * LAYERS
    for layer in reversed(range(LAYERS)):
        (own_inputs, inputs, query, keyval, mixed, logs, summed_one, ffn_in, pre_act, activated, summed_two) = stored[layer]
        attn_w, ffn_w = attn_full[layer], ffn_full[layer]
        w_query = attn_w[:, :width]
        w_keyval = attn_w[:, width : 3 * width]
        w_back_t = attn_w[:, 3 * width :]
        w_expand = ffn_w[:, : hidden * tensor]
        w_shrink_t = ffn_w[:, hidden * tensor :]
        unused_two, ffn_back = jax.vjp(layer_norm, summed_two, ffn_gain[layer], ffn_shift[layer])
        d_two, ffn_gain_part, ffn_shift_part = ffn_back(state_grad)
        d_two_low = d_two.astype(BF)
        shrink_grad_t = dot_left_t(d_two_low, activated)
        unused_act, gelu_back = jax.vjp(gelu_tanh, pre_act)
        d_pre = gelu_back(dot(d_two_low, w_shrink_t))[0].astype(BF)
        expand_grad = dot_left_t(ffn_in, d_pre)
        ffn_part = jnp.concatenate([expand_grad.astype(BF), shrink_grad_t.astype(BF)], axis=1)
        ffn_grads[layer] = lax.psum_scatter(ffn_part, "dp", scatter_dimension=0, tiled=True)
        d_normed = d_two + dot_right_t(d_pre, w_expand)
        unused_one, attn_back = jax.vjp(layer_norm, summed_one, attn_gain[layer], attn_shift[layer])
        d_one, attn_gain_part, attn_shift_part = attn_back(d_normed)
        d_one_low = d_one.astype(BF)
        back_grad_t = dot_left_t(d_one_low, mixed)
        d_mixed = dot(d_one_low, w_back_t).astype(BF)
        d_query, d_key, d_value = attend_backward(query, keyval, logs, d_mixed, tables)
        others = dot_right_t(d_key, w_keyval[:, :width]) + dot_right_t(d_value, w_keyval[:, width:])
        summed = lax.psum_scatter(others.astype(BF), "tensor", scatter_dimension=0, tiled=True)
        attn_part = jnp.concatenate(
            [
                dot_left_t(own_inputs, d_query).astype(BF),
                dot_left_t(inputs, d_key).astype(BF),
                dot_left_t(inputs, d_value).astype(BF),
                back_grad_t.astype(BF),
            ],
            axis=1,
        )
        attn_grads[layer] = lax.psum_scatter(attn_part, "dp", scatter_dimension=0, tiled=True)
        state_grad = d_one + dot_right_t(d_query, w_query) + summed.astype(F32)
        norm_parts[layer] = (attn_gain_part, attn_shift_part, ffn_gain_part, ffn_shift_part)

    def collect(parts, pieces):
        grads = jnp.stack(parts).reshape(LAYERS, depth, pieces, tensor, -1).transpose(3, 0, 1, 2, 4)
        own = lax.psum_scatter(grads, "tensor", scatter_dimension=0, tiled=False)
        return own.astype(F32)

    attn_own = collect(attn_grads, 4)
    ffn_own = collect(ffn_grads, 2)
    qkv_grad = attn_own[:, :, :3].reshape(LAYERS, depth, 3, head_local, HD)
    qkv_grad = qkv_grad.transpose(0, 1, 3, 2, 4).reshape(LAYERS, depth, 3 * chunk)
    out_w_grad = attn_own[:, :, 3].transpose(0, 2, 1)
    up_grad = ffn_own[:, :, 0]
    down_grad = ffn_own[:, :, 1].transpose(0, 2, 1)
    norm_sums = lax.psum(
        tuple(jnp.stack([norm_parts[l][k] for l in range(LAYERS)]) for k in range(4)),
        ("dp", "tensor"),
    )
    return (stream.astype(BF), state_grad, qkv_grad, out_w_grad, up_grad, down_grad) + tuple(norm_sums)


def solution(mesh):
    placed = (
        P(("dp", "tensor"), None),
        P(None, "dp", "tensor"),
        P(None, "tensor", "dp"),
        P(None, "dp", "tensor"),
        P(None, "tensor", "dp"),
        P(),
        P(),
        P(),
        P(),
        P(("dp", "tensor"), None),
        P("dp", None),
        P("dp", None),
        P("dp", "tensor", None, None),
    )
    return jax.shard_map(
        local,
        mesh=mesh,
        in_specs=placed,
        out_specs=(
            P(("dp", "tensor"), None),
            P(("dp", "tensor"), None),
            P(None, "dp", "tensor"),
            P(None, "tensor", "dp"),
            P(None, "dp", "tensor"),
            P(None, "tensor", "dp"),
            P(),
            P(),
            P(),
            P(),
        ),
        check_vma=False,
    )
```

time: 2590 us -> 1080 us (0.42)
  waiting for transfers between devices: 1360 us -> 545 us
  matrix products: 636 us -> 146 us
  local copies, waits for them, and re-layouts: 399 us -> 65.2 us
  Pallas kernels: 0 us -> 190 us
  other arithmetic: 76.5 us -> 31.6 us
  blocking collectives: 83.8 us -> 56.7 us
    reduce_scatter x12 -> x6, waiting for transfers between devices: 875 us -> 298 us  [the longest x2 155 us: local(): lax.psum_scatter(ffn_part, 'dp', scatter_dimension=0, tiled=True)]
    dot_general x64 -> x10, matrix products: 548 us -> 56.2 us  [dot(): return jnp.dot(left, right, preferred_element_type=F32)]
    broadcast_in_dim x48 -> x2, local copies, waits for them, and re-layouts: 336 us -> 1.78 us  [the longest x1 1.31 us: attention_tables(): bias_cols = jnp.repeat(bias_cols, BLK, axis=3)]
    all_gather x12 -> x8, waiting for transfers between devices: 473 us -> 229 us  [the longest x2 124 us: gather_tensor(): return lax.all_gather(shard, 'tensor', axis=0, tiled=True)]
    pallas_call x0 -> x4, Pallas kernels: none -> 190 us  [the longest x2 107 us: attend_backward(): pl.pallas_call(backward_kernel, grid_spec=pltpu.PrefetchScalarGridSpec(nu...]
    reduce_sum x15 -> x5, other arithmetic: 37.9 us -> 1.87 us  [the longest x1 0.88 us: attention_tables(): jnp.sum(jnp.where(wanted[:, :, None] == place[None, None, :], stored_at[N...]
    all_gather x4 -> x1, blocking collectives: 44.3 us -> 13.2 us  [local(): random_all = lax.all_gather(random_blocks[0], 'tensor', axis=0, tiled=True)]
  transfers between devices with their start and end apart: 28 -> 16, of which waited for: 20 -> 15; matrix products, arithmetic and copies ran while one was open for 16% -> 18% of each run, Pallas kernels for 0% -> 13%
where the time goes in v1:
time: 1080 us; the launch traced here: 1060 us
  waiting for transfers between devices  545 us (50%)
  Pallas kernels  190 us (18%)
  matrix products  146 us (14%)
  local copies, waits for them, and re-layouts  65.2 us (6%)
  blocking collectives  56.7 us (5%)
  other arithmetic  31.6 us (3%)
  between operations  15.5 us (1%)
  starting transfers between devices  11.1 us (1%)
    reduce_scatter x2, waiting for transfers between devices, local(): lax.psum_scatter(ffn_part, 'dp', scatter_dimension=0, tiled=True)  155 us
    all_gather x2, waiting for transfers between devices, gather_tensor(): return lax.all_gather(shard, 'tensor', axis=0, tiled=True)  124 us
    pallas_call x2, Pallas kernels, attend_backward(): pl.pallas_call(backward_kernel, grid_spec=pltpu.PrefetchScalarGridSpec(nu...  107 us
    pallas_call x2, Pallas kernels, attend_forward(): pl.pallas_call(forward_kernel, grid_spec=pltpu.PrefetchScalarGridSpec(num...  82.8 us
    reduce_scatter x2, waiting for transfers between devices, collect(): own = lax.psum_scatter(grads, 'tensor', scatter_dimension=0, tiled=False)  79.9 us
    all_gather x2, waiting for transfers between devices, spread(): gathered = lax.all_gather(shards, 'tensor', axis=0)  75 us
    reduce_scatter x2, waiting for transfers between devices, local(): lax.psum_scatter(others.astype(BF), 'tensor', scatter_dimension=0, tiled=...  62.9 us
    dot_general x10, matrix products, dot(): return jnp.dot(left, right, preferred_element_type=F32)  56.2 us
  transfers between devices with their start and end apart: 16, of which 15 were waited for; matrix products, arithmetic and copies ran while one was open for 18% of the time, Pallas kernels for 13%

profile of v1, /device:TPU:0, one launch (start us, length us, event | category | flops | bytes accessed | tf_op | source)
XLA Modules:
  0.0 1061.2 jit_solution(3570741847111510864)
XLA Ops:
  11.4 32.1 %all-gather.24.cloned.1.call-done = bf16[8,96,768]{2,1,0:T(8,128)(2,1)} async-done(((bf16[2,96,768]{2,1,0:T(8,128)(2,1)}), bf16[8,96,768]{2,1,0:T(8,128)(2,1)}) %all-gather.24.cloned.1.call-update) | async-done | bytes 1179664 | tf_op jit(solution)/shard_map/all_gather | solution.py:338
  43.5 3.5 reshape.400
  52.0 42.9 %all-gather.26.cloned.1.call-done = bf16[8,96,1536]{2,1,0:T(8,128)(2,1)} async-done(((bf16[2,96,1536]{2,1,0:T(8,128)(2,1)}), bf16[8,96,1536]{2,1,0:T(8,128)(2,1)}) %all-gather.26.cloned.1.call-update) | async-done | bytes 2359312 | tf_op jit(solution)/shard_map/all_gather | solution.py:338
  94.9 5.0 reshape.402
  99.9 3.0 copy.115
  109.1 13.2 %all-gather.1 = s32[1,12,32,3]{2,0,3,1:T(1,128)S(1)} all-gather(s32[1,3,32,3]{2,0,3,1:T(1,128)S(1)} %copy-done.35), channel_id=3, replica_groups=mesh['dp'=8,'tensor'=4] {'tensor'}, dimensions={1}, use_global_device_ids=true | all-gather | bytes 5760 | tf_op jit(solution)/shard_map/all_gather | solution.py:347
  129.1 5.8 all-gather.12.cloned.1.call-done
  134.9 2.9 fusion.54.q_ref
  137.9 62.0 %all-gather.14.cloned.1.call-done = bf16[2048,768]{1,0:T(8,128)(2,1)} async-done(((bf16[512,768]{1,0:T(8,128)(2,1)}), bf16[2048,768]{1,0:T(8,128)(2,1)}) %all-gather.14.cloned.1.call-update) | async-done | bytes 3145744 | tf_op jit(solution)/shard_map/all_gather | solution.py:299
  199.9 9.0 fusion.k_ref.v_ref
  208.9 41.4 %attend_forward.2 = (bf16[512,768]{1,0:T(8,128)(2,1)}, f32[8,1,768]{2,1,0:T(1,128)}) custom-call(s32[8,16]{1,0:T(8,128)} %select_reduce_fusion.keys_at, s32[8]{0:T(128)} %get-tuple-element.116.steps_of, bf16[512,768]{1,0:T(8,128)(2,1)} %fusion.54.q_ref, bf16[2048,1536]{1,0:T(8,128)(2,1)} %fusion.k_ref.v_ref, bf16[2048,1536]{1,0:T(8,128)(2,1)} %fusion.k_ref.v_ref, ...), custom_call_target="tpu_custom_call" | custom-call | flops 6442450944 | bytes 7864320 | tf_op jit(solution)/shard_map/attend_forward/pallas_call | solution.py:177
  250.2 2.4 fusion.91
  253.0 6.1 all-gather.16.cloned.1.call-done
  259.1 4.8 fusion.29
  264.2 4.0 fusion.92
  269.8 2.8 squeeze.30
  272.6 9.7 reduce-scatter.13.cloned.1.call-start
  286.4 13.8 %all-gather.18.cloned.1.call-done = bf16[768,3072]{1,0:T(8,128)(2,1)} async-done(((bf16[96,3072]{1,0:T(8,128)(2,1)}), bf16[768,3072]{1,0:T(8,128)(2,1)}) %all-gather.18.cloned.1.call-update) | async-done | bytes 4718608 | tf_op jit(solution)/shard_map/all_gather | solution.py:344
  300.2 3.2 multiply_convert_fusion.2.q_ref
  303.3 61.9 %all-gather.20.cloned.1.call-done = bf16[2048,768]{1,0:T(8,128)(2,1)} async-done(((bf16[512,768]{1,0:T(8,128)(2,1)}), bf16[2048,768]{1,0:T(8,128)(2,1)}) %all-gather.20.cloned.1.call-update) | async-done | bytes 3145744 | tf_op jit(solution)/shard_map/all_gather | solution.py:299
  365.2 9.0 convolution_convert_fusion.1.k_ref.v_ref
  374.2 41.5 %attend_forward.3 = (bf16[512,768]{1,0:T(8,128)(2,1)}, f32[8,1,768]{2,1,0:T(1,128)}) custom-call(s32[8,16]{1,0:T(8,128)} %select_reduce_fusion.keys_at, s32[8]{0:T(128)} %get-tuple-element.116.steps_of, bf16[512,768]{1,0:T(8,128)(2,1)} %multiply_convert_fusion.2.q_ref, bf16[2048,1536]{1,0:T(8,128)(2,1)} %convolution_convert_fusion.1.k_ref.v_ref, ...), custom_call_target="tpu_custom_call" | custom-call | flops 6442450944 | bytes 7864320 | tf_op jit(solution)/shard_map/attend_forward/pallas_call | solution.py:177
  415.7 2.4 fusion.93
  419.6 4.9 all-gather.22.cloned.1.call-done
  424.5 5.3 fusion.21
  430.6 4.0 fusion.94
  437.8 6.3 fusion.14
  444.2 3.7 multiply_reduce_fusion.1
  449.7 3.0 convolution_convert_fusion.16.d_ref
  452.7 53.6 %attend_backward.2 = (bf16[512,768]{1,0:T(8,128)(2,1)}, bf16[2048,768]{1,0:T(8,128)(2,1)}, bf16[2048,768]{1,0:T(8,128)(2,1)}) custom-call(s32[8,16]{1,0:T(8,128)} %select_reduce_fusion.keys_at, s32[8]{0:T(128)} %get-tuple-element.116.steps_of, bf16[512,768]{1,0:T(8,128)(2,1)} %multiply_convert_fusion.2.q_ref, ...), custom_call_target="tpu_custom_call" | custom-call | flops 16106127360 | bytes 14942208 | tf_op jit(solution)/shard_map/attend_backward/pallas_call | solution.py:218
  506.3 5.2 fusion.62
  511.4 5.4 add_convert_fusion.1
  517.3 2.3 convolution_convert_fusion.9
  521.6 4.7 convolution_convert_fusion.7
  526.3 2.7 convolution_convert_fusion.8
  528.9 2.5 pad_maximum_fusion.3
  531.4 6.7 copy.108
  538.4 47.5 %reduce-scatter.13.cloned.1.call-done = bf16[512,768]{1,0:T(8,128)(2,1)} async-done(((bf16[2048,768]{1,0:T(8,128)(2,1)}), bf16[512,768]{1,0:T(8,128)(2,1)}) %reduce-scatter.13.cloned.1.call-update) | async-done | bytes 786448 | tf_op jit(solution)/shard_map/reduce_scatter | solution.py:407
  585.9 3.7 multiply_reduce_fusion
  590.3 9.0 fusion.7
  599.4 3.2 multiply_reduce_fusion.2
  603.2 3.6 convolution_convert_fusion.15.d_ref
  606.8 53.7 %attend_backward.3 = (bf16[512,768]{1,0:T(8,128)(2,1)}, bf16[2048,768]{1,0:T(8,128)(2,1)}, bf16[2048,768]{1,0:T(8,128)(2,1)}) custom-call(s32[8,16]{1,0:T(8,128)} %select_reduce_fusion.keys_at, s32[8]{0:T(128)} %get-tuple-element.116.steps_of, bf16[512,768]{1,0:T(8,128)(2,1)} %fusion.54.q_ref, bf16[2048,1536]{1,0:T(8,128)(2,1)} %fusion.k_ref.v_ref, ...), custom_call_target="tpu_custom_call" | custom-call | flops 16106127360 | bytes 14942208 | tf_op jit(solution)/shard_map/attend_backward/pallas_call | solution.py:218
  660.5 2.3 fusion.51
  664.8 2.7 fusion.52
  667.5 2.7 fusion.53
  670.3 2.5 pad_maximum_fusion.2
  672.8 6.7 copy.106
  680.9 5.2 convolution_convert_fusion.3
  686.0 5.8 convolution_convert_fusion.2
  691.9 4.2 pad_maximum_fusion.1
  696.8 5.6 convolution_convert_fusion.5
  702.4 5.8 convolution_convert_fusion.4
  708.2 4.1 pad_maximum_fusion
  712.4 5.2 fusion.59
  717.6 5.4 add_convert_fusion
  724.5 17.0 %reduce-scatter.25.cloned.1.call-done = bf16[96,3072]{1,0:T(8,128)(2,1)} async-done(((bf16[768,3072]{1,0:T(8,128)(2,1)}), bf16[96,3072]{1,0:T(8,128)(2,1)}) %reduce-scatter.25.cloned.1.call-update) | async-done | bytes 589840
  744.7 77.1 %reduce-scatter.21.cloned.1.call-done = bf16[96,6144]{1,0:T(8,128)(2,1)} async-done(((bf16[768,6144]{1,0:T(8,128)(2,1)}), bf16[96,6144]{1,0:T(8,128)(2,1)}) %reduce-scatter.21.cloned.1.call-update) | async-done | bytes 1179664 | tf_op jit(solution)/shard_map/reduce_scatter | solution.py:398
  823.9 78.2 %reduce-scatter.19.cloned.1.call-done = bf16[96,6144]{1,0:T(8,128)(2,1)} async-done(((bf16[768,6144]{1,0:T(8,128)(2,1)}), bf16[96,6144]{1,0:T(8,128)(2,1)}) %reduce-scatter.19.cloned.1.call-update) | async-done | bytes 1179664 | tf_op jit(solution)/shard_map/reduce_scatter | solution.py:398
  906.8 43.5 %all-reduce = (f32[2,768]{1,0:T(2,128)}, f32[2,768]{1,0:T(2,128)}, f32[2,768]{1,0:T(2,128)}, f32[2,768]{1,0:T(2,128)}) all-reduce(f32[2,768]{1,0:T(2,128)S(1)} %pad_maximum_fusion.7, f32[2,768]{1,0:T(2,128)S(1)} %pad_maximum_fusion.8, f32[2,768]{1,0:T(2,128)S(1)} %pad_maximum_fusion.9, ...), channel_id=1, replica_groups=mesh['dp'=8,'tensor'=4] {'dp','tensor'}, use_global_device_ids=true, to_apply=%region_34.35 | all-reduce | flops 6144 | bytes 49152 | tf_op jit(solution)/shard_map/psum | solution.py:433
  950.3 15.4 %reduce-scatter.15.cloned.1.call-done = bf16[512,768]{1,0:T(8,128)(2,1)} async-done(((bf16[2048,768]{1,0:T(8,128)(2,1)}), bf16[512,768]{1,0:T(8,128)(2,1)}) %reduce-scatter.15.cloned.1.call-update) | async-done | bytes 786448 | tf_op jit(solution)/shard_map/reduce_scatter | solution.py:407
  965.7 3.5 convert_add_fusion
  969.1 34.0 %reduce-scatter.17.cloned.1.call-done = bf16[1,2,96,4,192]{2,4,1,3,0:T(8,128)(2,1)} async-done(((bf16[4,2,96,4,192]{2,4,1,3,0:T(8,128)(2,1)}), bf16[1,2,96,4,192]{2,4,1,3,0:T(8,128)(2,1)}) %reduce-scatter.17.cloned.1.call-update) | async-done | bytes 294928 | tf_op jit(solution)/shard_map/reduce_scatter | solution.py:423
  1006.0 45.9 %reduce-scatter.23.cloned.1.call-done = bf16[1,2,96,2,768]{4,2,1,3,0:T(8,128)(2,1)} async-done(((bf16[4,2,96,2,768]{4,2,1,3,0:T(8,128)(2,1)}), bf16[1,2,96,2,768]{4,2,1,3,0:T(8,128)(2,1)}) %reduce-scatter.23.cloned.1.call-update) | async-done | bytes 589840 | tf_op jit(solution)/shard_map/reduce_scatter | solution.py:423
  (256 shorter events, 59.8 us)
Async XLA Ops:
  7.2 3.2 copy-start.13
  7.2 3.2 copy-start.14
  7.2 36.3 %all-gather.24.cloned.1.call-start = ((), (), s32[]{:S(2)}) async-start(), calls=%async_computation.20 | async-start | bytes 1474560 | tf_op jit(solution)/shard_map/all_gather | solution.py:338
  10.4 84.5 %all-gather.26.cloned.1.call-start = ((), (), s32[]{:S(2)}) async-start(), calls=%async_computation.21 | async-start | bytes 2949120 | tf_op jit(solution)/shard_map/all_gather | solution.py:338
  11.3 123.6 %all-gather.12.cloned.1.call-start = ((), (), s32[]{:S(2)}) async-start(), calls=%async_computation.8 | async-start | bytes 5308416 | tf_op jit(solution)/shard_map/all_gather | solution.py:344
  51.4 148.5 %all-gather.14.cloned.1.call-start = ((), (), s32[]{:S(2)}) async-start(), calls=%async_computation.9 | async-start | bytes 3932160 | tf_op jit(solution)/shard_map/all_gather | solution.py:299
  52.0 207.1 %all-gather.16.cloned.1.call-start = ((), (), s32[]{:S(2)}) async-start(), calls=%async_computation.10 | async-start | bytes 10616832 | tf_op jit(solution)/shard_map/all_gather | solution.py:345
  104.7 4.4 copy-start.35
  106.5 193.7 %all-gather.18.cloned.1.call-start = ((), (), s32[]{:S(2)}) async-start(), calls=%async_computation.11 | async-start | bytes 5308416 | tf_op jit(solution)/shard_map/all_gather | solution.py:344
  107.2 19.7 %copy-start.31 = (f32[2,768]{1,0:T(2,128)S(1)}, f32[2,768]{1,0:T(2,128)}, u32[]{:S(2)}) copy-start(f32[2,768]{1,0:T(2,128)} %param.19) | copy-start | bytes 18436
  107.2 19.7 %copy-start.32 = (f32[2,768]{1,0:T(2,128)S(1)}, f32[2,768]{1,0:T(2,128)}, u32[]{:S(2)}) copy-start(f32[2,768]{1,0:T(2,128)} %param.18) | copy-start | bytes 18436
  107.2 20.4 %copy-start.33 = (f32[2,768]{1,0:T(2,128)S(1)}, f32[2,768]{1,0:T(2,128)}, u32[]{:S(2)}) copy-start(f32[2,768]{1,0:T(2,128)} %param.21) | copy-start | bytes 18436
  107.2 20.4 %copy-start.34 = (f32[2,768]{1,0:T(2,128)S(1)}, f32[2,768]{1,0:T(2,128)}, u32[]{:S(2)}) copy-start(f32[2,768]{1,0:T(2,128)} %param.20) | copy-start | bytes 18436
  107.2 27.7 %copy-start.12 = (bf16[512,768]{1,0:T(8,128)(2,1)S(1)}, bf16[512,768]{1,0:T(8,128)(2,1)}, u32[]{:S(2)}) copy-start(bf16[512,768]{1,0:T(8,128)(2,1)} %param.13) | copy-start | bytes 2359300
  109.1 256.1 %all-gather.20.cloned.1.call-start = ((), (), s32[]{:S(2)}) async-start(), calls=%async_computation.12 | async-start | bytes 3932160 | tf_op jit(solution)/shard_map/all_gather | solution.py:299
  127.6 136.3 %copy-start.26 = (f32[768]{0:T(1024)}, f32[768]{0:T(1024)S(1)}, u32[]{:S(2)}) copy-start(f32[768]{0:T(1024)S(1)} %get-tuple-element.128) | copy-start | bytes 9220
  127.6 136.4 %copy-start.36 = (f32[768]{0:T(1024)}, f32[768]{0:T(1024)S(1)}, u32[]{:S(2)}) copy-start(f32[768]{0:T(1024)S(1)} %get-tuple-element.89) | copy-start | bytes 9220
  128.2 140.3 %copy-start.22 = (f32[768]{0:T(1024)}, f32[768]{0:T(1024)S(1)}, u32[]{:S(2)}) copy-start(f32[768]{0:T(1024)S(1)} %get-tuple-element.85) | copy-start | bytes 9220
  253.0 11.0 %copy-start.17 = (f32[512]{0:T(512)}, f32[512]{0:T(512)S(1)}, u32[]{:S(2)}) copy-start(f32[512]{0:T(512)S(1)} %multiply_reduce_fusion.9) | copy-start | bytes 6148
  253.0 11.0 %copy-start.29 = (f32[512]{0:T(512)}, f32[512]{0:T(512)S(1)}, u32[]{:S(2)}) copy-start(f32[512]{0:T(512)S(1)} %fusion.76) | copy-start | bytes 6148
  259.1 5.1 copy-start.43
  264.2 4.0 copy-start.53
  268.5 4.1 copy-start.19
  268.5 4.1 copy-start.15
  269.7 154.8 %all-gather.22.cloned.1.call-start = ((), (), s32[]{:S(2)}) async-start(), calls=%async_computation.13 | async-start | bytes 10616832 | tf_op jit(solution)/shard_map/all_gather | solution.py:345
  272.6 313.3 %reduce-scatter.13.cloned.1.call-start = ((), (), s32[]{:S(2)}) async-start(), calls=%async_computation.14 | async-start | bytes 3932160 | tf_op jit(solution)/shard_map/reduce_scatter | solution.py:407
  374.2 41.5 %copy-start.16 = (f32[512]{0:T(512)S(1)}, f32[512]{0:T(512)}, u32[]{:S(2)}) copy-start(f32[512]{0:T(512)} %copy-done.15) | copy-start | bytes 6148
  374.2 41.5 %copy-start.23 = (f32[768]{0:T(1024)S(1)}, f32[768]{0:T(1024)}, u32[]{:S(2)}) copy-start(f32[768]{0:T(1024)} %copy-done.22) | copy-start | bytes 9220
  415.7 8.8 copy-start.28
  415.7 8.8 copy-start.38
  424.5 5.3 copy-start.1
  424.5 6.0 copy-start.44
  430.6 7.2 copy-start.54
  430.6 4.3 copy-start.3
  437.8 6.4 copy-start.6
  444.1 3.7 copy-start.56
  506.3 5.2 copy-start.58
  516.8 206.2 %reduce-scatter.27.cloned.1.call-start = ((), (), s32[]{:S(2)}) async-start(), calls=%async_computation.23 | async-start | bytes 5308416
  517.3 2.4 copy-start.11
  517.3 2.4 copy-start.49
  521.6 4.7 copy-start.55
  538.2 51.4 %copy-start.20 = (f32[512]{0:T(512)S(1)}, f32[512]{0:T(512)}, u32[]{:S(2)}) copy-start(f32[512]{0:T(512)} %copy-done.19) | copy-start | bytes 6148
  538.2 203.3 %reduce-scatter.25.cloned.1.call-start = ((), (), s32[]{:S(2)}) async-start(), calls=%async_computation.22 | async-start | bytes 5308416
  585.9 13.4 %slice-start = ((s8[9437184]{0:T(1024)(128)(4,1)}), s8[4194304]{0:T(1024)(128)(4,1)S(1)}, s32[]{:S(2)}) async-start(s8[9437184]{0:T(1024)(128)(4,1)} %bitcast.121), calls=%async_computation.24 | async-start | bytes 8388608
  590.2 9.1 copy-start.8
  590.2 9.1 copy-start.27
  590.2 9.1 copy-start.30
  590.2 9.1 slice-start.1
  590.2 9.1 slice-start.2
  599.3 3.2 copy-start.57
  599.4 3.2 copy-start.18
  603.2 59.6 %copy-start.4 = (f32[512,768]{1,0:T(8,128)}, f32[512,768]{1,0:T(8,128)S(1)}, u32[]{:S(2)}) copy-start(f32[512,768]{1,0:T(8,128)S(1)} %get-tuple-element.97) | copy-start | bytes 4718596
  660.5 3.3 copy-start.52
  664.8 2.7 copy-start.50
  679.5 142.2 %reduce-scatter.21.cloned.1.call-start = ((), (), s32[]{:S(2)}) async-start(), calls=%async_computation.18 | async-start | bytes 10616832 | tf_op jit(solution)/shard_map/reduce_scatter | solution.py:398
  680.9 5.2 copy-start.7
  696.1 6.3 copy-start.9
  696.1 206.0 %reduce-scatter.19.cloned.1.call-start = ((), (), s32[]{:S(2)}) async-start(), calls=%async_computation.17 | async-start | bytes 10616832 | tf_op jit(solution)/shard_map/reduce_scatter | solution.py:398
  712.4 5.2 copy-start.51
  712.4 253.3 %reduce-scatter.15.cloned.1.call-start = ((), (), s32[]{:S(2)}) async-start(), calls=%async_computation.15 | async-start | bytes 3932160 | tf_op jit(solution)/shard_map/reduce_scatter | solution.py:407
  723.0 280.2 %reduce-scatter.17.cloned.1.call-start = ((), (), s32[]{:S(2)}) async-start(), calls=%async_computation.16 | async-start | bytes 1966080 | tf_op jit(solution)/shard_map/reduce_scatter | solution.py:423
  744.6 307.3 %reduce-scatter.23.cloned.1.call-start = ((), (), s32[]{:S(2)}) async-start(), calls=%async_computation.19 | async-start | bytes 2949120 | tf_op jit(solution)/shard_map/reduce_scatter | solution.py:423
  905.9 59.7 %copy-start.5 = (f32[512,768]{1,0:T(8,128)S(1)}, f32[512,768]{1,0:T(8,128)}, u32[]{:S(2)}) copy-start(f32[512,768]{1,0:T(8,128)} %copy-done.4) | copy-start | bytes 4718596
  906.0 59.7 %copy-start.47 = (bf16[512,768]{1,0:T(8,128)(2,1)S(1)}, bf16[512,768]{1,0:T(8,128)(2,1)}, u32[]{:S(2)}) copy-start(bf16[512,768]{1,0:T(8,128)(2,1)} %get-tuple-element.27) | copy-start | bytes 2359300
  (14 other events, 19.3 us)
Sparse Core Ops, SparseCore 0:
  10.5 32.9 all-gather.23
  45.6 49.1 all-gather.25
  97.3 37.5 all-gather.11
  136.3 63.4 all-gather.13
  201.6 57.3 all-gather.15
  261.4 38.7 all-gather.17
  301.7 63.4 all-gather.19
  367.1 57.4 all-gather.21
  516.9 68.8 reduce-scatter.12
  589.2 53.6 reduce-scatter.26
  679.6 61.8 reduce-scatter.24
  744.9 76.8 reduce-scatter.20
  825.2 76.8 reduce-scatter.18
  904.2 61.3 reduce-scatter.14
  967.8 35.3 reduce-scatter.16
  1005.3 46.5 reduce-scatter.22

commit v2 on v1

--- a/solution.py
+++ b/solution.py
@@ -13,6 +13,10 @@
 WIDE = QUAD * HD
 STEP = 4
 STEPS = LONGEST // STEP
+
+ROW = 2
+DATA = ("hi", "row", "quad")
+EVERY = DATA + ("tensor",)
 
 NORM_EPSILON = 1e-12
 MASK_VALUE = -1e30
@@ -295,8 +299,18 @@
     return keys_at, steps_of, bias_rows, bias_cols
 
 
-def gather_tensor(shard):
-    return lax.all_gather(shard, "tensor", axis=0, tiled=True)
+def to_home(steps, parts):
+    pairs = []
+    for hi in range(steps):
+        for row in range(ROW):
+            for quad in range(QUAD):
+                side, core = quad // 2, quad % 2
+                plane = parts - 1 - side if core else side
+                for part in range(parts):
+                    source = ((hi * ROW + row) * QUAD + quad) * parts + part
+                    target = ((hi * ROW + row) * QUAD + part) * parts + plane
+                    pairs.append((source, target))
+    return pairs
 
 
 def local(
@@ -316,41 +330,63 @@
 ):
     own_rows, width = layer_input.shape
     tensor = lax.axis_size("tensor")
-    slot = lax.axis_index("tensor")
+    slot = lax.axis_index("quad")
+    plane = lax.axis_index("tensor")
     head_local = random_blocks.shape[1]
     chunk = head_local * HD
     depth = w_qkv.shape[1]
     hidden = w_up.shape[2]
     score_scale = HD ** (-0.5)
-
-    attn_shards = jnp.concatenate(
-        [
-            w_qkv.reshape(LAYERS, depth, head_local, 3, HD)
-            .transpose(0, 1, 3, 2, 4)
-            .reshape(LAYERS, depth, 3 * chunk),
-            w_out.transpose(0, 2, 1),
-        ],
-        axis=2,
-    )
-    ffn_shards = jnp.concatenate([w_up, w_down.transpose(0, 2, 1)], axis=2)
-
-    def spread(shards, pieces):
-        gathered = lax.all_gather(shards, "tensor", axis=0)
-        gathered = gathered.reshape(tensor, LAYERS, depth, pieces, -1)
-        return gathered.transpose(1, 2, 3, 0, 4).reshape(LAYERS, depth, -1)
-
-    attn_rows = spread(attn_shards, 4)
-    ffn_rows = spread(ffn_shards, 2)
-    attn_full = [lax.all_gather(attn_rows[l], "dp", axis=0, tiled=True) for l in range(LAYERS)]
-    ffn_full = [lax.all_gather(ffn_rows[l], "dp", axis=0, tiled=True) for l in range(LAYERS)]
+    moves = to_home(lax.axis_size("hi"), tensor)
+    moves_back = [(b, a) for a, b in moves]
+
+    def shifted(x, by):
+        return lax.ppermute(x, "tensor", [(i, (i + by) % tensor) for i in range(tensor)])
+
+    def spread(shard):
+        return [shard] + [shifted(shard, by) for by in range(1, tensor)]
+
+    def attn_rows(qkv, back):
+        qkv = qkv.reshape(depth, head_local, 3, HD).transpose(0, 2, 1, 3)
+        shard = jnp.concatenate([qkv.reshape(depth, 3 * chunk), back.T], axis=1)
+        parts = spread(shard)
+        return jnp.concatenate(
+            [part[:, p * chunk : (p + 1) * chunk] for p in range(4) for part in parts], axis=1
+        )
+
+    def ffn_rows(up, down):
+        parts = spread(jnp.concatenate([up, down.T], axis=1))
+        return jnp.concatenate(
+            [part[:, p * hidden : (p + 1) * hidden] for p in range(2) for part in parts], axis=1
+        )
+
+    def over_data(rows):
+        return lax.all_gather(rows, DATA, axis=0, tiled=True)
 
     random_all = lax.all_gather(random_blocks[0], "tensor", axis=0, tiled=True)
+    own_tokens = lax.ppermute(layer_input, EVERY, moves)
+    docs, group_blocks = doc_lengths.shape[1], block_deal.shape[1]
+    numbers = jnp.concatenate([doc_lengths[0], block_deal[0], random_all.reshape(-1)])
+    numbers = lax.ppermute(numbers, EVERY, moves)
+    attn_full = [over_data(attn_rows(w_qkv[0], w_out[0]))]
+    own_tokens, up_0, down_0 = lax.optimization_barrier((own_tokens, w_up[0], w_down[0]))
+    ffn_full = [over_data(ffn_rows(up_0, down_0))]
+
+    random_home = numbers[docs + group_blocks :].reshape(tensor, head_local, group_blocks, -1)
+    part_of = (plane - jnp.arange(tensor, dtype=jnp.int32)) % tensor
+    part_pick = (part_of[:, None] == jnp.arange(tensor, dtype=jnp.int32)[None, :]).astype(jnp.int32)
+    random_home = jnp.sum(part_pick[:, :, None, None, None] * random_home[None], axis=1)
+    random_home = random_home.reshape(tensor * head_local, group_blocks, -1)
     own_blocks = own_rows // BLK
     tables = attention_tables(
-        doc_lengths[0], block_deal[0], random_all, own_blocks, slot * own_blocks
-    )
-
-    stream = layer_input.astype(F32)
+        numbers[:docs],
+        numbers[docs : docs + group_blocks],
+        random_home,
+        own_blocks,
+        slot * own_blocks,
+    )
+
+    stream = own_tokens.astype(F32)
     stored = []
     for layer in range(LAYERS):
         attn_w, ffn_w = attn_full[layer], ffn_full[layer]
@@ -360,9 +396,15 @@
         w_expand = ffn_w[:, : hidden * tensor]
         w_shrink_t = ffn_w[:, hidden * tensor :]
         own_inputs = stream.astype(BF)
-        inputs = gather_tensor(own_inputs)
+        inputs = lax.all_gather(own_inputs, "quad", axis=0, tiled=True)
         query = (dot(own_inputs, w_query).astype(BF).astype(F32) * score_scale).astype(BF)
         keyval = dot(inputs, w_keyval).astype(BF)
+        if layer == 0:
+            query, later = lax.optimization_barrier((query, (out_grad, w_qkv, w_out, w_up, w_down)))
+            for other in range(1, LAYERS):
+                attn_full.append(over_data(attn_rows(later[1][other], later[2][other])))
+                ffn_full.append(over_data(ffn_rows(later[3][other], later[4][other])))
+            own_grad = lax.ppermute(later[0], EVERY, moves)
         mixed, logs = attend_forward(query, keyval, tables)
         summed_one = stream + dot_right_t(mixed, w_back_t)
         normed = layer_norm(summed_one, attn_gain[layer], attn_shift[layer])
@@ -374,8 +416,21 @@
             (own_inputs, inputs, query, keyval, mixed, logs, summed_one, ffn_in, pre_act, activated, summed_two)
         )
         stream = layer_norm(summed_two, ffn_gain[layer], ffn_shift[layer])
-
-    state_grad = out_grad.astype(F32)
+    layer_output = lax.ppermute(stream.astype(BF), EVERY, moves_back)
+
+    def sum_parts(rows, pieces):
+        parts = rows.reshape(depth, pieces, tensor, -1)
+        total = parts[:, :, 0].astype(F32)
+        for by in range(1, tensor):
+            total = total + shifted(parts[:, :, by].reshape(depth, -1), tensor - by).reshape(
+                depth, pieces, -1
+            ).astype(F32)
+        return total
+
+    def sum_data(part):
+        return lax.psum_scatter(part, DATA, scatter_dimension=0, tiled=True)
+
+    state_grad = own_grad.astype(F32)
     attn_grads = [None] * LAYERS
     ffn_grads = [None] * LAYERS
     norm_parts = [None] * LAYERS
@@ -395,75 +450,89 @@
         d_pre = gelu_back(dot(d_two_low, w_shrink_t))[0].astype(BF)
         expand_grad = dot_left_t(ffn_in, d_pre)
         ffn_part = jnp.concatenate([expand_grad.astype(BF), shrink_grad_t.astype(BF)], axis=1)
-        ffn_grads[layer] = lax.psum_scatter(ffn_part, "dp", scatter_dimension=0, tiled=True)
+        d_pre, ffn_part = lax.optimization_barrier((d_pre, ffn_part))
+        ffn_sum = sum_data(ffn_part)
         d_normed = d_two + dot_right_t(d_pre, w_expand)
         unused_one, attn_back = jax.vjp(layer_norm, summed_one, attn_gain[layer], attn_shift[layer])
         d_one, attn_gain_part, attn_shift_part = attn_back(d_normed)
         d_one_low = d_one.astype(BF)
-        back_grad_t = dot_left_t(d_one_low, mixed)
         d_mixed = dot(d_one_low, w_back_t).astype(BF)
+        if layer < LAYERS - 1:
+            d_mixed, attn_sum, ffn_grads[layer + 1] = lax.optimization_barrier(
+                (d_mixed, attn_sum, ffn_grads[layer + 1])
+            )
+            attn_grads[layer + 1] = sum_parts(attn_sum, 4)
         d_query, d_key, d_value = attend_backward(query, keyval, logs, d_mixed, tables)
+        (d_query, d_key, d_value), ffn_sum, attn_grads, layer_output = lax.optimization_barrier(
+            ((d_query, d_key, d_value), ffn_sum, attn_grads, layer_output)
+        )
+        ffn_grads[layer] = sum_parts(ffn_sum, 2)
         others = dot_right_t(d_key, w_keyval[:, :width]) + dot_right_t(d_value, w_keyval[:, width:])
-        summed = lax.psum_scatter(others.astype(BF), "tensor", scatter_dimension=0, tiled=True)
+        others = others.astype(BF)
+        d_query, d_key, d_value, others = lax.optimization_barrier((d_query, d_key, d_value, others))
+        summed = lax.psum_scatter(others, "quad", scatter_dimension=0, tiled=True)
         attn_part = jnp.concatenate(
             [
                 dot_left_t(own_inputs, d_query).astype(BF),
                 dot_left_t(inputs, d_key).astype(BF),
                 dot_left_t(inputs, d_value).astype(BF),
-                back_grad_t.astype(BF),
+                dot_left_t(d_one_low, mixed).astype(BF),
             ],
             axis=1,
         )
-        attn_grads[layer] = lax.psum_scatter(attn_part, "dp", scatter_dimension=0, tiled=True)
+        summed, attn_part = lax.optimization_barrier((summed, attn_part))
+        attn_sum = sum_data(attn_part)
         state_grad = d_one + dot_right_t(d_query, w_query) + summed.astype(F32)
         norm_parts[layer] = (attn_gain_part, attn_shift_part, ffn_gain_part, ffn_shift_part)
-
-    def collect(parts, pieces):
-        grads = jnp.stack(parts).reshape(LAYERS, depth, pieces, tensor, -1).transpose(3, 0, 1, 2, 4)
-        own = lax.psum_scatter(grads, "tensor", scatter_dimension=0, tiled=False)
-        return own.astype(F32)
-
-    attn_own = collect(attn_grads, 4)
-    ffn_own = collect(ffn_grads, 2)
+    norm_sums = lax.psum(
+        tuple(jnp.stack([norm_parts[l][k] for l in range(LAYERS)]) for k in range(4)), EVERY
+    )
+    attn_sum, ffn_grads, norm_sums = lax.optimization_barrier((attn_sum, ffn_grads, norm_sums))
+    attn_grads[0] = sum_parts(attn_sum, 4)
+    input_grad = lax.ppermute(state_grad.astype(BF), EVERY, moves_back).astype(F32)
+
+    attn_own = jnp.stack(attn_grads)
+    ffn_own = jnp.stack(ffn_grads)
     qkv_grad = attn_own[:, :, :3].reshape(LAYERS, depth, 3, head_local, HD)
     qkv_grad = qkv_grad.transpose(0, 1, 3, 2, 4).reshape(LAYERS, depth, 3 * chunk)
     out_w_grad = attn_own[:, :, 3].transpose(0, 2, 1)
     up_grad = ffn_own[:, :, 0]
     down_grad = ffn_own[:, :, 1].transpose(0, 2, 1)
-    norm_sums = lax.psum(
-        tuple(jnp.stack([norm_parts[l][k] for l in range(LAYERS)]) for k in range(4)),
-        ("dp", "tensor"),
-    )
-    return (stream.astype(BF), state_grad, qkv_grad, out_w_grad, up_grad, down_grad) + tuple(norm_sums)
+    return (layer_output, input_grad, qkv_grad, out_w_grad, up_grad, down_grad) + tuple(norm_sums)
 
 
 def solution(mesh):
+    devices = mesh.devices
+    tensor = devices.shape[1]
+    split = jax.sharding.Mesh(
+        devices.reshape(devices.shape[0] // (ROW * QUAD), ROW, QUAD, tensor), EVERY
+    )
     placed = (
-        P(("dp", "tensor"), None),
-        P(None, "dp", "tensor"),
-        P(None, "tensor", "dp"),
-        P(None, "dp", "tensor"),
-        P(None, "tensor", "dp"),
+        P(EVERY, None),
+        P(None, DATA, "tensor"),
+        P(None, "tensor", DATA),
+        P(None, DATA, "tensor"),
+        P(None, "tensor", DATA),
         P(),
         P(),
         P(),
         P(),
-        P(("dp", "tensor"), None),
-        P("dp", None),
-        P("dp", None),
-        P("dp", "tensor", None, None),
+        P(EVERY, None),
+        P(DATA, None),
+        P(DATA, None),
+        P(DATA, "tensor", None, None),
     )
     return jax.shard_map(
         local,
-        mesh=mesh,
+        mesh=split,
         in_specs=placed,
         out_specs=(
-            P(("dp", "tensor"), None),
-            P(("dp", "tensor"), None),
-            P(None, "dp", "tensor"),
-            P(None, "tensor", "dp"),
-            P(None, "dp", "tensor"),
-            P(None, "tensor", "dp"),
+            P(EVERY, None),
+            P(EVERY, None),
+            P(None, DATA, "tensor"),
+            P(None, "tensor", DATA),
+            P(None, DATA, "tensor"),
+            P(None, "tensor", DATA),
             P(),
             P(),
             P(),

time: 1080 us -> 833 us (0.77); the launches traced: 1060 us -> 825 us
  waiting for transfers between devices: 545 us -> 162 us
  starting transfers between devices: 11.1 us -> 92.1 us
  blocking collectives: 56.7 us -> 87.9 us
  Pallas kernels: 190 us -> 209 us
    reduce_scatter x6 -> x4, waiting for transfers between devices: 298 us -> 49.2 us  [the longest x2 49.1 us: local(): summed = lax.psum_scatter(others, 'quad', scatter_dimension=0, tiled=True)]
    all_gather x8 -> x6, waiting for transfers between devices: 229 us -> 16.2 us  [the longest x4 16.1 us: over_data(): return lax.all_gather(rows, DATA, axis=0, tiled=True)]
    ppermute x0 -> x29, waiting for transfers between devices: none -> 96.3 us  [the longest x24 96.3 us: shifted(): lax.ppermute(x, 'tensor', [(i, (i + by) % tensor) for i in range(tensor)])]
    ppermute x0 -> x29, starting transfers between devices: none -> 91.4 us  [the longest x24 66.8 us: shifted(): lax.ppermute(x, 'tensor', [(i, (i + by) % tensor) for i in range(tensor)])]
    psum x1, blocking collectives: 43.5 us -> 70.3 us  [local(): lax.psum(tuple((jnp.stack([norm_parts[l][k] for l in range(LAYERS)]) for...]
    unnamed x18 -> x14, waiting for transfers between devices: 17.8 us -> 0.2 us
    pallas_call x2, Pallas kernels: 107 us -> 119 us  [attend_backward(): pl.pallas_call(backward_kernel, grid_spec=pltpu.PrefetchScalarGridSpec(nu...]
    dot_general x12, matrix products: 47.8 us -> 59.7 us  [dot_right_t(): lax.dot_general(left, right, (((1,), (1,)), ((), ())), preferred_element_...]
  transfers between devices with their start and end apart: 16 -> 41, of which waited for: 15 -> 15; matrix products, arithmetic and copies ran while one was open for 18% -> 22% of each run, Pallas kernels for 13% -> 25%
where the time goes in v2:
time: 833 us; the launch traced here: 825 us
  Pallas kernels  209 us (25%)
  waiting for transfers between devices  162 us (19%)
  matrix products  151 us (18%)
  starting transfers between devices  92.1 us (11%)
  blocking collectives  87.9 us (11%)
  local copies, waits for them, and re-layouts  71.3 us (9%)
  other arithmetic  35.3 us (4%)
  between operations  16.5 us (2%)
    pallas_call x2, Pallas kernels, attend_backward(): pl.pallas_call(backward_kernel, grid_spec=pltpu.PrefetchScalarGridSpec(nu...  119 us
    ppermute x24, waiting for transfers between devices, shifted(): lax.ppermute(x, 'tensor', [(i, (i + by) % tensor) for i in range(tensor)])  96.3 us
    pallas_call x2, Pallas kernels, attend_forward(): pl.pallas_call(forward_kernel, grid_spec=pltpu.PrefetchScalarGridSpec(num...  90.2 us
    psum x1, blocking collectives, local(): lax.psum(tuple((jnp.stack([norm_parts[l][k] for l in range(LAYERS)]) for...  70.3 us
    ppermute x24, starting transfers between devices, shifted(): lax.ppermute(x, 'tensor', [(i, (i + by) % tensor) for i in range(tensor)])  66.8 us
    dot_general x12, matrix products, dot_right_t(): lax.dot_general(left, right, (((1,), (1,)), ((), ())), preferred_element_...  59.7 us
    dot_general x10, matrix products, dot(): return jnp.dot(left, right, preferred_element_type=F32)  56.8 us
    reduce_scatter x2, waiting for transfers between devices, local(): summed = lax.psum_scatter(others, 'quad', scatter_dimension=0, tiled=True)  49.1 us
  transfers between devices with their start and end apart: 41, of which 15 were waited for; matrix products, arithmetic and copies ran while one was open for 22% of the time, Pallas kernels for 25%

profile of v2, /device:TPU:0, one launch (start us, length us, event | category | flops | bytes accessed | tf_op | source)
XLA Modules:
  0.0 825.2 jit_solution(2771889193958751279)
XLA Ops:
  9.2 3.1 collective-permute-start.2
  16.2 4.0 collective-permute-done.2
  20.2 7.6 collective-permute-done.3
  31.0 34.5 %collective-permute-start.6 = (bf16[96,1536]{1,0:T(8,128)(2,1)S(1)}, bf16[96,1536]{1,0:T(8,128)(2,1)S(1)}, u32[]{:S(2)}, u32[]{:S(2)}) collective-permute-start(bf16[96,1536]{1,0:T(8,128)(2,1)S(1)} %pad_maximum_fusion.5), channel_id=1, source_target_pairs={{0,1},{1,2},{2,3},{3,0},{4,5},{5,6},{6,7},{7,4},{8,9},{9,10},{10,1... | collective-permute-start | bytes 884744 | tf_op jit(solution)/shard_map/ppermute | solution.py:344
  68.0 4.9 collective-permute-done.6
  72.9 12.5 %collective-permute-done.7 = bf16[96,1536]{1,0:T(8,128)(2,1)S(1)} collective-permute-done((bf16[96,1536]{1,0:T(8,128)(2,1)S(1)}, bf16[96,1536]{1,0:T(8,128)(2,1)S(1)}, u32[]{:S(2)}, u32[]{:S(2)}) %collective-permute-start.7) | collective-permute-done | bytes 294944 | tf_op jit(solution)/shard_map/ppermute | solution.py:344
  86.7 17.6 %all-gather = s32[1,12,32,3]{2,0,3,1:T(1,128)S(1)} all-gather(s32[1,3,32,3]{2,0,3,1:T(1,128)S(1)} %copy-done.57), channel_id=2, replica_groups=mesh['hi'=1,'row'=2,'quad'=4,'tensor'=4] {'tensor'}, dimensions={1}, use_global_device_ids=true | all-gather | bytes 5760 | tf_op jit(solution)/shard_map/all_gather | solution.py:366
  106.8 3.0 multiply_convert_fusion.3.q_ref
  110.1 3.3 collective-permute-start.9
  115.9 3.1 collective-permute-done.9
  119.0 10.5 %collective-permute-done.10 = bf16[96,768]{0,1:T(8,128)(2,1)S(1)} collective-permute-done((bf16[96,768]{0,1:T(8,128)(2,1)S(1)}, bf16[96,768]{0,1:T(8,128)(2,1)S(1)}, u32[]{:S(2)}, u32[]{:S(2)}) %collective-permute-start.10) | collective-permute-done | bytes 147488 | tf_op jit(solution)/shard_map/ppermute | solution.py:344
  137.8 9.0 %convolution_convert_fusion.1.k_ref.v_ref = bf16[2048,1536]{1,0:T(8,128)(2,1)} fusion(bf16[2048,768]{1,0:T(8,128)(2,1)} %all-gather.10.cloned.1.call-done, bf16[768,3072]{1,0:T(8,128)(2,1)} %all-gather.8.cloned.1.call-done), kind=kOutput, calls=%fused_computation.7 | convolution fusion | flops 4834983936 | bytes 11796480 | tf_op jit(solution)/shard_map/dot_general | solution.py:39
  146.8 45.1 %attend_forward.2 = (bf16[512,768]{1,0:T(8,128)(2,1)}, f32[8,1,768]{2,1,0:T(1,128)}) custom-call(s32[8,16]{1,0:T(8,128)} %select_reduce_fusion.keys_at, s32[8]{0:T(128)} %get-tuple-element.230.steps_of, bf16[512,768]{1,0:T(8,128)(2,1)} %multiply_convert_fusion.3.q_ref, bf16[2048,1536]{1,0:T(8,128)(2,1)} %convolution_convert_fusion.1.k_ref.v_ref, ...), custom_call_target="tpu_custom_call" | custom-call | flops 6442450944 | bytes 7864320 | tf_op jit(solution)/shard_map/attend_forward/pallas_call | solution.py:181
  194.6 4.9 fusion.28
  200.5 4.7 fusion.98
  209.9 3.0 collective-permute-start.14
  212.9 7.3 collective-permute-done.12
  220.8 10.3 %collective-permute-done.13 = bf16[96,1536]{1,0:T(8,128)(2,1)S(1)} collective-permute-done((bf16[96,1536]{1,0:T(8,128)(2,1)S(1)}, bf16[96,1536]{1,0:T(8,128)(2,1)S(1)}, u32[]{:S(2)}, u32[]{:S(2)}) %collective-permute-start.13) | collective-permute-done | bytes 294944 | tf_op jit(solution)/shard_map/ppermute | solution.py:344
  235.3 7.8 collective-permute-start.5
  243.1 3.2 multiply_convert_fusion.2.q_ref
  246.3 9.1 %convolution_convert_fusion.k_ref.v_ref = bf16[2048,1536]{1,0:T(8,128)(2,1)} fusion(bf16[2048,768]{1,0:T(8,128)(2,1)} %all-gather.16.cloned.1.call-done, bf16[768,3072]{1,0:T(8,128)(2,1)} %all-gather.14.cloned.1.call-done), kind=kOutput, calls=%fused_computation.6 | convolution fusion | flops 4834983936 | bytes 11796480 | tf_op jit(solution)/shard_map/dot_general | solution.py:39
  255.5 45.1 %attend_forward.3 = (bf16[512,768]{1,0:T(8,128)(2,1)}, f32[8,1,768]{2,1,0:T(1,128)}) custom-call(s32[8,16]{1,0:T(8,128)} %select_reduce_fusion.keys_at, s32[8]{0:T(128)} %get-tuple-element.230.steps_of, bf16[512,768]{1,0:T(8,128)(2,1)} %multiply_convert_fusion.2.q_ref, bf16[2048,1536]{1,0:T(8,128)(2,1)} %convolution_convert_fusion.k_ref.v_ref, ...), custom_call_target="tpu_custom_call" | custom-call | flops 6442450944 | bytes 7864320 | tf_op jit(solution)/shard_map/attend_forward/pallas_call | solution.py:181
  304.5 16.1 %all-gather.18.cloned.1.call-done = bf16[768,6144]{1,0:T(8,128)(2,1)} async-done(((bf16[96,6144]{1,0:T(8,128)(2,1)}), bf16[768,6144]{1,0:T(8,128)(2,1)}) %all-gather.18.cloned.1.call-update) | async-done | bytes 9437200 | tf_op jit(solution)/shard_map/all_gather | solution.py:364
  320.6 5.3 fusion.20
  326.6 4.0 fusion.100
  333.4 2.7 fusion.94
  336.2 3.3 convolution_convert_fusion.4
  339.5 6.3 fusion.13
  345.8 3.4 convolution_convert_fusion.5
  349.2 4.0 pad_maximum_fusion
  358.0 7.9 collective-permute-start.15
  365.9 9.4 %multiply_reduce_fusion.1 = (f32[768]{0:T(1024)S(1)}, f32[512]{0:T(512)S(1)}, f32[768]{0:T(1024)}, f32[512,768]{1,0:T(8,128)S(1)}) fusion(f32[512,768]{1,0:T(8,128)} %copy-done, f32[512]{0:T(512)S(1)} %copy-done.46, f32[512]{0:T(512)S(1)} %copy-done.28, f32[768]{0:T(1024)S(1)} %copy-done.42, bf16[512,3072]{1,0:T(8,128)(2,1)} %copy-done.79, ...), kind=kOutput, calls=%fused_computation.62 | convolution fusion | flops 2419849216 | bytes 12600320 | tf_op jit(solution)/shard_map/dot_general | solution.py:43
  376.0 3.6 convolution_convert_fusion.15.d_ref
  379.6 59.6 %attend_backward.2 = (bf16[512,768]{1,0:T(8,128)(2,1)}, bf16[2048,768]{1,0:T(8,128)(2,1)}, bf16[2048,768]{1,0:T(8,128)(2,1)}) custom-call(s32[8,16]{1,0:T(8,128)} %select_reduce_fusion.keys_at, s32[8]{0:T(128)} %get-tuple-element.230.steps_of, bf16[512,768]{1,0:T(8,128)(2,1)} %multiply_convert_fusion.2.q_ref, ...), custom_call_target="tpu_custom_call" | custom-call | flops 16106127360 | bytes 14942208 | tf_op jit(solution)/shard_map/attend_backward/pallas_call | solution.py:222
  439.2 5.2 fusion.56
  444.4 5.4 add_convert_fusion.1
  454.4 4.7 convolution_convert_fusion.12
  461.8 3.0 pad_maximum_fusion.2
  464.8 22.4 %reduce-scatter.13.cloned.1.call-done = bf16[512,768]{1,0:T(8,128)(2,1)} async-done(((bf16[2048,768]{1,0:T(8,128)(2,1)}), bf16[512,768]{1,0:T(8,128)(2,1)}) %reduce-scatter.13.cloned.1.call-update) | async-done | bytes 786448 | tf_op jit(solution)/shard_map/reduce_scatter | solution.py:473
  487.2 6.7 copy.143
  494.6 3.6 multiply_reduce_fusion
  498.9 9.4 %fusion.6 = bf16[512,3072]{1,0:T(8,128)(2,1)S(1)} fusion(f32[512,3072]{1,0:T(8,128)} %copy-done.75, bf16[768,6144]{1,0:T(8,128)(2,1)} %all-gather.12.cloned.1.call-done, f32[512,768]{1,0:T(8,128)S(1)} %get-tuple-element.207, f32[512]{0:T(512)S(1)} %negate_multiply_fusion.1), kind=kOutput, calls=%fused_computation.14 | convolution fusion | flops 2448162816 | bytes 15730688 | tf_op jit(solution)/shard_map/dot_general | solution.py:39
  510.1 3.4 convolution_convert_fusion.3
  513.5 3.3 convolution_convert_fusion.2
  516.8 4.1 pad_maximum_fusion.1
  523.1 5.1 slice_reduce_fusion.5
  528.2 3.3 collective-permute-start.16
  533.4 5.5 collective-permute-done.16
  539.3 17.4 %collective-permute-done.17 = bf16[96,1536]{1,0:T(8,128)(2,1)S(1)} collective-permute-done((bf16[96,1536]{1,0:T(8,128)(2,1)S(1)}, bf16[96,1536]{1,0:T(8,128)(2,1)S(1)}, u32[]{:S(2)}, u32[]{:S(2)}) %collective-permute-start.17) | collective-permute-done | bytes 294944 | tf_op jit(solution)/shard_map/ppermute | solution.py:344
  558.4 2.8 fusion.75
  561.2 8.6 %multiply_reduce_fusion.2 = (f32[768]{0:T(1024)S(1)}, f32[512]{0:T(512)S(1)}, f32[768]{0:T(1024)}, f32[512,768]{1,0:T(8,128)S(1)}) fusion(f32[512,768]{1,0:T(8,128)S(1)} %get-tuple-element.232, f32[512]{0:T(512)S(1)} %copy-done.44, f32[512]{0:T(512)S(1)} %copy-done.24, f32[768]{0:T(1024)S(1)} %copy-done.40, bf16[512,3072]{1,0:T(8,128)(2,1)} %copy-done.78, ...), kind=kOutput, calls=%fused_computation.63 | convolution fusion | flops 2419849216 | bytes 12600320 | tf_op jit(solution)/shard_map/dot_general | solution.py:43
  570.5 3.0 convolution_convert_fusion.14.d_ref
  579.3 59.6 %attend_backward.3 = (bf16[512,768]{1,0:T(8,128)(2,1)}, bf16[2048,768]{1,0:T(8,128)(2,1)}, bf16[2048,768]{1,0:T(8,128)(2,1)}) custom-call(s32[8,16]{1,0:T(8,128)} %select_reduce_fusion.keys_at, s32[8]{0:T(128)} %get-tuple-element.230.steps_of, bf16[512,768]{1,0:T(8,128)(2,1)} %multiply_convert_fusion.3.q_ref, ...), custom_call_target="tpu_custom_call" | custom-call | flops 16106127360 | bytes 14942208 | tf_op jit(solution)/shard_map/attend_backward/pallas_call | solution.py:222
  639.1 5.2 fusion.54
  644.2 5.4 add_convert_fusion
  654.3 4.7 convolution_convert_fusion.7
  661.6 2.8 pad_maximum_fusion.3
  664.4 26.7 %reduce-scatter.17.cloned.1.call-done = bf16[512,768]{1,0:T(8,128)(2,1)} async-done(((bf16[2048,768]{1,0:T(8,128)(2,1)}), bf16[512,768]{1,0:T(8,128)(2,1)}) %reduce-scatter.17.cloned.1.call-update) | async-done | bytes 786448 | tf_op jit(solution)/shard_map/reduce_scatter | solution.py:473
  691.2 6.6 copy.145
  700.6 3.4 add_convert_fusion.2
  704.0 7.5 collective-permute-start.22
  711.5 5.1 slice_reduce_fusion.2
  719.6 70.3 %all-reduce = (f32[2,768]{1,0:T(2,128)}, f32[2,768]{1,0:T(2,128)}, f32[2,768]{1,0:T(2,128)}, f32[2,768]{1,0:T(2,128)}) all-reduce(f32[2,768]{1,0:T(2,128)S(1)} %pad_maximum_fusion.10, f32[2,768]{1,0:T(2,128)S(1)} %pad_maximum_fusion.11, ...), channel_id=1, replica_groups=mesh['hi'=1,'row'=2,'quad'=4,'tensor'=4] {'hi','row','quad','tensor'}, use_global_device_ids=true, to_apply=%region_33.34 | all-reduce | flops 6144 | bytes 49152 | tf_op jit(solution)/shard_map/psum | solution.py:487
  802.8 11.1 %collective-permute-done.27 = bf16[96,768]{0,1:T(8,128)(2,1)S(1)} collective-permute-done((bf16[96,768]{0,1:T(8,128)(2,1)S(1)}, bf16[96,768]{0,1:T(8,128)(2,1)S(1)}, u32[]{:S(2)}, u32[]{:S(2)}) %collective-permute-start.27) | collective-permute-done | bytes 147488 | tf_op jit(solution)/shard_map/ppermute | solution.py:344
  (425 shorter events, 104.5 us)
Async XLA Ops:
  7.2 20.8 %copy-start.18 = (bf16[2,192,96]{2,1,0:T(8,128)(2,1)S(1)}, bf16[2,192,96]{2,1,0:T(8,128)(2,1)}, u32[]{:S(2)}) copy-start(bf16[2,192,96]{2,1,0:T(8,128)(2,1)} %param.15) | copy-start | bytes 221188
  7.2 99.6 %all-gather.8.cloned.1.call-start = ((), (), s32[]{:S(2)}) async-start(), calls=%async_computation.6 | async-start | bytes 5308416 | tf_op jit(solution)/shard_map/all_gather | solution.py:364
  9.2 11.0 %collective-permute-start.2 = (bf16[96,768]{0,1:T(8,128)(2,1)S(1)}, bf16[96,768]{0,1:T(8,128)(2,1)S(1)}, u32[]{:S(2)}, u32[]{:S(2)}) collective-permute-start(bf16[96,768]{0,1:T(8,128)(2,1)S(1)} %pad_maximum_fusion.8), channel_id=1, source_target_pairs={{0,1},{1,2},{2,3},{3,0},{4,5},{5,6},{6,7},{7,4},{8,9},{9,10},{10,1... | collective-permute-start | bytes 442376 | tf_op jit(solution)/shard_map/ppermute | solution.py:344
  12.3 15.5 %collective-permute-start.3 = (bf16[96,768]{0,1:T(8,128)(2,1)S(1)}, bf16[96,768]{0,1:T(8,128)(2,1)S(1)}, u32[]{:S(2)}, u32[]{:S(2)}) collective-permute-start(bf16[96,768]{0,1:T(8,128)(2,1)S(1)} %pad_maximum_fusion.8), channel_id=1, source_target_pairs={{0,2},{1,3},{2,0},{3,1},{4,6},{5,7},{6,4},{7,5},{8,10},{9,11},{10,... | collective-permute-start | bytes 442376 | tf_op jit(solution)/shard_map/ppermute | solution.py:344
  14.9 12.9 %collective-permute-start.4 = (bf16[96,768]{0,1:T(8,128)(2,1)S(1)}, bf16[96,768]{0,1:T(8,128)(2,1)S(1)}, u32[]{:S(2)}, u32[]{:S(2)}) collective-permute-start(bf16[96,768]{0,1:T(8,128)(2,1)S(1)} %pad_maximum_fusion.8), channel_id=1, source_target_pairs={{0,3},{1,0},{2,1},{3,2},{4,7},{5,4},{6,5},{7,6},{8,11},{9,8},{10,9... | collective-permute-start | bytes 442376 | tf_op jit(solution)/shard_map/ppermute | solution.py:344
  29.2 108.6 %all-gather.10.cloned.1.call-start = ((), (), s32[]{:S(2)}) async-start(), calls=%async_computation.7 | async-start | bytes 3932160 | tf_op jit(solution)/shard_map/all_gather | solution.py:399
  29.2 0.8 collective-permute-start.1
  30.9 163.7 %all-gather.12.cloned.1.call-start = ((), (), s32[]{:S(2)}) async-start(), calls=%async_computation.8 | async-start | bytes 10616832 | tf_op jit(solution)/shard_map/all_gather | solution.py:364
  31.0 41.9 %collective-permute-start.6 = (bf16[96,1536]{1,0:T(8,128)(2,1)S(1)}, bf16[96,1536]{1,0:T(8,128)(2,1)S(1)}, u32[]{:S(2)}, u32[]{:S(2)}) collective-permute-start(bf16[96,1536]{1,0:T(8,128)(2,1)S(1)} %pad_maximum_fusion.5), channel_id=1, source_target_pairs={{0,1},{1,2},{2,3},{3,0},{4,5},{5,6},{6,7},{7,4},{8,9},{9,10},{10,1... | collective-permute-start | bytes 884744 | tf_op jit(solution)/shard_map/ppermute | solution.py:344
  65.5 19.9 %collective-permute-start.7 = (bf16[96,1536]{1,0:T(8,128)(2,1)S(1)}, bf16[96,1536]{1,0:T(8,128)(2,1)S(1)}, u32[]{:S(2)}, u32[]{:S(2)}) collective-permute-start(bf16[96,1536]{1,0:T(8,128)(2,1)S(1)} %pad_maximum_fusion.5), channel_id=1, source_target_pairs={{0,2},{1,3},{2,0},{3,1},{4,6},{5,7},{6,4},{7,5},{8,10},{9,11},{10,... | collective-permute-start | bytes 884744 | tf_op jit(solution)/shard_map/ppermute | solution.py:344
  65.5 20.0 %collective-permute-start.8 = (bf16[96,1536]{1,0:T(8,128)(2,1)S(1)}, bf16[96,1536]{1,0:T(8,128)(2,1)S(1)}, u32[]{:S(2)}, u32[]{:S(2)}) collective-permute-start(bf16[96,1536]{1,0:T(8,128)(2,1)S(1)} %pad_maximum_fusion.5), channel_id=1, source_target_pairs={{0,3},{1,0},{2,1},{3,2},{4,7},{5,4},{6,5},{7,6},{8,11},{9,8},{10,9... | collective-permute-start | bytes 884744 | tf_op jit(solution)/shard_map/ppermute | solution.py:344
  67.9 18.8 %copy-start.57 = (s32[1,3,32,3]{2,0,3,1:T(1,128)S(1)}, s32[1,3,32,3]{2,0,3,1:T(1,128)}, u32[]{:S(2)}) copy-start(s32[1,3,32,3]{2,0,3,1:T(1,128)} %param.25) | copy-start | bytes 3460
  85.4 19.3 %copy-start.66 = (s32[1,4]{1,0:T(1,128)S(1)}, s32[1,4]{1,0:T(1,128)}, u32[]{:S(2)}) copy-start(s32[1,4]{1,0:T(1,128)} %param.23) | copy-start | bytes 52
  85.4 19.2 %copy-start.67 = (s32[1,32]{1,0:T(1,128)S(1)}, s32[1,32]{1,0:T(1,128)}, u32[]{:S(2)}) copy-start(s32[1,32]{1,0:T(1,128)} %param.24) | copy-start | bytes 388
  85.4 20.0 %copy-start.47 = (f32[2,768]{1,0:T(2,128)S(1)}, f32[2,768]{1,0:T(2,128)}, u32[]{:S(2)}) copy-start(f32[2,768]{1,0:T(2,128)} %param.19) | copy-start | bytes 18436
  85.5 20.0 %copy-start.48 = (f32[2,768]{1,0:T(2,128)S(1)}, f32[2,768]{1,0:T(2,128)}, u32[]{:S(2)}) copy-start(f32[2,768]{1,0:T(2,128)} %param.18) | copy-start | bytes 18436
  85.5 20.6 %copy-start.49 = (f32[2,768]{1,0:T(2,128)S(1)}, f32[2,768]{1,0:T(2,128)}, u32[]{:S(2)}) copy-start(f32[2,768]{1,0:T(2,128)} %param.21) | copy-start | bytes 18436
  85.5 20.6 %copy-start.50 = (f32[2,768]{1,0:T(2,128)S(1)}, f32[2,768]{1,0:T(2,128)}, u32[]{:S(2)}) copy-start(f32[2,768]{1,0:T(2,128)} %param.20) | copy-start | bytes 18436
  85.5 21.3 %copy-start.11 = (bf16[512,768]{1,0:T(8,128)(2,1)S(1)}, bf16[512,768]{1,0:T(8,128)(2,1)}, u32[]{:S(2)}) copy-start(bf16[512,768]{1,0:T(8,128)(2,1)} %copy-done.10) | copy-start | bytes 2359300
  86.7 156.5 %all-gather.14.cloned.1.call-start = ((), (), s32[]{:S(2)}) async-start(), calls=%async_computation.9 | async-start | bytes 5308416 | tf_op jit(solution)/shard_map/all_gather | solution.py:364
  104.8 26.4 %collective-permute-start = (s32[1188]{0:T(1024)S(1)}, s32[1188]{0:T(1024)S(1)}, u32[]{:S(2)}, u32[]{:S(2)}) collective-permute-start(s32[1188]{0:T(1024)S(1)} %concatenate.39), channel_id=1, source_target_pairs={{0,0},{1,4},{2,8},{3,12},{4,3},{5,7},{6,11},{7,15},{8,1},{9,5},{10... | collective-permute-start | bytes 14264 | tf_op jit(solution)/shard_map/ppermute | solution.py:370
  106.1 88.5 %copy-start.39 = (f32[768]{0:T(1024)}, f32[768]{0:T(1024)S(1)}, u32[]{:S(2)}) copy-start(f32[768]{0:T(1024)S(1)} %get-tuple-element.243) | copy-start | bytes 9220
  106.1 88.5 %copy-start.58 = (f32[768]{0:T(1024)}, f32[768]{0:T(1024)S(1)}, u32[]{:S(2)}) copy-start(f32[768]{0:T(1024)S(1)} %get-tuple-element.197) | copy-start | bytes 9220
  110.1 8.9 %collective-permute-start.9 = (bf16[96,768]{0,1:T(8,128)(2,1)S(1)}, bf16[96,768]{0,1:T(8,128)(2,1)S(1)}, u32[]{:S(2)}, u32[]{:S(2)}) collective-permute-start(bf16[96,768]{0,1:T(8,128)(2,1)S(1)} %pad_maximum_fusion.9), channel_id=1, source_target_pairs={{0,1},{1,2},{2,3},{3,0},{4,5},{5,6},{6,7},{7,4},{8,9},{9,10},{10,1... | collective-permute-start | bytes 442376 | tf_op jit(solution)/shard_map/ppermute | solution.py:344
  113.5 16.0 %collective-permute-start.10 = (bf16[96,768]{0,1:T(8,128)(2,1)S(1)}, bf16[96,768]{0,1:T(8,128)(2,1)S(1)}, u32[]{:S(2)}, u32[]{:S(2)}) collective-permute-start(bf16[96,768]{0,1:T(8,128)(2,1)S(1)} %pad_maximum_fusion.9), channel_id=1, source_target_pairs={{0,2},{1,3},{2,0},{3,1},{4,6},{5,7},{6,4},{7,5},{8,10},{9,11},{10,... | collective-permute-start | bytes 442376 | tf_op jit(solution)/shard_map/ppermute | solution.py:344
  115.8 13.7 %collective-permute-start.11 = (bf16[96,768]{0,1:T(8,128)(2,1)S(1)}, bf16[96,768]{0,1:T(8,128)(2,1)S(1)}, u32[]{:S(2)}, u32[]{:S(2)}) collective-permute-start(bf16[96,768]{0,1:T(8,128)(2,1)S(1)} %pad_maximum_fusion.9), channel_id=1, source_target_pairs={{0,3},{1,0},{2,1},{3,2},{4,7},{5,4},{6,5},{7,6},{8,11},{9,8},{10,9... | collective-permute-start | bytes 442376 | tf_op jit(solution)/shard_map/ppermute | solution.py:344
  130.9 115.5 %all-gather.16.cloned.1.call-start = ((), (), s32[]{:S(2)}) async-start(), calls=%async_computation.10 | async-start | bytes 3932160 | tf_op jit(solution)/shard_map/all_gather | solution.py:399
  205.3 95.3 %copy-start.21 = (f32[512]{0:T(512)}, f32[512]{0:T(512)S(1)}, u32[]{:S(2)}) copy-start(f32[512]{0:T(512)S(1)} %broadcast_multiply_fusion.2) | copy-start | bytes 6148
  205.6 94.9 %copy-start.25 = (f32[512]{0:T(512)}, f32[512]{0:T(512)S(1)}, u32[]{:S(2)}) copy-start(f32[512]{0:T(512)S(1)} %fusion.83) | copy-start | bytes 6148
  207.2 113.4 %all-gather.18.cloned.1.call-start = ((), (), s32[]{:S(2)}) async-start(), calls=%async_computation.11 | async-start | bytes 10616832 | tf_op jit(solution)/shard_map/all_gather | solution.py:364
  207.2 25.2 %copy-start.16 = (bf16[2,768,96]{1,2,0:T(8,128)(2,1)S(1)}, bf16[2,768,96]{1,2,0:T(8,128)(2,1)}, u32[]{:S(2)}) copy-start(bf16[2,768,96]{1,2,0:T(8,128)(2,1)} %param.17) | copy-start | bytes 884740
  208.3 11.9 %collective-permute-start.12 = (bf16[96,1536]{1,0:T(8,128)(2,1)S(1)}, bf16[96,1536]{1,0:T(8,128)(2,1)S(1)}, u32[]{:S(2)}, u32[]{:S(2)}) collective-permute-start(bf16[96,1536]{1,0:T(8,128)(2,1)S(1)} %pad_maximum_fusion.6), channel_id=1, source_target_pairs={{0,1},{1,2},{2,3},{3,0},{4,5},{5,6},{6,7},{7,4},{8,9},{9,10},{10,1... | collective-permute-start | bytes 884744 | tf_op jit(solution)/shard_map/ppermute | solution.py:344
  209.2 21.9 %collective-permute-start.13 = (bf16[96,1536]{1,0:T(8,128)(2,1)S(1)}, bf16[96,1536]{1,0:T(8,128)(2,1)S(1)}, u32[]{:S(2)}, u32[]{:S(2)}) collective-permute-start(bf16[96,1536]{1,0:T(8,128)(2,1)S(1)} %pad_maximum_fusion.6), channel_id=1, source_target_pairs={{0,2},{1,3},{2,0},{3,1},{4,6},{5,7},{6,4},{7,5},{8,10},{9,11},{10,... | collective-permute-start | bytes 884744 | tf_op jit(solution)/shard_map/ppermute | solution.py:344
  209.9 21.9 %collective-permute-start.14 = (bf16[96,1536]{1,0:T(8,128)(2,1)S(1)}, bf16[96,1536]{1,0:T(8,128)(2,1)S(1)}, u32[]{:S(2)}, u32[]{:S(2)}) collective-permute-start(bf16[96,1536]{1,0:T(8,128)(2,1)S(1)} %pad_maximum_fusion.6), channel_id=1, source_target_pairs={{0,3},{1,0},{2,1},{3,2},{4,7},{5,4},{6,5},{7,6},{8,11},{9,8},{10,9... | collective-permute-start | bytes 884744 | tf_op jit(solution)/shard_map/ppermute | solution.py:344
  235.2 204.0 %reduce-scatter.11.cloned.1.call-start = ((), (), s32[]{:S(2)}) async-start(), calls=%async_computation.12 | async-start | bytes 10616832 | tf_op jit(solution)/shard_map/reduce_scatter | solution.py:431
  235.3 95.7 %collective-permute-start.5 = (bf16[512,768]{1,0:T(8,128)(2,1)}, bf16[512,768]{1,0:T(8,128)(2,1)}, u32[]{:S(2)}, u32[]{:S(2)}) collective-permute-start(bf16[512,768]{1,0:T(8,128)(2,1)} %param.22), channel_id=1, source_target_pairs={{0,0},{1,4},{2,8},{3,12},{4,3},{5,7},{6,11},{7,15},{8,1},{9,5},{10... | collective-permute-start | bytes 2359304 | tf_op jit(solution)/shard_map/ppermute | solution.py:407
  303.0 17.6 %copy-start.41 = (f32[768]{0:T(1024)S(1)}, f32[768]{0:T(1024)}, u32[]{:S(2)}) copy-start(f32[768]{0:T(1024)} %get-tuple-element.244) | copy-start | bytes 9220
  303.0 17.6 %copy-start.60 = (f32[768]{0:T(1024)S(1)}, f32[768]{0:T(1024)}, u32[]{:S(2)}) copy-start(f32[768]{0:T(1024)} %get-tuple-element.196) | copy-start | bytes 9220
  303.0 42.7 %copy-start.27 = (f32[512]{0:T(512)}, f32[512]{0:T(512)S(1)}, u32[]{:S(2)}) copy-start(f32[512]{0:T(512)S(1)} %broadcast_multiply_fusion.1) | copy-start | bytes 6148
  304.5 21.5 %copy-start.33 = (f32[512]{0:T(512)}, f32[512]{0:T(512)S(1)}, u32[]{:S(2)}) copy-start(f32[512]{0:T(512)S(1)} %multiply_reduce_fusion.7) | copy-start | bytes 6148
  304.5 41.3 %copy-start.45 = (f32[512]{0:T(512)}, f32[512]{0:T(512)S(1)}, u32[]{:S(2)}) copy-start(f32[512]{0:T(512)S(1)} %fusion.84) | copy-start | bytes 6148
  353.3 133.9 %reduce-scatter.13.cloned.1.call-start = ((), (), s32[]{:S(2)}) async-start(), calls=%async_computation.13 | async-start | bytes 3932160 | tf_op jit(solution)/shard_map/reduce_scatter | solution.py:473
  358.0 17.3 %copy-start.34 = (f32[512]{0:T(512)S(1)}, f32[512]{0:T(512)}, u32[]{:S(2)}) copy-start(f32[512]{0:T(512)} %copy-done.33) | copy-start | bytes 6148
  358.0 17.3 %copy-start.2 = (f32[512,768]{1,0:T(8,128)S(1)}, f32[512,768]{1,0:T(8,128)}, u32[]{:S(2)}) copy-start(f32[512,768]{1,0:T(8,128)} %copy-done) | copy-start | bytes 4718596
  358.0 81.2 %collective-permute-start.15 = (bf16[512,768]{1,0:T(8,128)(2,1)}, bf16[512,768]{1,0:T(8,128)(2,1)}, u32[]{:S(2)}, u32[]{:S(2)}) collective-permute-start(bf16[512,768]{1,0:T(8,128)(2,1)} %get-tuple-element.214), channel_id=1, source_target_pairs={{0,0},{4,1},{8,2},{12,3},{3,4},{7,5},{11,6},{15,7},{1,8},{5,9},{9,... | collective-permute-start | bytes 2359304 | tf_op jit(solution)/shard_map/ppermute | solution.py:419
  449.8 123.6 %reduce-scatter.19.cloned.1.call-start = ((), (), s32[]{:S(2)}) async-start(), calls=%async_computation.16 | async-start | bytes 5308416
  493.9 145.1 %reduce-scatter.15.cloned.1.call-start = ((), (), s32[]{:S(2)}) async-start(), calls=%async_computation.14 | async-start | bytes 10616832 | tf_op jit(solution)/shard_map/reduce_scatter | solution.py:431
  494.6 18.9 %slice-start = ((s8[6291456]{0:T(1024)(128)(4,1)}), s8[2097152]{0:T(1024)(128)(4,1)S(1)}, s32[]{:S(2)}) async-start(s8[6291456]{0:T(1024)(128)(4,1)} %bitcast.211), calls=%async_computation.18 | async-start | bytes 4194304
  498.9 14.6 %copy-start.5 = (f32[512,768]{1,0:T(8,128)}, f32[512,768]{1,0:T(8,128)S(1)}, u32[]{:S(2)}) copy-start(f32[512,768]{1,0:T(8,128)S(1)} %get-tuple-element.207) | copy-start | bytes 4718596
  520.9 170.3 %reduce-scatter.17.cloned.1.call-start = ((), (), s32[]{:S(2)}) async-start(), calls=%async_computation.15 | async-start | bytes 3932160 | tf_op jit(solution)/shard_map/reduce_scatter | solution.py:473
  528.2 10.7 %collective-permute-start.16 = (bf16[96,1536]{1,0:T(8,128)(2,1)S(1)}, bf16[96,1536]{1,0:T(8,128)(2,1)S(1)}, u32[]{:S(2)}, u32[]{:S(2)}) collective-permute-start(bf16[96,1536]{1,0:T(8,128)(2,1)S(1)} %bitcast.191), channel_id=1, source_target_pairs={{0,3},{1,0},{2,1},{3,2},{4,7},{5,4},{6,5},{7,6},{8,11},{9,8},{10,9... | collective-permute-start | bytes 884744 | tf_op jit(solution)/shard_map/ppermute | solution.py:344
  531.5 25.2 %collective-permute-start.17 = (bf16[96,1536]{1,0:T(8,128)(2,1)S(1)}, bf16[96,1536]{1,0:T(8,128)(2,1)S(1)}, u32[]{:S(2)}, u32[]{:S(2)}) collective-permute-start(bf16[96,1536]{1,0:T(8,128)(2,1)S(1)} %bitcast.192), channel_id=1, source_target_pairs={{0,2},{1,3},{2,0},{3,1},{4,6},{5,7},{6,4},{7,5},{8,10},{9,11},{10,... | collective-permute-start | bytes 884744 | tf_op jit(solution)/shard_map/ppermute | solution.py:344
  532.3 24.7 %collective-permute-start.18 = (bf16[96,1536]{1,0:T(8,128)(2,1)}, bf16[96,1536]{1,0:T(8,128)(2,1)}, u32[]{:S(2)}, u32[]{:S(2)}) collective-permute-start(bf16[96,1536]{1,0:T(8,128)(2,1)} %bitcast.85), channel_id=1, source_target_pairs={{0,1},{1,2},{2,3},{3,0},{4,5},{5,6},{6,7},{7,4},{8,9},{9,10},{10,1... | collective-permute-start | bytes 884744 | tf_op jit(solution)/shard_map/ppermute | solution.py:344
  575.0 63.9 %collective-permute-start.19 = (bf16[96,768]{0,1:T(8,128)(2,1)S(1)}, bf16[96,768]{0,1:T(8,128)(2,1)S(1)}, u32[]{:S(2)}, u32[]{:S(2)}) collective-permute-start(bf16[96,768]{0,1:T(8,128)(2,1)S(1)} %bitcast.203), channel_id=1, source_target_pairs={{0,3},{1,0},{2,1},{3,2},{4,7},{5,4},{6,5},{7,6},{8,11},{9,8},{10,9... | collective-permute-start | bytes 442376 | tf_op jit(solution)/shard_map/ppermute | solution.py:344
  575.0 63.9 %collective-permute-start.20 = (bf16[96,768]{0,1:T(8,128)(2,1)S(1)}, bf16[96,768]{0,1:T(8,128)(2,1)S(1)}, u32[]{:S(2)}, u32[]{:S(2)}) collective-permute-start(bf16[96,768]{0,1:T(8,128)(2,1)S(1)} %bitcast.199), channel_id=1, source_target_pairs={{0,2},{1,3},{2,0},{3,1},{4,6},{5,7},{6,4},{7,5},{8,10},{9,11},{10,... | collective-permute-start | bytes 442376 | tf_op jit(solution)/shard_map/ppermute | solution.py:344
  577.4 61.5 %collective-permute-start.21 = (bf16[96,768]{0,1:T(8,128)(2,1)S(1)}, bf16[96,768]{0,1:T(8,128)(2,1)S(1)}, u32[]{:S(2)}, u32[]{:S(2)}) collective-permute-start(bf16[96,768]{0,1:T(8,128)(2,1)S(1)} %bitcast.195), channel_id=1, source_target_pairs={{0,1},{1,2},{2,3},{3,0},{4,5},{5,6},{6,7},{7,4},{8,9},{9,10},{10,1... | collective-permute-start | bytes 442376 | tf_op jit(solution)/shard_map/ppermute | solution.py:344
  649.6 144.5 %reduce-scatter.21.cloned.1.call-start = ((), (), s32[]{:S(2)}) async-start(), calls=%async_computation.17 | async-start | bytes 5308416
  704.0 87.7 %collective-permute-start.22 = (bf16[512,768]{1,0:T(8,128)(2,1)}, bf16[512,768]{1,0:T(8,128)(2,1)}, u32[]{:S(2)}, u32[]{:S(2)}) collective-permute-start(bf16[512,768]{1,0:T(8,128)(2,1)} %add_convert_fusion.2), channel_id=1, source_target_pairs={{0,0},{4,1},{8,2},{12,3},{3,4},{7,5},{11,6},{15,7},{1,8},{5,9},{9,... | collective-permute-start | bytes 2359304 | tf_op jit(solution)/shard_map/ppermute | solution.py:492
  716.6 73.3 %collective-permute-start.23 = (bf16[96,1536]{1,0:T(8,128)(2,1)S(1)}, bf16[96,1536]{1,0:T(8,128)(2,1)S(1)}, u32[]{:S(2)}, u32[]{:S(2)}) collective-permute-start(bf16[96,1536]{1,0:T(8,128)(2,1)S(1)} %bitcast.189), channel_id=1, source_target_pairs={{0,3},{1,0},{2,1},{3,2},{4,7},{5,4},{6,5},{7,6},{8,11},{9,8},{10,9... | collective-permute-start | bytes 884744 | tf_op jit(solution)/shard_map/ppermute | solution.py:344
  716.7 73.6 %collective-permute-start.24 = (bf16[96,1536]{1,0:T(8,128)(2,1)S(1)}, bf16[96,1536]{1,0:T(8,128)(2,1)S(1)}, u32[]{:S(2)}, u32[]{:S(2)}) collective-permute-start(bf16[96,1536]{1,0:T(8,128)(2,1)S(1)} %bitcast.190), channel_id=1, source_target_pairs={{0,2},{1,3},{2,0},{3,1},{4,6},{5,7},{6,4},{7,5},{8,10},{9,11},{10,... | collective-permute-start | bytes 884744 | tf_op jit(solution)/shard_map/ppermute | solution.py:344
  717.6 73.2 %collective-permute-start.25 = (bf16[96,1536]{1,0:T(8,128)(2,1)}, bf16[96,1536]{1,0:T(8,128)(2,1)S(1)}, u32[]{:S(2)}, u32[]{:S(2)}) collective-permute-start(bf16[96,1536]{1,0:T(8,128)(2,1)} %bitcast.91), channel_id=1, source_target_pairs={{0,1},{1,2},{2,3},{3,0},{4,5},{5,6},{6,7},{7,4},{8,9},{9,10},{10,1... | collective-permute-start | bytes 884744 | tf_op jit(solution)/shard_map/ppermute | solution.py:344
  795.7 7.1 collective-permute-start.26
  797.3 16.7 %collective-permute-start.27 = (bf16[96,768]{0,1:T(8,128)(2,1)S(1)}, bf16[96,768]{0,1:T(8,128)(2,1)S(1)}, u32[]{:S(2)}, u32[]{:S(2)}) collective-permute-start(bf16[96,768]{0,1:T(8,128)(2,1)S(1)} %bitcast.202), channel_id=1, source_target_pairs={{0,2},{1,3},{2,0},{3,1},{4,6},{5,7},{6,4},{7,5},{8,10},{9,11},{10,... | collective-permute-start | bytes 442376 | tf_op jit(solution)/shard_map/ppermute | solution.py:344
  797.3 16.7 %collective-permute-start.28 = (bf16[96,768]{0,1:T(8,128)(2,1)S(1)}, bf16[96,768]{0,1:T(8,128)(2,1)S(1)}, u32[]{:S(2)}, u32[]{:S(2)}) collective-permute-start(bf16[96,768]{0,1:T(8,128)(2,1)S(1)} %bitcast.198), channel_id=1, source_target_pairs={{0,1},{1,2},{2,3},{3,0},{4,5},{5,6},{6,7},{7,4},{8,9},{9,10},{10,1... | collective-permute-start | bytes 442376 | tf_op jit(solution)/shard_map/ppermute | solution.py:344
  (61 other events, 233.2 us)
Sparse Core Ops, SparseCore 0:
  29.3 51.5 all-gather.7
  83.0 28.4 all-gather.9
  114.0 58.8 all-gather.11
  175.2 38.8 all-gather.13
  215.5 28.4 all-gather.15
  245.8 74.7 all-gather.17
  353.4 82.5 reduce-scatter.10
  450.0 37.2 reduce-scatter.12
  494.0 53.7 reduce-scatter.18
  551.2 76.8 reduce-scatter.14
  649.7 41.4 reduce-scatter.16
  698.0 59.6 reduce-scatter.20

commit v3 on v2

v3 whole, which is shorter than its diff:
```python
import functools

import jax
import jax.numpy as jnp
from jax import lax
from jax.experimental import pallas as pl
from jax.experimental.pallas import tpu as pltpu
from jax.sharding import PartitionSpec as P

HD = 64
BLK = 64
LAYERS = 2
LONGEST = 16
QUAD = 4
WIDE = QUAD * HD
STEP = 4
STEPS = LONGEST // STEP

ROW = 2
DATA = ("hi", "row", "quad")
EVERY = DATA + ("tensor",)

NORM_EPSILON = 1e-12
MASK_VALUE = -1e30
BF = jnp.bfloat16
F32 = jnp.float32


def layer_norm(summed, norm_gain, norm_shift):
    row_mean = jnp.mean(summed, axis=-1, keepdims=True)
    centred = summed - row_mean
    row_var = jnp.mean(centred * centred, axis=-1, keepdims=True)
    return centred * lax.rsqrt(row_var + NORM_EPSILON) * norm_gain + norm_shift


def gelu_tanh(values):
    return jax.nn.gelu(values, approximate=True)


def dot(left, right):
    return jnp.dot(left, right, preferred_element_type=F32)


def dot_right_t(left, right):
    return lax.dot_general(left, right, (((1,), (1,)), ((), ())), preferred_element_type=F32)


def dot_left_t(left, right):
    return lax.dot_general(left, right, (((0,), (0,)), ((), ())), preferred_element_type=F32)


def head_diagonal(rows):
    lane_head = lax.broadcasted_iota(jnp.int32, rows.shape, 1) // HD
    return jnp.concatenate(
        [jnp.where(lane_head == h, rows, jnp.zeros_like(rows)) for h in range(QUAD)], axis=0
    )


def diagonal_rows(full):
    lane_head = lax.broadcasted_iota(jnp.int32, (HD, WIDE), 1) // HD
    out = full[:HD]
    for h in range(1, QUAD):
        out = jnp.where(lane_head == h, full[h * HD : (h + 1) * HD], out)
    return out


def key_rows(keys_at, b, count):
    return [pl.ds(pl.multiple_of(keys_at[b, i] * BLK, BLK), BLK) for i in range(count)]


def stacked(ref, places):
    return jnp.concatenate([ref[p, :] for p in places], axis=0)


def row_sums(x):
    return jnp.sum(x.reshape(x.shape[0] // 8, 8, WIDE), axis=0)


def for_steps(steps, body):
    for n in range(1, STEPS + 1):
        pl.when(steps == n)(functools.partial(body, n * STEP))


def forward_kernel(keys_at, steps_of, q_ref, k_ref, v_ref, bias_ref, out_ref, log_ref):
    def one_block(b, carry):
        rows = pl.ds(pl.multiple_of(b * BLK, BLK), BLK)

        def attend(count):
            places = key_rows(keys_at, b, count)
            query = head_diagonal(q_ref[rows, :])
            raw = dot_right_t(stacked(k_ref, places), query)
            scores, peak = [], None
            for i in range(count):
                piece = raw[i * BLK : (i + 1) * BLK] + bias_ref[b, i : i + 1, :]
                scores.append(piece)
                high = jnp.max(piece.reshape(BLK // 8, 8, WIDE), axis=0)
                peak = high if peak is None else jnp.maximum(peak, high)
            peak = jnp.max(peak, axis=0, keepdims=True)
            total, weights = None, []
            for piece in scores:
                exponent = jnp.exp(piece - peak)
                part = row_sums(exponent)
                total = part if total is None else total + part
                weights.append(exponent.astype(BF))
            total = jnp.sum(total, axis=0, keepdims=True)
            mix = dot_left_t(jnp.concatenate(weights, axis=0), stacked(v_ref, places))
            column = jnp.transpose(jnp.broadcast_to(total, (128, WIDE)))
            mix = mix / jnp.concatenate([column, column], axis=1)
            out_ref[rows, :] = diagonal_rows(mix).astype(BF)
            log_ref[b] = peak + jnp.log(total)

        for_steps(steps_of[b], attend)
        return carry

    lax.fori_loop(0, q_ref.shape[0] // BLK, one_block, 0)


def backward_kernel(
    keys_at, steps_of, q_ref, k_ref, v_ref, bias_ref, log_ref, d_ref, dq_ref, dk_ref, dv_ref, dkey, dvalue
):
    dkey[...] = jnp.zeros_like(dkey)
    dvalue[...] = jnp.zeros_like(dvalue)

    def one_block(b, carry):
        rows = pl.ds(pl.multiple_of(b * BLK, BLK), BLK)

        def attend(count):
            places = key_rows(keys_at, b, count)
            query = head_diagonal(q_ref[rows, :])
            d_mixed = head_diagonal(d_ref[rows, :])
            logs = log_ref[b]
            keys = stacked(k_ref, places)
            raw = dot_right_t(keys, query)
            back = dot_right_t(stacked(v_ref, places), d_mixed)
            probs, inner = [], None
            for i in range(count):
                at = slice(i * BLK, (i + 1) * BLK)
                prob = jnp.exp(raw[at] + (bias_ref[b, i : i + 1, :] - logs))
                probs.append(prob)
                part = row_sums(prob * back[at])
                inner = part if inner is None else inner + part
            grad = dot(jnp.concatenate([p.astype(BF) for p in probs], axis=0), d_mixed)
            for i, p in enumerate(places):
                dvalue[p, :] += grad[i * BLK : (i + 1) * BLK]
            inner = jnp.sum(inner, axis=0, keepdims=True)
            d_score = jnp.concatenate(
                [
                    (prob * (back[i * BLK : (i + 1) * BLK] - inner)).astype(BF)
                    for i, prob in enumerate(probs)
                ],
                axis=0,
            )
            grad = dot(d_score, query)
            for i, p in enumerate(places):
                dkey[p, :] += grad[i * BLK : (i + 1) * BLK]
            d_query = dot_left_t(d_score, keys)
            dq_ref[rows, :] = (diagonal_rows(d_query) * (HD**-0.5)).astype(BF)

        for_steps(steps_of[b], attend)
        return carry

    lax.fori_loop(0, q_ref.shape[0] // BLK, one_block, 0)
    dk_ref[...] = dkey[...].astype(BF)
    dv_ref[...] = dvalue[...].astype(BF)


SHORT = pl.CostEstimate(flops=1_000_000, bytes_accessed=1_000_000, transcendentals=0)
MESH_ID = pl.DeviceIdType.MESH
CALL_GATHER_FIRST, CALL_GATHER, CALL_REDUCE, CALL_NORMS = range(4)


def quad_places():
    me = lax.axis_index("quad")
    mate = me + 1 - 2 * (me % 2)
    return me, mate, (me + 2) % QUAD, (mate + 2) % QUAD


def greet(*peers):
    barrier = pltpu.get_barrier_semaphore()
    for peer in peers:
        pl.semaphore_signal(barrier, inc=1, device_id=peer, device_id_type=MESH_ID)
    pl.semaphore_wait(barrier, len(peers))


def block_at(block, size, start=0, rows=None):
    return pl.ds(pl.multiple_of(block * size + start, 16), size if rows is None else rows)


def gather_kernel(pieces, *refs):
    count = len(pieces)
    owns, outs = refs[:count], refs[count : 2 * count]
    keep_sem, mate_send, mate_recv, far_send, far_recv, on_send, on_recv = refs[2 * count :]
    me, mate, far, cross = quad_places()
    greet({"quad": mate}, {"quad": far})

    def send(source, target, sends, recvs, at, peer):
        return pltpu.make_async_remote_copy(
            src_ref=source,
            dst_ref=target,
            send_sem=sends.at[at],
            recv_sem=recvs.at[at],
            device_id={"quad": peer},
            device_id_type=MESH_ID,
        )

    parts = []
    for n in range(count):
        size = owns[n].shape[0]
        step = size // pieces[n]
        for p in range(pieces[n]):
            parts.append((n, size, p * step, step))
    to_far = [
        send(owns[n].at[pl.ds(start, step)], outs[n].at[block_at(me, size, start, step)], far_send, far_recv, i, far)
        for i, (n, size, start, step) in enumerate(parts)
    ]
    for copy in to_far:
        copy.start()
    to_mate = [
        send(owns[n], outs[n].at[block_at(me, owns[n].shape[0])], mate_send, mate_recv, n, mate)
        for n in range(count)
    ]
    for copy in to_mate:
        copy.start()
    kept = [
        pltpu.make_async_copy(owns[n], outs[n].at[block_at(me, owns[n].shape[0])], keep_sem.at[n])
        for n in range(count)
    ]
    for copy in kept:
        copy.start()
    onward = []
    for i, (n, size, start, step) in enumerate(parts):
        to_far[i].wait_recv()
        came = outs[n].at[block_at(far, size, start, step)]
        copy = send(came, came, on_send, on_recv, i, mate)
        copy.start()
        onward.append(copy)
    for copy in to_mate + onward:
        copy.wait()
    for copy in to_far:
        copy.wait_send()
    for copy in kept:
        copy.wait()


def quad_gather(arrays, pieces, call):
    count, total = len(arrays), sum(pieces)
    sems = [pltpu.SemaphoreType.DMA((k,)) for k in (count, count, count, total, total, total, total)]
    return pl.pallas_call(
        functools.partial(gather_kernel, pieces),
        out_shape=[jax.ShapeDtypeStruct((QUAD * x.shape[0],) + x.shape[1:], x.dtype) for x in arrays],
        in_specs=[pl.BlockSpec(memory_space=pltpu.VMEM)] * count,
        out_specs=[pl.BlockSpec(memory_space=pl.ANY)] * count,
        scratch_shapes=sems,
        compiler_params=pltpu.CompilerParams(collective_id=call, has_side_effects=True),
        cost_estimate=SHORT,
        name="quad_gather",
    )(*arrays)


REDUCE_PIECES = 4


def reduce_kernel(
    parts_ref, out_ref, near, relay, beyond, mate_send, mate_recv, own_send, own_recv, far_send, far_recv
):
    me, mate, far, cross = quad_places()
    greet({"quad": mate}, {"quad": far})
    size = out_ref.shape[0]
    step = size // REDUCE_PIECES

    def send(source, target, send_sem, recv_sem, peer):
        copy = pltpu.make_async_remote_copy(
            src_ref=source,
            dst_ref=target,
            send_sem=send_sem,
            recv_sem=recv_sem,
            device_id={"quad": peer},
            device_id_type=MESH_ID,
        )
        copy.start()
        return copy

    to_mate = [
        send(
            parts_ref.at[block_at(cross, size, p * step, step)],
            near.at[1, pl.ds(p * step, step)],
            mate_send.at[p],
            mate_recv.at[p],
            mate,
        )
        for p in range(REDUCE_PIECES)
    ]
    own = send(parts_ref.at[block_at(mate, size)], near.at[0], own_send, own_recv, mate)
    to_far = []
    for p in range(REDUCE_PIECES):
        rows = pl.ds(p * step, step)
        to_mate[p].wait_recv()
        mine = parts_ref[block_at(far, size, p * step, step), :].astype(F32)
        relay[rows, :] = (mine + near[1, rows, :].astype(F32)).astype(BF)
        to_far.append(send(relay.at[rows], beyond.at[rows], far_send.at[p], far_recv.at[p], far))
    own.wait_recv()
    for p in range(REDUCE_PIECES):
        rows = pl.ds(p * step, step)
        to_far[p].wait_recv()
        mine = parts_ref[block_at(me, size, p * step, step), :].astype(F32)
        out_ref[rows, :] = mine + near[0, rows, :].astype(F32) + beyond[rows, :].astype(F32)
    for copy in to_mate + [own] + to_far:
        copy.wait_send()


def quad_reduce(parts):
    rows, width = parts.shape[0] // QUAD, parts.shape[1]
    dma = pltpu.SemaphoreType.DMA
    return pl.pallas_call(
        reduce_kernel,
        out_shape=jax.ShapeDtypeStruct((rows, width), F32),
        in_specs=[pl.BlockSpec(memory_space=pltpu.VMEM)],
        out_specs=pl.BlockSpec(memory_space=pltpu.VMEM),
        scratch_shapes=[
            pltpu.VMEM((2, rows, width), BF),
            pltpu.VMEM((rows, width), BF),
            pltpu.VMEM((rows, width), BF),
            dma((REDUCE_PIECES,)),
            dma((REDUCE_PIECES,)),
            dma,
            dma,
            dma((REDUCE_PIECES,)),
            dma((REDUCE_PIECES,)),
        ],
        compiler_params=pltpu.CompilerParams(collective_id=CALL_REDUCE, has_side_effects=True),
        cost_estimate=SHORT,
        name="quad_reduce",
    )(parts)


def norms_kernel(hops, x_ref, out_ref, held, came, send_sem, recv_sem):
    peers = []
    for axis, bit in hops:
        at = lax.axis_index(axis)
        peers.append({axis: at + bit - 2 * bit * ((at // bit) % 2)})
    greet(*peers)
    for n, peer in enumerate(peers):
        source = x_ref if n == 0 else held.at[n]
        copy = pltpu.make_async_remote_copy(
            src_ref=source,
            dst_ref=came.at[n],
            send_sem=send_sem.at[n],
            recv_sem=recv_sem.at[n],
            device_id=peer,
            device_id_type=MESH_ID,
        )
        copy.start()
        copy.wait()
        total = source[...] + came[n]
        if n == len(peers) - 1:
            out_ref[...] = total
        else:
            held[n + 1] = total


def sum_everywhere(x):
    hops = []
    for axis in ("quad", "row", "tensor", "hi"):
        bit = 1
        while bit < lax.axis_size(axis):
            hops.append((axis, bit))
            bit *= 2
    vmem = pltpu.VMEM((len(hops),) + x.shape, x.dtype)
    return pl.pallas_call(
        functools.partial(norms_kernel, tuple(hops)),
        out_shape=jax.ShapeDtypeStruct(x.shape, x.dtype),
        in_specs=[pl.BlockSpec(memory_space=pltpu.VMEM)],
        out_specs=pl.BlockSpec(memory_space=pltpu.VMEM),
        scratch_shapes=[
            vmem,
            vmem,
            pltpu.SemaphoreType.DMA((len(hops),)),
            pltpu.SemaphoreType.DMA((len(hops),)),
        ],
        compiler_params=pltpu.CompilerParams(collective_id=CALL_NORMS, has_side_effects=True),
        cost_estimate=SHORT,
        name="sum_everywhere",
    )(x)


def attend_forward(query, keyval, tables):
    keys_at, steps_of, bias = tables
    own, width = query.shape
    quads = width // WIDE
    rows = keyval.shape[0]
    blocks = own // BLK
    return pl.pallas_call(
        forward_kernel,
        grid_spec=pltpu.PrefetchScalarGridSpec(
            num_scalar_prefetch=2,
            grid=(quads,),
            in_specs=[
                pl.BlockSpec((own, WIDE), lambda i, *_: (0, i)),
                pl.BlockSpec((rows, WIDE), lambda i, *_: (0, i)),
                pl.BlockSpec((rows, WIDE), lambda i, *_: (0, i + quads)),
                pl.BlockSpec((blocks, LONGEST, WIDE), lambda i, *_: (0, 0, i)),
            ],
            out_specs=[
                pl.BlockSpec((own, WIDE), lambda i, *_: (0, i)),
                pl.BlockSpec((blocks, 1, WIDE), lambda i, *_: (0, 0, i)),
            ],
        ),
        out_shape=[
            jax.ShapeDtypeStruct((own, width), BF),
            jax.ShapeDtypeStruct((blocks, 1, width), F32),
        ],
        cost_estimate=SHORT,
        name="attend_forward",
    )(keys_at, steps_of, query, keyval, keyval, bias)


def attend_backward(query, keyval, logs, d_mixed, tables):
    keys_at, steps_of, bias = tables
    own, width = query.shape
    quads = width // WIDE
    rows = keyval.shape[0]
    blocks = own // BLK
    return pl.pallas_call(
        backward_kernel,
        grid_spec=pltpu.PrefetchScalarGridSpec(
            num_scalar_prefetch=2,
            grid=(quads,),
            in_specs=[
                pl.BlockSpec((own, WIDE), lambda i, *_: (0, i)),
                pl.BlockSpec((rows, WIDE), lambda i, *_: (0, i)),
                pl.BlockSpec((rows, WIDE), lambda i, *_: (0, i + quads)),
                pl.BlockSpec((blocks, LONGEST, WIDE), lambda i, *_: (0, 0, i)),
                pl.BlockSpec((blocks, 1, WIDE), lambda i, *_: (0, 0, i)),
                pl.BlockSpec((own, WIDE), lambda i, *_: (0, i)),
            ],
            out_specs=[
                pl.BlockSpec((own, WIDE), lambda i, *_: (0, i)),
                pl.BlockSpec((rows, WIDE), lambda i, *_: (0, i)),
                pl.BlockSpec((rows, WIDE), lambda i, *_: (0, i)),
            ],
            scratch_shapes=[
                pltpu.VMEM((rows, WIDE), F32),
                pltpu.VMEM((rows, WIDE), F32),
            ],
        ),
        out_shape=[
            jax.ShapeDtypeStruct((own, width), BF),
            jax.ShapeDtypeStruct((rows, width), BF),
            jax.ShapeDtypeStruct((rows, width), BF),
        ],
        cost_estimate=SHORT,
        name="attend_backward",
    )(keys_at, steps_of, query, keyval, keyval, bias, logs, d_mixed)


def attention_tables(doc_lengths, block_deal, random_rows, own_blocks, first_own):
    blocks = block_deal.shape[0]
    doc_ends = jnp.cumsum(doc_lengths)
    doc_starts = doc_ends - doc_lengths
    place = jnp.arange(blocks, dtype=jnp.int32)
    stored_at = jnp.sum(
        jnp.where(block_deal[None, :] == place[:, None], place[None, :], 0), axis=1
    )
    own = lax.dynamic_slice(block_deal, (first_own,), (own_blocks,))
    doc_index = jnp.sum((own[:, None] >= doc_ends[None, :]).astype(jnp.int32), axis=1)
    doc_pick = (
        doc_index[:, None] == jnp.arange(doc_lengths.shape[0], dtype=jnp.int32)[None, :]
    ).astype(jnp.int32)
    first_block = jnp.sum(doc_pick * doc_starts[None, :], axis=1)
    doc_blocks = jnp.sum(doc_pick * doc_lengths[None, :], axis=1)
    local = own - first_block
    other = jnp.arange(LONGEST, dtype=jnp.int32)
    wanted = jnp.minimum(first_block[:, None] + other[None, :], blocks - 1)
    keys_at = jnp.sum(
        jnp.where(wanted[:, :, None] == place[None, None, :], stored_at[None, None, :], 0), axis=2
    )
    own_pick = (own[:, None] == place[None, :]).astype(jnp.int32)
    picks = jnp.sum(own_pick[None, :, :, None] * random_rows[:, None, :, :], axis=2)
    picks = jnp.remainder(picks, doc_blocks[None, :, None])
    random_hit = jnp.any(picks[:, :, :, None] == other[None, None, None, :], axis=2)
    inside = other[None, :] < doc_blocks[:, None]
    near = jnp.abs(local[:, None] - other[None, :]) <= 1
    everywhere = (local[:, None] < 2) | (other[None, :] < 2)
    allowed = inside[None] & ((near | everywhere)[None] | random_hit)
    bias = jnp.where(allowed, 0.0, MASK_VALUE).astype(F32)
    bias = jnp.repeat(bias.transpose(1, 2, 0), BLK, axis=2)
    steps_of = (doc_blocks + STEP - 1) // STEP
    return keys_at, steps_of, bias


def to_home(steps, parts):
    pairs = []
    for hi in range(steps):
        for row in range(ROW):
            for quad in range(QUAD):
                side, core = quad // 2, quad % 2
                plane = parts - 1 - side if core else side
                for part in range(parts):
                    source = ((hi * ROW + row) * QUAD + quad) * parts + part
                    target = ((hi * ROW + row) * QUAD + part) * parts + plane
                    pairs.append((source, target))
    return pairs


def local(
    layer_input,
    w_qkv,
    w_out,
    w_up,
    w_down,
    attn_gain,
    attn_shift,
    ffn_gain,
    ffn_shift,
    out_grad,
    doc_lengths,
    block_deal,
    random_blocks,
):
    own_rows, width = layer_input.shape
    tensor = lax.axis_size("tensor")
    slot = lax.axis_index("quad")
    plane = lax.axis_index("tensor")
    head_local = random_blocks.shape[1]
    chunk = head_local * HD
    depth = w_qkv.shape[1]
    hidden = w_up.shape[2]
    score_scale = HD ** (-0.5)
    moves = to_home(lax.axis_size("hi"), tensor)
    moves_back = [(b, a) for a, b in moves]

    def shifted(x, by):
        return lax.ppermute(x, "tensor", [(i, (i + by) % tensor) for i in range(tensor)])

    def spread(shard):
        return [shard] + [shifted(shard, by) for by in range(1, tensor)]

    def attn_rows(qkv, back):
        qkv = qkv.reshape(depth, head_local, 3, HD).transpose(0, 2, 1, 3)
        shard = jnp.concatenate([qkv.reshape(depth, 3 * chunk), back.T], axis=1)
        parts = spread(shard)
        return jnp.concatenate(
            [part[:, p * chunk : (p + 1) * chunk] for p in range(4) for part in parts], axis=1
        )

    def ffn_rows(up, down):
        parts = spread(jnp.concatenate([up, down.T], axis=1))
        return jnp.concatenate(
            [part[:, p * hidden : (p + 1) * hidden] for p in range(2) for part in parts], axis=1
        )

    def over_data(rows):
        return lax.all_gather(rows, DATA, axis=0, tiled=True)

    docs, group_blocks = doc_lengths.shape[1], block_deal.shape[1]
    numbers = jnp.concatenate([doc_lengths[0], block_deal[0], random_blocks[0].reshape(-1)])
    numbers = jnp.stack([numbers // BLK, numbers % BLK]).astype(BF)
    numbers = jnp.pad(numbers, ((0, 14), (0, width - numbers.shape[1])))
    own_numbers = lax.ppermute(numbers, EVERY, moves)
    own_tokens = lax.ppermute(layer_input, EVERY, moves)
    attn_full = [over_data(attn_rows(w_qkv[0], w_out[0]))]
    own_tokens, own_numbers, up_0, down_0 = lax.optimization_barrier(
        (own_tokens, own_numbers, w_up[0], w_down[0])
    )
    ffn_full = [over_data(ffn_rows(up_0, down_0))]

    inputs, numbers = quad_gather([own_tokens, own_numbers], [4, 1], CALL_GATHER_FIRST)
    numbers = numbers.reshape(QUAD, 16, width)[:, :2].astype(jnp.int32)
    numbers = numbers[:, 0] * BLK + numbers[:, 1]
    lengths, deal = numbers[0, :docs], numbers[0, docs : docs + group_blocks]
    random_home = numbers[:, docs + group_blocks :][:, : random_blocks.size]
    random_home = random_home.reshape(tensor, head_local, group_blocks, -1)
    part_of = (plane - jnp.arange(tensor, dtype=jnp.int32)) % tensor
    part_pick = (part_of[:, None] == jnp.arange(tensor, dtype=jnp.int32)[None, :]).astype(jnp.int32)
    random_home = jnp.sum(part_pick[:, :, None, None, None] * random_home[None], axis=1)
    random_home = random_home.reshape(tensor * head_local, group_blocks, -1)
    own_blocks = own_rows // BLK
    tables = attention_tables(
        lengths,
        deal,
        random_home,
        own_blocks,
        slot * own_blocks,
    )

    stream = own_tokens.astype(F32)
    stored = []
    for layer in range(LAYERS):
        attn_w, ffn_w = attn_full[layer], ffn_full[layer]
        w_query = attn_w[:, :width]
        w_keyval = attn_w[:, width : 3 * width]
        w_back_t = attn_w[:, 3 * width :]
        w_expand = ffn_w[:, : hidden * tensor]
        w_shrink_t = ffn_w[:, hidden * tensor :]
        own_inputs = stream.astype(BF)
        if layer > 0:
            (inputs,) = quad_gather([own_inputs], [4], CALL_GATHER)
        query = (dot(own_inputs, w_query).astype(BF).astype(F32) * score_scale).astype(BF)
        keyval = dot(inputs, w_keyval).astype(BF)
        if layer == 0:
            keyval, later = lax.optimization_barrier((keyval, (w_qkv, w_out, w_up, w_down)))
            later_rows = [
                (attn_rows(later[0][other], later[1][other]), ffn_rows(later[2][other], later[3][other]))
                for other in range(1, LAYERS)
            ]
        mixed, logs = attend_forward(query, keyval, tables)
        if layer == 0:
            mixed, later_rows, own_grad = lax.optimization_barrier((mixed, later_rows, out_grad))
            for attn_later, ffn_later in later_rows:
                attn_full.append(over_data(attn_later))
                ffn_full.append(over_data(ffn_later))
            own_grad = lax.ppermute(own_grad, EVERY, moves)
        summed_one = stream + dot_right_t(mixed, w_back_t)
        normed = layer_norm(summed_one, attn_gain[layer], attn_shift[layer])
        ffn_in = normed.astype(BF)
        pre_act = dot(ffn_in, w_expand)
        activated = gelu_tanh(pre_act).astype(BF)
        summed_two = normed + dot_right_t(activated, w_shrink_t)
        stored.append(
            (own_inputs, inputs, query, keyval, mixed, logs, summed_one, ffn_in, pre_act, activated, summed_two)
        )
        stream = layer_norm(summed_two, ffn_gain[layer], ffn_shift[layer])
    layer_output = lax.ppermute(stream.astype(BF), EVERY, moves_back)

    def sum_parts(rows, sizes):
        pieces, start = [], 0
        for size in sizes:
            pieces.append(rows[:, start : start + tensor * size].reshape(depth, tensor, size))
            start += tensor * size
        total = jnp.concatenate([p[:, 0] for p in pieces], axis=1).astype(F32)
        for by in range(1, tensor):
            part = jnp.concatenate([p[:, by] for p in pieces], axis=1)
            total = total + shifted(part, tensor - by).astype(F32)
        return total

    def sum_data(part):
        return lax.psum_scatter(part, DATA, scatter_dimension=0, tiled=True)

    state_grad = own_grad.astype(F32)
    attn_grads = [None] * LAYERS
    ffn_grads = [None] * LAYERS
    norm_parts = [None] * LAYERS
    for layer in reversed(range(LAYERS)):
        (own_inputs, inputs, query, keyval, mixed, logs, summed_one, ffn_in, pre_act, activated, summed_two) = stored[layer]
        attn_w, ffn_w = attn_full[layer], ffn_full[layer]
        w_query = attn_w[:, :width]
        w_keyval = attn_w[:, width : 3 * width]
        w_back_t = attn_w[:, 3 * width :]
        w_expand = ffn_w[:, : hidden * tensor]
        w_shrink_t = ffn_w[:, hidden * tensor :]
        unused_two, ffn_back = jax.vjp(layer_norm, summed_two, ffn_gain[layer], ffn_shift[layer])
        d_two, ffn_gain_part, ffn_shift_part = ffn_back(state_grad)
        d_two_low = d_two.astype(BF)
        shrink_grad_t = dot_left_t(d_two_low, activated)
        unused_act, gelu_back = jax.vjp(gelu_tanh, pre_act)
        d_pre = gelu_back(dot(d_two_low, w_shrink_t))[0].astype(BF)
        expand_grad = dot_left_t(ffn_in, d_pre)
        d_normed = d_two + dot_right_t(d_pre, w_expand)
        unused_one, attn_back = jax.vjp(layer_norm, summed_one, attn_gain[layer], attn_shift[layer])
        d_one, attn_gain_part, attn_shift_part = attn_back(d_normed)
        norm_parts[layer] = (attn_gain_part, attn_shift_part, ffn_gain_part, ffn_shift_part)
        d_one_low = d_one.astype(BF)
        ffn_part = jnp.concatenate(
            [
                expand_grad.astype(BF),
                shrink_grad_t.astype(BF),
                dot_left_t(d_one_low, mixed).astype(BF),
            ],
            axis=1,
        )
        d_one_low, ffn_part = lax.optimization_barrier((d_one_low, ffn_part))
        ffn_sum = sum_data(ffn_part)
        d_mixed = dot(d_one_low, w_back_t).astype(BF)
        if layer < LAYERS - 1:
            d_mixed, attn_sum, ffn_grads[layer + 1] = lax.optimization_barrier(
                (d_mixed, attn_sum, ffn_grads[layer + 1])
            )
            attn_grads[layer + 1] = sum_parts(attn_sum, (chunk,) * 3)
        if layer == 0:
            norm_sums = sum_everywhere(
                jnp.stack([norm_parts[l][k] for k in range(4) for l in range(LAYERS)])
            )
            d_mixed, norm_sums = lax.optimization_barrier((d_mixed, norm_sums))
        d_query, d_key, d_value = attend_backward(query, keyval, logs, d_mixed, tables)
        (d_query, d_key, d_value), ffn_sum, attn_grads, layer_output = lax.optimization_barrier(
            ((d_query, d_key, d_value), ffn_sum, attn_grads, layer_output)
        )
        ffn_grads[layer] = sum_parts(ffn_sum, (hidden, hidden, chunk))
        others = dot_right_t(d_key, w_keyval[:, :width]) + dot_right_t(d_value, w_keyval[:, width:])
        others = others.astype(BF)
        d_query, d_key, d_value, others = lax.optimization_barrier((d_query, d_key, d_value, others))
        attn_part = jnp.concatenate(
            [
                dot_left_t(own_inputs, d_query).astype(BF),
                dot_left_t(inputs, d_key).astype(BF),
                dot_left_t(inputs, d_value).astype(BF),
            ],
            axis=1,
        )
        others, attn_part = lax.optimization_barrier((others, attn_part))
        attn_sum = sum_data(attn_part)
        summed = quad_reduce(others)
        state_grad = d_one + dot_right_t(d_query, w_query) + summed
    attn_sum, ffn_grads = lax.optimization_barrier((attn_sum, ffn_grads))
    attn_grads[0] = sum_parts(attn_sum, (chunk,) * 3)
    input_grad = lax.ppermute(state_grad.astype(BF), EVERY, moves_back).astype(F32)

    qkv_grad = jnp.stack(attn_grads).reshape(LAYERS, depth, 3, head_local, HD)
    qkv_grad = qkv_grad.transpose(0, 1, 3, 2, 4).reshape(LAYERS, depth, 3 * chunk)
    ffn_own = jnp.stack(ffn_grads)
    up_grad = ffn_own[:, :, :hidden]
    down_grad = ffn_own[:, :, hidden : 2 * hidden].transpose(0, 2, 1)
    out_w_grad = ffn_own[:, :, 2 * hidden :].transpose(0, 2, 1)
    return (layer_output, input_grad, qkv_grad, out_w_grad, up_grad, down_grad) + tuple(
        norm_sums[k * LAYERS : (k + 1) * LAYERS] for k in range(4)
    )


def solution(mesh):
    devices = mesh.devices
    tensor = devices.shape[1]
    split = jax.sharding.Mesh(
        devices.reshape(devices.shape[0] // (ROW * QUAD), ROW, QUAD, tensor), EVERY
    )
    placed = (
        P(EVERY, None),
        P(None, DATA, "tensor"),
        P(None, "tensor", DATA),
        P(None, DATA, "tensor"),
        P(None, "tensor", DATA),
        P(),
        P(),
        P(),
        P(),
        P(EVERY, None),
        P(DATA, None),
        P(DATA, None),
        P(DATA, "tensor", None, None),
    )
    return jax.shard_map(
        local,
        mesh=split,
        in_specs=placed,
        out_specs=(
            P(EVERY, None),
            P(EVERY, None),
            P(None, DATA, "tensor"),
            P(None, "tensor", DATA),
            P(None, DATA, "tensor"),
            P(None, "tensor", DATA),
            P(),
            P(),
            P(),
            P(),
        ),
        check_vma=False,
    )
```

time: 833 us -> 779 us (0.935)
  blocking collectives: 87.9 us -> 0 us
  Pallas kernels: 209 us -> 241 us
  starting transfers between devices: 92.1 us -> 112 us
  matrix products: 151 us -> 133 us
  local copies, waits for them, and re-layouts: 71.3 us -> 53.4 us
  waiting for transfers between devices: 162 us -> 172 us
    pallas_call x0 -> x5, Pallas kernels: none -> 139 us  [the longest x2 62.3 us: quad_gather(): pl.pallas_call(functools.partial(gather_kernel, pieces), out_shape=[jax.S...]
    psum x1 -> x0, blocking collectives: 70.3 us -> none  [local(): lax.psum(tuple((jnp.stack([norm_parts[l][k] for l in range(LAYERS)]) for...]
    pallas_call x2, Pallas kernels: 119 us -> 54.8 us  [attend_backward(): pl.pallas_call(backward_kernel, grid_spec=pltpu.PrefetchScalarGridSpec(nu...]
    reduce_scatter x2, waiting for transfers between devices: 0.04 us -> 60.2 us  [sum_data(): return lax.psum_scatter(part, DATA, scatter_dimension=0, tiled=True)]
    reduce_scatter x2 -> x0, waiting for transfers between devices: 49.1 us -> none  [local(): summed = lax.psum_scatter(others, 'quad', scatter_dimension=0, tiled=True)]
    pallas_call x2, Pallas kernels: 90.2 us -> 46.7 us  [attend_forward(): pl.pallas_call(forward_kernel, grid_spec=pltpu.PrefetchScalarGridSpec(num...]
    ppermute x24, starting transfers between devices: 66.8 us -> 93.8 us  [shifted(): lax.ppermute(x, 'tensor', [(i, (i + by) % tensor) for i in range(tensor)])]
    ppermute x24, waiting for transfers between devices: 96.3 us -> 73.1 us  [shifted(): lax.ppermute(x, 'tensor', [(i, (i + by) % tensor) for i in range(tensor)])]
  transfers between devices with their start and end apart: 41 -> 37, of which waited for: 15 -> 14; matrix products, arithmetic and copies ran while one was open for 22% -> 16% of each run, Pallas kernels for 25% -> 28%
where the time goes in v3:
time: 779 us; the launch traced here: 768 us
  Pallas kernels  241 us (31%)
  waiting for transfers between devices  172 us (22%)
  matrix products  133 us (17%)
  starting transfers between devices  112 us (14%)
  local copies, waits for them, and re-layouts  53.4 us (7%)
  other arithmetic  40.6 us (5%)
  between operations  16.5 us (2%)
    ppermute x24, starting transfers between devices, shifted(): lax.ppermute(x, 'tensor', [(i, (i + by) % tensor) for i in range(tensor)])  93.8 us
    ppermute x24, waiting for transfers between devices, shifted(): lax.ppermute(x, 'tensor', [(i, (i + by) % tensor) for i in range(tensor)])  73.1 us
    pallas_call x2, Pallas kernels, quad_gather(): pl.pallas_call(functools.partial(gather_kernel, pieces), out_shape=[jax.S...  62.3 us
    reduce_scatter x2, waiting for transfers between devices, sum_data(): return lax.psum_scatter(part, DATA, scatter_dimension=0, tiled=True)  60.2 us
    pallas_call x2, Pallas kernels, quad_reduce(): pl.pallas_call(reduce_kernel, out_shape=jax.ShapeDtypeStruct((rows, width...  58.7 us
    dot_general x10, matrix products, dot(): return jnp.dot(left, right, preferred_element_type=F32)  55.8 us
    pallas_call x2, Pallas kernels, attend_backward(): pl.pallas_call(backward_kernel, grid_spec=pltpu.PrefetchScalarGridSpec(nu...  54.8 us
    dot_general x12, matrix products, dot_right_t(): lax.dot_general(left, right, (((1,), (1,)), ((), ())), preferred_element_...  48.9 us
  transfers between devices with their start and end apart: 37, of which 14 were waited for; matrix products, arithmetic and copies ran while one was open for 16% of the time, Pallas kernels for 28%

profile of v3, /device:TPU:0, one launch (start us, length us, event | category | flops | bytes accessed | tf_op | source)
XLA Modules:
  0.0 768.3 jit_solution(4104329365058531542)
XLA Ops:
  9.2 5.1 collective-permute-start.4
  15.3 12.6 %collective-permute-done.2 = bf16[96,768]{0,1:T(8,128)(2,1)S(1)} collective-permute-done((bf16[96,768]{0,1:T(8,128)(2,1)S(1)}, bf16[96,768]{0,1:T(8,128)(2,1)S(1)}, u32[]{:S(2)}, u32[]{:S(2)}) %collective-permute-start.2) | collective-permute-done | bytes 147488 | tf_op jit(solution)/shard_map/ppermute | solution.py:533
  27.9 3.1 collective-permute-done.3
  35.5 30.4 %collective-permute-start.12 = (bf16[96,1536]{1,0:T(8,128)(2,1)S(1)}, bf16[96,1536]{1,0:T(8,128)(2,1)S(1)}, u32[]{:S(2)}, u32[]{:S(2)}) collective-permute-start(bf16[96,1536]{1,0:T(8,128)(2,1)S(1)} %pad_maximum_fusion.13), channel_id=1, source_target_pairs={{0,1},{1,2},{2,3},{3,0},{4,5},{5,6},{6,7},{7,4},{8,9},{9,10},{10,1... | collective-permute-start | bytes 884744 | tf_op jit(solution)/shard_map/ppermute | solution.py:533
  67.5 5.9 collective-permute-done.12
  73.3 14.6 %collective-permute-done.13 = bf16[96,1536]{1,0:T(8,128)(2,1)S(1)} collective-permute-done((bf16[96,1536]{1,0:T(8,128)(2,1)S(1)}, bf16[96,1536]{1,0:T(8,128)(2,1)S(1)}, u32[]{:S(2)}, u32[]{:S(2)}) %collective-permute-start.13) | collective-permute-done | bytes 294944 | tf_op jit(solution)/shard_map/ppermute | solution.py:533
  89.3 31.6 %quad_gather.2 = (bf16[2048,768]{1,0:T(8,128)(2,1)}, bf16[64,768]{1,0:T(8,128)(2,1)}) custom-call(bf16[512,768]{1,0:T(8,128)(2,1)} %copy-done.16, bf16[16,768]{1,0:T(8,128)(2,1)} %copy-done.27), custom_call_target="tpu_custom_call" | custom-call | flops 1000000 | bytes 1000000 | tf_op jit(solution)/shard_map/quad_gather/pallas_call | solution.py:248
  127.7 9.1 %convolution_convert_fusion.1.k_ref.v_ref = bf16[2048,1536]{1,0:T(8,128)(2,1)} fusion(bf16[2048,768]{1,0:T(8,128)(2,1)} %get-tuple-element.73, bf16[768,3072]{1,0:T(8,128)(2,1)} %all-gather.5.cloned.1.call-done), kind=kOutput, calls=%fused_computation.7 | convolution fusion | flops 4834983936 | bytes 11796480 | tf_op jit(solution)/shard_map/dot_general | solution.py:41
  137.7 6.8 collective-permute-start.7
  145.8 3.3 collective-permute-start.10
  150.2 2.9 multiply_convert_fusion.3.q_ref
  153.2 23.2 %attend_forward.2 = (bf16[512,768]{1,0:T(8,128)(2,1)}, f32[8,1,768]{2,1,0:T(1,128)}) custom-call(s32[8,16]{1,0:T(8,128)} %select_reduce_fusion.keys_at, s32[8]{0:T(128)} %get-tuple-element.284.steps_of, bf16[512,768]{1,0:T(8,128)(2,1)} %multiply_convert_fusion.3.q_ref, bf16[2048,1536]{1,0:T(8,128)(2,1)} %convolution_convert_fusion.1.k_ref.v_ref, ...), custom_call_target="tpu_custom_call" | custom-call | flops 1000000 | bytes 1000000 | tf_op jit(solution)/shard_map/attend_forward/pallas_call | solution.py:392
  188.9 7.4 collective-permute-start.11
  196.3 2.8 fusion.110
  199.5 5.2 fusion.28
  204.8 4.0 fusion.111
  210.4 30.7 %quad_gather.3 = bf16[2048,768]{1,0:T(8,128)(2,1)} custom-call(bf16[512,768]{1,0:T(8,128)(2,1)} %fusion.51.refs_0_), custom_call_target="tpu_custom_call" | custom-call | flops 1000000 | bytes 1000000 | tf_op jit(solution)/shard_map/quad_gather/pallas_call | solution.py:248
  241.0 7.3 all-gather.9.cloned.1.call-done
  248.4 3.1 multiply_convert_fusion.2.q_ref
  251.4 8.5 %convolution_convert_fusion.k_ref.v_ref = bf16[2048,1536]{1,0:T(8,128)(2,1)} fusion(bf16[2048,768]{1,0:T(8,128)(2,1)S(1)} %copy-done.6, bf16[768,3072]{1,0:T(8,128)(2,1)} %all-gather.9.cloned.1.call-done), kind=kOutput, calls=%fused_computation.6 | convolution fusion | flops 4834983936 | bytes 11796480 | tf_op jit(solution)/shard_map/dot_general | solution.py:41
  260.0 23.5 %attend_forward.3 = (bf16[512,768]{1,0:T(8,128)(2,1)}, f32[8,1,768]{2,1,0:T(1,128)}) custom-call(s32[8,16]{1,0:T(8,128)} %select_reduce_fusion.keys_at, s32[8]{0:T(128)} %get-tuple-element.284.steps_of, bf16[512,768]{1,0:T(8,128)(2,1)} %multiply_convert_fusion.2.q_ref, bf16[2048,1536]{1,0:T(8,128)(2,1)} %convolution_convert_fusion.k_ref.v_ref, ...), custom_call_target="tpu_custom_call" | custom-call | flops 1000000 | bytes 1000000 | tf_op jit(solution)/shard_map/attend_forward/pallas_call | solution.py:392
  286.2 24.8 %all-gather.11.cloned.1.call-done = bf16[768,6144]{1,0:T(8,128)(2,1)} async-done(((bf16[96,6144]{1,0:T(8,128)(2,1)}), bf16[768,6144]{1,0:T(8,128)(2,1)}) %all-gather.11.cloned.1.call-update) | async-done | bytes 9437200 | tf_op jit(solution)/shard_map/all_gather | solution.py:553
  311.1 5.3 fusion.20
  316.4 4.0 fusion.113
  322.5 2.7 fusion.97
  325.3 3.3 convolution_convert_fusion.4
  328.6 6.1 fusion.13
  336.3 3.5 convolution_convert_fusion.5
  339.9 5.0 multiply_reduce_fusion.1
  349.0 8.0 %pad_maximum_fusion = bf16[768,6912]{1,0:T(8,128)(2,1)} fusion(bf16[768,768]{1,0:T(8,128)(2,1)S(1)} %convolution_convert_fusion.13, bf16[768,3072]{1,0:T(8,128)(2,1)S(1)} %convolution_convert_fusion.4, bf16[768,3072]{1,0:T(8,128)(2,1)S(1)} %convolution_convert_fusion.5), kind=kLoop, calls=%fused_computation | loop fusion | flops 31850496 | bytes 21233664 | tf_op jit(solution)/shard_map/concatenate | solution.py:663
  357.0 7.4 collective-permute-start.15
  364.5 3.6 convolution_convert_fusion.15.d_ref
  368.1 27.7 %attend_backward.2 = (bf16[512,768]{1,0:T(8,128)(2,1)}, bf16[2048,768]{1,0:T(8,128)(2,1)}, bf16[2048,768]{1,0:T(8,128)(2,1)}) custom-call(s32[8,16]{1,0:T(8,128)} %select_reduce_fusion.keys_at, s32[8]{0:T(128)} %get-tuple-element.284.steps_of, bf16[512,768]{1,0:T(8,128)(2,1)} %multiply_convert_fusion.2.q_ref, ...), custom_call_target="tpu_custom_call" | custom-call | flops 1000000 | bytes 1000000 | tf_op jit(solution)/shard_map/attend_backward/pallas_call | solution.py:423
  395.8 47.1 %reduce-scatter.9.cloned.1.call-done = bf16[96,6912]{1,0:T(8,128)(2,1)} async-done(((bf16[768,6912]{1,0:T(8,128)(2,1)}), bf16[96,6912]{1,0:T(8,128)(2,1)}) %reduce-scatter.9.cloned.1.call-update) | async-done | bytes 1327120 | tf_op jit(solution)/shard_map/reduce_scatter | solution.py:637
  442.9 5.0 fusion.56
  447.9 5.6 add_convert_fusion.1.parts_ref
  455.4 2.7 convolution_convert_fusion.11
  458.1 2.7 convolution_convert_fusion.10
  462.8 24.5 %quad_reduce.2 = f32[512,768]{1,0:T(8,128)} custom-call(bf16[2048,768]{1,0:T(8,128)(2,1)} %add_convert_fusion.1.parts_ref), custom_call_target="tpu_custom_call" | custom-call | flops 1000000 | bytes 1000000 | tf_op jit(solution)/shard_map/quad_reduce/pallas_call | solution.py:314
  487.3 3.3 multiply_reduce_fusion
  491.2 5.9 copy.201
  497.2 9.0 %fusion.6 = bf16[512,3072]{1,0:T(8,128)(2,1)S(1)} fusion(f32[512,3072]{1,0:T(8,128)} %copy-done.45, bf16[768,6144]{1,0:T(8,128)(2,1)} %all-gather.7.cloned.1.call-done, f32[512,768]{1,0:T(8,128)S(1)} %get-tuple-element.205, f32[512]{0:T(512)S(1)} %negate_multiply_fusion.1), kind=kOutput, calls=%fused_computation.14 | convolution fusion | flops 2448162816 | bytes 15730688 | tf_op jit(solution)/shard_map/dot_general | solution.py:41
  506.3 3.2 multiply_reduce_fusion.2
  513.1 3.4 convolution_convert_fusion.3
  516.6 3.3 convolution_convert_fusion.2
  519.9 8.0 %pad_maximum_fusion.1 = bf16[768,6912]{1,0:T(8,128)(2,1)} fusion(bf16[768,768]{1,0:T(8,128)(2,1)S(1)} %convolution_convert_fusion.9, bf16[768,3072]{1,0:T(8,128)(2,1)S(1)} %convolution_convert_fusion.2, bf16[768,3072]{1,0:T(8,128)(2,1)S(1)} %convolution_convert_fusion.3), kind=kLoop, calls=%fused_computation.1 | loop fusion | flops 31850496 | bytes 21233664 | tf_op jit(solution)/shard_map/concatenate | solution.py:663
  537.8 2.9 convolution_convert_fusion.14.d_ref
  540.7 5.1 collective-permute-done.18
  545.8 5.8 collective-permute-done.16
  551.7 15.3 %collective-permute-done.17 = bf16[96,1728]{1,0:T(8,128)(2,1)S(1)} collective-permute-done((bf16[96,1728]{1,0:T(8,128)(2,1)S(1)}, bf16[96,1728]{1,0:T(8,128)(2,1)S(1)}, u32[]{:S(2)}, u32[]{:S(2)}) %collective-permute-start.17) | collective-permute-done | bytes 331808 | tf_op jit(solution)/shard_map/ppermute | solution.py:533
  572.5 18.4 %sum_everywhere.1 = f32[8,768]{1,0:T(8,128)} custom-call(f32[8,768]{1,0:T(8,128)} %stack.36.x_ref), custom_call_target="tpu_custom_call" | custom-call | flops 1000000 | bytes 1000000 | tf_op jit(solution)/shard_map/sum_everywhere/pallas_call | solution.py:369
  590.9 27.1 %attend_backward.3 = (bf16[512,768]{1,0:T(8,128)(2,1)}, bf16[2048,768]{1,0:T(8,128)(2,1)}, bf16[2048,768]{1,0:T(8,128)(2,1)}) custom-call(s32[8,16]{1,0:T(8,128)} %select_reduce_fusion.keys_at, s32[8]{0:T(128)} %get-tuple-element.284.steps_of, bf16[512,768]{1,0:T(8,128)(2,1)} %multiply_convert_fusion.3.q_ref, ...), custom_call_target="tpu_custom_call" | custom-call | flops 1000000 | bytes 1000000 | tf_op jit(solution)/shard_map/attend_backward/pallas_call | solution.py:423
  618.8 13.1 %reduce-scatter.11.cloned.1.call-done = bf16[96,6912]{1,0:T(8,128)(2,1)} async-done(((bf16[768,6912]{1,0:T(8,128)(2,1)}), bf16[96,6912]{1,0:T(8,128)(2,1)}) %reduce-scatter.11.cloned.1.call-update) | async-done | bytes 1327120 | tf_op jit(solution)/shard_map/reduce_scatter | solution.py:637
  631.9 5.2 fusion.54
  637.1 5.7 add_convert_fusion.parts_ref
  644.7 2.9 convolution_convert_fusion.7
  647.6 2.9 convolution_convert_fusion.6
  650.9 4.0 copy.203
  664.6 34.2 %quad_reduce.3 = f32[512,768]{1,0:T(8,128)} custom-call(bf16[2048,768]{1,0:T(8,128)(2,1)} %add_convert_fusion.parts_ref), custom_call_target="tpu_custom_call" | custom-call | flops 1000000 | bytes 1000000 | tf_op jit(solution)/shard_map/quad_reduce/pallas_call | solution.py:314
  698.9 2.8 add_convert_fusion.2
  705.8 5.9 reduce-scatter.15.cloned.1.call-done
  714.0 13.8 %collective-permute-start.26 = (bf16[96,576]{0,1:T(8,128)(2,1)S(1)}, bf16[96,576]{0,1:T(8,128)(2,1)S(1)}, u32[]{:S(2)}, u32[]{:S(2)}) collective-permute-start(bf16[96,576]{0,1:T(8,128)(2,1)S(1)} %pad_maximum_fusion.19), channel_id=1, source_target_pairs={{0,3},{1,0},{2,1},{3,2},{4,7},{5,4},{6,5},{7,6},{8,11},{9,8},{10,9... | collective-permute-start | bytes 331784 | tf_op jit(solution)/shard_map/ppermute | solution.py:533
  727.8 16.6 %collective-permute-start.27 = (bf16[96,576]{0,1:T(8,128)(2,1)S(1)}, bf16[96,576]{0,1:T(8,128)(2,1)S(1)}, u32[]{:S(2)}, u32[]{:S(2)}) collective-permute-start(bf16[96,576]{0,1:T(8,128)(2,1)S(1)} %pad_maximum_fusion.20), channel_id=1, source_target_pairs={{0,2},{1,3},{2,0},{3,1},{4,6},{5,7},{6,4},{7,5},{8,10},{9,11},{10,... | collective-permute-start | bytes 331784 | tf_op jit(solution)/shard_map/ppermute | solution.py:533
  747.7 10.1 %collective-permute-done.27 = bf16[96,576]{0,1:T(8,128)(2,1)S(1)} collective-permute-done((bf16[96,576]{0,1:T(8,128)(2,1)S(1)}, bf16[96,576]{0,1:T(8,128)(2,1)S(1)}, u32[]{:S(2)}, u32[]{:S(2)}) %collective-permute-start.27) | collective-permute-done | bytes 110624 | tf_op jit(solution)/shard_map/ppermute | solution.py:533
  (392 shorter events, 93.9 us)
Async XLA Ops:
  7.2 24.1 %copy-start.25 = (bf16[2,192,96]{2,1,0:T(8,128)(2,1)S(1)}, bf16[2,192,96]{2,1,0:T(8,128)(2,1)}, u32[]{:S(2)}) copy-start(bf16[2,192,96]{2,1,0:T(8,128)(2,1)} %param.15) | copy-start | bytes 221188
  7.2 120.5 %all-gather.5.cloned.1.call-start = ((), (), s32[]{:S(2)}) async-start(), calls=%async_computation.4 | async-start | bytes 5308416 | tf_op jit(solution)/shard_map/all_gather | solution.py:553
  9.2 21.8 %collective-permute-start.4 = (bf16[96,768]{0,1:T(8,128)(2,1)S(1)}, bf16[96,768]{0,1:T(8,128)(2,1)S(1)}, u32[]{:S(2)}, u32[]{:S(2)}) collective-permute-start(bf16[96,768]{0,1:T(8,128)(2,1)S(1)} %pad_maximum_fusion.14), channel_id=1, source_target_pairs={{0,3},{1,0},{2,1},{3,2},{4,7},{5,4},{6,5},{7,6},{8,11},{9,8},{10,9... | collective-permute-start | bytes 442376 | tf_op jit(solution)/shard_map/ppermute | solution.py:533
  14.3 16.7 %collective-permute-start.3 = (bf16[96,768]{0,1:T(8,128)(2,1)S(1)}, bf16[96,768]{0,1:T(8,128)(2,1)S(1)}, u32[]{:S(2)}, u32[]{:S(2)}) collective-permute-start(bf16[96,768]{0,1:T(8,128)(2,1)S(1)} %pad_maximum_fusion.14), channel_id=1, source_target_pairs={{0,2},{1,3},{2,0},{3,1},{4,6},{5,7},{6,4},{7,5},{8,10},{9,11},{10,... | collective-permute-start | bytes 442376 | tf_op jit(solution)/shard_map/ppermute | solution.py:533
  14.3 13.6 %collective-permute-start.2 = (bf16[96,768]{0,1:T(8,128)(2,1)S(1)}, bf16[96,768]{0,1:T(8,128)(2,1)S(1)}, u32[]{:S(2)}, u32[]{:S(2)}) collective-permute-start(bf16[96,768]{0,1:T(8,128)(2,1)S(1)} %pad_maximum_fusion.14), channel_id=1, source_target_pairs={{0,1},{1,2},{2,3},{3,0},{4,5},{5,6},{6,7},{7,4},{8,9},{9,10},{10,1... | collective-permute-start | bytes 442376 | tf_op jit(solution)/shard_map/ppermute | solution.py:533
  31.1 4.3 copy-start.22
  32.4 167.1 %all-gather.7.cloned.1.call-start = ((), (), s32[]{:S(2)}) async-start(), calls=%async_computation.5 | async-start | bytes 10616832 | tf_op jit(solution)/shard_map/all_gather | solution.py:553
  32.5 3.0 collective-permute-start
  34.7 0.7 collective-permute-start.1
  35.4 53.7 %copy-start.27 = (bf16[16,768]{1,0:T(8,128)(2,1)}, bf16[16,768]{1,0:T(8,128)(2,1)S(1)}, u32[]{:S(2)}) copy-start(bf16[16,768]{1,0:T(8,128)(2,1)S(1)} %collective-permute-done.1.refs_1_) | copy-start | bytes 73732
  35.5 53.7 %copy-start.16 = (bf16[512,768]{1,0:T(8,128)(2,1)}, bf16[512,768]{1,0:T(8,128)(2,1)S(1)}, u32[]{:S(2)}) copy-start(bf16[512,768]{1,0:T(8,128)(2,1)S(1)} %collective-permute-done.refs_0_) | copy-start | bytes 2359300
  35.5 37.8 %collective-permute-start.12 = (bf16[96,1536]{1,0:T(8,128)(2,1)S(1)}, bf16[96,1536]{1,0:T(8,128)(2,1)S(1)}, u32[]{:S(2)}, u32[]{:S(2)}) collective-permute-start(bf16[96,1536]{1,0:T(8,128)(2,1)S(1)} %pad_maximum_fusion.13), channel_id=1, source_target_pairs={{0,1},{1,2},{2,3},{3,0},{4,5},{5,6},{6,7},{7,4},{8,9},{9,10},{10,1... | collective-permute-start | bytes 884744 | tf_op jit(solution)/shard_map/ppermute | solution.py:533
  65.9 22.1 %collective-permute-start.14 = (bf16[96,1536]{1,0:T(8,128)(2,1)S(1)}, bf16[96,1536]{1,0:T(8,128)(2,1)S(1)}, u32[]{:S(2)}, u32[]{:S(2)}) collective-permute-start(bf16[96,1536]{1,0:T(8,128)(2,1)S(1)} %pad_maximum_fusion.13), channel_id=1, source_target_pairs={{0,3},{1,0},{2,1},{3,2},{4,7},{5,4},{6,5},{7,6},{8,11},{9,8},{10,9... | collective-permute-start | bytes 884744 | tf_op jit(solution)/shard_map/ppermute | solution.py:533
  65.9 22.1 %collective-permute-start.13 = (bf16[96,1536]{1,0:T(8,128)(2,1)S(1)}, bf16[96,1536]{1,0:T(8,128)(2,1)S(1)}, u32[]{:S(2)}, u32[]{:S(2)}) collective-permute-start(bf16[96,1536]{1,0:T(8,128)(2,1)S(1)} %pad_maximum_fusion.13), channel_id=1, source_target_pairs={{0,2},{1,3},{2,0},{3,1},{4,6},{5,7},{6,4},{7,5},{8,10},{9,11},{10,... | collective-permute-start | bytes 884744 | tf_op jit(solution)/shard_map/ppermute | solution.py:533
  89.2 159.2 %all-gather.9.cloned.1.call-start = ((), (), s32[]{:S(2)}) async-start(), calls=%async_computation.6 | async-start | bytes 5308416 | tf_op jit(solution)/shard_map/all_gather | solution.py:553
  127.7 9.1 %copy-start.24 = (bf16[2,96,576]{2,1,0:T(8,128)(2,1)S(1)}, bf16[2,96,576]{2,1,0:T(8,128)(2,1)}, u32[]{:S(2)}) copy-start(bf16[2,96,576]{2,1,0:T(8,128)(2,1)} %param.14) | copy-start | bytes 663556
  136.8 13.5 %copy-start.17 = (bf16[512,768]{1,0:T(8,128)(2,1)S(1)}, bf16[512,768]{1,0:T(8,128)(2,1)}, u32[]{:S(2)}) copy-start(bf16[512,768]{1,0:T(8,128)(2,1)} %copy-done.16) | copy-start | bytes 2359300
  137.7 40.3 %collective-permute-start.7 = (bf16[96,768]{0,1:T(8,128)(2,1)}, bf16[96,768]{0,1:T(8,128)(2,1)}, u32[]{:S(2)}, u32[]{:S(2)}) collective-permute-start(bf16[96,768]{0,1:T(8,128)(2,1)} %pad_maximum_fusion.15), channel_id=1, source_target_pairs={{0,3},{1,0},{2,1},{3,2},{4,7},{5,4},{6,5},{7,6},{8,11},{9,8},{10,9... | collective-permute-start | bytes 442376 | tf_op jit(solution)/shard_map/ppermute | solution.py:533
  144.5 32.8 %collective-permute-start.6 = (bf16[96,768]{0,1:T(8,128)(2,1)}, bf16[96,768]{0,1:T(8,128)(2,1)}, u32[]{:S(2)}, u32[]{:S(2)}) collective-permute-start(bf16[96,768]{0,1:T(8,128)(2,1)} %pad_maximum_fusion.15), channel_id=1, source_target_pairs={{0,2},{1,3},{2,0},{3,1},{4,6},{5,7},{6,4},{7,5},{8,10},{9,11},{10,... | collective-permute-start | bytes 442376 | tf_op jit(solution)/shard_map/ppermute | solution.py:533
  144.5 31.9 %collective-permute-start.5 = (bf16[96,768]{0,1:T(8,128)(2,1)}, bf16[96,768]{0,1:T(8,128)(2,1)}, u32[]{:S(2)}, u32[]{:S(2)}) collective-permute-start(bf16[96,768]{0,1:T(8,128)(2,1)} %pad_maximum_fusion.15), channel_id=1, source_target_pairs={{0,1},{1,2},{2,3},{3,0},{4,5},{5,6},{6,7},{7,4},{8,9},{9,10},{10,1... | collective-permute-start | bytes 442376 | tf_op jit(solution)/shard_map/ppermute | solution.py:533
  145.8 41.0 %collective-permute-start.10 = (bf16[96,1536]{1,0:T(8,128)(2,1)}, bf16[96,1536]{1,0:T(8,128)(2,1)S(1)}, u32[]{:S(2)}, u32[]{:S(2)}) collective-permute-start(bf16[96,1536]{1,0:T(8,128)(2,1)} %pad_maximum_fusion.12), channel_id=1, source_target_pairs={{0,3},{1,0},{2,1},{3,2},{4,7},{5,4},{6,5},{7,6},{8,11},{9,8},{10,9... | collective-permute-start | bytes 884744 | tf_op jit(solution)/shard_map/ppermute | solution.py:533
  149.1 37.7 %collective-permute-start.9 = (bf16[96,1536]{1,0:T(8,128)(2,1)}, bf16[96,1536]{1,0:T(8,128)(2,1)S(1)}, u32[]{:S(2)}, u32[]{:S(2)}) collective-permute-start(bf16[96,1536]{1,0:T(8,128)(2,1)} %pad_maximum_fusion.12), channel_id=1, source_target_pairs={{0,2},{1,3},{2,0},{3,1},{4,6},{5,7},{6,4},{7,5},{8,10},{9,11},{10,... | collective-permute-start | bytes 884744 | tf_op jit(solution)/shard_map/ppermute | solution.py:533
  176.4 10.4 %collective-permute-start.8 = (bf16[96,1536]{1,0:T(8,128)(2,1)}, bf16[96,1536]{1,0:T(8,128)(2,1)S(1)}, u32[]{:S(2)}, u32[]{:S(2)}) collective-permute-start(bf16[96,1536]{1,0:T(8,128)(2,1)} %pad_maximum_fusion.12), channel_id=1, source_target_pairs={{0,1},{1,2},{2,3},{3,0},{4,5},{5,6},{6,7},{7,4},{8,9},{9,10},{10,1... | collective-permute-start | bytes 884744 | tf_op jit(solution)/shard_map/ppermute | solution.py:533
  188.2 122.9 %all-gather.11.cloned.1.call-start = ((), (), s32[]{:S(2)}) async-start(), calls=%async_computation.7 | async-start | bytes 10616832 | tf_op jit(solution)/shard_map/all_gather | solution.py:553
  188.8 254.1 %reduce-scatter.9.cloned.1.call-start = ((), (), s32[]{:S(2)}) async-start(), calls=%async_computation.8 | async-start | bytes 11943936 | tf_op jit(solution)/shard_map/reduce_scatter | solution.py:637
  188.9 131.8 %collective-permute-start.11 = (bf16[512,768]{1,0:T(8,128)(2,1)}, bf16[512,768]{1,0:T(8,128)(2,1)}, u32[]{:S(2)}, u32[]{:S(2)}) collective-permute-start(bf16[512,768]{1,0:T(8,128)(2,1)} %param.22), channel_id=1, source_target_pairs={{0,0},{1,4},{2,8},{3,12},{4,3},{5,7},{6,11},{7,15},{8,1},{9,5},{10... | collective-permute-start | bytes 2359304 | tf_op jit(solution)/shard_map/ppermute | solution.py:612
  199.2 5.6 copy-start
  199.5 5.3 copy-start.35
  210.4 38.0 %copy-start.8 = (bf16[512,768]{1,0:T(8,128)(2,1)S(1)}, bf16[512,768]{1,0:T(8,128)(2,1)}, u32[]{:S(2)}) copy-start(bf16[512,768]{1,0:T(8,128)(2,1)} %fusion.51.refs_0_) | copy-start | bytes 2359300
  285.9 53.9 %copy-start.2 = (f32[512,768]{1,0:T(8,128)}, f32[512,768]{1,0:T(8,128)S(1)}, u32[]{:S(2)}) copy-start(f32[512,768]{1,0:T(8,128)S(1)} %get-tuple-element.290) | copy-start | bytes 4718596
  311.1 5.3 copy-start.36
  357.0 211.0 %reduce-scatter.13.cloned.1.call-start = ((), (), s32[]{:S(2)}) async-start(), calls=%async_computation.10 | async-start | bytes 3981312
  357.0 38.8 %collective-permute-start.15 = (bf16[512,768]{1,0:T(8,128)(2,1)}, bf16[512,768]{1,0:T(8,128)(2,1)}, u32[]{:S(2)}, u32[]{:S(2)}) collective-permute-start(bf16[512,768]{1,0:T(8,128)(2,1)} %get-tuple-element.214), channel_id=1, source_target_pairs={{0,0},{4,1},{8,2},{12,3},{3,4},{7,5},{11,6},{15,7},{1,8},{5,9},{9,... | collective-permute-start | bytes 2359304 | tf_op jit(solution)/shard_map/ppermute | solution.py:623
  442.9 5.0 copy-start.41
  447.9 5.6 copy-start.9
  447.9 5.6 copy-start.15
  491.2 15.1 %slice-start.2 = ((s8[9437184]{0:T(1024)(128)(4,1)}), s8[1048576]{0:T(1024)(128)(4,1)S(1)}, s32[]{:S(2)}) async-start(s8[9437184]{0:T(1024)(128)(4,1)} %bitcast.285), calls=%async_computation.14 | async-start | bytes 2097152
  497.1 134.8 %reduce-scatter.11.cloned.1.call-start = ((), (), s32[]{:S(2)}) async-start(), calls=%async_computation.9 | async-start | bytes 11943936 | tf_op jit(solution)/shard_map/reduce_scatter | solution.py:637
  497.2 9.1 %copy-start.1 = (f32[512,768]{1,0:T(8,128)S(1)}, f32[512,768]{1,0:T(8,128)}, u32[]{:S(2)}) copy-start(f32[512,768]{1,0:T(8,128)} %copy-done) | copy-start | bytes 4718596
  497.2 9.1 %slice-start.3 = ((s8[9437184]{0:T(1024)(128)(4,1)}), s8[4194304]{0:T(1024)(128)(4,1)S(1)}, s32[]{:S(2)}) async-start(s8[9437184]{0:T(1024)(128)(4,1)} %bitcast.285), calls=%async_computation.15 | async-start | bytes 8388608
  497.2 9.1 %slice-start.4 = ((s8[9437184]{0:T(1024)(128)(4,1)}), s8[4194304]{0:T(1024)(128)(4,1)S(1)}, s32[]{:S(2)}) async-start(s8[9437184]{0:T(1024)(128)(4,1)} %bitcast.285), calls=%async_computation.16 | async-start | bytes 8388608
  511.3 5.3 slice-start.5
  527.9 183.8 %reduce-scatter.15.cloned.1.call-start = ((), (), s32[]{:S(2)}) async-start(), calls=%async_computation.11 | async-start | bytes 3981312
  533.0 4.8 copy-start.20
  533.0 12.8 %collective-permute-start.18 = (bf16[96,1728]{1,0:T(8,128)(2,1)S(1)}, bf16[96,1728]{1,0:T(8,128)(2,1)S(1)}, u32[]{:S(2)}, u32[]{:S(2)}) collective-permute-start(bf16[96,1728]{1,0:T(8,128)(2,1)S(1)} %pad_maximum_fusion.8), channel_id=1, source_target_pairs={{0,1},{1,2},{2,3},{3,0},{4,5},{5,6},{6,7},{7,4},{8,9},{9,10},{10,1... | collective-permute-start | bytes 995336 | tf_op jit(solution)/shard_map/ppermute | solution.py:533
  534.6 17.1 %collective-permute-start.16 = (bf16[96,1728]{1,0:T(8,128)(2,1)S(1)}, bf16[96,1728]{1,0:T(8,128)(2,1)S(1)}, u32[]{:S(2)}, u32[]{:S(2)}) collective-permute-start(bf16[96,1728]{1,0:T(8,128)(2,1)S(1)} %pad_maximum_fusion.6), channel_id=1, source_target_pairs={{0,3},{1,0},{2,1},{3,2},{4,7},{5,4},{6,5},{7,6},{8,11},{9,8},{10,9... | collective-permute-start | bytes 995336 | tf_op jit(solution)/shard_map/ppermute | solution.py:533
  537.0 29.9 %collective-permute-start.17 = (bf16[96,1728]{1,0:T(8,128)(2,1)S(1)}, bf16[96,1728]{1,0:T(8,128)(2,1)S(1)}, u32[]{:S(2)}, u32[]{:S(2)}) collective-permute-start(bf16[96,1728]{1,0:T(8,128)(2,1)S(1)} %pad_maximum_fusion.7), channel_id=1, source_target_pairs={{0,2},{1,3},{2,0},{3,1},{4,6},{5,7},{6,4},{7,5},{8,10},{9,11},{10,... | collective-permute-start | bytes 995336 | tf_op jit(solution)/shard_map/ppermute | solution.py:533
  569.5 48.5 %collective-permute-start.19 = (bf16[96,576]{0,1:T(8,128)(2,1)S(1)}, bf16[96,576]{0,1:T(8,128)(2,1)S(1)}, u32[]{:S(2)}, u32[]{:S(2)}) collective-permute-start(bf16[96,576]{0,1:T(8,128)(2,1)S(1)} %pad_maximum_fusion.16), channel_id=1, source_target_pairs={{0,3},{1,0},{2,1},{3,2},{4,7},{5,4},{6,5},{7,6},{8,11},{9,8},{10,9... | collective-permute-start | bytes 331784 | tf_op jit(solution)/shard_map/ppermute | solution.py:533
  571.1 46.9 %collective-permute-start.20 = (bf16[96,576]{0,1:T(8,128)(2,1)S(1)}, bf16[96,576]{0,1:T(8,128)(2,1)S(1)}, u32[]{:S(2)}, u32[]{:S(2)}) collective-permute-start(bf16[96,576]{0,1:T(8,128)(2,1)S(1)} %pad_maximum_fusion.17), channel_id=1, source_target_pairs={{0,2},{1,3},{2,0},{3,1},{4,6},{5,7},{6,4},{7,5},{8,10},{9,11},{10,... | collective-permute-start | bytes 331784 | tf_op jit(solution)/shard_map/ppermute | solution.py:533
  571.2 46.8 %collective-permute-start.21 = (bf16[96,576]{0,1:T(8,128)(2,1)S(1)}, bf16[96,576]{0,1:T(8,128)(2,1)S(1)}, u32[]{:S(2)}, u32[]{:S(2)}) collective-permute-start(bf16[96,576]{0,1:T(8,128)(2,1)S(1)} %pad_maximum_fusion.18), channel_id=1, source_target_pairs={{0,1},{1,2},{2,3},{3,0},{4,5},{5,6},{6,7},{7,4},{8,9},{9,10},{10,1... | collective-permute-start | bytes 331784 | tf_op jit(solution)/shard_map/ppermute | solution.py:533
  631.9 5.2 copy-start.38
  637.1 5.7 copy-start.18
  637.1 5.7 copy-start.43
  637.1 6.6 copy-start.39
  659.9 43.2 %collective-permute-start.25 = (bf16[96,1728]{1,0:T(8,128)(2,1)S(1)}, bf16[96,1728]{1,0:T(8,128)(2,1)}, u32[]{:S(2)}, u32[]{:S(2)}) collective-permute-start(bf16[96,1728]{1,0:T(8,128)(2,1)S(1)} %pad_maximum_fusion.11), channel_id=1, source_target_pairs={{0,1},{1,2},{2,3},{3,0},{4,5},{5,6},{6,7},{7,4},{8,9},{9,10},{10,1... | collective-permute-start | bytes 995336 | tf_op jit(solution)/shard_map/ppermute | solution.py:533
  661.5 41.6 %collective-permute-start.23 = (bf16[96,1728]{1,0:T(8,128)(2,1)S(1)}, bf16[96,1728]{1,0:T(8,128)(2,1)}, u32[]{:S(2)}, u32[]{:S(2)}) collective-permute-start(bf16[96,1728]{1,0:T(8,128)(2,1)S(1)} %pad_maximum_fusion.9), channel_id=1, source_target_pairs={{0,3},{1,0},{2,1},{3,2},{4,7},{5,4},{6,5},{7,6},{8,11},{9,8},{10,9... | collective-permute-start | bytes 995336 | tf_op jit(solution)/shard_map/ppermute | solution.py:533
  663.9 34.9 %copy-start.4 = (f32[512,768]{1,0:T(8,128)S(1)}, f32[512,768]{1,0:T(8,128)}, u32[]{:S(2)}) copy-start(f32[512,768]{1,0:T(8,128)} %copy-done.3) | copy-start | bytes 4718596
  663.9 39.2 %collective-permute-start.24 = (bf16[96,1728]{1,0:T(8,128)(2,1)S(1)}, bf16[96,1728]{1,0:T(8,128)(2,1)}, u32[]{:S(2)}, u32[]{:S(2)}) collective-permute-start(bf16[96,1728]{1,0:T(8,128)(2,1)S(1)} %pad_maximum_fusion.10), channel_id=1, source_target_pairs={{0,2},{1,3},{2,0},{3,1},{4,6},{5,7},{6,4},{7,5},{8,10},{9,11},{10,... | collective-permute-start | bytes 995336 | tf_op jit(solution)/shard_map/ppermute | solution.py:533
  701.7 2.8 collective-permute-start.22
  705.8 7.3 copy-start.5
  714.0 33.7 %collective-permute-start.26 = (bf16[96,576]{0,1:T(8,128)(2,1)S(1)}, bf16[96,576]{0,1:T(8,128)(2,1)S(1)}, u32[]{:S(2)}, u32[]{:S(2)}) collective-permute-start(bf16[96,576]{0,1:T(8,128)(2,1)S(1)} %pad_maximum_fusion.19), channel_id=1, source_target_pairs={{0,3},{1,0},{2,1},{3,2},{4,7},{5,4},{6,5},{7,6},{8,11},{9,8},{10,9... | collective-permute-start | bytes 331784 | tf_op jit(solution)/shard_map/ppermute | solution.py:533
  727.8 29.9 %collective-permute-start.27 = (bf16[96,576]{0,1:T(8,128)(2,1)S(1)}, bf16[96,576]{0,1:T(8,128)(2,1)S(1)}, u32[]{:S(2)}, u32[]{:S(2)}) collective-permute-start(bf16[96,576]{0,1:T(8,128)(2,1)S(1)} %pad_maximum_fusion.20), channel_id=1, source_target_pairs={{0,2},{1,3},{2,0},{3,1},{4,6},{5,7},{6,4},{7,5},{8,10},{9,11},{10,... | collective-permute-start | bytes 331784 | tf_op jit(solution)/shard_map/ppermute | solution.py:533
  744.5 13.3 %copy-start.14 = (f32[96,576]{0,1:T(8,128)S(1)}, f32[96,576]{0,1:T(8,128)}, u32[]{:S(2)}) copy-start(f32[96,576]{0,1:T(8,128)} %convert_add_fusion.4) | copy-start | bytes 663556
  744.5 13.2 %collective-permute-start.28 = (bf16[96,576]{0,1:T(8,128)(2,1)S(1)}, bf16[96,576]{0,1:T(8,128)(2,1)S(1)}, u32[]{:S(2)}, u32[]{:S(2)}) collective-permute-start(bf16[96,576]{0,1:T(8,128)(2,1)S(1)} %pad_maximum_fusion.21), channel_id=1, source_target_pairs={{0,1},{1,2},{2,3},{3,0},{4,5},{5,6},{6,7},{7,4},{8,9},{9,10},{10,1... | collective-permute-start | bytes 331784 | tf_op jit(solution)/shard_map/ppermute | solution.py:533
  (27 other events, 57.2 us)
Sparse Core Ops, SparseCore 0:
  32.6 50.9 all-gather.4
  89.3 70.0 all-gather.6
  188.3 60.0 all-gather.8
  250.1 60.9 all-gather.10
  357.1 85.6 reduce-scatter.8
  497.2 47.8 reduce-scatter.12
  548.7 83.1 reduce-scatter.10
  655.0 56.6 reduce-scatter.14

commit v4 on v3

--- a/solution.py
+++ b/solution.py
@@ -116,7 +116,25 @@
 
 
 def backward_kernel(
-    keys_at, steps_of, q_ref, k_ref, v_ref, bias_ref, log_ref, d_ref, dq_ref, dk_ref, dv_ref, dkey, dvalue
+    keys_at,
+    steps_of,
+    q_ref,
+    k_ref,
+    v_ref,
+    bias_ref,
+    log_ref,
+    d_ref,
+    own_ref,
+    in_ref,
+    wk_ref,
+    wv_ref,
+    dq_ref,
+    others_ref,
+    grad_ref,
+    dkey,
+    dvalue,
+    low,
+    back_sum,
 ):
     dkey[...] = jnp.zeros_like(dkey)
     dvalue[...] = jnp.zeros_like(dvalue)
@@ -160,13 +178,28 @@
         return carry
 
     lax.fori_loop(0, q_ref.shape[0] // BLK, one_block, 0)
-    dk_ref[...] = dkey[...].astype(BF)
-    dv_ref[...] = dvalue[...].astype(BF)
+
+    low[0] = dkey[...].astype(BF)
+    low[1] = dvalue[...].astype(BF)
+    grad_ref[:, :WIDE] = dot_left_t(own_ref[...], dq_ref[...]).astype(BF)
+    grad_ref[:, WIDE : 2 * WIDE] = dot_left_t(in_ref[...], low[0]).astype(BF)
+    grad_ref[:, 2 * WIDE :] = dot_left_t(in_ref[...], low[1]).astype(BF)
+    quad = pl.program_id(0)
+
+    def others(r, carry):
+        at = pl.ds(pl.multiple_of(r * WIDE, WIDE), WIDE)
+        part = dot_right_t(low[0, at, :], wk_ref[...]) + dot_right_t(low[1, at, :], wv_ref[...])
+        so_far = jnp.where(quad == 0, jnp.zeros_like(part), back_sum[at, :]) + part
+        back_sum[at, :] = so_far
+        others_ref[at, :] = so_far.astype(BF)
+        return carry
+
+    lax.fori_loop(0, in_ref.shape[0] // WIDE, others, 0)
 
 
 SHORT = pl.CostEstimate(flops=1_000_000, bytes_accessed=1_000_000, transcendentals=0)
 MESH_ID = pl.DeviceIdType.MESH
-CALL_GATHER_FIRST, CALL_GATHER, CALL_REDUCE, CALL_NORMS = range(4)
+CALL_GATHER_FIRST, CALL_GATHER, CALL_REDUCE, CALL_NORMS, CALL_ROWS, CALL_LINE_FFN, CALL_LINE_ATTN, CALL_BOTH = range(8)
 
 
 def quad_places():
@@ -261,10 +294,22 @@
 
 
 def reduce_kernel(
-    parts_ref, out_ref, near, relay, beyond, mate_send, mate_recv, own_send, own_recv, far_send, far_recv
+    parts_ref,
+    out_ref,
+    near,
+    relay,
+    beyond,
+    mate_send,
+    mate_recv,
+    own_send,
+    own_recv,
+    far_send,
+    far_recv,
+    greeted=False,
 ):
     me, mate, far, cross = quad_places()
-    greet({"quad": mate}, {"quad": far})
+    if not greeted:
+        greet({"quad": mate}, {"quad": far})
     size = out_ref.shape[0]
     step = size // REDUCE_PIECES
 
@@ -308,29 +353,49 @@
         copy.wait_send()
 
 
+def reduce_scratch(rows, width):
+    one, each = pltpu.SemaphoreType.DMA, pltpu.SemaphoreType.DMA((REDUCE_PIECES,))
+    low = pltpu.VMEM((rows, width), BF)
+    return [pltpu.VMEM((2, rows, width), BF), low, low, each, each, one, one, each, each]
+
+
 def quad_reduce(parts):
     rows, width = parts.shape[0] // QUAD, parts.shape[1]
-    dma = pltpu.SemaphoreType.DMA
     return pl.pallas_call(
         reduce_kernel,
         out_shape=jax.ShapeDtypeStruct((rows, width), F32),
         in_specs=[pl.BlockSpec(memory_space=pltpu.VMEM)],
         out_specs=pl.BlockSpec(memory_space=pltpu.VMEM),
-        scratch_shapes=[
-            pltpu.VMEM((2, rows, width), BF),
-            pltpu.VMEM((rows, width), BF),
-            pltpu.VMEM((rows, width), BF),
-            dma((REDUCE_PIECES,)),
-            dma((REDUCE_PIECES,)),
-            dma,
-            dma,
-            dma((REDUCE_PIECES,)),
-            dma((REDUCE_PIECES,)),
-        ],
+        scratch_shapes=reduce_scratch(rows, width),
         compiler_params=pltpu.CompilerParams(collective_id=CALL_REDUCE, has_side_effects=True),
         cost_estimate=SHORT,
         name="quad_reduce",
     )(parts)
+
+
+def both_kernel(sizes, planes, parts_ref, x_ref, out_ref, line_ref, *scratch):
+    me, mate, far, cross = quad_places()
+    greet({"quad": mate}, {"quad": far}, *line_peers(planes))
+    held, came, send_sem, recv_sem = scratch[:4]
+    copies = line_start(sizes, planes, x_ref, held, came, send_sem, recv_sem)
+    reduce_kernel(parts_ref, out_ref, *scratch[4:], greeted=True)
+    line_finish(sizes, planes, x_ref, line_ref, came, copies)
+
+
+def quad_reduce_and_line(parts, lines, sizes, planes):
+    rows, width = parts.shape[0] // QUAD, parts.shape[1]
+    shape = (lines.shape[0], sum(sizes))
+    vmem = pl.BlockSpec(memory_space=pltpu.VMEM)
+    return pl.pallas_call(
+        functools.partial(both_kernel, sizes, planes),
+        out_shape=[jax.ShapeDtypeStruct((rows, width), F32), jax.ShapeDtypeStruct(shape, F32)],
+        in_specs=[vmem, vmem],
+        out_specs=[vmem, vmem],
+        scratch_shapes=line_scratch(shape, planes) + reduce_scratch(rows, width),
+        compiler_params=pltpu.CompilerParams(collective_id=CALL_BOTH, has_side_effects=True),
+        cost_estimate=SHORT,
+        name="quad_reduce_and_line",
+    )(parts, lines)
 
 
 def norms_kernel(hops, x_ref, out_ref, held, came, send_sem, recv_sem):
@@ -381,6 +446,181 @@
         cost_estimate=SHORT,
         name="sum_everywhere",
     )(x)
+
+
+def rows_kernel(parts, own_ref, out_ref, keep_sem, line_send, line_recv, send_sem, recv_sem):
+    me, mate, far, cross = quad_places()
+    row, plane = lax.axis_index("row"), lax.axis_index("tensor")
+    other = 1 - row
+    line = [{"tensor": (plane + by) % parts} for by in range(1, parts)]
+    to_x, to_y, to_mate = {"quad": far}, {"row": other}, {"quad": mate}
+    greet(*line, to_x, to_y, to_mate)
+    size, width = own_ref.shape
+
+    def block(at_row, at_quad, part):
+        return out_ref.at[block_at(at_row * QUAD + at_quad, size), pl.ds(part * width, width)]
+
+    used = []
+
+    def send(source, target, peer, n):
+        copy = pltpu.make_async_remote_copy(
+            src_ref=source,
+            dst_ref=target,
+            send_sem=send_sem.at[n],
+            recv_sem=recv_sem.at[n],
+            device_id=peer,
+            device_id_type=MESH_ID,
+        )
+        copy.start()
+        used.append(copy)
+        return copy
+
+    along = []
+    for by in range(1, parts):
+        copy = pltpu.make_async_remote_copy(
+            src_ref=own_ref,
+            dst_ref=block(row, me, by),
+            send_sem=line_send.at[by - 1],
+            recv_sem=line_recv.at[by - 1],
+            device_id=line[by - 1],
+            device_id_type=MESH_ID,
+        )
+        copy.start()
+        along.append(copy)
+    keep = pltpu.make_async_copy(own_ref, block(row, me, 0), keep_sem)
+    keep.start()
+    near_x, near_y, beyond, mates = [], [], [], []
+    for part in range(parts + 1):
+        if part < parts:
+            if part:
+                along[part - 1].wait_recv()
+            source = own_ref if part == 0 else block(row, me, part)
+            target = block(row, me, part)
+            near_x.append(send(source, target, to_x, part))
+            near_y.append(send(source, target, to_y, parts + part))
+            mates.append(send(source, target, to_mate, 2 * parts + part))
+        if part:
+            done = part - 1
+            from_x, from_y = block(row, far, done), block(other, me, done)
+            near_x[done].wait_recv()
+            near_y[done].wait_recv()
+            if done % 2:
+                beyond.append(send(from_y, from_y, to_x, 3 * parts + done))
+            else:
+                beyond.append(send(from_x, from_x, to_y, 3 * parts + done))
+            mates.append(send(from_x, from_x, to_mate, 4 * parts + done))
+            mates.append(send(from_y, from_y, to_mate, 5 * parts + done))
+    for part in range(parts):
+        beyond[part].wait_recv()
+        came = block(other, far, part)
+        mates.append(send(came, came, to_mate, 6 * parts + part))
+    for copy in mates:
+        copy.wait_recv()
+    for copy in along + used:
+        copy.wait_send()
+    keep.wait()
+
+
+def gather_rows(rows, parts):
+    size, width = rows.shape
+    dma = pltpu.SemaphoreType.DMA
+    return pl.pallas_call(
+        functools.partial(rows_kernel, parts),
+        out_shape=jax.ShapeDtypeStruct((ROW * QUAD * size, parts * width), rows.dtype),
+        in_specs=[pl.BlockSpec(memory_space=pltpu.VMEM)],
+        out_specs=pl.BlockSpec(memory_space=pl.ANY),
+        scratch_shapes=[dma, dma((parts - 1,)), dma((parts - 1,)), dma((7 * parts,)), dma((7 * parts,))],
+        compiler_params=pltpu.CompilerParams(collective_id=CALL_ROWS, has_side_effects=True),
+        cost_estimate=SHORT,
+        name="gather_rows",
+    )(rows)
+
+
+def regroup_kernel(parts, kinds, x_ref, out_ref):
+    size = x_ref.shape[1] // (parts * kinds)
+    for kind in range(kinds):
+        for part in range(parts):
+            to, at = (kind * parts + part) * size, (part * kinds + kind) * size
+            out_ref[:, to : to + size] = x_ref[:, at : at + size]
+
+
+def regroup(rows, parts, kinds):
+    block = pl.BlockSpec((rows.shape[0] // 4, rows.shape[1]), lambda i: (i, 0))
+    return pl.pallas_call(
+        functools.partial(regroup_kernel, parts, kinds),
+        out_shape=jax.ShapeDtypeStruct(rows.shape, rows.dtype),
+        grid=(4,),
+        in_specs=[block],
+        out_specs=block,
+        cost_estimate=SHORT,
+        name="regroup",
+    )(rows)
+
+
+def line_peers(parts):
+    plane = lax.axis_index("tensor")
+    return [{"tensor": (plane + by) % parts} for by in range(1, parts)]
+
+
+def line_pick(sizes, parts, x_ref, part):
+    columns, start = [], 0
+    for size in sizes:
+        columns.append(x_ref[:, start + part * size : start + (part + 1) * size])
+        start += parts * size
+    return jnp.concatenate(columns, axis=1)
+
+
+def line_start(sizes, parts, x_ref, held, came, send_sem, recv_sem):
+    plane = lax.axis_index("tensor")
+    copies = []
+    for by in range(1, parts):
+        held[by - 1] = line_pick(sizes, parts, x_ref, by)
+        copy = pltpu.make_async_remote_copy(
+            src_ref=held.at[by - 1],
+            dst_ref=came.at[by - 1],
+            send_sem=send_sem.at[by - 1],
+            recv_sem=recv_sem.at[by - 1],
+            device_id={"tensor": (plane + parts - by) % parts},
+            device_id_type=MESH_ID,
+        )
+        copy.start()
+        copies.append(copy)
+    return copies
+
+
+def line_finish(sizes, parts, x_ref, out_ref, came, copies):
+    total = line_pick(sizes, parts, x_ref, 0).astype(F32)
+    for by in range(1, parts):
+        copies[by - 1].wait_recv()
+        total = total + came[by - 1].astype(F32)
+    out_ref[...] = total
+    for copy in copies:
+        copy.wait_send()
+
+
+def line_scratch(shape, parts):
+    dma = pltpu.SemaphoreType.DMA((parts - 1,))
+    return [pltpu.VMEM((parts - 1,) + shape, BF), pltpu.VMEM((parts - 1,) + shape, BF), dma, dma]
+
+
+def parts_kernel(sizes, parts, x_ref, out_ref, held, came, send_sem, recv_sem):
+    greet(*line_peers(parts))
+    copies = line_start(sizes, parts, x_ref, held, came, send_sem, recv_sem)
+    line_finish(sizes, parts, x_ref, out_ref, came, copies)
+
+
+def sum_line(rows, sizes, parts, call):
+    shape = (rows.shape[0], sum(sizes))
+    return pl.pallas_call(
+        functools.partial(parts_kernel, sizes, parts),
+        out_shape=jax.ShapeDtypeStruct(shape, F32),
+        in_specs=[pl.BlockSpec(memory_space=pltpu.VMEM)],
+        out_specs=pl.BlockSpec(memory_space=pltpu.VMEM),
+        scratch_shapes=line_scratch(shape, parts),
+        compiler_params=pltpu.CompilerParams(collective_id=call, has_side_effects=True),
+        cost_estimate=SHORT,
+        name="sum_line",
+    )(rows)
 
 
 def attend_forward(query, keyval, tables):
@@ -414,12 +654,13 @@
     )(keys_at, steps_of, query, keyval, keyval, bias)
 
 
-def attend_backward(query, keyval, logs, d_mixed, tables):
+def attend_backward(query, keyval, logs, d_mixed, tables, own_inputs, inputs, w_keyval):
     keys_at, steps_of, bias = tables
     own, width = query.shape
     quads = width // WIDE
-    rows = keyval.shape[0]
+    rows, depth = inputs.shape
     blocks = own // BLK
+    once = pl.Buffered(1)
     return pl.pallas_call(
         backward_kernel,
         grid_spec=pltpu.PrefetchScalarGridSpec(
@@ -432,25 +673,31 @@
                 pl.BlockSpec((blocks, LONGEST, WIDE), lambda i, *_: (0, 0, i)),
                 pl.BlockSpec((blocks, 1, WIDE), lambda i, *_: (0, 0, i)),
                 pl.BlockSpec((own, WIDE), lambda i, *_: (0, i)),
+                pl.BlockSpec((own, depth), lambda i, *_: (0, 0), pipeline_mode=once),
+                pl.BlockSpec((rows, depth), lambda i, *_: (0, 0), pipeline_mode=once),
+                pl.BlockSpec((depth, WIDE), lambda i, *_: (0, i)),
+                pl.BlockSpec((depth, WIDE), lambda i, *_: (0, i + quads)),
             ],
             out_specs=[
                 pl.BlockSpec((own, WIDE), lambda i, *_: (0, i)),
-                pl.BlockSpec((rows, WIDE), lambda i, *_: (0, i)),
-                pl.BlockSpec((rows, WIDE), lambda i, *_: (0, i)),
+                pl.BlockSpec((rows, depth), lambda i, *_: (0, 0)),
+                pl.BlockSpec((depth, 3 * WIDE), lambda i, *_: (0, i)),
             ],
             scratch_shapes=[
                 pltpu.VMEM((rows, WIDE), F32),
                 pltpu.VMEM((rows, WIDE), F32),
+                pltpu.VMEM((2, rows, WIDE), BF),
+                pltpu.VMEM((rows, depth), F32),
             ],
         ),
         out_shape=[
             jax.ShapeDtypeStruct((own, width), BF),
-            jax.ShapeDtypeStruct((rows, width), BF),
-            jax.ShapeDtypeStruct((rows, width), BF),
+            jax.ShapeDtypeStruct((rows, depth), BF),
+            jax.ShapeDtypeStruct((depth, 3 * width), BF),
         ],
         cost_estimate=SHORT,
         name="attend_backward",
-    )(keys_at, steps_of, query, keyval, keyval, bias, logs, d_mixed)
+    )(keys_at, steps_of, query, keyval, keyval, bias, logs, d_mixed, own_inputs, inputs, w_keyval, w_keyval)
 
 
 def attention_tables(doc_lengths, block_deal, random_rows, own_blocks, first_own):
@@ -535,19 +782,19 @@
     def spread(shard):
         return [shard] + [shifted(shard, by) for by in range(1, tensor)]
 
+    def by_kind(parts, kinds):
+        rows = jnp.stack([part.reshape(depth, kinds, -1) for part in parts], axis=2)
+        return rows.reshape(depth, -1)
+
+    def attn_shard(qkv, back):
+        qkv = qkv.reshape(depth, head_local, 3, HD).transpose(0, 2, 1, 3)
+        return jnp.concatenate([qkv.reshape(depth, 3 * chunk), back.T], axis=1)
+
     def attn_rows(qkv, back):
-        qkv = qkv.reshape(depth, head_local, 3, HD).transpose(0, 2, 1, 3)
-        shard = jnp.concatenate([qkv.reshape(depth, 3 * chunk), back.T], axis=1)
-        parts = spread(shard)
-        return jnp.concatenate(
-            [part[:, p * chunk : (p + 1) * chunk] for p in range(4) for part in parts], axis=1
-        )
+        return by_kind(spread(attn_shard(qkv, back)), 4)
 
     def ffn_rows(up, down):
-        parts = spread(jnp.concatenate([up, down.T], axis=1))
-        return jnp.concatenate(
-            [part[:, p * hidden : (p + 1) * hidden] for p in range(2) for part in parts], axis=1
-        )
+        return by_kind(spread(jnp.concatenate([up, down.T], axis=1)), 2)
 
     def over_data(rows):
         return lax.all_gather(rows, DATA, axis=0, tiled=True)
@@ -558,13 +805,22 @@
     numbers = jnp.pad(numbers, ((0, 14), (0, width - numbers.shape[1])))
     own_numbers = lax.ppermute(numbers, EVERY, moves)
     own_tokens = lax.ppermute(layer_input, EVERY, moves)
-    attn_full = [over_data(attn_rows(w_qkv[0], w_out[0]))]
-    own_tokens, own_numbers, up_0, down_0 = lax.optimization_barrier(
-        (own_tokens, own_numbers, w_up[0], w_down[0])
-    )
-    ffn_full = [over_data(ffn_rows(up_0, down_0))]
+    if lax.axis_size("hi") == 1:
+        rows = gather_rows(attn_shard(w_qkv[0], w_out[0]), tensor)
+        rows, own_tokens, own_numbers, up_0, down_0 = lax.optimization_barrier(
+            (rows, own_tokens, own_numbers, w_up[0], w_down[0])
+        )
+        attn_full = [regroup(rows, tensor, 4)]
+    else:
+        attn_full = [over_data(attn_rows(w_qkv[0], w_out[0]))]
+        own_tokens, own_numbers, up_0, down_0 = lax.optimization_barrier(
+            (own_tokens, own_numbers, w_up[0], w_down[0])
+        )
+    first_rows = ffn_rows(up_0, down_0)
 
     inputs, numbers = quad_gather([own_tokens, own_numbers], [4, 1], CALL_GATHER_FIRST)
+    inputs, first_rows = lax.optimization_barrier((inputs, first_rows))
+    ffn_full = [over_data(first_rows)]
     numbers = numbers.reshape(QUAD, 16, width)[:, :2].astype(jnp.int32)
     numbers = numbers[:, 0] * BLK + numbers[:, 1]
     lengths, deal = numbers[0, :docs], numbers[0, docs : docs + group_blocks]
@@ -597,18 +853,17 @@
             (inputs,) = quad_gather([own_inputs], [4], CALL_GATHER)
         query = (dot(own_inputs, w_query).astype(BF).astype(F32) * score_scale).astype(BF)
         keyval = dot(inputs, w_keyval).astype(BF)
+        if layer < LAYERS - 1:
+            keyval, following = lax.optimization_barrier(
+                (keyval, [w[layer + 1] for w in (w_qkv, w_out, w_up, w_down)])
+            )
+            attn_next, ffn_next = attn_rows(*following[:2]), ffn_rows(*following[2:])
+        mixed, logs = attend_forward(query, keyval, tables)
+        if layer < LAYERS - 1:
+            mixed, attn_next = lax.optimization_barrier((mixed, attn_next))
+            attn_full.append(over_data(attn_next))
         if layer == 0:
-            keyval, later = lax.optimization_barrier((keyval, (w_qkv, w_out, w_up, w_down)))
-            later_rows = [
-                (attn_rows(later[0][other], later[1][other]), ffn_rows(later[2][other], later[3][other]))
-                for other in range(1, LAYERS)
-            ]
-        mixed, logs = attend_forward(query, keyval, tables)
-        if layer == 0:
-            mixed, later_rows, own_grad = lax.optimization_barrier((mixed, later_rows, out_grad))
-            for attn_later, ffn_later in later_rows:
-                attn_full.append(over_data(attn_later))
-                ffn_full.append(over_data(ffn_later))
+            mixed, own_grad = lax.optimization_barrier((mixed, out_grad))
             own_grad = lax.ppermute(own_grad, EVERY, moves)
         summed_one = stream + dot_right_t(mixed, w_back_t)
         normed = layer_norm(summed_one, attn_gain[layer], attn_shift[layer])
@@ -616,27 +871,24 @@
         pre_act = dot(ffn_in, w_expand)
         activated = gelu_tanh(pre_act).astype(BF)
         summed_two = normed + dot_right_t(activated, w_shrink_t)
+        if layer < LAYERS - 1:
+            summed_two, ffn_next = lax.optimization_barrier((summed_two, ffn_next))
+            ffn_full.append(over_data(ffn_next))
         stored.append(
             (own_inputs, inputs, query, keyval, mixed, logs, summed_one, ffn_in, pre_act, activated, summed_two)
         )
         stream = layer_norm(summed_two, ffn_gain[layer], ffn_shift[layer])
     layer_output = lax.ppermute(stream.astype(BF), EVERY, moves_back)
 
-    def sum_parts(rows, sizes):
-        pieces, start = [], 0
-        for size in sizes:
-            pieces.append(rows[:, start : start + tensor * size].reshape(depth, tensor, size))
-            start += tensor * size
-        total = jnp.concatenate([p[:, 0] for p in pieces], axis=1).astype(F32)
-        for by in range(1, tensor):
-            part = jnp.concatenate([p[:, by] for p in pieces], axis=1)
-            total = total + shifted(part, tensor - by).astype(F32)
-        return total
+    def by_piece(rows):
+        rows = rows.reshape(depth, -1, 3, WIDE).transpose(0, 2, 1, 3)
+        return rows.reshape(depth, 3 * width)
 
     def sum_data(part):
         return lax.psum_scatter(part, DATA, scatter_dimension=0, tiled=True)
 
     state_grad = own_grad.astype(F32)
+    attn_sums = [None] * LAYERS
     attn_grads = [None] * LAYERS
     ffn_grads = [None] * LAYERS
     norm_parts = [None] * LAYERS
@@ -672,38 +924,35 @@
         ffn_sum = sum_data(ffn_part)
         d_mixed = dot(d_one_low, w_back_t).astype(BF)
         if layer < LAYERS - 1:
-            d_mixed, attn_sum, ffn_grads[layer + 1] = lax.optimization_barrier(
-                (d_mixed, attn_sum, ffn_grads[layer + 1])
+            d_mixed, attn_sums[layer + 1] = lax.optimization_barrier((d_mixed, attn_sums[layer + 1]))
+        d_query, others, attn_part = attend_backward(
+            query, keyval, logs, d_mixed, tables, own_inputs, inputs, w_keyval
+        )
+        if layer == 0:
+            norms = jnp.stack([norm_parts[l][k] for k in range(4) for l in range(LAYERS)])
+            norms, others = lax.optimization_barrier((norms, others))
+            norm_sums = sum_everywhere(norms)
+            norm_sums, ffn_last = lax.optimization_barrier((norm_sums, ffn_last))
+            ffn_grads[1] = sum_line(ffn_last, (hidden, hidden, chunk), tensor, CALL_LINE_FFN)
+            others, ffn_sum, attn_part, norm_sums, ffn_grads[1] = lax.optimization_barrier(
+                (others, ffn_sum, attn_part, norm_sums, ffn_grads[1])
             )
-            attn_grads[layer + 1] = sum_parts(attn_sum, (chunk,) * 3)
+        else:
+            others, layer_output = lax.optimization_barrier((others, layer_output))
         if layer == 0:
-            norm_sums = sum_everywhere(
-                jnp.stack([norm_parts[l][k] for k in range(4) for l in range(LAYERS)])
-            )
-            d_mixed, norm_sums = lax.optimization_barrier((d_mixed, norm_sums))
-        d_query, d_key, d_value = attend_backward(query, keyval, logs, d_mixed, tables)
-        (d_query, d_key, d_value), ffn_sum, attn_grads, layer_output = lax.optimization_barrier(
-            ((d_query, d_key, d_value), ffn_sum, attn_grads, layer_output)
-        )
-        ffn_grads[layer] = sum_parts(ffn_sum, (hidden, hidden, chunk))
-        others = dot_right_t(d_key, w_keyval[:, :width]) + dot_right_t(d_value, w_keyval[:, width:])
-        others = others.astype(BF)
-        d_query, d_key, d_value, others = lax.optimization_barrier((d_query, d_key, d_value, others))
-        attn_part = jnp.concatenate(
-            [
-                dot_left_t(own_inputs, d_query).astype(BF),
-                dot_left_t(inputs, d_key).astype(BF),
-                dot_left_t(inputs, d_value).astype(BF),
-            ],
-            axis=1,
-        )
-        others, attn_part = lax.optimization_barrier((others, attn_part))
-        attn_sum = sum_data(attn_part)
-        summed = quad_reduce(others)
+            summed, ffn_grads[0] = quad_reduce_and_line(others, ffn_sum, (hidden, hidden, chunk), tensor)
+        else:
+            summed = quad_reduce(others)
+            summed, ffn_sum, attn_part = lax.optimization_barrier((summed, ffn_sum, attn_part))
+        ffn_last = ffn_sum
+        attn_sums[layer] = sum_data(attn_part)
         state_grad = d_one + dot_right_t(d_query, w_query) + summed
-    attn_sum, ffn_grads = lax.optimization_barrier((attn_sum, ffn_grads))
-    attn_grads[0] = sum_parts(attn_sum, (chunk,) * 3)
     input_grad = lax.ppermute(state_grad.astype(BF), EVERY, moves_back).astype(F32)
+    for layer in reversed(range(LAYERS)):
+        attn_sums[layer], ffn_grads, attn_grads = lax.optimization_barrier(
+            (attn_sums[layer], ffn_grads, attn_grads)
+        )
+        attn_grads[layer] = sum_line(by_piece(attn_sums[layer]), (chunk,) * 3, tensor, CALL_LINE_ATTN)
 
     qkv_grad = jnp.stack(attn_grads).reshape(LAYERS, depth, 3, head_local, HD)
     qkv_grad = qkv_grad.transpose(0, 1, 3, 2, 4).reshape(LAYERS, depth, 3 * chunk)

time: 779 us -> 729 us (0.936)
  Pallas kernels: 241 us -> 445 us
  waiting for transfers between devices: 172 us -> 29.1 us
  starting transfers between devices: 112 us -> 39.7 us
  matrix products: 133 us -> 100 us
    pallas_call x0 -> x6, Pallas kernels: none -> 177 us  [the longest x3 92.6 us: sum_line(): pl.pallas_call(functools.partial(parts_kernel, sizes, parts), out_shape=j...]
    ppermute x24 -> x9, starting transfers between devices: 93.8 us -> 19.1 us  [shifted(): lax.ppermute(x, 'tensor', [(i, (i + by) % tensor) for i in range(tensor)])]
    ppermute x24 -> x9, waiting for transfers between devices: 73.1 us -> 18.5 us  [shifted(): lax.ppermute(x, 'tensor', [(i, (i + by) % tensor) for i in range(tensor)])]
    reduce_scatter x2 -> x4, waiting for transfers between devices: 60.2 us -> 10.4 us  [sum_data(): return lax.psum_scatter(part, DATA, scatter_dimension=0, tiled=True)]
    pallas_call x2, Pallas kernels: 54.8 us -> 96.6 us  [attend_backward(): pl.pallas_call(backward_kernel, grid_spec=pltpu.PrefetchScalarGridSpec(nu...]
    all_gather x4 -> x3, waiting for transfers between devices: 32.2 us -> 0.04 us  [over_data(): return lax.all_gather(rows, DATA, axis=0, tiled=True)]
    pallas_call x2 -> x1, Pallas kernels: 58.7 us -> 36.3 us  [quad_reduce(): pl.pallas_call(reduce_kernel, out_shape=jax.ShapeDtypeStruct((rows, width...]
    unnamed x179 -> x85, local copies, waits for them, and re-layouts: 34 us -> 12.1 us
  transfers between devices with their start and end apart: 37 -> 21, of which waited for: 14 -> 4; matrix products, arithmetic and copies ran while one was open for 16% -> 18% of each run, Pallas kernels for 28% -> 60%
where the time goes in v4:
time: 729 us; the launch traced here: 719 us
  Pallas kernels  445 us (61%)
  matrix products  100 us (14%)
  local copies, waits for them, and re-layouts  47.6 us (7%)
  other arithmetic  42.3 us (6%)
  starting transfers between devices  39.7 us (5%)
  waiting for transfers between devices  29.1 us (4%)
  between operations  15.8 us (2%)
    pallas_call x2, Pallas kernels, attend_backward(): pl.pallas_call(backward_kernel, grid_spec=pltpu.PrefetchScalarGridSpec(nu...  96.6 us
    pallas_call x3, Pallas kernels, sum_line(): pl.pallas_call(functools.partial(parts_kernel, sizes, parts), out_shape=j...  92.6 us
    pallas_call x2, Pallas kernels, quad_gather(): pl.pallas_call(functools.partial(gather_kernel, pieces), out_shape=[jax.S...  64.5 us
    dot_general x10, matrix products, dot(): return jnp.dot(left, right, preferred_element_type=F32)  54.4 us
    pallas_call x2, Pallas kernels, attend_forward(): pl.pallas_call(forward_kernel, grid_spec=pltpu.PrefetchScalarGridSpec(num...  50.6 us
    pallas_call x1, Pallas kernels, gather_rows(): pl.pallas_call(functools.partial(rows_kernel, parts), out_shape=jax.Shape...  43.3 us
    pallas_call x1, Pallas kernels, quad_reduce(): pl.pallas_call(reduce_kernel, out_shape=jax.ShapeDtypeStruct((rows, width...  36.3 us
    pallas_call x1, Pallas kernels, quad_reduce_and_line(): pl.pallas_call(functools.partial(both_kernel, sizes, planes), out_shape=[...  35.8 us
  transfers between devices with their start and end apart: 21, of which 4 were waited for; matrix products, arithmetic and copies ran while one was open for 18% of the time, Pallas kernels for 60%

profile of v4, /device:TPU:0, one launch (start us, length us, event | category | flops | bytes accessed | tf_op | source)
XLA Modules:
  0.0 719.1 jit_solution(11721929711305401955)
XLA Ops:
  7.2 1.9 collective-permute-start
  13.1 1.6 fusion.92
  17.2 43.3 %gather_rows.1.x_ref = bf16[768,3072]{1,0:T(8,128)(2,1)} custom-call(bf16[96,768]{1,0:T(8,128)(2,1)} %pad_maximum_fusion.10.own_ref), custom_call_target="tpu_custom_call" | custom-call | flops 1000000 | bytes 1000000 | tf_op jit(solution)/shard_map/gather_rows/pallas_call | solution.py:527
  60.6 9.2 %collective-permute-start.4 = (bf16[96,1536]{1,0:T(8,128)(2,1)S(1)}, bf16[96,1536]{1,0:T(8,128)(2,1)S(1)}, u32[]{:S(2)}, u32[]{:S(2)}) collective-permute-start(bf16[96,1536]{1,0:T(8,128)(2,1)S(1)} %pad_maximum_fusion.7), channel_id=1, source_target_pairs={{0,3},{1,0},{2,1},{3,2},{4,7},{5,4},{6,5},{7,6},{8,11},{9,8},{10,9... | collective-permute-start | bytes 884744 | tf_op jit(solution)/shard_map/ppermute | solution.py:780
  70.7 22.9 %quad_gather.2 = (bf16[2048,768]{1,0:T(8,128)(2,1)}, bf16[64,768]{1,0:T(8,128)(2,1)}) custom-call(bf16[512,768]{1,0:T(8,128)(2,1)} %copy-done.6, bf16[16,768]{1,0:T(8,128)(2,1)} %copy-done.25), custom_call_target="tpu_custom_call" | custom-call | flops 1000000 | bytes 1000000 | tf_op jit(solution)/shard_map/quad_gather/pallas_call | solution.py:281
  94.0 2.2 stack_reshape.49
  96.2 2.8 pad_maximum_fusion.2
  99.1 1.7 reshape.672
  102.5 5.5 regroup.1
  110.8 3.2 multiply_convert_fusion.3.q_ref
  113.9 8.6 %convolution_convert_fusion.1.k_ref.v_ref = bf16[2048,1536]{1,0:T(8,128)(2,1)} fusion(bf16[2048,768]{1,0:T(8,128)(2,1)S(1)} %copy-done.9, bf16[768,3072]{1,0:T(8,128)(2,1)} %regroup.1), kind=kOutput, calls=%fused_computation.7 | convolution fusion | flops 4834983936 | bytes 11796480 | tf_op jit(solution)/shard_map/dot_general | solution.py:41
  122.6 3.3 collective-permute-start.7
  127.0 2.2 collective-permute-start.5
  131.8 25.3 %attend_forward.2 = (bf16[512,768]{1,0:T(8,128)(2,1)}, f32[8,1,768]{2,1,0:T(1,128)}) custom-call(s32[8,16]{1,0:T(8,128)} %select_reduce_fusion.keys_at, s32[8]{0:T(128)} %get-tuple-element.212.steps_of, bf16[512,768]{1,0:T(8,128)(2,1)} %multiply_convert_fusion.3.q_ref, bf16[2048,1536]{1,0:T(8,128)(2,1)} %convolution_convert_fusion.1.k_ref.v_ref, ...), custom_call_target="tpu_custom_call" | custom-call | flops 1000000 | bytes 1000000 | tf_op jit(solution)/shard_map/attend_forward/pallas_call | solution.py:632
  159.5 1.9 reshape.676
  161.6 1.8 collective-permute-start.10
  165.1 2.4 fusion.95
  167.9 3.0 collective-permute-done.10
  170.9 2.9 stack_reshape.55
  173.7 15.4 %collective-permute-done.9 = bf16[96,1536]{1,0:T(8,128)(2,1)S(1)} collective-permute-done((bf16[96,1536]{1,0:T(8,128)(2,1)S(1)}, bf16[96,1536]{1,0:T(8,128)(2,1)S(1)}, u32[]{:S(2)}, u32[]{:S(2)}) %collective-permute-start.9) | collective-permute-done | bytes 294944 | tf_op jit(solution)/shard_map/ppermute | solution.py:780
  191.0 4.0 pad_maximum_fusion.3
  195.0 1.7 reshape.677
  196.7 4.8 fusion.28
  201.5 2.7 copy-done.35
  204.2 3.9 fusion.40
  208.2 7.5 %collective-permute-start.11 = (bf16[512,768]{1,0:T(8,128)(2,1)}, bf16[512,768]{1,0:T(8,128)(2,1)}, u32[]{:S(2)}, u32[]{:S(2)}) collective-permute-start(bf16[512,768]{1,0:T(8,128)(2,1)} %param.22), channel_id=1, source_target_pairs={{0,0},{1,4},{2,8},{3,12},{4,3},{5,7},{6,11},{7,15},{8,1},{9,5},{10... | collective-permute-start | bytes 2359304 | tf_op jit(solution)/shard_map/ppermute | solution.py:867
  217.4 41.6 %quad_gather.3.in_ref = bf16[2048,768]{1,0:T(8,128)(2,1)} custom-call(bf16[512,768]{1,0:T(8,128)(2,1)} %fusion.49.refs_0_.own_ref), custom_call_target="tpu_custom_call" | custom-call | flops 1000000 | bytes 1000000 | tf_op jit(solution)/shard_map/quad_gather/pallas_call | solution.py:281
  259.0 3.2 multiply_convert_fusion.2.q_ref
  262.3 8.8 %convolution_convert_fusion.k_ref.v_ref = bf16[2048,1536]{1,0:T(8,128)(2,1)} fusion(bf16[2048,768]{1,0:T(8,128)(2,1)S(1)} %copy-done, bf16[768,3072]{1,0:T(8,128)(2,1)} %all-gather.6.cloned.1.call-done), kind=kOutput, calls=%fused_computation.6 | convolution fusion | flops 4834983936 | bytes 11796480 | tf_op jit(solution)/shard_map/dot_general | solution.py:41
  271.0 25.3 %attend_forward.3 = (bf16[512,768]{1,0:T(8,128)(2,1)}, f32[8,1,768]{2,1,0:T(1,128)}) custom-call(s32[8,16]{1,0:T(8,128)} %select_reduce_fusion.keys_at, s32[8]{0:T(128)} %get-tuple-element.212.steps_of, bf16[512,768]{1,0:T(8,128)(2,1)} %multiply_convert_fusion.2.q_ref, bf16[2048,1536]{1,0:T(8,128)(2,1)} %convolution_convert_fusion.k_ref.v_ref, ...), custom_call_target="tpu_custom_call" | custom-call | flops 1000000 | bytes 1000000 | tf_op jit(solution)/shard_map/attend_forward/pallas_call | solution.py:632
  296.3 2.4 fusion.96
  299.1 4.9 fusion.20
  304.4 4.0 fusion.97
  308.7 1.8 fusion.37
  310.6 2.7 fusion.91
  313.3 3.6 convolution_convert_fusion.4
  317.0 6.1 fusion.13
  324.7 3.3 convolution_convert_fusion.5
  328.1 5.0 multiply_reduce_fusion.1
  333.1 2.0 fusion.90
  337.2 8.0 %pad_maximum_fusion = bf16[768,6912]{1,0:T(8,128)(2,1)} fusion(bf16[768,768]{1,0:T(8,128)(2,1)S(1)} %convolution_convert_fusion.7, bf16[768,3072]{1,0:T(8,128)(2,1)S(1)} %convolution_convert_fusion.4, bf16[768,3072]{1,0:T(8,128)(2,1)S(1)} %convolution_convert_fusion.5), kind=kLoop, calls=%fused_computation | loop fusion | flops 31850496 | bytes 21233664 | tf_op jit(solution)/shard_map/concatenate | solution.py:915
  345.3 7.7 %collective-permute-start.12 = (bf16[512,768]{1,0:T(8,128)(2,1)}, bf16[512,768]{1,0:T(8,128)(2,1)}, u32[]{:S(2)}, u32[]{:S(2)}) collective-permute-start(bf16[512,768]{1,0:T(8,128)(2,1)} %get-tuple-element.192), channel_id=1, source_target_pairs={{0,0},{4,1},{8,2},{12,3},{3,4},{7,5},{11,6},{15,7},{1,8},{5,9},{9,... | collective-permute-start | bytes 2359304 | tf_op jit(solution)/shard_map/ppermute | solution.py:881
  353.0 3.3 slice.184.wk_ref.wv_ref
  356.3 3.3 convolution_convert_fusion.9.d_ref
  359.6 49.1 %attend_backward.2 = (bf16[512,768]{1,0:T(8,128)(2,1)}, bf16[2048,768]{1,0:T(8,128)(2,1)}, bf16[768,2304]{1,0:T(8,128)(2,1)}) custom-call(s32[8,16]{1,0:T(8,128)} %select_reduce_fusion.keys_at, s32[8]{0:T(128)} %get-tuple-element.212.steps_of, bf16[512,768]{1,0:T(8,128)(2,1)} %multiply_convert_fusion.2.q_ref, ...), custom_call_target="tpu_custom_call" | custom-call | flops 1000000 | bytes 1000000 | tf_op jit(solution)/shard_map/attend_backward/pallas_call | solution.py:664
  408.7 36.3 %quad_reduce.1 = f32[512,768]{1,0:T(8,128)} custom-call(bf16[2048,768]{1,0:T(8,128)(2,1)} %get-tuple-element.96.parts_ref), custom_call_target="tpu_custom_call" | custom-call | flops 1000000 | bytes 1000000 | tf_op jit(solution)/shard_map/quad_reduce/pallas_call | solution.py:364
  446.7 3.2 multiply_reduce_fusion
  450.9 8.5 %fusion.6 = bf16[512,3072]{1,0:T(8,128)(2,1)S(1)} fusion(f32[512,3072]{1,0:T(8,128)} %copy-done.35, bf16[768,6144]{1,0:T(8,128)(2,1)} %all-gather.4.cloned.1.call-done, f32[512,768]{1,0:T(8,128)S(1)} %get-tuple-element.183, f32[512]{0:T(512)S(1)} %negate_multiply_fusion.1), kind=kOutput, calls=%fused_computation.14 | convolution fusion | flops 2448162816 | bytes 15730688 | tf_op jit(solution)/shard_map/dot_general | solution.py:41
  459.4 5.9 multiply_reduce_fusion.3
  468.1 3.4 convolution_convert_fusion.3
  471.5 3.3 convolution_convert_fusion.2
  474.8 8.0 %pad_maximum_fusion.1 = bf16[768,6912]{1,0:T(8,128)(2,1)} fusion(bf16[768,768]{1,0:T(8,128)(2,1)S(1)} %convolution_convert_fusion.6, bf16[768,3072]{1,0:T(8,128)(2,1)S(1)} %convolution_convert_fusion.2, bf16[768,3072]{1,0:T(8,128)(2,1)S(1)} %convolution_convert_fusion.3), kind=kLoop, calls=%fused_computation.1 | loop fusion | flops 31850496 | bytes 21233664 | tf_op jit(solution)/shard_map/concatenate | solution.py:915
  483.1 3.3 slice.178.wk_ref.wv_ref
  487.1 2.9 convolution_convert_fusion.8.d_ref
  490.1 8.8 %reduce-scatter.7.cloned.1.call-done = bf16[96,2304]{1,0:T(8,128)(2,1)} async-done(((bf16[768,2304]{1,0:T(8,128)(2,1)}), bf16[96,2304]{1,0:T(8,128)(2,1)}) %reduce-scatter.7.cloned.1.call-update) | async-done | bytes 442384 | tf_op jit(solution)/shard_map/reduce_scatter | solution.py:888
  498.8 47.5 %attend_backward.3 = (bf16[512,768]{1,0:T(8,128)(2,1)}, bf16[2048,768]{1,0:T(8,128)(2,1)}, bf16[768,2304]{1,0:T(8,128)(2,1)}) custom-call(s32[8,16]{1,0:T(8,128)} %select_reduce_fusion.keys_at, s32[8]{0:T(128)} %get-tuple-element.212.steps_of, bf16[512,768]{1,0:T(8,128)(2,1)} %multiply_convert_fusion.3.q_ref, ...), custom_call_target="tpu_custom_call" | custom-call | flops 1000000 | bytes 1000000 | tf_op jit(solution)/shard_map/attend_backward/pallas_call | solution.py:664
  546.4 19.4 %sum_everywhere.1 = f32[8,768]{1,0:T(8,128)} custom-call(f32[8,768]{1,0:T(8,128)} %stack.48.x_ref), custom_call_target="tpu_custom_call" | custom-call | flops 1000000 | bytes 1000000 | tf_op jit(solution)/shard_map/sum_everywhere/pallas_call | solution.py:434
  565.8 33.7 %sum_line.3 = f32[96,1728]{1,0:T(8,128)} custom-call(bf16[96,6912]{1,0:T(8,128)(2,1)} %reduce-scatter.5.cloned.1.call-done.x_ref), custom_call_target="tpu_custom_call" | custom-call | flops 1000000 | bytes 1000000 | tf_op jit(solution)/shard_map/sum_line/pallas_call | solution.py:614
  599.6 35.8 %quad_reduce_and_line.1 = (f32[512,768]{1,0:T(8,128)}, f32[96,1728]{1,0:T(8,128)}) custom-call(bf16[2048,768]{1,0:T(8,128)(2,1)} %get-tuple-element.113.parts_ref, bf16[96,6912]{1,0:T(8,128)(2,1)} %reduce-scatter.9.cloned.1.call-done.x_ref), custom_call_target="tpu_custom_call" | custom-call | flops 1000000 | bytes 1000000 | tf_op jit(solution)/shard_map/quad_reduce_and_line/pallas_call | solution.py:389
  635.4 3.5 add_convert_fusion
  638.9 2.0 collective-permute-start.13
  642.7 43.0 %sum_line.4 = f32[96,576]{1,0:T(8,128)} custom-call(bf16[96,2304]{1,0:T(8,128)(2,1)} %reshape.687.x_ref), custom_call_target="tpu_custom_call" | custom-call | flops 1000000 | bytes 1000000 | tf_op jit(solution)/shard_map/sum_line/pallas_call | solution.py:614
  690.7 15.9 %sum_line.5 = f32[96,576]{1,0:T(8,128)} custom-call(bf16[96,2304]{1,0:T(8,128)(2,1)} %reshape.689.x_ref), custom_call_target="tpu_custom_call" | custom-call | flops 1000000 | bytes 1000000 | tf_op jit(solution)/shard_map/sum_line/pallas_call | solution.py:614
  709.7 2.1 copy.108
  (233 shorter events, 44.6 us)
Async XLA Ops:
  7.2 7.9 %copy-start.21 = (bf16[2,96,768]{2,1,0:T(8,128)(2,1)S(1)}, bf16[2,96,768]{2,1,0:T(8,128)(2,1)}, u32[]{:S(2)}) copy-start(bf16[2,96,768]{2,1,0:T(8,128)(2,1)} %param.16) | copy-start | bytes 884740
  7.2 8.6 %copy-start.22 = (bf16[2,768,96]{1,2,0:T(8,128)(2,1)S(1)}, bf16[2,768,96]{1,2,0:T(8,128)(2,1)}, u32[]{:S(2)}) copy-start(bf16[2,768,96]{1,2,0:T(8,128)(2,1)} %param.17) | copy-start | bytes 884740
  7.2 189.5 %all-gather.4.cloned.1.call-start = ((), (), s32[]{:S(2)}) async-start(), calls=%async_computation.4 | async-start | bytes 10616832 | tf_op jit(solution)/shard_map/all_gather | solution.py:800
  7.2 53.3 %collective-permute-start = (bf16[512,768]{1,0:T(8,128)(2,1)}, bf16[512,768]{1,0:T(8,128)(2,1)S(1)}, u32[]{:S(2)}, u32[]{:S(2)}) collective-permute-start(bf16[512,768]{1,0:T(8,128)(2,1)} %param.13), channel_id=1, source_target_pairs={{0,0},{1,4},{2,8},{3,12},{4,3},{5,7},{6,11},{7,15},{8,1},{9,5},{10... | collective-permute-start | bytes 2359304 | tf_op jit(solution)/shard_map/ppermute | solution.py:807
  10.9 49.6 %collective-permute-start.1 = (bf16[16,768]{1,0:T(8,128)(2,1)S(1)}, bf16[16,768]{1,0:T(8,128)(2,1)S(1)}, u32[]{:S(2)}, u32[]{:S(2)}) collective-permute-start(bf16[16,768]{1,0:T(8,128)(2,1)S(1)} %fusion.69), channel_id=1, source_target_pairs={{0,0},{1,4},{2,8},{3,12},{4,3},{5,7},{6,11},{7,15},{8,1},{9,5},{10... | collective-permute-start | bytes 73736 | tf_op jit(solution)/shard_map/ppermute | solution.py:806
  60.6 10.1 %copy-start.25 = (bf16[16,768]{1,0:T(8,128)(2,1)}, bf16[16,768]{1,0:T(8,128)(2,1)S(1)}, u32[]{:S(2)}) copy-start(bf16[16,768]{1,0:T(8,128)(2,1)S(1)} %collective-permute-done.1.refs_1_) | copy-start | bytes 73732
  60.6 10.1 %copy-start.6 = (bf16[512,768]{1,0:T(8,128)(2,1)}, bf16[512,768]{1,0:T(8,128)(2,1)S(1)}, u32[]{:S(2)}) copy-start(bf16[512,768]{1,0:T(8,128)(2,1)S(1)} %collective-permute-done.refs_0_.own_ref) | copy-start | bytes 2359300
  60.6 33.0 %collective-permute-start.4 = (bf16[96,1536]{1,0:T(8,128)(2,1)S(1)}, bf16[96,1536]{1,0:T(8,128)(2,1)S(1)}, u32[]{:S(2)}, u32[]{:S(2)}) collective-permute-start(bf16[96,1536]{1,0:T(8,128)(2,1)S(1)} %pad_maximum_fusion.7), channel_id=1, source_target_pairs={{0,3},{1,0},{2,1},{3,2},{4,7},{5,4},{6,5},{7,6},{8,11},{9,8},{10,9... | collective-permute-start | bytes 884744 | tf_op jit(solution)/shard_map/ppermute | solution.py:780
  69.9 24.0 %collective-permute-start.3 = (bf16[96,1536]{1,0:T(8,128)(2,1)S(1)}, bf16[96,1536]{1,0:T(8,128)(2,1)S(1)}, u32[]{:S(2)}, u32[]{:S(2)}) collective-permute-start(bf16[96,1536]{1,0:T(8,128)(2,1)S(1)} %pad_maximum_fusion.7), channel_id=1, source_target_pairs={{0,2},{1,3},{2,0},{3,1},{4,6},{5,7},{6,4},{7,5},{8,10},{9,11},{10,... | collective-permute-start | bytes 884744 | tf_op jit(solution)/shard_map/ppermute | solution.py:780
  69.9 24.2 %collective-permute-start.2 = (bf16[96,1536]{1,0:T(8,128)(2,1)S(1)}, bf16[96,1536]{1,0:T(8,128)(2,1)}, u32[]{:S(2)}, u32[]{:S(2)}) collective-permute-start(bf16[96,1536]{1,0:T(8,128)(2,1)S(1)} %pad_maximum_fusion.7), channel_id=1, source_target_pairs={{0,1},{1,2},{2,3},{3,0},{4,5},{5,6},{6,7},{7,4},{8,9},{9,10},{10,1... | collective-permute-start | bytes 884744 | tf_op jit(solution)/shard_map/ppermute | solution.py:780
  99.0 1.8 copy-start.18
  100.8 158.2 %all-gather.6.cloned.1.call-start = ((), (), s32[]{:S(2)}) async-start(), calls=%async_computation.5 | async-start | bytes 5308416 | tf_op jit(solution)/shard_map/all_gather | solution.py:800
  102.5 8.3 %copy-start.7 = (bf16[512,768]{1,0:T(8,128)(2,1)S(1)}, bf16[512,768]{1,0:T(8,128)(2,1)}, u32[]{:S(2)}) copy-start(bf16[512,768]{1,0:T(8,128)(2,1)} %copy-done.6) | copy-start | bytes 2359300
  110.8 3.2 copy-start.9
  113.9 8.6 %copy-start.23 = (bf16[192,96]{1,0:T(8,128)(2,1)S(1)}, bf16[192,96]{1,0:T(8,128)(2,1)}, u32[]{:S(2)}) copy-start(bf16[192,96]{1,0:T(8,128)(2,1)} %get-tuple-element.80) | copy-start | bytes 110596
  122.6 34.5 %collective-permute-start.7 = (bf16[96,768]{0,1:T(8,128)(2,1)S(1)}, bf16[96,768]{0,1:T(8,128)(2,1)S(1)}, u32[]{:S(2)}, u32[]{:S(2)}) collective-permute-start(bf16[96,768]{0,1:T(8,128)(2,1)S(1)} %pad_maximum_fusion.9), channel_id=1, source_target_pairs={{0,3},{1,0},{2,1},{3,2},{4,7},{5,4},{6,5},{7,6},{8,11},{9,8},{10,9... | collective-permute-start | bytes 442376 | tf_op jit(solution)/shard_map/ppermute | solution.py:780
  125.9 31.4 %collective-permute-start.6 = (bf16[96,768]{0,1:T(8,128)(2,1)S(1)}, bf16[96,768]{0,1:T(8,128)(2,1)S(1)}, u32[]{:S(2)}, u32[]{:S(2)}) collective-permute-start(bf16[96,768]{0,1:T(8,128)(2,1)S(1)} %pad_maximum_fusion.9), channel_id=1, source_target_pairs={{0,2},{1,3},{2,0},{3,1},{4,6},{5,7},{6,4},{7,5},{8,10},{9,11},{10,... | collective-permute-start | bytes 442376 | tf_op jit(solution)/shard_map/ppermute | solution.py:780
  127.0 30.5 %collective-permute-start.5 = (bf16[96,768]{0,1:T(8,128)(2,1)S(1)}, bf16[96,768]{0,1:T(8,128)(2,1)S(1)}, u32[]{:S(2)}, u32[]{:S(2)}) collective-permute-start(bf16[96,768]{0,1:T(8,128)(2,1)S(1)} %pad_maximum_fusion.9), channel_id=1, source_target_pairs={{0,1},{1,2},{2,3},{3,0},{4,5},{5,6},{6,7},{7,4},{8,9},{9,10},{10,1... | collective-permute-start | bytes 442376 | tf_op jit(solution)/shard_map/ppermute | solution.py:780
  158.4 3.0 copy-start.26
  158.4 3.0 copy-start.27
  158.4 3.1 copy-start.16
  158.5 3.1 copy-start.17
  159.5 5.6 copy-start.8
  161.4 137.7 %all-gather.8.cloned.1.call-start = ((), (), s32[]{:S(2)}) async-start(), calls=%async_computation.6 | async-start | bytes 10616832 | tf_op jit(solution)/shard_map/all_gather | solution.py:800
  161.6 9.3 %collective-permute-start.10 = (bf16[96,1536]{1,0:T(8,128)(2,1)S(1)}, bf16[96,1536]{1,0:T(8,128)(2,1)}, u32[]{:S(2)}, u32[]{:S(2)}) collective-permute-start(bf16[96,1536]{1,0:T(8,128)(2,1)S(1)} %pad_maximum_fusion.8), channel_id=1, source_target_pairs={{0,3},{1,0},{2,1},{3,2},{4,7},{5,4},{6,5},{7,6},{8,11},{9,8},{10,9... | collective-permute-start | bytes 884744 | tf_op jit(solution)/shard_map/ppermute | solution.py:780
  163.4 25.8 %collective-permute-start.9 = (bf16[96,1536]{1,0:T(8,128)(2,1)S(1)}, bf16[96,1536]{1,0:T(8,128)(2,1)S(1)}, u32[]{:S(2)}, u32[]{:S(2)}) collective-permute-start(bf16[96,1536]{1,0:T(8,128)(2,1)S(1)} %pad_maximum_fusion.8), channel_id=1, source_target_pairs={{0,2},{1,3},{2,0},{3,1},{4,6},{5,7},{6,4},{7,5},{8,10},{9,11},{10,... | collective-permute-start | bytes 884744 | tf_op jit(solution)/shard_map/ppermute | solution.py:780
  164.0 26.0 %collective-permute-start.8 = (bf16[96,1536]{1,0:T(8,128)(2,1)S(1)}, bf16[96,1536]{1,0:T(8,128)(2,1)S(1)}, u32[]{:S(2)}, u32[]{:S(2)}) collective-permute-start(bf16[96,1536]{1,0:T(8,128)(2,1)S(1)} %pad_maximum_fusion.8), channel_id=1, source_target_pairs={{0,1},{1,2},{2,3},{3,0},{4,5},{5,6},{6,7},{7,4},{8,9},{9,10},{10,1... | collective-permute-start | bytes 884744 | tf_op jit(solution)/shard_map/ppermute | solution.py:780
  167.5 34.0 %copy-start.2 = (f32[512,768]{1,0:T(8,128)}, f32[512,768]{1,0:T(8,128)S(1)}, u32[]{:S(2)}) copy-start(f32[512,768]{1,0:T(8,128)S(1)} %get-tuple-element.214) | copy-start | bytes 4718596
  196.7 7.5 %copy-start.30 = (bf16[768,6144]{1,0:T(8,128)(2,1)S(1)}, bf16[768,6144]{1,0:T(8,128)(2,1)}, u32[]{:S(2)}) copy-start(bf16[768,6144]{1,0:T(8,128)(2,1)} %all-gather.4.cloned.1.call-done) | copy-start | bytes 28311556
  201.5 2.7 copy-start.35
  204.2 4.0 copy-start.28
  204.2 4.0 copy-start.29
  208.1 238.6 %reduce-scatter.5.cloned.1.call-start = ((), (), s32[]{:S(2)}) async-start(), calls=%async_computation.7 | async-start | bytes 11943936 | tf_op jit(solution)/shard_map/reduce_scatter | solution.py:888
  208.2 100.5 %collective-permute-start.11 = (bf16[512,768]{1,0:T(8,128)(2,1)}, bf16[512,768]{1,0:T(8,128)(2,1)}, u32[]{:S(2)}, u32[]{:S(2)}) collective-permute-start(bf16[512,768]{1,0:T(8,128)(2,1)} %param.22), channel_id=1, source_target_pairs={{0,0},{1,4},{2,8},{3,12},{4,3},{5,7},{6,11},{7,15},{8,1},{9,5},{10... | collective-permute-start | bytes 2359304 | tf_op jit(solution)/shard_map/ppermute | solution.py:867
  217.4 41.6 %copy-start.1 = (bf16[512,768]{1,0:T(8,128)(2,1)S(1)}, bf16[512,768]{1,0:T(8,128)(2,1)}, u32[]{:S(2)}) copy-start(bf16[512,768]{1,0:T(8,128)(2,1)} %fusion.49.refs_0_.own_ref) | copy-start | bytes 2359300
  259.0 3.2 copy-start
  298.7 29.3 %copy-start.4 = (f32[512,768]{1,0:T(8,128)}, f32[512,768]{1,0:T(8,128)S(1)}, u32[]{:S(2)}) copy-start(f32[512,768]{1,0:T(8,128)S(1)} %get-tuple-element.216) | copy-start | bytes 4718596
  299.1 5.3 copy-start.31
  323.1 1.6 copy-start.36
  335.1 1.3 copy-start.33
  335.3 0.9 copy-start.14
  345.2 153.6 %reduce-scatter.7.cloned.1.call-start = ((), (), s32[]{:S(2)}) async-start(), calls=%async_computation.8 | async-start | bytes 3981312 | tf_op jit(solution)/shard_map/reduce_scatter | solution.py:888
  345.3 11.0 %copy-start.15 = (bf16[512,768]{1,0:T(8,128)(2,1)S(1)}, bf16[512,768]{1,0:T(8,128)(2,1)}, u32[]{:S(2)}) copy-start(bf16[512,768]{1,0:T(8,128)(2,1)} %copy-done.14) | copy-start | bytes 2359300
  345.3 63.4 %collective-permute-start.12 = (bf16[512,768]{1,0:T(8,128)(2,1)}, bf16[512,768]{1,0:T(8,128)(2,1)}, u32[]{:S(2)}, u32[]{:S(2)}) collective-permute-start(bf16[512,768]{1,0:T(8,128)(2,1)} %get-tuple-element.192), channel_id=1, source_target_pairs={{0,0},{4,1},{8,2},{12,3},{3,4},{7,5},{11,6},{15,7},{1,8},{5,9},{9,... | collective-permute-start | bytes 2359304 | tf_op jit(solution)/shard_map/ppermute | solution.py:881
  450.6 148.9 %reduce-scatter.9.cloned.1.call-start = ((), (), s32[]{:S(2)}) async-start(), calls=%async_computation.9 | async-start | bytes 11943936 | tf_op jit(solution)/shard_map/reduce_scatter | solution.py:888
  450.9 8.6 %copy-start.3 = (f32[512,768]{1,0:T(8,128)S(1)}, f32[512,768]{1,0:T(8,128)}, u32[]{:S(2)}) copy-start(f32[512,768]{1,0:T(8,128)} %copy-done.2) | copy-start | bytes 4718596
  466.0 1.2 copy-start.32
  466.0 5.5 slice-start
  466.2 0.9 copy-start.12
  468.1 3.5 slice-start.1
  482.8 4.3 copy-start.13
  482.8 204.7 %reduce-scatter.11.cloned.1.call-start = ((), (), s32[]{:S(2)}) async-start(), calls=%async_computation.10 | async-start | bytes 3981312 | tf_op jit(solution)/shard_map/reduce_scatter | solution.py:888
  599.5 35.8 %copy-start.34 = (bf16[512,768]{1,0:T(8,128)(2,1)S(1)}, bf16[512,768]{1,0:T(8,128)(2,1)}, u32[]{:S(2)}) copy-start(bf16[512,768]{1,0:T(8,128)(2,1)} %get-tuple-element.104) | copy-start | bytes 2359300
  635.4 5.6 copy-start.19
  638.9 47.4 %collective-permute-start.13 = (bf16[512,768]{1,0:T(8,128)(2,1)}, bf16[512,768]{1,0:T(8,128)(2,1)S(1)}, u32[]{:S(2)}, u32[]{:S(2)}) collective-permute-start(bf16[512,768]{1,0:T(8,128)(2,1)} %add_convert_fusion), channel_id=1, source_target_pairs={{0,0},{4,1},{8,2},{12,3},{3,4},{7,5},{11,6},{15,7},{1,8},{5,9},{9,... | collective-permute-start | bytes 2359304 | tf_op jit(solution)/shard_map/ppermute | solution.py:950
  641.2 44.5 %copy-start.24 = (f32[8,768]{1,0:T(8,128)S(1)}, f32[8,768]{1,0:T(8,128)}, u32[]{:S(2)}) copy-start(f32[8,768]{1,0:T(8,128)} %sum_everywhere.1) | copy-start | bytes 73732
  642.7 44.9 %copy-start.5 = (f32[96,1728]{1,0:T(8,128)S(1)}, f32[96,1728]{1,0:T(8,128)}, u32[]{:S(2)}) copy-start(f32[96,1728]{1,0:T(8,128)} %sum_line.3) | copy-start | bytes 1990660
  642.7 44.9 %copy-start.10 = (f32[96,1728]{1,0:T(8,128)S(1)}, f32[96,1728]{1,0:T(8,128)}, u32[]{:S(2)}) copy-start(f32[96,1728]{1,0:T(8,128)} %get-tuple-element.125) | copy-start | bytes 1990660
  687.6 1.1 copy-start.11
  687.6 1.4 copy-start.20
Sparse Core Ops, SparseCore 0:
  100.9 60.2 all-gather.3
  163.1 38.7 all-gather.5
  208.2 81.3 all-gather.7
  345.4 101.2 reduce-scatter.4
  450.7 48.0 reduce-scatter.6
  502.2 83.1 reduce-scatter.8
  599.7 46.9 reduce-scatter.10

commit v5 on v4

--- a/solution.py
+++ b/solution.py
@@ -219,12 +219,60 @@
     return pl.ds(pl.multiple_of(block * size + start, 16), size if rows is None else rows)
 
 
-def gather_kernel(pieces, *refs):
-    count = len(pieces)
-    owns, outs = refs[:count], refs[count : 2 * count]
-    keep_sem, mate_send, mate_recv, far_send, far_recv, on_send, on_recv = refs[2 * count :]
+def line_peers(parts):
+    plane = lax.axis_index("tensor")
+    return [{"tensor": (plane + by) % parts} for by in range(1, parts)]
+
+
+def lines_start(parts, groups, owns, outs, keep_sem, send_sem, recv_sem):
+    peers = line_peers(parts)
+    copies, kept, n = [], [], 0
+    for count, out in zip(groups, outs):
+        for kind in range(count):
+            own = owns[n]
+            width = own.shape[1]
+            kept.append(
+                pltpu.make_async_copy(own, out.at[:, pl.ds(kind * parts * width, width)], keep_sem.at[n])
+            )
+            kept[-1].start()
+            for by in range(1, parts):
+                copy = pltpu.make_async_remote_copy(
+                    src_ref=own,
+                    dst_ref=out.at[:, pl.ds((kind * parts + by) * width, width)],
+                    send_sem=send_sem.at[n, by - 1],
+                    recv_sem=recv_sem.at[n, by - 1],
+                    device_id=peers[by - 1],
+                    device_id_type=MESH_ID,
+                )
+                copy.start()
+                copies.append(copy)
+            n += 1
+    return copies, kept
+
+
+def lines_finish(copies, kept):
+    for copy in copies + kept:
+        copy.wait()
+
+
+def lines_shapes(parts, groups):
+    owns = [own for group in groups for own in group]
+    shapes = [
+        jax.ShapeDtypeStruct((group[0].shape[0], parts * len(group) * group[0].shape[1]), BF)
+        for group in groups
+    ]
+    dma, count = pltpu.SemaphoreType.DMA, max(len(owns), 1)
+    return owns, shapes, [dma((count,)), dma((count, parts - 1)), dma((count, parts - 1))]
+
+
+def gather_kernel(pieces, parts_along, groups, *refs):
+    count, lines = len(pieces), sum(groups)
+    at = [count, count + lines, 2 * count + lines, 2 * count + lines + len(groups)]
+    owns, line_owns = refs[: at[0]], refs[at[0] : at[1]]
+    outs, line_outs = refs[at[1] : at[2]], refs[at[2] : at[3]]
+    keep_sem, mate_send, mate_recv, far_send, far_recv, on_send, on_recv = refs[at[3] : at[3] + 7]
     me, mate, far, cross = quad_places()
-    greet({"quad": mate}, {"quad": far})
+    greet({"quad": mate}, {"quad": far}, *(line_peers(parts_along) if groups else []))
 
     def send(source, target, sends, recvs, at, peer):
         return pltpu.make_async_remote_copy(
@@ -254,6 +302,7 @@
     ]
     for copy in to_mate:
         copy.start()
+    along = lines_start(parts_along, groups, line_owns, line_outs, *refs[at[3] + 7 :])
     kept = [
         pltpu.make_async_copy(owns[n], outs[n].at[block_at(me, owns[n].shape[0])], keep_sem.at[n])
         for n in range(count)
@@ -273,21 +322,24 @@
         copy.wait_send()
     for copy in kept:
         copy.wait()
-
-
-def quad_gather(arrays, pieces, call):
+    lines_finish(*along)
+
+
+def quad_gather(arrays, pieces, call, parts=1, groups=()):
     count, total = len(arrays), sum(pieces)
     sems = [pltpu.SemaphoreType.DMA((k,)) for k in (count, count, count, total, total, total, total)]
+    owns, shapes, line_sems = lines_shapes(max(parts, 2), groups)
     return pl.pallas_call(
-        functools.partial(gather_kernel, pieces),
-        out_shape=[jax.ShapeDtypeStruct((QUAD * x.shape[0],) + x.shape[1:], x.dtype) for x in arrays],
-        in_specs=[pl.BlockSpec(memory_space=pltpu.VMEM)] * count,
-        out_specs=[pl.BlockSpec(memory_space=pl.ANY)] * count,
-        scratch_shapes=sems,
+        functools.partial(gather_kernel, pieces, parts, tuple(len(g) for g in groups)),
+        out_shape=[jax.ShapeDtypeStruct((QUAD * x.shape[0],) + x.shape[1:], x.dtype) for x in arrays]
+        + shapes,
+        in_specs=[pl.BlockSpec(memory_space=pltpu.VMEM)] * (count + len(owns)),
+        out_specs=[pl.BlockSpec(memory_space=pl.ANY)] * (count + len(shapes)),
+        scratch_shapes=sems + line_sems,
         compiler_params=pltpu.CompilerParams(collective_id=call, has_side_effects=True),
         cost_estimate=SHORT,
         name="quad_gather",
-    )(*arrays)
+    )(*arrays, *owns)
 
 
 REDUCE_PIECES = 4
@@ -448,7 +500,11 @@
     )(x)
 
 
-def rows_kernel(parts, own_ref, out_ref, keep_sem, line_send, line_recv, send_sem, recv_sem):
+def rows_kernel(parts, groups, own_ref, *refs):
+    lines = sum(groups)
+    line_owns, out_ref, line_outs = refs[:lines], refs[lines], refs[lines + 1 : lines + 1 + len(groups)]
+    keep_sem, line_send, line_recv, send_sem, recv_sem = refs[lines + 1 + len(groups) :][:5]
+    line_sems = refs[lines + 1 + len(groups) :][5:]
     me, mate, far, cross = quad_places()
     row, plane = lax.axis_index("row"), lax.axis_index("tensor")
     other = 1 - row
@@ -489,6 +545,7 @@
         along.append(copy)
     keep = pltpu.make_async_copy(own_ref, block(row, me, 0), keep_sem)
     keep.start()
+    only_line = lines_start(parts, groups, line_owns, line_outs, *line_sems)
     near_x, near_y, beyond, mates = [], [], [], []
     for part in range(parts + 1):
         if part < parts:
@@ -519,21 +576,24 @@
     for copy in along + used:
         copy.wait_send()
     keep.wait()
-
-
-def gather_rows(rows, parts):
+    lines_finish(*only_line)
+
+
+def gather_rows(rows, parts, groups):
     size, width = rows.shape
     dma = pltpu.SemaphoreType.DMA
+    owns, shapes, line_sems = lines_shapes(parts, groups)
     return pl.pallas_call(
-        functools.partial(rows_kernel, parts),
-        out_shape=jax.ShapeDtypeStruct((ROW * QUAD * size, parts * width), rows.dtype),
-        in_specs=[pl.BlockSpec(memory_space=pltpu.VMEM)],
-        out_specs=pl.BlockSpec(memory_space=pl.ANY),
-        scratch_shapes=[dma, dma((parts - 1,)), dma((parts - 1,)), dma((7 * parts,)), dma((7 * parts,))],
+        functools.partial(rows_kernel, parts, tuple(len(g) for g in groups)),
+        out_shape=[jax.ShapeDtypeStruct((ROW * QUAD * size, parts * width), rows.dtype)] + shapes,
+        in_specs=[pl.BlockSpec(memory_space=pltpu.VMEM)] * (1 + len(owns)),
+        out_specs=[pl.BlockSpec(memory_space=pl.ANY)] * (1 + len(shapes)),
+        scratch_shapes=[dma, dma((parts - 1,)), dma((parts - 1,)), dma((7 * parts,)), dma((7 * parts,))]
+        + line_sems,
         compiler_params=pltpu.CompilerParams(collective_id=CALL_ROWS, has_side_effects=True),
         cost_estimate=SHORT,
         name="gather_rows",
-    )(rows)
+    )(rows, *owns)
 
 
 def regroup_kernel(parts, kinds, x_ref, out_ref):
@@ -545,21 +605,17 @@
 
 
 def regroup(rows, parts, kinds):
-    block = pl.BlockSpec((rows.shape[0] // 4, rows.shape[1]), lambda i: (i, 0))
+    steps = max(rows.shape[0] // 192, 1)
+    block = pl.BlockSpec((rows.shape[0] // steps, rows.shape[1]), lambda i: (i, 0))
     return pl.pallas_call(
         functools.partial(regroup_kernel, parts, kinds),
         out_shape=jax.ShapeDtypeStruct(rows.shape, rows.dtype),
-        grid=(4,),
+        grid=(steps,),
         in_specs=[block],
         out_specs=block,
         cost_estimate=SHORT,
         name="regroup",
     )(rows)
-
-
-def line_peers(parts):
-    plane = lax.axis_index("tensor")
-    return [{"tensor": (plane + by) % parts} for by in range(1, parts)]
 
 
 def line_pick(sizes, parts, x_ref, part):
@@ -790,12 +846,6 @@
         qkv = qkv.reshape(depth, head_local, 3, HD).transpose(0, 2, 1, 3)
         return jnp.concatenate([qkv.reshape(depth, 3 * chunk), back.T], axis=1)
 
-    def attn_rows(qkv, back):
-        return by_kind(spread(attn_shard(qkv, back)), 4)
-
-    def ffn_rows(up, down):
-        return by_kind(spread(jnp.concatenate([up, down.T], axis=1)), 2)
-
     def over_data(rows):
         return lax.all_gather(rows, DATA, axis=0, tiled=True)
 
@@ -805,22 +855,24 @@
     numbers = jnp.pad(numbers, ((0, 14), (0, width - numbers.shape[1])))
     own_numbers = lax.ppermute(numbers, EVERY, moves)
     own_tokens = lax.ppermute(layer_input, EVERY, moves)
+    ffn_shards = [w_up[0], w_down[0].T]
     if lax.axis_size("hi") == 1:
-        rows = gather_rows(attn_shard(w_qkv[0], w_out[0]), tensor)
-        rows, own_tokens, own_numbers, up_0, down_0 = lax.optimization_barrier(
-            (rows, own_tokens, own_numbers, w_up[0], w_down[0])
+        rows, first_rows = gather_rows(attn_shard(w_qkv[0], w_out[0]), tensor, [ffn_shards])
+        rows, first_rows, own_tokens, own_numbers = lax.optimization_barrier(
+            (rows, first_rows, own_tokens, own_numbers)
         )
         attn_full = [regroup(rows, tensor, 4)]
     else:
-        attn_full = [over_data(attn_rows(w_qkv[0], w_out[0]))]
-        own_tokens, own_numbers, up_0, down_0 = lax.optimization_barrier(
-            (own_tokens, own_numbers, w_up[0], w_down[0])
-        )
-    first_rows = ffn_rows(up_0, down_0)
-
-    inputs, numbers = quad_gather([own_tokens, own_numbers], [4, 1], CALL_GATHER_FIRST)
-    inputs, first_rows = lax.optimization_barrier((inputs, first_rows))
+        attn_full = [over_data(by_kind(spread(attn_shard(w_qkv[0], w_out[0])), 4))]
+        first_rows = by_kind(spread(jnp.concatenate(ffn_shards, axis=1)), 2)
     ffn_full = [over_data(first_rows)]
+
+    groups = []
+    for layer in range(1, LAYERS):
+        groups += [[attn_shard(w_qkv[layer], w_out[layer])], [w_up[layer], w_down[layer].T]]
+    inputs, numbers, *later = quad_gather(
+        [own_tokens, own_numbers], [4, 1], CALL_GATHER_FIRST, tensor, groups
+    )
     numbers = numbers.reshape(QUAD, 16, width)[:, :2].astype(jnp.int32)
     numbers = numbers[:, 0] * BLK + numbers[:, 1]
     lengths, deal = numbers[0, :docs], numbers[0, docs : docs + group_blocks]
@@ -854,14 +906,9 @@
         query = (dot(own_inputs, w_query).astype(BF).astype(F32) * score_scale).astype(BF)
         keyval = dot(inputs, w_keyval).astype(BF)
         if layer < LAYERS - 1:
-            keyval, following = lax.optimization_barrier(
-                (keyval, [w[layer + 1] for w in (w_qkv, w_out, w_up, w_down)])
-            )
-            attn_next, ffn_next = attn_rows(*following[:2]), ffn_rows(*following[2:])
+            attn_full.append(over_data(regroup(later[2 * layer], tensor, 4)))
+            ffn_full.append(over_data(later[2 * layer + 1]))
         mixed, logs = attend_forward(query, keyval, tables)
-        if layer < LAYERS - 1:
-            mixed, attn_next = lax.optimization_barrier((mixed, attn_next))
-            attn_full.append(over_data(attn_next))
         if layer == 0:
             mixed, own_grad = lax.optimization_barrier((mixed, out_grad))
             own_grad = lax.ppermute(own_grad, EVERY, moves)
@@ -871,9 +918,6 @@
         pre_act = dot(ffn_in, w_expand)
         activated = gelu_tanh(pre_act).astype(BF)
         summed_two = normed + dot_right_t(activated, w_shrink_t)
-        if layer < LAYERS - 1:
-            summed_two, ffn_next = lax.optimization_barrier((summed_two, ffn_next))
-            ffn_full.append(over_data(ffn_next))
         stored.append(
             (own_inputs, inputs, query, keyval, mixed, logs, summed_one, ffn_in, pre_act, activated, summed_two)
         )
@@ -929,13 +973,12 @@
             query, keyval, logs, d_mixed, tables, own_inputs, inputs, w_keyval
         )
         if layer == 0:
-            norms = jnp.stack([norm_parts[l][k] for k in range(4) for l in range(LAYERS)])
-            norms, others = lax.optimization_barrier((norms, others))
-            norm_sums = sum_everywhere(norms)
-            norm_sums, ffn_last = lax.optimization_barrier((norm_sums, ffn_last))
+            others, ffn_last = lax.optimization_barrier((others, ffn_last))
             ffn_grads[1] = sum_line(ffn_last, (hidden, hidden, chunk), tensor, CALL_LINE_FFN)
-            others, ffn_sum, attn_part, norm_sums, ffn_grads[1] = lax.optimization_barrier(
-                (others, ffn_sum, attn_part, norm_sums, ffn_grads[1])
+            attn_sums[1], ffn_grads[1] = lax.optimization_barrier((attn_sums[1], ffn_grads[1]))
+            attn_grads[1] = sum_line(by_piece(attn_sums[1]), (chunk,) * 3, tensor, CALL_LINE_ATTN)
+            others, ffn_sum, attn_part, ffn_grads[1], attn_grads[1] = lax.optimization_barrier(
+                (others, ffn_sum, attn_part, ffn_grads[1], attn_grads[1])
             )
         else:
             others, layer_output = lax.optimization_barrier((others, layer_output))
@@ -948,11 +991,11 @@
         attn_sums[layer] = sum_data(attn_part)
         state_grad = d_one + dot_right_t(d_query, w_query) + summed
     input_grad = lax.ppermute(state_grad.astype(BF), EVERY, moves_back).astype(F32)
-    for layer in reversed(range(LAYERS)):
-        attn_sums[layer], ffn_grads, attn_grads = lax.optimization_barrier(
-            (attn_sums[layer], ffn_grads, attn_grads)
-        )
-        attn_grads[layer] = sum_line(by_piece(attn_sums[layer]), (chunk,) * 3, tensor, CALL_LINE_ATTN)
+    norms = jnp.stack([norm_parts[l][k] for k in range(4) for l in range(LAYERS)])
+    norms, state_grad = lax.optimization_barrier((norms, state_grad))
+    norm_sums = sum_everywhere(norms)
+    attn_sums[0], norm_sums = lax.optimization_barrier((attn_sums[0], norm_sums))
+    attn_grads[0] = sum_line(by_piece(attn_sums[0]), (chunk,) * 3, tensor, CALL_LINE_ATTN)
 
     qkv_grad = jnp.stack(attn_grads).reshape(LAYERS, depth, 3, head_local, HD)
     qkv_grad = qkv_grad.transpose(0, 1, 3, 2, 4).reshape(LAYERS, depth, 3 * chunk)

time: 729 us -> 694 us (0.952)
  starting transfers between devices: 39.7 us -> 19.7 us
  local copies, waits for them, and re-layouts: 47.6 us -> 30.5 us
  Pallas kernels: 445 us -> 457 us
    pallas_call x3, Pallas kernels: 92.6 us -> 65.3 us  [sum_line(): pl.pallas_call(functools.partial(parts_kernel, sizes, parts), out_shape=j...]
    pallas_call x3, Pallas kernels: 108 us -> 128 us  [the longest x2 67.4 us: quad_gather(): pl.pallas_call(functools.partial(gather_kernel, pieces, parts, tuple((len...]
    ppermute x9 -> x0, starting transfers between devices: 19.1 us -> none  [shifted(): lax.ppermute(x, 'tensor', [(i, (i + by) % tensor) for i in range(tensor)])]
    ppermute x9 -> x0, waiting for transfers between devices: 18.5 us -> none  [shifted(): lax.ppermute(x, 'tensor', [(i, (i + by) % tensor) for i in range(tensor)])]
    all_gather x3, waiting for transfers between devices: 0.04 us -> 15.7 us  [over_data(): return lax.all_gather(rows, DATA, axis=0, tiled=True)]
    pallas_call x1, Pallas kernels: 19.4 us -> 33 us  [sum_everywhere(): pl.pallas_call(functools.partial(norms_kernel, tuple(hops)), out_shape=ja...]
    another operation x13 -> x0, local copies, waits for them, and re-layouts: 9.99 us -> none  [by_kind(): rows = jnp.stack([part.reshape(depth, kinds, -1) for part in parts], axis=2)]
    another operation x6 -> x3, other arithmetic: 8.5 us -> 0.94 us  [the longest x3 7.56 us: by_kind(): rows = jnp.stack([part.reshape(depth, kinds, -1) for part in parts], axis=2)]
  transfers between devices with their start and end apart: 21 -> 12, of which waited for: 4 -> 2; matrix products, arithmetic and copies ran while one was open for 18% -> 17% of each run, Pallas kernels for 60% -> 64%
where the time goes in v5:
time: 694 us; the launch traced here: 685 us
  Pallas kernels  457 us (66%)
  matrix products  101 us (15%)
  other arithmetic  35.3 us (5%)
  local copies, waits for them, and re-layouts  30.5 us (4%)
  waiting for transfers between devices  26.1 us (4%)
  starting transfers between devices  19.7 us (3%)
  between operations  15.3 us (2%)
    pallas_call x2, Pallas kernels, attend_backward(): pl.pallas_call(backward_kernel, grid_spec=pltpu.PrefetchScalarGridSpec(nu...  96 us
    pallas_call x2, Pallas kernels, quad_gather(): pl.pallas_call(functools.partial(gather_kernel, pieces, parts, tuple((len...  67.4 us
    pallas_call x3, Pallas kernels, sum_line(): pl.pallas_call(functools.partial(parts_kernel, sizes, parts), out_shape=j...  65.3 us
    pallas_call x1, Pallas kernels, gather_rows(): pl.pallas_call(functools.partial(rows_kernel, parts, tuple((len(g) for g...  60.1 us
    dot_general x10, matrix products, dot(): return jnp.dot(left, right, preferred_element_type=F32)  55.2 us
    pallas_call x2, Pallas kernels, attend_forward(): pl.pallas_call(forward_kernel, grid_spec=pltpu.PrefetchScalarGridSpec(num...  50.5 us
    pallas_call x1, Pallas kernels, quad_reduce_and_line(): pl.pallas_call(functools.partial(both_kernel, sizes, planes), out_shape=[...  39.9 us
    pallas_call x1, Pallas kernels, quad_reduce(): pl.pallas_call(reduce_kernel, out_shape=jax.ShapeDtypeStruct((rows, width...  37.2 us
  transfers between devices with their start and end apart: 12, of which 2 were waited for; matrix products, arithmetic and copies ran while one was open for 17% of the time, Pallas kernels for 64%

profile of v5, /device:TPU:0, one launch (start us, length us, event | category | flops | bytes accessed | tf_op | source)
XLA Modules:
  0.0 685.1 jit_solution(8128849150474740288)
XLA Ops:
  7.2 1.9 collective-permute-start
  12.5 1.0 fusion.92
  16.1 60.1 %gather_rows.1 = (bf16[768,3072]{1,0:T(8,128)(2,1)}, bf16[96,6144]{1,0:T(8,128)(2,1)}) custom-call(bf16[96,768]{1,0:T(8,128)(2,1)} %pad_maximum_fusion.4.own_ref, bf16[96,768]{1,0:T(8,128)(2,1)} %get-tuple-element.174.refs_0_, bf16[96,768]{1,0:T(8,128)(2,1)} %get-tuple-element.172.refs_1_), custom_call_target="tpu_custom_call" | custom-call | flops 1000000 | bytes 1000000 | tf_op jit(solution)/shard_map/gather_rows/pallas_call | solution.py:586
  77.5 41.6 %quad_gather.2 = (bf16[2048,768]{1,0:T(8,128)(2,1)}, bf16[64,768]{1,0:T(8,128)(2,1)}, bf16[96,3072]{1,0:T(8,128)(2,1)}, bf16[96,6144]{1,0:T(8,128)(2,1)}) custom-call(bf16[512,768]{1,0:T(8,128)(2,1)} %copy-done.6, bf16[16,768]{1,0:T(8,128)(2,1)} %copy-done.19, bf16[96,768]{1,0:T(8,128)(2,1)} %pad_maximum_fusion.5.refs_2_, ...), custom_call_target="tpu_custom_call" | custom-call | flops 1000000 | bytes 1000000 | tf_op jit(solution)/shard_map/quad_gather/pallas_call | solution.py:332
  119.1 2.1 regroup.3
  126.8 1.0 reshape.661.bias_ref
  127.8 5.5 regroup.2
  133.5 0.9 select_reduce_fusion.keys_at
  134.4 3.1 multiply_convert_fusion.3.q_ref
  137.5 8.6 %convolution_convert_fusion.1.k_ref.v_ref = bf16[2048,1536]{1,0:T(8,128)(2,1)} fusion(bf16[2048,768]{1,0:T(8,128)(2,1)S(1)} %copy-done.8, bf16[768,3072]{1,0:T(8,128)(2,1)} %regroup.2), kind=kOutput, calls=%fused_computation.7 | convolution fusion | flops 4834983936 | bytes 11796480 | tf_op jit(solution)/shard_map/dot_general | solution.py:41
  146.1 25.2 %attend_forward.2 = (bf16[512,768]{1,0:T(8,128)(2,1)}, f32[8,1,768]{2,1,0:T(1,128)}) custom-call(s32[8,16]{1,0:T(8,128)} %select_reduce_fusion.keys_at, s32[8]{0:T(128)} %get-tuple-element.188.steps_of, bf16[512,768]{1,0:T(8,128)(2,1)} %multiply_convert_fusion.3.q_ref, bf16[2048,1536]{1,0:T(8,128)(2,1)} %convolution_convert_fusion.1.k_ref.v_ref, ...), custom_call_target="tpu_custom_call" | custom-call | flops 1000000 | bytes 1000000 | tf_op jit(solution)/shard_map/attend_forward/pallas_call | solution.py:688
  171.3 7.4 %collective-permute-start.2 = (bf16[512,768]{1,0:T(8,128)(2,1)}, bf16[512,768]{1,0:T(8,128)(2,1)}, u32[]{:S(2)}, u32[]{:S(2)}) collective-permute-start(bf16[512,768]{1,0:T(8,128)(2,1)} %param.22), channel_id=1, source_target_pairs={{0,0},{1,4},{2,8},{3,12},{4,3},{5,7},{6,11},{7,15},{8,1},{9,5},{10... | collective-permute-start | bytes 2359304 | tf_op jit(solution)/shard_map/ppermute | solution.py:914
  178.7 2.4 fusion.96
  181.5 5.2 fusion.28
  186.9 4.0 fusion.97
  191.2 1.2 fusion.49.refs_0_.own_ref
  192.5 25.8 %quad_gather.3.in_ref = bf16[2048,768]{1,0:T(8,128)(2,1)} custom-call(bf16[512,768]{1,0:T(8,128)(2,1)} %fusion.49.refs_0_.own_ref), custom_call_target="tpu_custom_call" | custom-call | flops 1000000 | bytes 1000000 | tf_op jit(solution)/shard_map/quad_gather/pallas_call | solution.py:332
  218.3 3.1 multiply_convert_fusion.2.q_ref
  221.4 8.9 %convolution_convert_fusion.k_ref.v_ref = bf16[2048,1536]{1,0:T(8,128)(2,1)} fusion(bf16[2048,768]{1,0:T(8,128)(2,1)S(1)} %copy-done, bf16[768,3072]{1,0:T(8,128)(2,1)} %all-gather.6.cloned.1.call-done), kind=kOutput, calls=%fused_computation.6 | convolution fusion | flops 4834983936 | bytes 11796480 | tf_op jit(solution)/shard_map/dot_general | solution.py:41
  230.4 25.2 %attend_forward.3 = (bf16[512,768]{1,0:T(8,128)(2,1)}, f32[8,1,768]{2,1,0:T(1,128)}) custom-call(s32[8,16]{1,0:T(8,128)} %select_reduce_fusion.keys_at, s32[8]{0:T(128)} %get-tuple-element.188.steps_of, bf16[512,768]{1,0:T(8,128)(2,1)} %multiply_convert_fusion.2.q_ref, bf16[2048,1536]{1,0:T(8,128)(2,1)} %convolution_convert_fusion.k_ref.v_ref, ...), custom_call_target="tpu_custom_call" | custom-call | flops 1000000 | bytes 1000000 | tf_op jit(solution)/shard_map/attend_forward/pallas_call | solution.py:688
  255.6 2.4 fusion.98
  258.4 15.6 %all-gather.8.cloned.1.call-done = bf16[768,6144]{1,0:T(8,128)(2,1)} async-done(((bf16[96,6144]{1,0:T(8,128)(2,1)}), bf16[768,6144]{1,0:T(8,128)(2,1)}) %all-gather.8.cloned.1.call-update) | async-done | bytes 9437200 | tf_op jit(solution)/shard_map/all_gather | solution.py:850
  274.0 5.2 fusion.20
  279.3 4.0 fusion.99
  283.6 1.8 fusion.37
  285.4 2.7 fusion.91
  288.2 3.3 convolution_convert_fusion.4
  291.4 6.1 fusion.13
  297.6 1.6 copy-done.29
  299.2 3.5 convolution_convert_fusion.5
  302.7 5.0 multiply_reduce_fusion.1
  307.7 2.0 fusion.90
  310.0 0.9 copy-done.13
  311.8 8.0 %pad_maximum_fusion = bf16[768,6912]{1,0:T(8,128)(2,1)} fusion(bf16[768,768]{1,0:T(8,128)(2,1)S(1)} %convolution_convert_fusion.7, bf16[768,3072]{1,0:T(8,128)(2,1)S(1)} %convolution_convert_fusion.4, bf16[768,3072]{1,0:T(8,128)(2,1)S(1)} %convolution_convert_fusion.5), kind=kLoop, calls=%fused_computation | loop fusion | flops 31850496 | bytes 21233664 | tf_op jit(solution)/shard_map/concatenate | solution.py:959
  319.9 7.6 %collective-permute-start.3 = (bf16[512,768]{1,0:T(8,128)(2,1)}, bf16[512,768]{1,0:T(8,128)(2,1)}, u32[]{:S(2)}, u32[]{:S(2)}) collective-permute-start(bf16[512,768]{1,0:T(8,128)(2,1)} %get-tuple-element.168), channel_id=1, source_target_pairs={{0,0},{4,1},{8,2},{12,3},{3,4},{7,5},{11,6},{15,7},{1,8},{5,9},{9,... | collective-permute-start | bytes 2359304 | tf_op jit(solution)/shard_map/ppermute | solution.py:925
  327.5 3.9 slice.184.wk_ref.wv_ref
  331.5 3.2 convolution_convert_fusion.9.d_ref
  334.7 48.3 %attend_backward.2 = (bf16[512,768]{1,0:T(8,128)(2,1)}, bf16[2048,768]{1,0:T(8,128)(2,1)}, bf16[768,2304]{1,0:T(8,128)(2,1)}) custom-call(s32[8,16]{1,0:T(8,128)} %select_reduce_fusion.keys_at, s32[8]{0:T(128)} %get-tuple-element.188.steps_of, bf16[512,768]{1,0:T(8,128)(2,1)} %multiply_convert_fusion.2.q_ref, ...), custom_call_target="tpu_custom_call" | custom-call | flops 1000000 | bytes 1000000 | tf_op jit(solution)/shard_map/attend_backward/pallas_call | solution.py:720
  383.0 37.2 %quad_reduce.1 = f32[512,768]{1,0:T(8,128)} custom-call(bf16[2048,768]{1,0:T(8,128)(2,1)} %get-tuple-element.76.parts_ref), custom_call_target="tpu_custom_call" | custom-call | flops 1000000 | bytes 1000000 | tf_op jit(solution)/shard_map/quad_reduce/pallas_call | solution.py:416
  420.3 3.2 multiply_reduce_fusion
  424.3 8.9 %fusion.6 = bf16[512,3072]{1,0:T(8,128)(2,1)S(1)} fusion(f32[512,3072]{1,0:T(8,128)} %copy-done.28, bf16[768,6144]{1,0:T(8,128)(2,1)} %all-gather.4.cloned.1.call-done, f32[512,768]{1,0:T(8,128)S(1)} %get-tuple-element.159, f32[512]{0:T(512)S(1)} %negate_multiply_fusion.1), kind=kOutput, calls=%fused_computation.14 | convolution fusion | flops 2448162816 | bytes 15730688 | tf_op jit(solution)/shard_map/dot_general | solution.py:41
  433.2 5.8 multiply_reduce_fusion.2
  441.7 3.4 convolution_convert_fusion.3
  445.2 3.3 convolution_convert_fusion.2
  448.4 8.0 %pad_maximum_fusion.1 = bf16[768,6912]{1,0:T(8,128)(2,1)} fusion(bf16[768,768]{1,0:T(8,128)(2,1)S(1)} %convolution_convert_fusion.6, bf16[768,3072]{1,0:T(8,128)(2,1)S(1)} %convolution_convert_fusion.2, bf16[768,3072]{1,0:T(8,128)(2,1)S(1)} %convolution_convert_fusion.3), kind=kLoop, calls=%fused_computation.1 | loop fusion | flops 31850496 | bytes 21233664 | tf_op jit(solution)/shard_map/concatenate | solution.py:959
  456.5 3.3 slice.178.wk_ref.wv_ref
  459.9 2.9 convolution_convert_fusion.8.d_ref
  462.8 9.6 %reduce-scatter.7.cloned.1.call-done = bf16[96,2304]{1,0:T(8,128)(2,1)} async-done(((bf16[768,2304]{1,0:T(8,128)(2,1)}), bf16[96,2304]{1,0:T(8,128)(2,1)}) %reduce-scatter.7.cloned.1.call-update) | async-done | bytes 442384 | tf_op jit(solution)/shard_map/reduce_scatter | solution.py:932
  472.4 47.7 %attend_backward.3 = (bf16[512,768]{1,0:T(8,128)(2,1)}, bf16[2048,768]{1,0:T(8,128)(2,1)}, bf16[768,2304]{1,0:T(8,128)(2,1)}) custom-call(s32[8,16]{1,0:T(8,128)} %select_reduce_fusion.keys_at, s32[8]{0:T(128)} %get-tuple-element.188.steps_of, bf16[512,768]{1,0:T(8,128)(2,1)} %multiply_convert_fusion.3.q_ref, ...), custom_call_target="tpu_custom_call" | custom-call | flops 1000000 | bytes 1000000 | tf_op jit(solution)/shard_map/attend_backward/pallas_call | solution.py:720
  520.1 35.1 %sum_line.3 = f32[96,1728]{1,0:T(8,128)} custom-call(bf16[96,6912]{1,0:T(8,128)(2,1)} %reduce-scatter.5.cloned.1.call-done.x_ref), custom_call_target="tpu_custom_call" | custom-call | flops 1000000 | bytes 1000000 | tf_op jit(solution)/shard_map/sum_line/pallas_call | solution.py:670
  555.7 1.3 reshape.663.x_ref
  557.0 14.3 %sum_line.4 = f32[96,576]{1,0:T(8,128)} custom-call(bf16[96,2304]{1,0:T(8,128)(2,1)} %reshape.663.x_ref), custom_call_target="tpu_custom_call" | custom-call | flops 1000000 | bytes 1000000 | tf_op jit(solution)/shard_map/sum_line/pallas_call | solution.py:670
  571.3 39.9 %quad_reduce_and_line.1 = (f32[512,768]{1,0:T(8,128)}, f32[96,1728]{1,0:T(8,128)}) custom-call(bf16[2048,768]{1,0:T(8,128)(2,1)} %get-tuple-element.94.parts_ref, bf16[96,6912]{1,0:T(8,128)(2,1)} %reduce-scatter.9.cloned.1.call-done.x_ref), custom_call_target="tpu_custom_call" | custom-call | flops 1000000 | bytes 1000000 | tf_op jit(solution)/shard_map/quad_reduce_and_line/pallas_call | solution.py:441
  611.3 4.0 add_add_fusion.4
  615.3 1.8 collective-permute-start.4
  618.8 33.0 %sum_everywhere.1 = f32[8,768]{1,0:T(8,128)} custom-call(f32[8,768]{1,0:T(8,128)} %stack.36.x_ref), custom_call_target="tpu_custom_call" | custom-call | flops 1000000 | bytes 1000000 | tf_op jit(solution)/shard_map/sum_everywhere/pallas_call | solution.py:486
  651.8 1.1 fusion.62
  652.9 1.3 convert_element_type.156
  654.2 1.5 reshape.672
  656.0 1.3 reshape.673.x_ref
  657.3 15.9 %sum_line.5 = f32[96,576]{1,0:T(8,128)} custom-call(bf16[96,2304]{1,0:T(8,128)(2,1)} %reshape.673.x_ref), custom_call_target="tpu_custom_call" | custom-call | flops 1000000 | bytes 1000000 | tf_op jit(solution)/shard_map/sum_line/pallas_call | solution.py:670
  673.2 1.1 copy.70
  674.4 1.0 copy.73
  676.0 2.1 copy.84
  (182 shorter events, 22.1 us)
Async XLA Ops:
  7.2 6.7 copy-start.16
  7.2 7.4 %copy-start.17 = (bf16[2,768,96]{1,2,0:T(8,128)(2,1)S(1)}, bf16[2,768,96]{1,2,0:T(8,128)(2,1)}, u32[]{:S(2)}) copy-start(bf16[2,768,96]{1,2,0:T(8,128)(2,1)} %param.17) | copy-start | bytes 884740
  7.2 174.3 %all-gather.4.cloned.1.call-start = ((), (), s32[]{:S(2)}) async-start(), calls=%async_computation.4 | async-start | bytes 10616832 | tf_op jit(solution)/shard_map/all_gather | solution.py:850
  7.2 69.0 %collective-permute-start = (bf16[512,768]{1,0:T(8,128)(2,1)}, bf16[512,768]{1,0:T(8,128)(2,1)S(1)}, u32[]{:S(2)}, u32[]{:S(2)}) collective-permute-start(bf16[512,768]{1,0:T(8,128)(2,1)} %param.13), channel_id=1, source_target_pairs={{0,0},{1,4},{2,8},{3,12},{4,3},{5,7},{6,11},{7,15},{8,1},{9,5},{10... | collective-permute-start | bytes 2359304 | tf_op jit(solution)/shard_map/ppermute | solution.py:857
  10.9 65.3 %collective-permute-start.1 = (bf16[16,768]{1,0:T(8,128)(2,1)S(1)}, bf16[16,768]{1,0:T(8,128)(2,1)S(1)}, u32[]{:S(2)}, u32[]{:S(2)}) collective-permute-start(bf16[16,768]{1,0:T(8,128)(2,1)S(1)} %fusion.69), channel_id=1, source_target_pairs={{0,0},{1,4},{2,8},{3,12},{4,3},{5,7},{6,11},{7,15},{8,1},{9,5},{10... | collective-permute-start | bytes 73736 | tf_op jit(solution)/shard_map/ppermute | solution.py:856
  76.2 1.3 copy-start.19
  76.2 1.3 copy-start.6
  76.2 142.1 %all-gather.6.cloned.1.call-start = ((), (), s32[]{:S(2)}) async-start(), calls=%async_computation.5 | async-start | bytes 5308416 | tf_op jit(solution)/shard_map/all_gather | solution.py:850
  119.1 3.0 copy-start.20
  119.1 3.0 copy-start.21
  119.1 3.0 copy-start.22
  119.1 3.0 copy-start.23
  121.2 152.8 %all-gather.8.cloned.1.call-start = ((), (), s32[]{:S(2)}) async-start(), calls=%async_computation.6 | async-start | bytes 10616832 | tf_op jit(solution)/shard_map/all_gather | solution.py:850
  122.0 298.3 %reduce-scatter.5.cloned.1.call-start = ((), (), s32[]{:S(2)}) async-start(), calls=%async_computation.7 | async-start | bytes 11943936 | tf_op jit(solution)/shard_map/reduce_scatter | solution.py:932
  127.8 6.6 copy-start.7
  134.4 3.1 copy-start.8
  171.3 112.3 %collective-permute-start.2 = (bf16[512,768]{1,0:T(8,128)(2,1)}, bf16[512,768]{1,0:T(8,128)(2,1)}, u32[]{:S(2)}, u32[]{:S(2)}) collective-permute-start(bf16[512,768]{1,0:T(8,128)(2,1)} %param.22), channel_id=1, source_target_pairs={{0,0},{1,4},{2,8},{3,12},{4,3},{5,7},{6,11},{7,15},{8,1},{9,5},{10... | collective-permute-start | bytes 2359304 | tf_op jit(solution)/shard_map/ppermute | solution.py:914
  181.1 5.6 copy-start.2
  181.5 5.4 copy-start.24
  186.9 4.0 copy-start.28
  192.4 25.9 %copy-start.1 = (bf16[512,768]{1,0:T(8,128)(2,1)S(1)}, bf16[512,768]{1,0:T(8,128)(2,1)}, u32[]{:S(2)}) copy-start(bf16[512,768]{1,0:T(8,128)(2,1)} %fusion.49.refs_0_.own_ref) | copy-start | bytes 2359300
  218.3 3.1 copy-start
  258.0 44.7 %copy-start.4 = (f32[512,768]{1,0:T(8,128)}, f32[512,768]{1,0:T(8,128)S(1)}, u32[]{:S(2)}) copy-start(f32[512,768]{1,0:T(8,128)S(1)} %get-tuple-element.194) | copy-start | bytes 4718596
  274.0 5.3 copy-start.25
  297.5 1.6 copy-start.29
  309.8 1.3 copy-start.27
  309.9 0.9 copy-start.13
  319.9 152.5 %reduce-scatter.7.cloned.1.call-start = ((), (), s32[]{:S(2)}) async-start(), calls=%async_computation.8 | async-start | bytes 3981312 | tf_op jit(solution)/shard_map/reduce_scatter | solution.py:932
  319.9 11.6 %copy-start.14 = (bf16[512,768]{1,0:T(8,128)(2,1)S(1)}, bf16[512,768]{1,0:T(8,128)(2,1)}, u32[]{:S(2)}) copy-start(bf16[512,768]{1,0:T(8,128)(2,1)} %copy-done.13) | copy-start | bytes 2359300
  319.9 63.1 %collective-permute-start.3 = (bf16[512,768]{1,0:T(8,128)(2,1)}, bf16[512,768]{1,0:T(8,128)(2,1)}, u32[]{:S(2)}, u32[]{:S(2)}) collective-permute-start(bf16[512,768]{1,0:T(8,128)(2,1)} %get-tuple-element.168), channel_id=1, source_target_pairs={{0,0},{4,1},{8,2},{12,3},{3,4},{7,5},{11,6},{15,7},{1,8},{5,9},{9,... | collective-permute-start | bytes 2359304 | tf_op jit(solution)/shard_map/ppermute | solution.py:925
  424.2 147.1 %reduce-scatter.9.cloned.1.call-start = ((), (), s32[]{:S(2)}) async-start(), calls=%async_computation.9 | async-start | bytes 11943936 | tf_op jit(solution)/shard_map/reduce_scatter | solution.py:932
  424.2 8.9 %copy-start.3 = (f32[512,768]{1,0:T(8,128)S(1)}, f32[512,768]{1,0:T(8,128)}, u32[]{:S(2)}) copy-start(f32[512,768]{1,0:T(8,128)} %copy-done.2) | copy-start | bytes 4718596
  439.7 1.2 copy-start.26
  439.7 5.5 slice-start
  439.9 0.9 copy-start.11
  441.7 3.4 slice-start.1
  456.5 3.4 copy-start.12
  456.5 197.7 %reduce-scatter.11.cloned.1.call-start = ((), (), s32[]{:S(2)}) async-start(), calls=%async_computation.10 | async-start | bytes 3981312 | tf_op jit(solution)/shard_map/reduce_scatter | solution.py:932
  520.1 35.1 %copy-start.15 = (bf16[96,2304]{1,0:T(8,128)(2,1)S(1)}, bf16[96,2304]{1,0:T(8,128)(2,1)}, u32[]{:S(2)}) copy-start(bf16[96,2304]{1,0:T(8,128)(2,1)} %reduce-scatter.7.cloned.1.call-done) | copy-start | bytes 1327108
  611.3 6.5 copy-start.10
  611.3 6.7 copy-start.5
  611.3 6.7 copy-start.9
  615.3 37.7 %collective-permute-start.4 = (bf16[512,768]{1,0:T(8,128)(2,1)}, bf16[512,768]{1,0:T(8,128)(2,1)S(1)}, u32[]{:S(2)}, u32[]{:S(2)}) collective-permute-start(bf16[512,768]{1,0:T(8,128)(2,1)} %add_add_fusion.4), channel_id=1, source_target_pairs={{0,0},{4,1},{8,2},{12,3},{3,4},{7,5},{11,6},{15,7},{1,8},{5,9},{9,... | collective-permute-start | bytes 2359304 | tf_op jit(solution)/shard_map/ppermute | solution.py:993
  674.3 1.1 copy-start.18
Sparse Core Ops, SparseCore 0:
  76.4 70.3 all-gather.3
  149.2 58.7 all-gather.5
  209.9 64.0 all-gather.7
  320.0 99.9 reduce-scatter.4
  424.3 48.0 reduce-scatter.6
  475.8 82.5 reduce-scatter.8
  571.4 49.6 reduce-scatter.10

commit v6 on v5

--- a/solution.py
+++ b/solution.py
@@ -425,29 +425,36 @@
     )(parts)
 
 
-def both_kernel(sizes, planes, parts_ref, x_ref, out_ref, line_ref, *scratch):
+def both_kernel(sizes, planes, parts_ref, *refs):
+    count = len(sizes)
+    x_refs, out_ref, line_refs, scratch = refs[:count], refs[count], refs[count + 1 :][:count], refs[2 * count + 1 :]
     me, mate, far, cross = quad_places()
     greet({"quad": mate}, {"quad": far}, *line_peers(planes))
-    held, came, send_sem, recv_sem = scratch[:4]
-    copies = line_start(sizes, planes, x_ref, held, came, send_sem, recv_sem)
-    reduce_kernel(parts_ref, out_ref, *scratch[4:], greeted=True)
-    line_finish(sizes, planes, x_ref, line_ref, came, copies)
-
-
-def quad_reduce_and_line(parts, lines, sizes, planes):
+    lines = []
+    for n in range(count):
+        held, came, send_sem, recv_sem = scratch[4 * n : 4 * n + 4]
+        lines.append((came, line_start(sizes[n], planes, x_refs[n], held, came, send_sem, recv_sem)))
+    reduce_kernel(parts_ref, out_ref, *scratch[4 * count :], greeted=True)
+    for n in range(count):
+        line_finish(sizes[n], planes, x_refs[n], line_refs[n], *lines[n])
+
+
+def quad_reduce_and_lines(parts, lines, sizes, planes):
     rows, width = parts.shape[0] // QUAD, parts.shape[1]
-    shape = (lines.shape[0], sum(sizes))
-    vmem = pl.BlockSpec(memory_space=pltpu.VMEM)
+    shapes = [(x.shape[0], sum(own)) for x, own in zip(lines, sizes)]
+    vmem, count = pl.BlockSpec(memory_space=pltpu.VMEM), len(lines)
     return pl.pallas_call(
-        functools.partial(both_kernel, sizes, planes),
-        out_shape=[jax.ShapeDtypeStruct((rows, width), F32), jax.ShapeDtypeStruct(shape, F32)],
-        in_specs=[vmem, vmem],
-        out_specs=[vmem, vmem],
-        scratch_shapes=line_scratch(shape, planes) + reduce_scratch(rows, width),
+        functools.partial(both_kernel, tuple(sizes), planes),
+        out_shape=[jax.ShapeDtypeStruct((rows, width), F32)]
+        + [jax.ShapeDtypeStruct(shape, F32) for shape in shapes],
+        in_specs=[vmem] * (1 + count),
+        out_specs=[vmem] * (1 + count),
+        scratch_shapes=sum([line_scratch(shape, planes) for shape in shapes], [])
+        + reduce_scratch(rows, width),
         compiler_params=pltpu.CompilerParams(collective_id=CALL_BOTH, has_side_effects=True),
         cost_estimate=SHORT,
-        name="quad_reduce_and_line",
-    )(parts, lines)
+        name="quad_reduce_and_lines",
+    )(parts, *lines)
 
 
 def norms_kernel(hops, x_ref, out_ref, held, came, send_sem, recv_sem):
@@ -756,6 +763,45 @@
     )(keys_at, steps_of, query, keyval, keyval, bias, logs, d_mixed, own_inputs, inputs, w_keyval, w_keyval)
 
 
+def weights_kernel(steps, ffn_ref, two_ref, one_ref, pre_ref, act_ref, mixed_ref, out_ref, left):
+    i = pl.program_id(0)
+    for start, ref in ((0, ffn_ref), (steps, two_ref), (2 * steps, one_ref)):
+
+        @pl.when(i == start)
+        def _():
+            left[...] = jnp.transpose(ref[...])
+
+    for start, ref in ((0, pre_ref), (steps, act_ref), (2 * steps, mixed_ref)):
+
+        @pl.when((i >= start) & (i < start + steps))
+        def _():
+            out_ref[...] = dot(left[...], ref[...]).astype(BF)
+
+
+def weight_grads(ffn_in, d_two, d_one, d_pre, activated, mixed):
+    own, depth = ffn_in.shape
+    steps = d_pre.shape[1] // depth
+    last = steps - 1
+    whole = pl.BlockSpec((own, depth), lambda i: (0, 0), pipeline_mode=pl.Buffered(1))
+    return pl.pallas_call(
+        functools.partial(weights_kernel, steps),
+        grid=(2 * steps + 1,),
+        in_specs=[
+            whole,
+            whole,
+            whole,
+            pl.BlockSpec((own, depth), lambda i: (0, jnp.minimum(i, last))),
+            pl.BlockSpec((own, depth), lambda i: (0, jnp.clip(i - steps, 0, last))),
+            whole,
+        ],
+        out_specs=pl.BlockSpec((depth, depth), lambda i: (0, i)),
+        out_shape=jax.ShapeDtypeStruct((depth, (2 * steps + 1) * depth), BF),
+        scratch_shapes=[pltpu.VMEM((depth, own), BF)],
+        cost_estimate=SHORT,
+        name="weight_grads",
+    )(ffn_in, d_two, d_one, d_pre, activated, mixed)
+
+
 def attention_tables(doc_lengths, block_deal, random_rows, own_blocks, first_own):
     blocks = block_deal.shape[0]
     doc_ends = jnp.cumsum(doc_lengths)
@@ -947,55 +993,52 @@
         unused_two, ffn_back = jax.vjp(layer_norm, summed_two, ffn_gain[layer], ffn_shift[layer])
         d_two, ffn_gain_part, ffn_shift_part = ffn_back(state_grad)
         d_two_low = d_two.astype(BF)
-        shrink_grad_t = dot_left_t(d_two_low, activated)
         unused_act, gelu_back = jax.vjp(gelu_tanh, pre_act)
         d_pre = gelu_back(dot(d_two_low, w_shrink_t))[0].astype(BF)
-        expand_grad = dot_left_t(ffn_in, d_pre)
         d_normed = d_two + dot_right_t(d_pre, w_expand)
         unused_one, attn_back = jax.vjp(layer_norm, summed_one, attn_gain[layer], attn_shift[layer])
         d_one, attn_gain_part, attn_shift_part = attn_back(d_normed)
         norm_parts[layer] = (attn_gain_part, attn_shift_part, ffn_gain_part, ffn_shift_part)
         d_one_low = d_one.astype(BF)
-        ffn_part = jnp.concatenate(
-            [
-                expand_grad.astype(BF),
-                shrink_grad_t.astype(BF),
-                dot_left_t(d_one_low, mixed).astype(BF),
-            ],
-            axis=1,
-        )
+        ffn_part = weight_grads(ffn_in, d_two_low, d_one_low, d_pre, activated, mixed)
         d_one_low, ffn_part = lax.optimization_barrier((d_one_low, ffn_part))
         ffn_sum = sum_data(ffn_part)
         d_mixed = dot(d_one_low, w_back_t).astype(BF)
         if layer < LAYERS - 1:
-            d_mixed, attn_sums[layer + 1] = lax.optimization_barrier((d_mixed, attn_sums[layer + 1]))
+            norms = jnp.stack([norm_parts[l][k] for k in range(4) for l in range(LAYERS)])
+            d_mixed, norms = lax.optimization_barrier((d_mixed, norms))
+            norm_sums = sum_everywhere(norms)
+            d_mixed, norm_sums, attn_sums[layer + 1] = lax.optimization_barrier(
+                (d_mixed, norm_sums, attn_sums[layer + 1])
+            )
         d_query, others, attn_part = attend_backward(
             query, keyval, logs, d_mixed, tables, own_inputs, inputs, w_keyval
         )
         if layer == 0:
             others, ffn_last = lax.optimization_barrier((others, ffn_last))
             ffn_grads[1] = sum_line(ffn_last, (hidden, hidden, chunk), tensor, CALL_LINE_FFN)
-            attn_sums[1], ffn_grads[1] = lax.optimization_barrier((attn_sums[1], ffn_grads[1]))
-            attn_grads[1] = sum_line(by_piece(attn_sums[1]), (chunk,) * 3, tensor, CALL_LINE_ATTN)
-            others, ffn_sum, attn_part, ffn_grads[1], attn_grads[1] = lax.optimization_barrier(
-                (others, ffn_sum, attn_part, ffn_grads[1], attn_grads[1])
+            others, ffn_sum, attn_part, ffn_grads[1] = lax.optimization_barrier(
+                (others, ffn_sum, attn_part, ffn_grads[1])
             )
         else:
             others, layer_output = lax.optimization_barrier((others, layer_output))
         if layer == 0:
-            summed, ffn_grads[0] = quad_reduce_and_line(others, ffn_sum, (hidden, hidden, chunk), tensor)
+            summed, ffn_grads[0], attn_grads[1] = quad_reduce_and_lines(
+                others,
+                [ffn_sum, by_piece(attn_sums[1])],
+                [(hidden, hidden, chunk), (chunk,) * 3],
+                tensor,
+            )
         else:
             summed = quad_reduce(others)
             summed, ffn_sum, attn_part = lax.optimization_barrier((summed, ffn_sum, attn_part))
         ffn_last = ffn_sum
         attn_sums[layer] = sum_data(attn_part)
         state_grad = d_one + dot_right_t(d_query, w_query) + summed
-    input_grad = lax.ppermute(state_grad.astype(BF), EVERY, moves_back).astype(F32)
-    norms = jnp.stack([norm_parts[l][k] for k in range(4) for l in range(LAYERS)])
-    norms, state_grad = lax.optimization_barrier((norms, state_grad))
-    norm_sums = sum_everywhere(norms)
-    attn_sums[0], norm_sums = lax.optimization_barrier((attn_sums[0], norm_sums))
+    input_grad = lax.ppermute(state_grad.astype(BF), EVERY, moves_back)
     attn_grads[0] = sum_line(by_piece(attn_sums[0]), (chunk,) * 3, tensor, CALL_LINE_ATTN)
+    input_grad, attn_grads = lax.optimization_barrier((input_grad, attn_grads))
+    input_grad = input_grad.astype(F32)
 
     qkv_grad = jnp.stack(attn_grads).reshape(LAYERS, depth, 3, head_local, HD)
     qkv_grad = qkv_grad.transpose(0, 1, 3, 2, 4).reshape(LAYERS, depth, 3 * chunk)

time: 694 us -> 677 us (0.976)
  Pallas kernels: 457 us -> 477 us
  matrix products: 101 us -> 86.2 us
  other arithmetic: 35.3 us -> 21.5 us
  waiting for transfers between devices: 26.1 us -> 15 us
    pallas_call x1 -> x3, Pallas kernels: 39.9 us -> 75.7 us  [the longest x1 48 us: quad_reduce_and_lines(): pl.pallas_call(functools.partial(both_kernel, tuple(sizes), planes), out_...]
    pallas_call x1, Pallas kernels: 33 us -> 11.9 us  [sum_everywhere(): pl.pallas_call(functools.partial(norms_kernel, tuple(hops)), out_shape=ja...]
    concatenate x2 -> x0, other arithmetic: 16 us -> none  [local(): jnp.concatenate([expand_grad.astype(BF), shrink_grad_t.astype(BF), dot_le...]
    dot_general x6 -> x0, matrix products: 15.1 us -> none  [dot_left_t(): lax.dot_general(left, right, (((0,), (0,)), ((), ())), preferred_element_...]
    pallas_call x3 -> x2, Pallas kernels: 65.3 us -> 77.2 us  [sum_line(): pl.pallas_call(functools.partial(parts_kernel, sizes, parts), out_shape=j...]
    reduce_scatter x4, waiting for transfers between devices: 9.64 us -> 0.06 us  [sum_data(): return lax.psum_scatter(part, DATA, scatter_dimension=0, tiled=True)]
  transfers between devices with their start and end apart: 12 -> 12, of which waited for: 2 -> 1; matrix products, arithmetic and copies ran while one was open for 17% -> 17% of each run, Pallas kernels for 64% -> 70%
where the time goes in v6:
time: 677 us; the launch traced here: 665 us
  Pallas kernels  477 us (70%)
  matrix products  86.2 us (13%)
  local copies, waits for them, and re-layouts  30.3 us (4%)
  other arithmetic  21.5 us (3%)
  starting transfers between devices  20.2 us (3%)
  between operations  15.2 us (2%)
  waiting for transfers between devices  15 us (2%)
    pallas_call x2, Pallas kernels, attend_backward(): pl.pallas_call(backward_kernel, grid_spec=pltpu.PrefetchScalarGridSpec(nu...  90.7 us
    pallas_call x2, Pallas kernels, sum_line(): pl.pallas_call(functools.partial(parts_kernel, sizes, parts), out_shape=j...  77.2 us
    pallas_call x2, Pallas kernels, quad_gather(): pl.pallas_call(functools.partial(gather_kernel, pieces, parts, tuple((len...  66.9 us
    dot_general x10, matrix products, dot(): return jnp.dot(left, right, preferred_element_type=F32)  61.9 us
    pallas_call x1, Pallas kernels, gather_rows(): pl.pallas_call(functools.partial(rows_kernel, parts, tuple((len(g) for g...  60.1 us
    pallas_call x1, Pallas kernels, quad_reduce_and_lines(): pl.pallas_call(functools.partial(both_kernel, tuple(sizes), planes), out_...  48 us
    pallas_call x2, Pallas kernels, attend_forward(): pl.pallas_call(forward_kernel, grid_spec=pltpu.PrefetchScalarGridSpec(num...  44.4 us
    pallas_call x1, Pallas kernels, quad_reduce(): pl.pallas_call(reduce_kernel, out_shape=jax.ShapeDtypeStruct((rows, width...  42.2 us
  transfers between devices with their start and end apart: 12, of which 1 were waited for; matrix products, arithmetic and copies ran while one was open for 17% of the time, Pallas kernels for 70%

profile of v6, /device:TPU:0, one launch (start us, length us, event | category | flops | bytes accessed | tf_op | source)
XLA Modules:
  0.0 665.2 jit_solution(18193266081238166308)
XLA Ops:
  7.2 1.9 collective-permute-start
  11.6 0.8 fusion.89
  12.5 1.0 fusion.88
  16.1 60.1 %gather_rows.1 = (bf16[768,3072]{1,0:T(8,128)(2,1)}, bf16[96,6144]{1,0:T(8,128)(2,1)}) custom-call(bf16[96,768]{1,0:T(8,128)(2,1)} %pad_maximum_fusion.2.own_ref, bf16[96,768]{1,0:T(8,128)(2,1)} %get-tuple-element.176.refs_0_, bf16[96,768]{1,0:T(8,128)(2,1)} %get-tuple-element.174.refs_1_), custom_call_target="tpu_custom_call" | custom-call | flops 1000000 | bytes 1000000 | tf_op jit(solution)/shard_map/gather_rows/pallas_call | solution.py:593
  77.5 41.6 %quad_gather.2 = (bf16[2048,768]{1,0:T(8,128)(2,1)}, bf16[64,768]{1,0:T(8,128)(2,1)}, bf16[96,3072]{1,0:T(8,128)(2,1)}, bf16[96,6144]{1,0:T(8,128)(2,1)}) custom-call(bf16[512,768]{1,0:T(8,128)(2,1)} %copy-done.5, bf16[16,768]{1,0:T(8,128)(2,1)} %copy-done.24, bf16[96,768]{1,0:T(8,128)(2,1)} %pad_maximum_fusion.3.refs_2_, ...), custom_call_target="tpu_custom_call" | custom-call | flops 1000000 | bytes 1000000 | tf_op jit(solution)/shard_map/quad_gather/pallas_call | solution.py:332
  119.1 2.1 regroup.3
  126.8 1.0 reshape.661.bias_ref
  127.8 5.5 regroup.2
  133.5 0.9 select_reduce_fusion.keys_at
  134.4 3.1 multiply_convert_fusion.3.q_ref
  137.5 8.6 %convolution_convert_fusion.1.k_ref.v_ref = bf16[2048,1536]{1,0:T(8,128)(2,1)} fusion(bf16[2048,768]{1,0:T(8,128)(2,1)S(1)} %copy-done.16, bf16[768,3072]{1,0:T(8,128)(2,1)} %regroup.2), kind=kOutput, calls=%fused_computation.5 | convolution fusion | flops 4834983936 | bytes 11796480 | tf_op jit(solution)/shard_map/dot_general | solution.py:41
  146.1 22.2 %attend_forward.2 = (bf16[512,768]{1,0:T(8,128)(2,1)}, f32[8,1,768]{2,1,0:T(1,128)}) custom-call(s32[8,16]{1,0:T(8,128)} %select_reduce_fusion.keys_at, s32[8]{0:T(128)} %get-tuple-element.190.steps_of, bf16[512,768]{1,0:T(8,128)(2,1)} %multiply_convert_fusion.3.q_ref, bf16[2048,1536]{1,0:T(8,128)(2,1)} %convolution_convert_fusion.1.k_ref.v_ref, ...), custom_call_target="tpu_custom_call" | custom-call | flops 1000000 | bytes 1000000 | tf_op jit(solution)/shard_map/attend_forward/pallas_call | solution.py:695
  168.4 7.9 %collective-permute-start.2 = (bf16[512,768]{1,0:T(8,128)(2,1)}, bf16[512,768]{1,0:T(8,128)(2,1)}, u32[]{:S(2)}, u32[]{:S(2)}) collective-permute-start(bf16[512,768]{1,0:T(8,128)(2,1)} %param.22), channel_id=1, source_target_pairs={{0,0},{1,4},{2,8},{3,12},{4,3},{5,7},{6,11},{7,15},{8,1},{9,5},{10... | collective-permute-start | bytes 2359304 | tf_op jit(solution)/shard_map/ppermute | solution.py:960
  176.3 2.4 fusion.92
  179.4 9.1 %multiply_convert_fusion.1 = (bf16[512,3072]{1,0:T(8,128)(2,1)S(1)}, f32[512,3072]{1,0:T(8,128)}) fusion(bf16[512,768]{1,0:T(8,128)(2,1)S(1)} %fusion.48.ffn_ref, bf16[768,6144]{1,0:T(8,128)(2,1)} %all-gather.4.cloned.1.call-done), kind=kOutput, calls=%fused_computation.21 | convolution fusion | flops 2430074880 | bytes 14942208 | tf_op jit(solution)/shard_map/dot_general | solution.py:41
  188.5 2.8 fusion.93
  191.6 1.2 fusion.49.refs_0_.own_ref
  192.8 25.3 %quad_gather.3.in_ref = bf16[2048,768]{1,0:T(8,128)(2,1)} custom-call(bf16[512,768]{1,0:T(8,128)(2,1)} %fusion.49.refs_0_.own_ref), custom_call_target="tpu_custom_call" | custom-call | flops 1000000 | bytes 1000000 | tf_op jit(solution)/shard_map/quad_gather/pallas_call | solution.py:332
  218.2 3.5 multiply_convert_fusion.2.q_ref
  221.7 9.1 %convolution_convert_fusion.k_ref.v_ref = bf16[2048,1536]{1,0:T(8,128)(2,1)} fusion(bf16[2048,768]{1,0:T(8,128)(2,1)S(1)} %copy-done.3, bf16[768,3072]{1,0:T(8,128)(2,1)} %all-gather.6.cloned.1.call-done), kind=kOutput, calls=%fused_computation.4 | convolution fusion | flops 4834983936 | bytes 11796480 | tf_op jit(solution)/shard_map/dot_general | solution.py:41
  230.7 22.2 %attend_forward.3 = (bf16[512,768]{1,0:T(8,128)(2,1)}, f32[8,1,768]{2,1,0:T(1,128)}) custom-call(s32[8,16]{1,0:T(8,128)} %select_reduce_fusion.keys_at, s32[8]{0:T(128)} %get-tuple-element.190.steps_of, bf16[512,768]{1,0:T(8,128)(2,1)} %multiply_convert_fusion.2.q_ref, bf16[2048,1536]{1,0:T(8,128)(2,1)} %convolution_convert_fusion.k_ref.v_ref, ...), custom_call_target="tpu_custom_call" | custom-call | flops 1000000 | bytes 1000000 | tf_op jit(solution)/shard_map/attend_forward/pallas_call | solution.py:695
  252.9 2.4 fusion.94
  255.7 0.8 copy-done.1
  256.5 1.2 fusion.50.ffn_ref
  257.8 14.1 %all-gather.8.cloned.1.call-done = bf16[768,6144]{1,0:T(8,128)(2,1)} async-done(((bf16[96,6144]{1,0:T(8,128)(2,1)}), bf16[768,6144]{1,0:T(8,128)(2,1)}) %all-gather.8.cloned.1.call-update) | async-done | bytes 9437200 | tf_op jit(solution)/shard_map/all_gather | solution.py:896
  271.9 5.8 multiply_convert_fusion
  277.7 2.8 fusion.95
  280.9 1.8 fusion.37
  282.7 2.8 fusion.87
  285.6 0.9 copy-done.9
  286.5 6.5 fusion.13.pre_ref
  293.0 3.2 multiply_reduce_fusion.1
  296.9 1.1 copy-done
  298.0 1.0 add_convert_fusion.4.one_ref
  299.1 13.6 %weight_grads.2 = bf16[768,6912]{1,0:T(8,128)(2,1)} custom-call(bf16[512,768]{1,0:T(8,128)(2,1)} %fusion.50.ffn_ref, bf16[512,768]{1,0:T(8,128)(2,1)} %copy-done.9, bf16[512,768]{1,0:T(8,128)(2,1)} %add_convert_fusion.4.one_ref, bf16[512,3072]{1,0:T(8,128)(2,1)} %copy-done.14, bf16[512,3072]{1,0:T(8,128)(2,1)} %copy-done.13, ...), custom_call_target="tpu_custom_call" | custom-call | flops 1000000 | bytes 1000000 | tf_op jit(solution)/shard_map/weight_grads/pallas_call | solution.py:786
  312.7 7.6 %collective-permute-start.3 = (bf16[512,768]{1,0:T(8,128)(2,1)}, bf16[512,768]{1,0:T(8,128)(2,1)}, u32[]{:S(2)}, u32[]{:S(2)}) collective-permute-start(bf16[512,768]{1,0:T(8,128)(2,1)} %get-tuple-element.170), channel_id=1, source_target_pairs={{0,0},{4,1},{8,2},{12,3},{3,4},{7,5},{11,6},{15,7},{1,8},{5,9},{9,... | collective-permute-start | bytes 2359304 | tf_op jit(solution)/shard_map/ppermute | solution.py:971
  320.4 3.9 slice.184.wk_ref.wv_ref
  324.3 3.2 convolution_convert_fusion.3.d_ref
  327.4 45.4 %attend_backward.2 = (bf16[512,768]{1,0:T(8,128)(2,1)}, bf16[2048,768]{1,0:T(8,128)(2,1)}, bf16[768,2304]{1,0:T(8,128)(2,1)}) custom-call(s32[8,16]{1,0:T(8,128)} %select_reduce_fusion.keys_at, s32[8]{0:T(128)} %get-tuple-element.190.steps_of, bf16[512,768]{1,0:T(8,128)(2,1)} %multiply_convert_fusion.2.q_ref, ...), custom_call_target="tpu_custom_call" | custom-call | flops 1000000 | bytes 1000000 | tf_op jit(solution)/shard_map/attend_backward/pallas_call | solution.py:727
  372.8 42.2 %quad_reduce.1 = f32[512,768]{1,0:T(8,128)} custom-call(bf16[2048,768]{1,0:T(8,128)(2,1)} %get-tuple-element.77.parts_ref), custom_call_target="tpu_custom_call" | custom-call | flops 1000000 | bytes 1000000 | tf_op jit(solution)/shard_map/quad_reduce/pallas_call | solution.py:416
  415.1 3.7 multiply_reduce_fusion
  419.6 0.9 copy-done.10
  420.5 9.9 %fusion.6.pre_ref = bf16[512,3072]{1,0:T(8,128)(2,1)S(1)} fusion(f32[512,3072]{1,0:T(8,128)} %get-tuple-element.194, bf16[512,768]{1,0:T(8,128)(2,1)S(1)} %add_convert_fusion.3.two_ref, bf16[768,6144]{1,0:T(8,128)(2,1)} %all-gather.4.cloned.1.call-done), kind=kOutput, calls=%fused_computation.12 | convolution fusion | flops 2447376384 | bytes 14942208 | tf_op jit(solution)/shard_map/dot_general | solution.py:41
  430.5 3.2 multiply_reduce_fusion.2
  434.3 1.0 add_convert_fusion.2.one_ref
  435.4 14.1 %weight_grads.3 = bf16[768,6912]{1,0:T(8,128)(2,1)} custom-call(bf16[512,768]{1,0:T(8,128)(2,1)} %copy-done.7, bf16[512,768]{1,0:T(8,128)(2,1)} %copy-done.10, bf16[512,768]{1,0:T(8,128)(2,1)} %add_convert_fusion.2.one_ref, bf16[512,3072]{1,0:T(8,128)(2,1)} %copy-done.15, bf16[512,3072]{1,0:T(8,128)(2,1)} %copy-done.12, ...), custom_call_target="tpu_custom_call" | custom-call | flops 1000000 | bytes 1000000 | tf_op jit(solution)/shard_map/weight_grads/pallas_call | solution.py:786
  449.6 3.3 slice.178.wk_ref.wv_ref
  453.6 3.2 convolution_convert_fusion.2.d_ref
  456.7 11.9 %sum_everywhere.1 = f32[8,768]{1,0:T(8,128)} custom-call(f32[8,768]{1,0:T(8,128)} %stack.36.x_ref), custom_call_target="tpu_custom_call" | custom-call | flops 1000000 | bytes 1000000 | tf_op jit(solution)/shard_map/sum_everywhere/pallas_call | solution.py:493
  468.7 45.4 %attend_backward.3 = (bf16[512,768]{1,0:T(8,128)(2,1)}, bf16[2048,768]{1,0:T(8,128)(2,1)}, bf16[768,2304]{1,0:T(8,128)(2,1)}) custom-call(s32[8,16]{1,0:T(8,128)} %select_reduce_fusion.keys_at, s32[8]{0:T(128)} %get-tuple-element.190.steps_of, bf16[512,768]{1,0:T(8,128)(2,1)} %multiply_convert_fusion.3.q_ref, ...), custom_call_target="tpu_custom_call" | custom-call | flops 1000000 | bytes 1000000 | tf_op jit(solution)/shard_map/attend_backward/pallas_call | solution.py:727
  514.1 38.0 %sum_line.2 = f32[96,1728]{1,0:T(8,128)} custom-call(bf16[96,6912]{1,0:T(8,128)(2,1)} %reduce-scatter.5.cloned.1.call-done.x_ref), custom_call_target="tpu_custom_call" | custom-call | flops 1000000 | bytes 1000000 | tf_op jit(solution)/shard_map/sum_line/pallas_call | solution.py:677
  552.1 1.0 copy-done.19
  553.5 1.3 reshape.671.refs_1_
  554.8 48.0 %quad_reduce_and_lines.1 = (f32[512,768]{1,0:T(8,128)}, f32[96,1728]{1,0:T(8,128)}, f32[96,576]{1,0:T(8,128)}) custom-call(bf16[2048,768]{1,0:T(8,128)(2,1)} %get-tuple-element.94.parts_ref, bf16[96,6912]{1,0:T(8,128)(2,1)} %reduce-scatter.9.cloned.1.call-done.refs_0_, bf16[96,2304]{1,0:T(8,128)(2,1)} %reshape.671.refs_1_), custom_call_target="tpu_custom_call" | custom-call | flops 1000000 | bytes 1000000 | tf_op jit(solution)/shard_map/quad_reduce_and_lines/pallas_call | solution.py:446
  602.8 3.9 add_convert_fusion
  606.7 1.8 collective-permute-start.4
  609.1 0.8 copy.68
  609.9 1.1 fusion.62
  611.0 1.5 reshape.672
  612.9 1.3 reshape.673.x_ref
  614.1 39.2 %sum_line.3 = f32[96,576]{1,0:T(8,128)} custom-call(bf16[96,2304]{1,0:T(8,128)(2,1)} %reshape.673.x_ref), custom_call_target="tpu_custom_call" | custom-call | flops 1000000 | bytes 1000000 | tf_op jit(solution)/shard_map/sum_line/pallas_call | solution.py:677
  653.4 1.3 convert_element_type.132
  655.1 1.0 copy.67
  656.1 2.1 copy.76
  (184 shorter events, 18.6 us)
Async XLA Ops:
  7.2 6.7 %copy-start.20 = (bf16[2,96,768]{2,1,0:T(8,128)(2,1)S(1)}, bf16[2,96,768]{2,1,0:T(8,128)(2,1)}, u32[]{:S(2)}) copy-start(bf16[2,96,768]{2,1,0:T(8,128)(2,1)} %param.16) | copy-start | bytes 884740
  7.2 7.4 %copy-start.21 = (bf16[2,768,96]{1,2,0:T(8,128)(2,1)S(1)}, bf16[2,768,96]{1,2,0:T(8,128)(2,1)}, u32[]{:S(2)}) copy-start(bf16[2,768,96]{1,2,0:T(8,128)(2,1)} %param.17) | copy-start | bytes 884740
  7.2 172.2 %all-gather.4.cloned.1.call-start = ((), (), s32[]{:S(2)}) async-start(), calls=%async_computation.4 | async-start | bytes 10616832 | tf_op jit(solution)/shard_map/all_gather | solution.py:896
  7.2 69.0 %collective-permute-start = (bf16[512,768]{1,0:T(8,128)(2,1)}, bf16[512,768]{1,0:T(8,128)(2,1)S(1)}, u32[]{:S(2)}, u32[]{:S(2)}) collective-permute-start(bf16[512,768]{1,0:T(8,128)(2,1)} %param.13), channel_id=1, source_target_pairs={{0,0},{1,4},{2,8},{3,12},{4,3},{5,7},{6,11},{7,15},{8,1},{9,5},{10... | collective-permute-start | bytes 2359304 | tf_op jit(solution)/shard_map/ppermute | solution.py:903
  10.9 65.3 %collective-permute-start.1 = (bf16[16,768]{1,0:T(8,128)(2,1)S(1)}, bf16[16,768]{1,0:T(8,128)(2,1)S(1)}, u32[]{:S(2)}, u32[]{:S(2)}) collective-permute-start(bf16[16,768]{1,0:T(8,128)(2,1)S(1)} %fusion.69), channel_id=1, source_target_pairs={{0,0},{1,4},{2,8},{3,12},{4,3},{5,7},{6,11},{7,15},{8,1},{9,5},{10... | collective-permute-start | bytes 73736 | tf_op jit(solution)/shard_map/ppermute | solution.py:902
  76.2 1.3 copy-start.24
  76.2 1.3 copy-start.5
  76.2 141.9 %all-gather.6.cloned.1.call-start = ((), (), s32[]{:S(2)}) async-start(), calls=%async_computation.5 | async-start | bytes 5308416 | tf_op jit(solution)/shard_map/all_gather | solution.py:896
  119.1 3.0 copy-start.25
  119.1 3.0 copy-start.26
  119.1 3.0 copy-start.27
  119.1 3.0 copy-start.28
  121.2 150.7 %all-gather.8.cloned.1.call-start = ((), (), s32[]{:S(2)}) async-start(), calls=%async_computation.6 | async-start | bytes 10616832 | tf_op jit(solution)/shard_map/all_gather | solution.py:896
  122.0 293.1 %reduce-scatter.5.cloned.1.call-start = ((), (), s32[]{:S(2)}) async-start(), calls=%async_computation.7 | async-start | bytes 11943936 | tf_op jit(solution)/shard_map/reduce_scatter | solution.py:978
  127.8 6.6 copy-start.6
  134.4 3.1 copy-start.16
  168.4 112.5 %collective-permute-start.2 = (bf16[512,768]{1,0:T(8,128)(2,1)}, bf16[512,768]{1,0:T(8,128)(2,1)}, u32[]{:S(2)}, u32[]{:S(2)}) collective-permute-start(bf16[512,768]{1,0:T(8,128)(2,1)} %param.22), channel_id=1, source_target_pairs={{0,0},{1,4},{2,8},{3,12},{4,3},{5,7},{6,11},{7,15},{8,1},{9,5},{10... | collective-permute-start | bytes 2359304 | tf_op jit(solution)/shard_map/ppermute | solution.py:960
  179.3 9.2 %copy-start.7 = (bf16[512,768]{1,0:T(8,128)(2,1)}, bf16[512,768]{1,0:T(8,128)(2,1)S(1)}, u32[]{:S(2)}) copy-start(bf16[512,768]{1,0:T(8,128)(2,1)S(1)} %fusion.48.ffn_ref) | copy-start | bytes 2359300
  179.4 9.1 %copy-start.29 = (bf16[768,6144]{1,0:T(8,128)(2,1)S(1)}, bf16[768,6144]{1,0:T(8,128)(2,1)}, u32[]{:S(2)}) copy-start(bf16[768,6144]{1,0:T(8,128)(2,1)} %all-gather.4.cloned.1.call-done) | copy-start | bytes 28311556
  188.5 2.8 copy-start.12
  218.2 3.5 copy-start.3
  255.4 1.1 copy-start.1
  271.9 5.8 copy-start.2
  271.9 5.8 copy-start.30
  277.7 2.8 copy-start.13
  285.6 0.9 copy-start.9
  293.0 3.2 copy-start.14
  296.9 1.1 copy-start
  312.7 156.0 %reduce-scatter.7.cloned.1.call-start = ((), (), s32[]{:S(2)}) async-start(), calls=%async_computation.8 | async-start | bytes 3981312 | tf_op jit(solution)/shard_map/reduce_scatter | solution.py:978
  312.7 11.5 %copy-start.11 = (bf16[512,768]{1,0:T(8,128)(2,1)S(1)}, bf16[512,768]{1,0:T(8,128)(2,1)}, u32[]{:S(2)}) copy-start(bf16[512,768]{1,0:T(8,128)(2,1)} %add_convert_fusion.4.one_ref) | copy-start | bytes 2359300
  312.7 60.1 %collective-permute-start.3 = (bf16[512,768]{1,0:T(8,128)(2,1)}, bf16[512,768]{1,0:T(8,128)(2,1)}, u32[]{:S(2)}, u32[]{:S(2)}) collective-permute-start(bf16[512,768]{1,0:T(8,128)(2,1)} %get-tuple-element.170), channel_id=1, source_target_pairs={{0,0},{4,1},{8,2},{12,3},{3,4},{7,5},{11,6},{15,7},{1,8},{5,9},{9,... | collective-permute-start | bytes 2359304 | tf_op jit(solution)/shard_map/ppermute | solution.py:971
  415.0 137.0 %reduce-scatter.9.cloned.1.call-start = ((), (), s32[]{:S(2)}) async-start(), calls=%async_computation.9 | async-start | bytes 11943936 | tf_op jit(solution)/shard_map/reduce_scatter | solution.py:978
  418.8 11.6 %slice-start = ((s8[9437184]{0:T(1024)(128)(4,1)}), s8[4194304]{0:T(1024)(128)(4,1)S(1)}, s32[]{:S(2)}) async-start(s8[9437184]{0:T(1024)(128)(4,1)} %bitcast.100), calls=%async_computation.11 | async-start | bytes 8388608
  419.6 0.9 copy-start.10
  420.5 9.9 %slice-start.1 = ((s8[9437184]{0:T(1024)(128)(4,1)}), s8[4194304]{0:T(1024)(128)(4,1)S(1)}, s32[]{:S(2)}) async-start(s8[9437184]{0:T(1024)(128)(4,1)} %bitcast.100), calls=%async_computation.12 | async-start | bytes 8388608
  420.5 10.0 %slice-start.2 = ((s8[9437184]{0:T(1024)(128)(4,1)}), s8[1048576]{0:T(1024)(128)(4,1)S(1)}, s32[]{:S(2)}) async-start(s8[9437184]{0:T(1024)(128)(4,1)} %bitcast.100), calls=%async_computation.13 | async-start | bytes 2097152
  430.5 3.2 copy-start.15
  449.5 4.1 copy-start.8
  449.5 161.5 %reduce-scatter.11.cloned.1.call-start = ((), (), s32[]{:S(2)}) async-start(), calls=%async_computation.10 | async-start | bytes 3981312 | tf_op jit(solution)/shard_map/reduce_scatter | solution.py:978
  552.0 1.0 copy-start.19
  602.8 5.7 copy-start.23
  602.8 6.3 copy-start.4
  602.8 6.3 copy-start.17
  606.7 46.7 %collective-permute-start.4 = (bf16[512,768]{1,0:T(8,128)(2,1)}, bf16[512,768]{1,0:T(8,128)(2,1)S(1)}, u32[]{:S(2)}, u32[]{:S(2)}) collective-permute-start(bf16[512,768]{1,0:T(8,128)(2,1)} %add_convert_fusion), channel_id=1, source_target_pairs={{0,0},{4,1},{8,2},{12,3},{3,4},{7,5},{11,6},{15,7},{1,8},{5,9},{9,... | collective-permute-start | bytes 2359304 | tf_op jit(solution)/shard_map/ppermute | solution.py:1038
  614.1 40.5 %copy-start.22 = (f32[96,576]{1,0:T(8,128)S(1)}, f32[96,576]{1,0:T(8,128)}, u32[]{:S(2)}) copy-start(f32[96,576]{1,0:T(8,128)} %get-tuple-element.102) | copy-start | bytes 663556
  653.4 1.4 copy-start.18
Sparse Core Ops, SparseCore 0:
  76.4 70.3 all-gather.3
  149.2 56.6 all-gather.5
  207.8 64.0 all-gather.7
  312.8 100.0 reduce-scatter.4
  416.2 46.0 reduce-scatter.6
  465.7 83.1 reduce-scatter.8
  552.3 52.0 reduce-scatter.10

commit v7 on v6

--- a/solution.py
+++ b/solution.py
@@ -717,7 +717,7 @@
     )(keys_at, steps_of, query, keyval, keyval, bias)
 
 
-def attend_backward(query, keyval, logs, d_mixed, tables, own_inputs, inputs, w_keyval):
+def attend_backward(query, keyval, logs, d_mixed, tables, own_inputs, inputs, attn_w):
     keys_at, steps_of, bias = tables
     own, width = query.shape
     quads = width // WIDE
@@ -738,8 +738,8 @@
                 pl.BlockSpec((own, WIDE), lambda i, *_: (0, i)),
                 pl.BlockSpec((own, depth), lambda i, *_: (0, 0), pipeline_mode=once),
                 pl.BlockSpec((rows, depth), lambda i, *_: (0, 0), pipeline_mode=once),
-                pl.BlockSpec((depth, WIDE), lambda i, *_: (0, i)),
                 pl.BlockSpec((depth, WIDE), lambda i, *_: (0, i + quads)),
+                pl.BlockSpec((depth, WIDE), lambda i, *_: (0, i + 2 * quads)),
             ],
             out_specs=[
                 pl.BlockSpec((own, WIDE), lambda i, *_: (0, i)),
@@ -760,7 +760,7 @@
         ],
         cost_estimate=SHORT,
         name="attend_backward",
-    )(keys_at, steps_of, query, keyval, keyval, bias, logs, d_mixed, own_inputs, inputs, w_keyval, w_keyval)
+    )(keys_at, steps_of, query, keyval, keyval, bias, logs, d_mixed, own_inputs, inputs, attn_w, attn_w)
 
 
 def weights_kernel(steps, ffn_ref, two_ref, one_ref, pre_ref, act_ref, mixed_ref, out_ref, left):
@@ -969,6 +969,14 @@
         )
         stream = layer_norm(summed_two, ffn_gain[layer], ffn_shift[layer])
     layer_output = lax.ppermute(stream.astype(BF), EVERY, moves_back)
+
+    def line_parts(rows, sizes):
+        pieces, start = [], 0
+        for size in sizes:
+            pieces.append(rows[:, start : start + tensor * size].reshape(depth, tensor, size))
+            start += tensor * size
+        parts = [jnp.concatenate([p[:, by] for p in pieces], axis=1) for by in range(tensor)]
+        return parts[:1] + [shifted(parts[by], tensor - by) for by in range(1, tensor)]
 
     def by_piece(rows):
         rows = rows.reshape(depth, -1, 3, WIDE).transpose(0, 2, 1, 3)
@@ -1011,23 +1019,24 @@
             d_mixed, norm_sums, attn_sums[layer + 1] = lax.optimization_barrier(
                 (d_mixed, norm_sums, attn_sums[layer + 1])
             )
+        if layer == 0:
+            d_mixed, ffn_last = lax.optimization_barrier((d_mixed, ffn_last))
+            moving = line_parts(ffn_last, (hidden, hidden, chunk))
         d_query, others, attn_part = attend_backward(
-            query, keyval, logs, d_mixed, tables, own_inputs, inputs, w_keyval
+            query, keyval, logs, d_mixed, tables, own_inputs, inputs, attn_w
         )
         if layer == 0:
-            others, ffn_last = lax.optimization_barrier((others, ffn_last))
-            ffn_grads[1] = sum_line(ffn_last, (hidden, hidden, chunk), tensor, CALL_LINE_FFN)
-            others, ffn_sum, attn_part, ffn_grads[1] = lax.optimization_barrier(
-                (others, ffn_sum, attn_part, ffn_grads[1])
+            others, attn_sums[1] = lax.optimization_barrier((others, attn_sums[1]))
+            attn_grads[1] = sum_line(by_piece(attn_sums[1]), (chunk,) * 3, tensor, CALL_LINE_ATTN)
+            others, ffn_sum, attn_part, attn_grads[1], moving = lax.optimization_barrier(
+                (others, ffn_sum, attn_part, attn_grads[1], moving)
             )
+            ffn_grads[1] = sum(part.astype(F32) for part in moving)
         else:
             others, layer_output = lax.optimization_barrier((others, layer_output))
         if layer == 0:
-            summed, ffn_grads[0], attn_grads[1] = quad_reduce_and_lines(
-                others,
-                [ffn_sum, by_piece(attn_sums[1])],
-                [(hidden, hidden, chunk), (chunk,) * 3],
-                tensor,
+            summed, ffn_grads[0] = quad_reduce_and_lines(
+                others, [ffn_sum], [(hidden, hidden, chunk)], tensor
             )
         else:
             summed = quad_reduce(others)

time: 677 us -> 667 us (0.985)
  Pallas kernels: 477 us -> 462 us
    pallas_call x2, Pallas kernels: 77.2 us -> 49.1 us  [sum_line(): pl.pallas_call(functools.partial(parts_kernel, sizes, parts), out_shape=j...]
    pallas_call x2, Pallas kernels: 90.7 us -> 106 us  [attend_backward(): pl.pallas_call(backward_kernel, grid_spec=pltpu.PrefetchScalarGridSpec(nu...]
    pallas_call x2, Pallas kernels: 44.4 us -> 56.6 us  [attend_forward(): pl.pallas_call(forward_kernel, grid_spec=pltpu.PrefetchScalarGridSpec(num...]
    pallas_call x1, Pallas kernels: 48 us -> 37.8 us  [quad_reduce_and_lines(): pl.pallas_call(functools.partial(both_kernel, tuple(sizes), planes), out_...]
  transfers between devices with their start and end apart: 12 -> 15, of which waited for: 1 -> 3; matrix products, arithmetic and copies ran while one was open for 17% -> 17% of each run, Pallas kernels for 70% -> 68%
where the time goes in v7:
time: 667 us; the launch traced here: 657 us
  Pallas kernels  462 us (69%)
  matrix products  84.1 us (13%)
  local copies, waits for them, and re-layouts  28.6 us (4%)
  other arithmetic  27.7 us (4%)
  starting transfers between devices  24.5 us (4%)
  between operations  15.5 us (2%)
  waiting for transfers between devices  15.1 us (2%)
    pallas_call x2, Pallas kernels, attend_backward(): pl.pallas_call(backward_kernel, grid_spec=pltpu.PrefetchScalarGridSpec(nu...  106 us
    pallas_call x1, Pallas kernels, gather_rows(): pl.pallas_call(functools.partial(rows_kernel, parts, tuple((len(g) for g...  65.6 us
    dot_general x10, matrix products, dot(): return jnp.dot(left, right, preferred_element_type=F32)  61.1 us
    pallas_call x2, Pallas kernels, quad_gather(): pl.pallas_call(functools.partial(gather_kernel, pieces, parts, tuple((len...  61.1 us
    pallas_call x2, Pallas kernels, attend_forward(): pl.pallas_call(forward_kernel, grid_spec=pltpu.PrefetchScalarGridSpec(num...  56.6 us
    pallas_call x2, Pallas kernels, sum_line(): pl.pallas_call(functools.partial(parts_kernel, sizes, parts), out_shape=j...  49.1 us
    pallas_call x1, Pallas kernels, quad_reduce_and_lines(): pl.pallas_call(functools.partial(both_kernel, tuple(sizes), planes), out_...  37.8 us
    pallas_call x1, Pallas kernels, quad_reduce(): pl.pallas_call(reduce_kernel, out_shape=jax.ShapeDtypeStruct((rows, width...  37.7 us
  transfers between devices with their start and end apart: 15, of which 3 were waited for; matrix products, arithmetic and copies ran while one was open for 17% of the time, Pallas kernels for 68%

profile of v7, /device:TPU:0, one launch (start us, length us, event | category | flops | bytes accessed | tf_op | source)
XLA Modules:
  0.0 657.0 jit_solution(4796751040297210384)
XLA Ops:
  9.7 1.8 collective-permute-start
  12.4 1.0 fusion.92
  16.0 65.6 %gather_rows.1 = (bf16[768,3072]{1,0:T(8,128)(2,1)}, bf16[96,6144]{1,0:T(8,128)(2,1)}) custom-call(bf16[96,768]{1,0:T(8,128)(2,1)} %pad_maximum_fusion.6.own_ref, bf16[96,768]{1,0:T(8,128)(2,1)} %get-tuple-element.196.refs_0_, bf16[96,768]{1,0:T(8,128)(2,1)} %get-tuple-element.194.refs_1_), custom_call_target="tpu_custom_call" | custom-call | flops 1000000 | bytes 1000000 | tf_op jit(solution)/shard_map/gather_rows/pallas_call | solution.py:593
  82.8 41.1 %quad_gather.2 = (bf16[2048,768]{1,0:T(8,128)(2,1)}, bf16[64,768]{1,0:T(8,128)(2,1)}, bf16[96,3072]{1,0:T(8,128)(2,1)}, bf16[96,6144]{1,0:T(8,128)(2,1)}) custom-call(bf16[512,768]{1,0:T(8,128)(2,1)} %copy-done.4, bf16[16,768]{1,0:T(8,128)(2,1)} %copy-done.22, bf16[96,768]{1,0:T(8,128)(2,1)} %pad_maximum_fusion.7.refs_2_, ...), custom_call_target="tpu_custom_call" | custom-call | flops 1000000 | bytes 1000000 | tf_op jit(solution)/shard_map/quad_gather/pallas_call | solution.py:332
  124.0 2.1 regroup.3
  131.7 1.0 reshape.670.bias_ref
  132.7 5.5 regroup.2.wk_ref.wv_ref
  138.4 0.9 select_reduce_fusion.keys_at
  139.3 3.1 multiply_convert_fusion.3.q_ref
  142.4 8.6 %convolution_convert_fusion.1.k_ref.v_ref = bf16[2048,1536]{1,0:T(8,128)(2,1)} fusion(bf16[2048,768]{1,0:T(8,128)(2,1)S(1)} %copy-done.14, bf16[768,3072]{1,0:T(8,128)(2,1)} %regroup.2.wk_ref.wv_ref), kind=kOutput, calls=%fused_computation.5 | convolution fusion | flops 4834983936 | bytes 11796480 | tf_op jit(solution)/shard_map/dot_general | solution.py:41
  151.0 28.3 %attend_forward.2 = (bf16[512,768]{1,0:T(8,128)(2,1)}, f32[8,1,768]{2,1,0:T(1,128)}) custom-call(s32[8,16]{1,0:T(8,128)} %select_reduce_fusion.keys_at, s32[8]{0:T(128)} %get-tuple-element.214.steps_of, bf16[512,768]{1,0:T(8,128)(2,1)} %multiply_convert_fusion.3.q_ref, bf16[2048,1536]{1,0:T(8,128)(2,1)} %convolution_convert_fusion.1.k_ref.v_ref, ...), custom_call_target="tpu_custom_call" | custom-call | flops 1000000 | bytes 1000000 | tf_op jit(solution)/shard_map/attend_forward/pallas_call | solution.py:695
  179.3 7.6 %collective-permute-start.2 = (bf16[512,768]{1,0:T(8,128)(2,1)}, bf16[512,768]{1,0:T(8,128)(2,1)}, u32[]{:S(2)}, u32[]{:S(2)}) collective-permute-start(bf16[512,768]{1,0:T(8,128)(2,1)} %param.22), channel_id=1, source_target_pairs={{0,0},{1,4},{2,8},{3,12},{4,3},{5,7},{6,11},{7,15},{8,1},{9,5},{10... | collective-permute-start | bytes 2359304 | tf_op jit(solution)/shard_map/ppermute | solution.py:960
  186.9 2.4 fusion.97
  190.0 9.1 %multiply_convert_fusion.1 = (bf16[512,3072]{1,0:T(8,128)(2,1)S(1)}, f32[512,3072]{1,0:T(8,128)}) fusion(bf16[512,768]{1,0:T(8,128)(2,1)S(1)} %fusion.50.ffn_ref, bf16[768,6144]{1,0:T(8,128)(2,1)} %all-gather.4.cloned.1.call-done), kind=kOutput, calls=%fused_computation.21 | convolution fusion | flops 2430074880 | bytes 14942208 | tf_op jit(solution)/shard_map/dot_general | solution.py:41
  199.1 2.8 fusion.98
  202.2 1.2 fusion.51.refs_0_.own_ref
  203.4 20.0 %quad_gather.3.in_ref = bf16[2048,768]{1,0:T(8,128)(2,1)} custom-call(bf16[512,768]{1,0:T(8,128)(2,1)} %fusion.51.refs_0_.own_ref), custom_call_target="tpu_custom_call" | custom-call | flops 1000000 | bytes 1000000 | tf_op jit(solution)/shard_map/quad_gather/pallas_call | solution.py:332
  223.4 3.3 multiply_convert_fusion.2.q_ref
  226.8 8.9 %convolution_convert_fusion.k_ref.v_ref = bf16[2048,1536]{1,0:T(8,128)(2,1)} fusion(bf16[2048,768]{1,0:T(8,128)(2,1)S(1)} %copy-done.3, bf16[768,3072]{1,0:T(8,128)(2,1)} %all-gather.6.cloned.1.call-done.wk_ref.wv_ref), kind=kOutput, calls=%fused_computation.4 | convolution fusion | flops 4834983936 | bytes 11796480 | tf_op jit(solution)/shard_map/dot_general | solution.py:41
  235.7 28.3 %attend_forward.3 = (bf16[512,768]{1,0:T(8,128)(2,1)}, f32[8,1,768]{2,1,0:T(1,128)}) custom-call(s32[8,16]{1,0:T(8,128)} %select_reduce_fusion.keys_at, s32[8]{0:T(128)} %get-tuple-element.214.steps_of, bf16[512,768]{1,0:T(8,128)(2,1)} %multiply_convert_fusion.2.q_ref, bf16[2048,1536]{1,0:T(8,128)(2,1)} %convolution_convert_fusion.k_ref.v_ref, ...), custom_call_target="tpu_custom_call" | custom-call | flops 1000000 | bytes 1000000 | tf_op jit(solution)/shard_map/attend_forward/pallas_call | solution.py:695
  264.0 2.6 fusion.99
  267.7 1.2 fusion.52.ffn_ref
  268.9 9.2 %all-gather.8.cloned.1.call-done = bf16[768,6144]{1,0:T(8,128)(2,1)} async-done(((bf16[96,6144]{1,0:T(8,128)(2,1)}), bf16[768,6144]{1,0:T(8,128)(2,1)}) %all-gather.8.cloned.1.call-update) | async-done | bytes 9437200 | tf_op jit(solution)/shard_map/all_gather | solution.py:896
  278.1 5.8 multiply_convert_fusion
  283.9 2.8 fusion.100
  287.1 1.8 fusion.39
  288.9 2.8 fusion.88
  292.7 6.5 fusion.13.pre_ref
  299.3 3.2 multiply_reduce_fusion.1
  303.1 1.1 copy-done
  304.3 1.0 add_convert_fusion.4.one_ref
  305.3 13.6 %weight_grads.2 = bf16[768,6912]{1,0:T(8,128)(2,1)} custom-call(bf16[512,768]{1,0:T(8,128)(2,1)} %fusion.52.ffn_ref, bf16[512,768]{1,0:T(8,128)(2,1)} %copy-done.8, bf16[512,768]{1,0:T(8,128)(2,1)} %add_convert_fusion.4.one_ref, bf16[512,3072]{1,0:T(8,128)(2,1)} %copy-done.12, bf16[512,3072]{1,0:T(8,128)(2,1)} %copy-done.11, ...), custom_call_target="tpu_custom_call" | custom-call | flops 1000000 | bytes 1000000 | tf_op jit(solution)/shard_map/weight_grads/pallas_call | solution.py:786
  319.0 7.5 %collective-permute-start.3 = (bf16[512,768]{1,0:T(8,128)(2,1)}, bf16[512,768]{1,0:T(8,128)(2,1)}, u32[]{:S(2)}, u32[]{:S(2)}) collective-permute-start(bf16[512,768]{1,0:T(8,128)(2,1)} %get-tuple-element.180), channel_id=1, source_target_pairs={{0,0},{4,1},{8,2},{12,3},{3,4},{7,5},{11,6},{15,7},{1,8},{5,9},{9,... | collective-permute-start | bytes 2359304 | tf_op jit(solution)/shard_map/ppermute | solution.py:971
  326.4 3.5 convolution_convert_fusion.3.d_ref
  329.9 53.5 %attend_backward.2 = (bf16[512,768]{1,0:T(8,128)(2,1)}, bf16[2048,768]{1,0:T(8,128)(2,1)}, bf16[768,2304]{1,0:T(8,128)(2,1)}) custom-call(s32[8,16]{1,0:T(8,128)} %select_reduce_fusion.keys_at, s32[8]{0:T(128)} %get-tuple-element.214.steps_of, bf16[512,768]{1,0:T(8,128)(2,1)} %multiply_convert_fusion.2.q_ref, ...), custom_call_target="tpu_custom_call" | custom-call | flops 1000000 | bytes 1000000 | tf_op jit(solution)/shard_map/attend_backward/pallas_call | solution.py:727
  383.5 37.7 %quad_reduce.1 = f32[512,768]{1,0:T(8,128)} custom-call(bf16[2048,768]{1,0:T(8,128)(2,1)} %get-tuple-element.82.parts_ref), custom_call_target="tpu_custom_call" | custom-call | flops 1000000 | bytes 1000000 | tf_op jit(solution)/shard_map/quad_reduce/pallas_call | solution.py:416
  421.3 3.7 multiply_reduce_fusion
  425.9 0.9 copy-done.9
  426.8 9.4 %fusion.6.pre_ref = bf16[512,3072]{1,0:T(8,128)(2,1)S(1)} fusion(f32[512,3072]{1,0:T(8,128)} %get-tuple-element.218, bf16[512,768]{1,0:T(8,128)(2,1)S(1)} %add_convert_fusion.3.two_ref, bf16[768,6144]{1,0:T(8,128)(2,1)} %all-gather.4.cloned.1.call-done), kind=kOutput, calls=%fused_computation.12 | convolution fusion | flops 2447376384 | bytes 14942208 | tf_op jit(solution)/shard_map/dot_general | solution.py:41
  436.2 3.2 multiply_reduce_fusion.2
  440.0 1.0 add_convert_fusion.2.one_ref
  441.1 13.7 %weight_grads.3 = bf16[768,6912]{1,0:T(8,128)(2,1)} custom-call(bf16[512,768]{1,0:T(8,128)(2,1)} %copy-done.6, bf16[512,768]{1,0:T(8,128)(2,1)} %copy-done.9, bf16[512,768]{1,0:T(8,128)(2,1)} %add_convert_fusion.2.one_ref, bf16[512,3072]{1,0:T(8,128)(2,1)} %copy-done.13, bf16[512,3072]{1,0:T(8,128)(2,1)} %copy-done.10, ...), custom_call_target="tpu_custom_call" | custom-call | flops 1000000 | bytes 1000000 | tf_op jit(solution)/shard_map/weight_grads/pallas_call | solution.py:786
  455.9 2.9 convolution_convert_fusion.2.d_ref
  458.8 13.3 %sum_everywhere.1 = f32[8,768]{1,0:T(8,128)} custom-call(f32[8,768]{1,0:T(8,128)} %stack.36.x_ref), custom_call_target="tpu_custom_call" | custom-call | flops 1000000 | bytes 1000000 | tf_op jit(solution)/shard_map/sum_everywhere/pallas_call | solution.py:493
  472.1 1.4 fusion.89
  478.2 4.0 collective-permute-start.4
  484.5 52.0 %attend_backward.3 = (bf16[512,768]{1,0:T(8,128)(2,1)}, bf16[2048,768]{1,0:T(8,128)(2,1)}, bf16[768,2304]{1,0:T(8,128)(2,1)}) custom-call(s32[8,16]{1,0:T(8,128)} %select_reduce_fusion.keys_at, s32[8]{0:T(128)} %get-tuple-element.214.steps_of, bf16[512,768]{1,0:T(8,128)(2,1)} %multiply_convert_fusion.3.q_ref, ...), custom_call_target="tpu_custom_call" | custom-call | flops 1000000 | bytes 1000000 | tf_op jit(solution)/shard_map/attend_backward/pallas_call | solution.py:727
  537.0 1.3 reshape.680.x_ref
  538.3 12.1 %sum_line.2 = f32[96,576]{1,0:T(8,128)} custom-call(bf16[96,2304]{1,0:T(8,128)(2,1)} %reshape.680.x_ref), custom_call_target="tpu_custom_call" | custom-call | flops 1000000 | bytes 1000000 | tf_op jit(solution)/shard_map/sum_line/pallas_call | solution.py:677
  550.5 2.1 reduce-scatter.9.cloned.1.call-done.refs_0_
  552.7 2.3 fusion.62
  555.0 37.8 %quad_reduce_and_lines.1 = (f32[512,768]{1,0:T(8,128)}, f32[96,1728]{1,0:T(8,128)}) custom-call(bf16[2048,768]{1,0:T(8,128)(2,1)} %get-tuple-element.102.parts_ref, bf16[96,6912]{1,0:T(8,128)(2,1)} %reduce-scatter.9.cloned.1.call-done.refs_0_), custom_call_target="tpu_custom_call" | custom-call | flops 1000000 | bytes 1000000 | tf_op jit(solution)/shard_map/quad_reduce_and_lines/pallas_call | solution.py:446
  592.7 2.6 add_convert_fusion
  595.3 1.9 collective-permute-start.7
  597.8 1.3 add_bitcast_fusion
  600.0 1.1 fusion.65
  601.1 2.9 reduce-scatter.11.cloned.1.call-done
  604.1 1.5 reshape.684
  605.9 1.3 reshape.685.x_ref
  607.2 37.0 %sum_line.3 = f32[96,576]{1,0:T(8,128)} custom-call(bf16[96,2304]{1,0:T(8,128)(2,1)} %reshape.685.x_ref), custom_call_target="tpu_custom_call" | custom-call | flops 1000000 | bytes 1000000 | tf_op jit(solution)/shard_map/sum_line/pallas_call | solution.py:677
  644.2 1.1 copy.88
  645.6 1.0 copy.91
  646.6 1.3 convert_element_type.144
  647.8 2.1 copy.136
  (211 shorter events, 29.0 us)
Async XLA Ops:
  7.2 6.6 %copy-start.18 = (bf16[2,96,768]{2,1,0:T(8,128)(2,1)S(1)}, bf16[2,96,768]{2,1,0:T(8,128)(2,1)}, u32[]{:S(2)}) copy-start(bf16[2,96,768]{2,1,0:T(8,128)(2,1)} %param.16) | copy-start | bytes 884740
  7.2 7.3 %copy-start.19 = (bf16[2,768,96]{1,2,0:T(8,128)(2,1)S(1)}, bf16[2,768,96]{1,2,0:T(8,128)(2,1)}, u32[]{:S(2)}) copy-start(bf16[2,768,96]{1,2,0:T(8,128)(2,1)} %param.17) | copy-start | bytes 884740
  7.2 182.8 %all-gather.4.cloned.1.call-start = ((), (), s32[]{:S(2)}) async-start(), calls=%async_computation.4 | async-start | bytes 10616832 | tf_op jit(solution)/shard_map/all_gather | solution.py:896
  9.0 72.5 %collective-permute-start.1 = (bf16[16,768]{1,0:T(8,128)(2,1)S(1)}, bf16[16,768]{1,0:T(8,128)(2,1)S(1)}, u32[]{:S(2)}, u32[]{:S(2)}) collective-permute-start(bf16[16,768]{1,0:T(8,128)(2,1)S(1)} %fusion.72), channel_id=1, source_target_pairs={{0,0},{1,4},{2,8},{3,12},{4,3},{5,7},{6,11},{7,15},{8,1},{9,5},{10... | collective-permute-start | bytes 73736 | tf_op jit(solution)/shard_map/ppermute | solution.py:902
  9.7 71.9 %collective-permute-start = (bf16[512,768]{1,0:T(8,128)(2,1)}, bf16[512,768]{1,0:T(8,128)(2,1)S(1)}, u32[]{:S(2)}, u32[]{:S(2)}) collective-permute-start(bf16[512,768]{1,0:T(8,128)(2,1)} %param.13), channel_id=1, source_target_pairs={{0,0},{1,4},{2,8},{3,12},{4,3},{5,7},{6,11},{7,15},{8,1},{9,5},{10... | collective-permute-start | bytes 2359304 | tf_op jit(solution)/shard_map/ppermute | solution.py:903
  81.6 1.3 copy-start.22
  81.6 1.3 copy-start.4
  81.6 141.8 %all-gather.6.cloned.1.call-start = ((), (), s32[]{:S(2)}) async-start(), calls=%async_computation.5 | async-start | bytes 5308416 | tf_op jit(solution)/shard_map/all_gather | solution.py:896
  124.0 3.0 copy-start.23
  124.0 3.0 copy-start.24
  124.0 3.0 copy-start.25
  124.0 3.0 copy-start.26
  126.1 152.0 %all-gather.8.cloned.1.call-start = ((), (), s32[]{:S(2)}) async-start(), calls=%async_computation.6 | async-start | bytes 10616832 | tf_op jit(solution)/shard_map/all_gather | solution.py:896
  126.9 294.4 %reduce-scatter.5.cloned.1.call-start = ((), (), s32[]{:S(2)}) async-start(), calls=%async_computation.7 | async-start | bytes 11943936 | tf_op jit(solution)/shard_map/reduce_scatter | solution.py:986
  132.7 6.6 %copy-start.5 = (bf16[512,768]{1,0:T(8,128)(2,1)S(1)}, bf16[512,768]{1,0:T(8,128)(2,1)}, u32[]{:S(2)}) copy-start(bf16[512,768]{1,0:T(8,128)(2,1)} %copy-done.4) | copy-start | bytes 2359300
  139.3 3.1 copy-start.14
  179.3 107.8 %collective-permute-start.2 = (bf16[512,768]{1,0:T(8,128)(2,1)}, bf16[512,768]{1,0:T(8,128)(2,1)}, u32[]{:S(2)}, u32[]{:S(2)}) collective-permute-start(bf16[512,768]{1,0:T(8,128)(2,1)} %param.22), channel_id=1, source_target_pairs={{0,0},{1,4},{2,8},{3,12},{4,3},{5,7},{6,11},{7,15},{8,1},{9,5},{10... | collective-permute-start | bytes 2359304 | tf_op jit(solution)/shard_map/ppermute | solution.py:960
  190.0 9.1 %copy-start.6 = (bf16[512,768]{1,0:T(8,128)(2,1)}, bf16[512,768]{1,0:T(8,128)(2,1)S(1)}, u32[]{:S(2)}) copy-start(bf16[512,768]{1,0:T(8,128)(2,1)S(1)} %fusion.50.ffn_ref) | copy-start | bytes 2359300
  190.0 9.1 %copy-start.27 = (bf16[768,6144]{1,0:T(8,128)(2,1)S(1)}, bf16[768,6144]{1,0:T(8,128)(2,1)}, u32[]{:S(2)}) copy-start(bf16[768,6144]{1,0:T(8,128)(2,1)} %all-gather.4.cloned.1.call-done) | copy-start | bytes 28311556
  199.1 2.8 copy-start.10
  223.4 3.3 copy-start.3
  266.6 1.1 copy-start.1
  278.1 5.8 copy-start.2
  278.1 5.8 copy-start.28
  283.9 2.8 copy-start.11
  291.8 0.9 copy-start.8
  299.3 3.2 copy-start.12
  303.1 1.1 copy-start
  318.9 153.2 %reduce-scatter.7.cloned.1.call-start = ((), (), s32[]{:S(2)}) async-start(), calls=%async_computation.8 | async-start | bytes 3981312 | tf_op jit(solution)/shard_map/reduce_scatter | solution.py:986
  319.0 64.5 %collective-permute-start.3 = (bf16[512,768]{1,0:T(8,128)(2,1)}, bf16[512,768]{1,0:T(8,128)(2,1)}, u32[]{:S(2)}, u32[]{:S(2)}) collective-permute-start(bf16[512,768]{1,0:T(8,128)(2,1)} %get-tuple-element.180), channel_id=1, source_target_pairs={{0,0},{4,1},{8,2},{12,3},{3,4},{7,5},{11,6},{15,7},{1,8},{5,9},{9,... | collective-permute-start | bytes 2359304 | tf_op jit(solution)/shard_map/ppermute | solution.py:971
  421.3 131.4 %reduce-scatter.9.cloned.1.call-start = ((), (), s32[]{:S(2)}) async-start(), calls=%async_computation.9 | async-start | bytes 11943936 | tf_op jit(solution)/shard_map/reduce_scatter | solution.py:986
  425.0 11.1 %slice-start.1 = ((s8[9437184]{0:T(1024)(128)(4,1)}), s8[4194304]{0:T(1024)(128)(4,1)S(1)}, s32[]{:S(2)}) async-start(s8[9437184]{0:T(1024)(128)(4,1)} %bitcast.147), calls=%async_computation.12 | async-start | bytes 8388608
  425.9 0.9 copy-start.9
  426.8 9.4 %slice-start.2 = ((s8[9437184]{0:T(1024)(128)(4,1)}), s8[4194304]{0:T(1024)(128)(4,1)S(1)}, s32[]{:S(2)}) async-start(s8[9437184]{0:T(1024)(128)(4,1)} %bitcast.147), calls=%async_computation.13 | async-start | bytes 8388608
  426.8 9.4 %slice-start.3 = ((s8[9437184]{0:T(1024)(128)(4,1)}), s8[1048576]{0:T(1024)(128)(4,1)S(1)}, s32[]{:S(2)}) async-start(s8[9437184]{0:T(1024)(128)(4,1)} %bitcast.147), calls=%async_computation.14 | async-start | bytes 2097152
  436.2 3.2 copy-start.13
  454.8 1.1 copy-start.7
  454.8 149.3 %reduce-scatter.11.cloned.1.call-start = ((), (), s32[]{:S(2)}) async-start(), calls=%async_computation.10 | async-start | bytes 3981312 | tf_op jit(solution)/shard_map/reduce_scatter | solution.py:986
  472.1 1.8 slice-start
  476.5 1.0 copy-start.20
  478.2 72.3 %collective-permute-start.4 = (bf16[96,1728]{1,0:T(8,128)(2,1)}, bf16[96,1728]{1,0:T(8,128)(2,1)}, u32[]{:S(2)}, u32[]{:S(2)}) collective-permute-start(bf16[96,1728]{1,0:T(8,128)(2,1)} %pad_maximum_fusion.3), channel_id=1, source_target_pairs={{0,3},{1,0},{2,1},{3,2},{4,7},{5,4},{6,5},{7,6},{8,11},{9,8},{10,9... | collective-permute-start | bytes 995336 | tf_op jit(solution)/shard_map/ppermute | solution.py:882
  483.0 67.5 %collective-permute-start.5 = (bf16[96,1728]{1,0:T(8,128)(2,1)}, bf16[96,1728]{1,0:T(8,128)(2,1)}, u32[]{:S(2)}, u32[]{:S(2)}) collective-permute-start(bf16[96,1728]{1,0:T(8,128)(2,1)} %pad_maximum_fusion.4), channel_id=1, source_target_pairs={{0,2},{1,3},{2,0},{3,1},{4,6},{5,7},{6,4},{7,5},{8,10},{9,11},{10,... | collective-permute-start | bytes 995336 | tf_op jit(solution)/shard_map/ppermute | solution.py:882
  483.7 66.8 %collective-permute-start.6 = (bf16[96,1728]{1,0:T(8,128)(2,1)}, bf16[96,1728]{1,0:T(8,128)(2,1)}, u32[]{:S(2)}, u32[]{:S(2)}) collective-permute-start(bf16[96,1728]{1,0:T(8,128)(2,1)} %pad_maximum_fusion.5), channel_id=1, source_target_pairs={{0,1},{1,2},{2,3},{3,0},{4,5},{5,6},{6,7},{7,4},{8,9},{9,10},{10,1... | collective-permute-start | bytes 995336 | tf_op jit(solution)/shard_map/ppermute | solution.py:882
  484.5 52.1 %copy-start.17 = (bf16[96,2304]{1,0:T(8,128)(2,1)S(1)}, bf16[96,2304]{1,0:T(8,128)(2,1)}, u32[]{:S(2)}) copy-start(bf16[96,2304]{1,0:T(8,128)(2,1)} %reduce-scatter.7.cloned.1.call-done) | copy-start | bytes 1327108
  592.7 4.5 copy-start.21
  595.3 3.9 copy-start.15
  595.3 48.9 %collective-permute-start.7 = (bf16[512,768]{1,0:T(8,128)(2,1)}, bf16[512,768]{1,0:T(8,128)(2,1)S(1)}, u32[]{:S(2)}, u32[]{:S(2)}) collective-permute-start(bf16[512,768]{1,0:T(8,128)(2,1)} %add_convert_fusion), channel_id=1, source_target_pairs={{0,0},{4,1},{8,2},{12,3},{3,4},{7,5},{11,6},{15,7},{1,8},{5,9},{9,... | collective-permute-start | bytes 2359304 | tf_op jit(solution)/shard_map/ppermute | solution.py:1047
  605.6 39.7 %copy-start.16 = (f32[96,576]{1,0:T(8,128)S(1)}, f32[96,576]{1,0:T(8,128)}, u32[]{:S(2)}) copy-start(f32[96,576]{1,0:T(8,128)} %sum_line.2) | copy-start | bytes 663556
Sparse Core Ops, SparseCore 0:
  81.7 69.8 all-gather.3
  154.1 53.1 all-gather.5
  209.2 68.8 all-gather.7
  319.0 99.9 reduce-scatter.4
  422.4 44.4 reduce-scatter.6
  470.3 82.3 reduce-scatter.8
  556.1 47.9 reduce-scatter.10

commit v8 on v7

--- a/solution.py
+++ b/solution.py
@@ -342,7 +342,7 @@
     )(*arrays, *owns)
 
 
-REDUCE_PIECES = 4
+REDUCE_PIECES = 8
 
 
 def reduce_kernel(
@@ -917,7 +917,7 @@
     for layer in range(1, LAYERS):
         groups += [[attn_shard(w_qkv[layer], w_out[layer])], [w_up[layer], w_down[layer].T]]
     inputs, numbers, *later = quad_gather(
-        [own_tokens, own_numbers], [4, 1], CALL_GATHER_FIRST, tensor, groups
+        [own_tokens, own_numbers], [8, 1], CALL_GATHER_FIRST, tensor, groups
     )
     numbers = numbers.reshape(QUAD, 16, width)[:, :2].astype(jnp.int32)
     numbers = numbers[:, 0] * BLK + numbers[:, 1]
@@ -948,7 +948,7 @@
         w_shrink_t = ffn_w[:, hidden * tensor :]
         own_inputs = stream.astype(BF)
         if layer > 0:
-            (inputs,) = quad_gather([own_inputs], [4], CALL_GATHER)
+            (inputs,) = quad_gather([own_inputs], [8], CALL_GATHER)
         query = (dot(own_inputs, w_query).astype(BF).astype(F32) * score_scale).astype(BF)
         keyval = dot(inputs, w_keyval).astype(BF)
         if layer < LAYERS - 1:

time: 667 us -> 667 us (level)
  Pallas kernels: 462 us -> 453 us
  waiting for transfers between devices: 15.1 us -> 23.8 us
    pallas_call x2, Pallas kernels: 56.6 us -> 47.4 us  [attend_forward(): pl.pallas_call(forward_kernel, grid_spec=pltpu.PrefetchScalarGridSpec(num...]
    pallas_call x2, Pallas kernels: 106 us -> 96.5 us  [attend_backward(): pl.pallas_call(backward_kernel, grid_spec=pltpu.PrefetchScalarGridSpec(nu...]
  transfers between devices with their start and end apart: 15 -> 15, of which waited for: 3 -> 4; matrix products, arithmetic and copies ran while one was open for 17% -> 17% of each run, Pallas kernels for 68% -> 67%
where the time goes in v8:
time: 667 us; the launch traced here: 657 us
  Pallas kernels  453 us (68%)
  matrix products  83.9 us (13%)
  local copies, waits for them, and re-layouts  28.6 us (4%)
  other arithmetic  27.7 us (4%)
  starting transfers between devices  24.5 us (4%)
  waiting for transfers between devices  23.8 us (4%)
  between operations  15.4 us (2%)
    pallas_call x2, Pallas kernels, attend_backward(): pl.pallas_call(backward_kernel, grid_spec=pltpu.PrefetchScalarGridSpec(nu...  96.5 us
    pallas_call x2, Pallas kernels, quad_gather(): pl.pallas_call(functools.partial(gather_kernel, pieces, parts, tuple((len...  65.7 us
    pallas_call x1, Pallas kernels, gather_rows(): pl.pallas_call(functools.partial(rows_kernel, parts, tuple((len(g) for g...  65.6 us
    dot_general x10, matrix products, dot(): return jnp.dot(left, right, preferred_element_type=F32)  61.1 us
    pallas_call x2, Pallas kernels, sum_line(): pl.pallas_call(functools.partial(parts_kernel, sizes, parts), out_shape=j...  53.7 us
    pallas_call x2, Pallas kernels, attend_forward(): pl.pallas_call(forward_kernel, grid_spec=pltpu.PrefetchScalarGridSpec(num...  47.4 us
    pallas_call x1, Pallas kernels, quad_reduce_and_lines(): pl.pallas_call(functools.partial(both_kernel, tuple(sizes), planes), out_...  37.9 us
    pallas_call x1, Pallas kernels, quad_reduce(): pl.pallas_call(reduce_kernel, out_shape=jax.ShapeDtypeStruct((rows, width...  35.3 us
  transfers between devices with their start and end apart: 15, of which 4 were waited for; matrix products, arithmetic and copies ran while one was open for 17% of the time, Pallas kernels for 67%

profile of v8, /device:TPU:0, one launch (start us, length us, event | category | flops | bytes accessed | tf_op | source)
XLA Modules:
  0.0 657.4 jit_solution(14994369775154222169)
XLA Ops:
  9.7 1.8 collective-permute-start
  12.4 1.0 fusion.92
  16.0 65.6 %gather_rows.1 = (bf16[768,3072]{1,0:T(8,128)(2,1)}, bf16[96,6144]{1,0:T(8,128)(2,1)}) custom-call(bf16[96,768]{1,0:T(8,128)(2,1)} %pad_maximum_fusion.6.own_ref, bf16[96,768]{1,0:T(8,128)(2,1)} %get-tuple-element.196.refs_0_, bf16[96,768]{1,0:T(8,128)(2,1)} %get-tuple-element.194.refs_1_), custom_call_target="tpu_custom_call" | custom-call | flops 1000000 | bytes 1000000 | tf_op jit(solution)/shard_map/gather_rows/pallas_call | solution.py:593
  82.8 41.3 %quad_gather.2 = (bf16[2048,768]{1,0:T(8,128)(2,1)}, bf16[64,768]{1,0:T(8,128)(2,1)}, bf16[96,3072]{1,0:T(8,128)(2,1)}, bf16[96,6144]{1,0:T(8,128)(2,1)}) custom-call(bf16[512,768]{1,0:T(8,128)(2,1)} %copy-done.4, bf16[16,768]{1,0:T(8,128)(2,1)} %copy-done.22, bf16[96,768]{1,0:T(8,128)(2,1)} %pad_maximum_fusion.7.refs_2_, ...), custom_call_target="tpu_custom_call" | custom-call | flops 1000000 | bytes 1000000 | tf_op jit(solution)/shard_map/quad_gather/pallas_call | solution.py:332
  124.2 2.1 regroup.3
  131.8 1.0 reshape.670.bias_ref
  132.9 5.5 regroup.2.wk_ref.wv_ref
  139.5 3.1 multiply_convert_fusion.3.q_ref
  142.6 8.6 %convolution_convert_fusion.1.k_ref.v_ref = bf16[2048,1536]{1,0:T(8,128)(2,1)} fusion(bf16[2048,768]{1,0:T(8,128)(2,1)S(1)} %copy-done.14, bf16[768,3072]{1,0:T(8,128)(2,1)} %regroup.2.wk_ref.wv_ref), kind=kOutput, calls=%fused_computation.5 | convolution fusion | flops 4834983936 | bytes 11796480 | tf_op jit(solution)/shard_map/dot_general | solution.py:41
  151.1 23.7 %attend_forward.2 = (bf16[512,768]{1,0:T(8,128)(2,1)}, f32[8,1,768]{2,1,0:T(1,128)}) custom-call(s32[8,16]{1,0:T(8,128)} %select_reduce_fusion.keys_at, s32[8]{0:T(128)} %get-tuple-element.214.steps_of, bf16[512,768]{1,0:T(8,128)(2,1)} %multiply_convert_fusion.3.q_ref, bf16[2048,1536]{1,0:T(8,128)(2,1)} %convolution_convert_fusion.1.k_ref.v_ref, ...), custom_call_target="tpu_custom_call" | custom-call | flops 1000000 | bytes 1000000 | tf_op jit(solution)/shard_map/attend_forward/pallas_call | solution.py:695
  174.9 7.6 %collective-permute-start.2 = (bf16[512,768]{1,0:T(8,128)(2,1)}, bf16[512,768]{1,0:T(8,128)(2,1)}, u32[]{:S(2)}, u32[]{:S(2)}) collective-permute-start(bf16[512,768]{1,0:T(8,128)(2,1)} %param.22), channel_id=1, source_target_pairs={{0,0},{1,4},{2,8},{3,12},{4,3},{5,7},{6,11},{7,15},{8,1},{9,5},{10... | collective-permute-start | bytes 2359304 | tf_op jit(solution)/shard_map/ppermute | solution.py:960
  182.5 2.5 fusion.97
  185.7 9.1 %multiply_convert_fusion.1 = (bf16[512,3072]{1,0:T(8,128)(2,1)S(1)}, f32[512,3072]{1,0:T(8,128)}) fusion(bf16[512,768]{1,0:T(8,128)(2,1)S(1)} %fusion.50.ffn_ref, bf16[768,6144]{1,0:T(8,128)(2,1)} %all-gather.4.cloned.1.call-done), kind=kOutput, calls=%fused_computation.21 | convolution fusion | flops 2430074880 | bytes 14942208 | tf_op jit(solution)/shard_map/dot_general | solution.py:41
  194.7 2.8 fusion.98
  197.8 1.2 fusion.51.refs_0_.own_ref
  199.1 24.4 %quad_gather.3.in_ref = bf16[2048,768]{1,0:T(8,128)(2,1)} custom-call(bf16[512,768]{1,0:T(8,128)(2,1)} %fusion.51.refs_0_.own_ref), custom_call_target="tpu_custom_call" | custom-call | flops 1000000 | bytes 1000000 | tf_op jit(solution)/shard_map/quad_gather/pallas_call | solution.py:332
  223.5 3.3 multiply_convert_fusion.2.q_ref
  226.9 9.0 %convolution_convert_fusion.k_ref.v_ref = bf16[2048,1536]{1,0:T(8,128)(2,1)} fusion(bf16[2048,768]{1,0:T(8,128)(2,1)S(1)} %copy-done.3, bf16[768,3072]{1,0:T(8,128)(2,1)} %all-gather.6.cloned.1.call-done.wk_ref.wv_ref), kind=kOutput, calls=%fused_computation.4 | convolution fusion | flops 4834983936 | bytes 11796480 | tf_op jit(solution)/shard_map/dot_general | solution.py:41
  235.9 23.7 %attend_forward.3 = (bf16[512,768]{1,0:T(8,128)(2,1)}, f32[8,1,768]{2,1,0:T(1,128)}) custom-call(s32[8,16]{1,0:T(8,128)} %select_reduce_fusion.keys_at, s32[8]{0:T(128)} %get-tuple-element.214.steps_of, bf16[512,768]{1,0:T(8,128)(2,1)} %multiply_convert_fusion.2.q_ref, bf16[2048,1536]{1,0:T(8,128)(2,1)} %convolution_convert_fusion.k_ref.v_ref, ...), custom_call_target="tpu_custom_call" | custom-call | flops 1000000 | bytes 1000000 | tf_op jit(solution)/shard_map/attend_forward/pallas_call | solution.py:695
  259.6 2.4 fusion.99
  263.2 1.2 fusion.52.ffn_ref
  264.4 13.3 %all-gather.8.cloned.1.call-done = bf16[768,6144]{1,0:T(8,128)(2,1)} async-done(((bf16[96,6144]{1,0:T(8,128)(2,1)}), bf16[768,6144]{1,0:T(8,128)(2,1)}) %all-gather.8.cloned.1.call-update) | async-done | bytes 9437200 | tf_op jit(solution)/shard_map/all_gather | solution.py:896
  277.7 5.8 multiply_convert_fusion
  283.6 2.8 fusion.100
  286.7 1.8 fusion.39
  288.5 2.8 fusion.88
  292.3 6.5 fusion.13.pre_ref
  298.9 3.2 multiply_reduce_fusion.1
  302.8 1.1 copy-done
  303.9 1.0 add_convert_fusion.4.one_ref
  304.9 13.6 %weight_grads.2 = bf16[768,6912]{1,0:T(8,128)(2,1)} custom-call(bf16[512,768]{1,0:T(8,128)(2,1)} %fusion.52.ffn_ref, bf16[512,768]{1,0:T(8,128)(2,1)} %copy-done.8, bf16[512,768]{1,0:T(8,128)(2,1)} %add_convert_fusion.4.one_ref, bf16[512,3072]{1,0:T(8,128)(2,1)} %copy-done.12, bf16[512,3072]{1,0:T(8,128)(2,1)} %copy-done.11, ...), custom_call_target="tpu_custom_call" | custom-call | flops 1000000 | bytes 1000000 | tf_op jit(solution)/shard_map/weight_grads/pallas_call | solution.py:786
  318.6 7.5 %collective-permute-start.3 = (bf16[512,768]{1,0:T(8,128)(2,1)}, bf16[512,768]{1,0:T(8,128)(2,1)}, u32[]{:S(2)}, u32[]{:S(2)}) collective-permute-start(bf16[512,768]{1,0:T(8,128)(2,1)} %get-tuple-element.180), channel_id=1, source_target_pairs={{0,0},{4,1},{8,2},{12,3},{3,4},{7,5},{11,6},{15,7},{1,8},{5,9},{9,... | collective-permute-start | bytes 2359304 | tf_op jit(solution)/shard_map/ppermute | solution.py:971
  326.1 3.8 convolution_convert_fusion.3.d_ref
  329.8 48.5 %attend_backward.2 = (bf16[512,768]{1,0:T(8,128)(2,1)}, bf16[2048,768]{1,0:T(8,128)(2,1)}, bf16[768,2304]{1,0:T(8,128)(2,1)}) custom-call(s32[8,16]{1,0:T(8,128)} %select_reduce_fusion.keys_at, s32[8]{0:T(128)} %get-tuple-element.214.steps_of, bf16[512,768]{1,0:T(8,128)(2,1)} %multiply_convert_fusion.2.q_ref, ...), custom_call_target="tpu_custom_call" | custom-call | flops 1000000 | bytes 1000000 | tf_op jit(solution)/shard_map/attend_backward/pallas_call | solution.py:727
  378.4 35.3 %quad_reduce.1 = f32[512,768]{1,0:T(8,128)} custom-call(bf16[2048,768]{1,0:T(8,128)(2,1)} %get-tuple-element.82.parts_ref), custom_call_target="tpu_custom_call" | custom-call | flops 1000000 | bytes 1000000 | tf_op jit(solution)/shard_map/quad_reduce/pallas_call | solution.py:416
  413.6 3.0 reduce-scatter.5.cloned.1.call-done
  416.7 3.7 multiply_reduce_fusion
  422.1 9.0 %fusion.6.pre_ref = bf16[512,3072]{1,0:T(8,128)(2,1)S(1)} fusion(f32[512,3072]{1,0:T(8,128)} %get-tuple-element.218, bf16[512,768]{1,0:T(8,128)(2,1)S(1)} %add_convert_fusion.3.two_ref, bf16[768,6144]{1,0:T(8,128)(2,1)} %all-gather.4.cloned.1.call-done), kind=kOutput, calls=%fused_computation.12 | convolution fusion | flops 2447376384 | bytes 14942208 | tf_op jit(solution)/shard_map/dot_general | solution.py:41
  431.2 3.2 multiply_reduce_fusion.2
  435.0 1.0 add_convert_fusion.2.one_ref
  436.0 13.7 %weight_grads.3 = bf16[768,6912]{1,0:T(8,128)(2,1)} custom-call(bf16[512,768]{1,0:T(8,128)(2,1)} %copy-done.6, bf16[512,768]{1,0:T(8,128)(2,1)} %copy-done.9, bf16[512,768]{1,0:T(8,128)(2,1)} %add_convert_fusion.2.one_ref, bf16[512,3072]{1,0:T(8,128)(2,1)} %copy-done.13, bf16[512,3072]{1,0:T(8,128)(2,1)} %copy-done.10, ...), custom_call_target="tpu_custom_call" | custom-call | flops 1000000 | bytes 1000000 | tf_op jit(solution)/shard_map/weight_grads/pallas_call | solution.py:786
  450.9 3.0 convolution_convert_fusion.2.d_ref
  453.9 16.5 %sum_everywhere.1 = f32[8,768]{1,0:T(8,128)} custom-call(f32[8,768]{1,0:T(8,128)} %stack.36.x_ref), custom_call_target="tpu_custom_call" | custom-call | flops 1000000 | bytes 1000000 | tf_op jit(solution)/shard_map/sum_everywhere/pallas_call | solution.py:493
  470.4 1.4 fusion.89
  476.5 3.0 collective-permute-start.4
  481.8 0.9 collective-permute-start.6
  482.7 48.0 %attend_backward.3 = (bf16[512,768]{1,0:T(8,128)(2,1)}, bf16[2048,768]{1,0:T(8,128)(2,1)}, bf16[768,2304]{1,0:T(8,128)(2,1)}) custom-call(s32[8,16]{1,0:T(8,128)} %select_reduce_fusion.keys_at, s32[8]{0:T(128)} %get-tuple-element.214.steps_of, bf16[512,768]{1,0:T(8,128)(2,1)} %multiply_convert_fusion.3.q_ref, ...), custom_call_target="tpu_custom_call" | custom-call | flops 1000000 | bytes 1000000 | tf_op jit(solution)/shard_map/attend_backward/pallas_call | solution.py:727
  531.2 1.3 reshape.680.x_ref
  532.5 16.6 %sum_line.2 = f32[96,576]{1,0:T(8,128)} custom-call(bf16[96,2304]{1,0:T(8,128)(2,1)} %reshape.680.x_ref), custom_call_target="tpu_custom_call" | custom-call | flops 1000000 | bytes 1000000 | tf_op jit(solution)/shard_map/sum_line/pallas_call | solution.py:677
  549.1 3.8 reduce-scatter.9.cloned.1.call-done.refs_0_
  553.0 2.3 fusion.62
  555.3 37.9 %quad_reduce_and_lines.1 = (f32[512,768]{1,0:T(8,128)}, f32[96,1728]{1,0:T(8,128)}) custom-call(bf16[2048,768]{1,0:T(8,128)(2,1)} %get-tuple-element.102.parts_ref, bf16[96,6912]{1,0:T(8,128)(2,1)} %reduce-scatter.9.cloned.1.call-done.refs_0_), custom_call_target="tpu_custom_call" | custom-call | flops 1000000 | bytes 1000000 | tf_op jit(solution)/shard_map/quad_reduce_and_lines/pallas_call | solution.py:446
  593.2 2.6 add_convert_fusion
  595.8 1.9 collective-permute-start.7
  598.3 1.3 add_bitcast_fusion
  600.5 1.1 fusion.65
  601.6 2.8 reduce-scatter.11.cloned.1.call-done
  604.4 1.5 reshape.684
  606.2 1.3 reshape.685.x_ref
  607.5 37.1 %sum_line.3 = f32[96,576]{1,0:T(8,128)} custom-call(bf16[96,2304]{1,0:T(8,128)(2,1)} %reshape.685.x_ref), custom_call_target="tpu_custom_call" | custom-call | flops 1000000 | bytes 1000000 | tf_op jit(solution)/shard_map/sum_line/pallas_call | solution.py:677
  644.6 1.1 copy.88
  646.0 1.0 copy.91
  647.0 1.3 convert_element_type.144
  648.3 2.1 copy.136
  (211 shorter events, 30.8 us)
Async XLA Ops:
  7.2 6.6 %copy-start.18 = (bf16[2,96,768]{2,1,0:T(8,128)(2,1)S(1)}, bf16[2,96,768]{2,1,0:T(8,128)(2,1)}, u32[]{:S(2)}) copy-start(bf16[2,96,768]{2,1,0:T(8,128)(2,1)} %param.16) | copy-start | bytes 884740
  7.2 7.3 %copy-start.19 = (bf16[2,768,96]{1,2,0:T(8,128)(2,1)S(1)}, bf16[2,768,96]{1,2,0:T(8,128)(2,1)}, u32[]{:S(2)}) copy-start(bf16[2,768,96]{1,2,0:T(8,128)(2,1)} %param.17) | copy-start | bytes 884740
  7.2 178.4 %all-gather.4.cloned.1.call-start = ((), (), s32[]{:S(2)}) async-start(), calls=%async_computation.4 | async-start | bytes 10616832 | tf_op jit(solution)/shard_map/all_gather | solution.py:896
  9.0 72.5 %collective-permute-start.1 = (bf16[16,768]{1,0:T(8,128)(2,1)S(1)}, bf16[16,768]{1,0:T(8,128)(2,1)S(1)}, u32[]{:S(2)}, u32[]{:S(2)}) collective-permute-start(bf16[16,768]{1,0:T(8,128)(2,1)S(1)} %fusion.72), channel_id=1, source_target_pairs={{0,0},{1,4},{2,8},{3,12},{4,3},{5,7},{6,11},{7,15},{8,1},{9,5},{10... | collective-permute-start | bytes 73736 | tf_op jit(solution)/shard_map/ppermute | solution.py:902
  9.7 71.9 %collective-permute-start = (bf16[512,768]{1,0:T(8,128)(2,1)}, bf16[512,768]{1,0:T(8,128)(2,1)S(1)}, u32[]{:S(2)}, u32[]{:S(2)}) collective-permute-start(bf16[512,768]{1,0:T(8,128)(2,1)} %param.13), channel_id=1, source_target_pairs={{0,0},{1,4},{2,8},{3,12},{4,3},{5,7},{6,11},{7,15},{8,1},{9,5},{10... | collective-permute-start | bytes 2359304 | tf_op jit(solution)/shard_map/ppermute | solution.py:903
  81.6 1.3 copy-start.22
  81.6 1.3 copy-start.4
  81.6 141.9 %all-gather.6.cloned.1.call-start = ((), (), s32[]{:S(2)}) async-start(), calls=%async_computation.5 | async-start | bytes 5308416 | tf_op jit(solution)/shard_map/all_gather | solution.py:896
  124.1 3.0 copy-start.23
  124.1 3.0 copy-start.24
  124.2 3.0 copy-start.25
  124.2 3.0 copy-start.26
  126.3 151.5 %all-gather.8.cloned.1.call-start = ((), (), s32[]{:S(2)}) async-start(), calls=%async_computation.6 | async-start | bytes 10616832 | tf_op jit(solution)/shard_map/all_gather | solution.py:896
  127.0 289.6 %reduce-scatter.5.cloned.1.call-start = ((), (), s32[]{:S(2)}) async-start(), calls=%async_computation.7 | async-start | bytes 11943936 | tf_op jit(solution)/shard_map/reduce_scatter | solution.py:986
  132.9 6.6 %copy-start.5 = (bf16[512,768]{1,0:T(8,128)(2,1)S(1)}, bf16[512,768]{1,0:T(8,128)(2,1)}, u32[]{:S(2)}) copy-start(bf16[512,768]{1,0:T(8,128)(2,1)} %copy-done.4) | copy-start | bytes 2359300
  139.5 3.1 copy-start.14
  174.9 111.9 %collective-permute-start.2 = (bf16[512,768]{1,0:T(8,128)(2,1)}, bf16[512,768]{1,0:T(8,128)(2,1)}, u32[]{:S(2)}, u32[]{:S(2)}) collective-permute-start(bf16[512,768]{1,0:T(8,128)(2,1)} %param.22), channel_id=1, source_target_pairs={{0,0},{1,4},{2,8},{3,12},{4,3},{5,7},{6,11},{7,15},{8,1},{9,5},{10... | collective-permute-start | bytes 2359304 | tf_op jit(solution)/shard_map/ppermute | solution.py:960
  185.6 9.1 %copy-start.6 = (bf16[512,768]{1,0:T(8,128)(2,1)}, bf16[512,768]{1,0:T(8,128)(2,1)S(1)}, u32[]{:S(2)}) copy-start(bf16[512,768]{1,0:T(8,128)(2,1)S(1)} %fusion.50.ffn_ref) | copy-start | bytes 2359300
  185.7 9.1 %copy-start.27 = (bf16[768,6144]{1,0:T(8,128)(2,1)S(1)}, bf16[768,6144]{1,0:T(8,128)(2,1)}, u32[]{:S(2)}) copy-start(bf16[768,6144]{1,0:T(8,128)(2,1)} %all-gather.4.cloned.1.call-done) | copy-start | bytes 28311556
  194.7 2.8 copy-start.10
  223.5 3.4 copy-start.3
  262.0 1.1 copy-start.1
  277.7 5.8 copy-start.2
  277.7 5.8 copy-start.28
  283.5 2.8 copy-start.11
  291.5 0.9 copy-start.8
  298.9 3.2 copy-start.12
  302.7 1.1 copy-start
  318.5 151.9 %reduce-scatter.7.cloned.1.call-start = ((), (), s32[]{:S(2)}) async-start(), calls=%async_computation.8 | async-start | bytes 3981312 | tf_op jit(solution)/shard_map/reduce_scatter | solution.py:986
  318.6 59.8 %collective-permute-start.3 = (bf16[512,768]{1,0:T(8,128)(2,1)}, bf16[512,768]{1,0:T(8,128)(2,1)}, u32[]{:S(2)}, u32[]{:S(2)}) collective-permute-start(bf16[512,768]{1,0:T(8,128)(2,1)} %get-tuple-element.180), channel_id=1, source_target_pairs={{0,0},{4,1},{8,2},{12,3},{3,4},{7,5},{11,6},{15,7},{1,8},{5,9},{9,... | collective-permute-start | bytes 2359304 | tf_op jit(solution)/shard_map/ppermute | solution.py:971
  416.6 136.3 %reduce-scatter.9.cloned.1.call-start = ((), (), s32[]{:S(2)}) async-start(), calls=%async_computation.9 | async-start | bytes 11943936 | tf_op jit(solution)/shard_map/reduce_scatter | solution.py:986
  420.4 10.7 %slice-start.1 = ((s8[9437184]{0:T(1024)(128)(4,1)}), s8[4194304]{0:T(1024)(128)(4,1)S(1)}, s32[]{:S(2)}) async-start(s8[9437184]{0:T(1024)(128)(4,1)} %bitcast.147), calls=%async_computation.12 | async-start | bytes 8388608
  421.2 0.9 copy-start.9
  422.1 9.0 %slice-start.2 = ((s8[9437184]{0:T(1024)(128)(4,1)}), s8[4194304]{0:T(1024)(128)(4,1)S(1)}, s32[]{:S(2)}) async-start(s8[9437184]{0:T(1024)(128)(4,1)} %bitcast.147), calls=%async_computation.13 | async-start | bytes 8388608
  422.1 9.0 %slice-start.3 = ((s8[9437184]{0:T(1024)(128)(4,1)}), s8[1048576]{0:T(1024)(128)(4,1)S(1)}, s32[]{:S(2)}) async-start(s8[9437184]{0:T(1024)(128)(4,1)} %bitcast.147), calls=%async_computation.14 | async-start | bytes 2097152
  431.2 3.2 copy-start.13
  449.7 1.1 copy-start.7
  449.8 154.6 %reduce-scatter.11.cloned.1.call-start = ((), (), s32[]{:S(2)}) async-start(), calls=%async_computation.10 | async-start | bytes 3981312 | tf_op jit(solution)/shard_map/reduce_scatter | solution.py:986
  470.4 1.8 slice-start
  474.7 1.0 copy-start.20
  476.5 72.6 %collective-permute-start.4 = (bf16[96,1728]{1,0:T(8,128)(2,1)}, bf16[96,1728]{1,0:T(8,128)(2,1)}, u32[]{:S(2)}, u32[]{:S(2)}) collective-permute-start(bf16[96,1728]{1,0:T(8,128)(2,1)} %pad_maximum_fusion.3), channel_id=1, source_target_pairs={{0,3},{1,0},{2,1},{3,2},{4,7},{5,4},{6,5},{7,6},{8,11},{9,8},{10,9... | collective-permute-start | bytes 995336 | tf_op jit(solution)/shard_map/ppermute | solution.py:882
  480.2 68.9 %collective-permute-start.5 = (bf16[96,1728]{1,0:T(8,128)(2,1)}, bf16[96,1728]{1,0:T(8,128)(2,1)}, u32[]{:S(2)}, u32[]{:S(2)}) collective-permute-start(bf16[96,1728]{1,0:T(8,128)(2,1)} %pad_maximum_fusion.4), channel_id=1, source_target_pairs={{0,2},{1,3},{2,0},{3,1},{4,6},{5,7},{6,4},{7,5},{8,10},{9,11},{10,... | collective-permute-start | bytes 995336 | tf_op jit(solution)/shard_map/ppermute | solution.py:882
  481.8 67.4 %collective-permute-start.6 = (bf16[96,1728]{1,0:T(8,128)(2,1)}, bf16[96,1728]{1,0:T(8,128)(2,1)}, u32[]{:S(2)}, u32[]{:S(2)}) collective-permute-start(bf16[96,1728]{1,0:T(8,128)(2,1)} %pad_maximum_fusion.5), channel_id=1, source_target_pairs={{0,1},{1,2},{2,3},{3,0},{4,5},{5,6},{6,7},{7,4},{8,9},{9,10},{10,1... | collective-permute-start | bytes 995336 | tf_op jit(solution)/shard_map/ppermute | solution.py:882
  482.7 48.0 %copy-start.17 = (bf16[96,2304]{1,0:T(8,128)(2,1)S(1)}, bf16[96,2304]{1,0:T(8,128)(2,1)}, u32[]{:S(2)}) copy-start(bf16[96,2304]{1,0:T(8,128)(2,1)} %reduce-scatter.7.cloned.1.call-done) | copy-start | bytes 1327108
  593.2 4.5 copy-start.21
  595.8 3.9 copy-start.15
  595.8 48.9 %collective-permute-start.7 = (bf16[512,768]{1,0:T(8,128)(2,1)}, bf16[512,768]{1,0:T(8,128)(2,1)S(1)}, u32[]{:S(2)}, u32[]{:S(2)}) collective-permute-start(bf16[512,768]{1,0:T(8,128)(2,1)} %add_convert_fusion), channel_id=1, source_target_pairs={{0,0},{4,1},{8,2},{12,3},{3,4},{7,5},{11,6},{15,7},{1,8},{5,9},{9,... | collective-permute-start | bytes 2359304 | tf_op jit(solution)/shard_map/ppermute | solution.py:1047
  606.0 39.8 %copy-start.16 = (f32[96,576]{1,0:T(8,128)S(1)}, f32[96,576]{1,0:T(8,128)}, u32[]{:S(2)}) copy-start(f32[96,576]{1,0:T(8,128)} %sum_line.2) | copy-start | bytes 663556
Sparse Core Ops, SparseCore 0:
  81.7 69.8 all-gather.3
  154.1 55.2 all-gather.5
  211.4 66.3 all-gather.7
  318.7 97.9 reduce-scatter.4
  419.9 47.2 reduce-scatter.6
  470.6 82.3 reduce-scatter.8
  556.4 47.9 reduce-scatter.10
